TPU v7x, 32 devices: a whole 2x2x4 slice. The times are simulated.
32 devices in a mesh: dp: 8 (over z, y), seq: 4 (over x, core).
Axes of the slice: x: 2, y: 2, z: 4, core: 2. Of those that a mesh axis runs over, the one named last changes fastest.
Arguments:
- layer_input: bfloat16 [8, 1024, 2048], P('dp', 'seq'), may hold values from -6 to 6
- pic_starts: int32 [8, 2], P('dp'), may hold values from 0 to 768, as said below
- skip_mask: int32 [8, 1024], P('dp', 'seq'), may hold values 0 or 1
- gain_attn: float32 [2048], P(('dp', 'seq')), may hold values from 0.1 to 1.9
- w_query: bfloat16 [2048, 2048], P(('dp', 'seq')), may hold values from -0.125 to 0.125
- w_key: bfloat16 [2048, 512], P(('dp', 'seq')), may hold values from -0.125 to 0.125
- w_value: bfloat16 [2048, 512], P(('dp', 'seq')), may hold values from -0.125 to 0.125
- w_out: bfloat16 [2048, 2048], P(None, ('dp', 'seq')), may hold values from -1 to 1
- gain_ffn: float32 [2048], P(('dp', 'seq')), may hold values from 0.1 to 1.9
- w_gate: bfloat16 [2048, 5632], P(('dp', 'seq')), may hold values from -0.125 to 0.125
- w_up: bfloat16 [2048, 5632], P(('dp', 'seq')), may hold values from -0.125 to 0.125
- w_down: bfloat16 [5632, 2048], P(None, ('dp', 'seq')), may hold values from -0.078125 to 0.078125
- cotangent: bfloat16 [8, 1024, 2048], P('dp', 'seq'), may hold values from -6 to 6
Outputs:
- out_hidden: bfloat16 [8, 1024, 2048], P('dp', 'seq')
- grad_input: float32 [8, 1024, 2048], P('dp', 'seq')
- grad_gain_attn: float32 [2048], P(('dp', 'seq'))
- grad_w_query: float32 [2048, 2048], P(('dp', 'seq'))
- grad_w_key: float32 [2048, 512], P(('dp', 'seq'))
- grad_w_value: float32 [2048, 512], P(('dp', 'seq'))
- grad_w_out: float32 [2048, 2048], P(None, ('dp', 'seq'))
- grad_gain_ffn: float32 [2048], P(('dp', 'seq'))
- grad_w_gate: float32 [2048, 5632], P(('dp', 'seq'))
- grad_w_up: float32 [2048, 5632], P(('dp', 'seq'))
- grad_w_down: float32 [5632, 2048], P(None, ('dp', 'seq'))
Inputs may be any that keep to these rules, and one draw needn't show every extreme that they name: `pic_starts`: piece j of a sequence starts between j * 512 and (j + 1) * 512 - 256, so pieces of one sequence never intersect.
All inputs are finite; a program needn't handle non-finite values. No bound on the sum of `skip_mask` on one device may be relied on, other than what follows from the above.
Results may differ from a plain program's by a relative error of at most 0.039.
Values may be sent and summed in bfloat16 or wider, within the bound.
A program may use at most 640 MiB of HBM per device.

v0:
```python
import jax
import jax.numpy as jnp
from jax import lax
from jax.sharding import PartitionSpec as P

H = 16
KV = 4
DH = 128
FF = 5632
PIC = 256
NPIC = 2


EPS = 1e-05


def rotary_tables(positions, head_dim):
    half_dim = head_dim // 2
    inverse = 10000.0 ** (-(jnp.arange(half_dim, dtype=jnp.float32) * 2.0 / head_dim))
    angles = positions.astype(jnp.float32)[:, None] * inverse[None, :]
    return (jnp.cos(angles), jnp.sin(angles))


def table_view(values, table):
    half_dim = values.shape[-1] // 2
    return table.reshape((table.shape[0],) + (1,) * (values.ndim - 3) + (half_dim,))


def rotate(values, cos_table, sin_table):
    half_dim = values.shape[-1] // 2
    cos_part = table_view(values, cos_table)
    sin_part = table_view(values, sin_table)
    first_half = values[..., :half_dim]
    second = values[..., half_dim:]
    return jnp.concatenate(
        [first_half * cos_part - second * sin_part, second * cos_part + first_half * sin_part],
        axis=-1,
    )


def rotate_back(values, cos_table, sin_table):
    half_dim = values.shape[-1] // 2
    cos_part = table_view(values, cos_table)
    sin_part = table_view(values, sin_table)
    first_half = values[..., :half_dim]
    second = values[..., half_dim:]
    return jnp.concatenate(
        [first_half * cos_part + second * sin_part, second * cos_part - first_half * sin_part],
        axis=-1,
    )


def picture_ids(positions, starts):
    inside = (positions[None, None, :] >= starts[:, :, None]) & (
        positions[None, None, :] < starts[:, :, None] + PIC
    )
    labels = jnp.arange(1, NPIC + 1, dtype=jnp.int32)
    return jnp.sum(jnp.where(inside, labels[None, :, None], 0), axis=1)


def visible(query_pos, key_pos, starts):
    query_ids = picture_ids(query_pos, starts)
    key_ids = picture_ids(key_pos, starts)
    causal = key_pos[None, None, :] <= query_pos[None, :, None]
    same_piece = (query_ids[:, :, None] == key_ids[:, None, :]) & (query_ids[:, :, None] > 0)
    return causal | same_piece


def rms_scale(rows_in):
    return lax.rsqrt(jnp.mean(rows_in * rows_in, axis=-1, keepdims=True) + EPS)


def dot_plain(left, right):
    return jnp.dot(left, right, preferred_element_type=jnp.float32)


def dot_last(left, right):
    return lax.dot_general(
        left, right, (((1,), (1,)), ((), ())), preferred_element_type=jnp.float32
    )


def dot_first(left, right):
    return lax.dot_general(
        left, right, (((0,), (0,)), ((), ())), preferred_element_type=jnp.float32
    )


def per_device(
    layer_input,
    pic_starts,
    skip_mask,
    gain_attn,
    w_query,
    w_key,
    w_value,
    w_out,
    gain_ffn,
    w_gate,
    w_up,
    w_down,
    cotangent,
):
    seq_count, local_len, width = layer_input.shape
    total_len = local_len * lax.axis_size("seq")
    tok_rows = seq_count * local_len
    groups = H // KV
    scale = DH ** (-0.5)
    query_width = H * DH
    key_width = KV * DH
    tokens = layer_input.reshape(tok_rows, width).astype(jnp.float32)
    keep = (1 - skip_mask).astype(jnp.float32).reshape(tok_rows, 1)
    positions = lax.axis_index("seq") * local_len + jnp.arange(local_len, dtype=jnp.int32)
    cos_table, sin_table = rotary_tables(positions, DH)
    allowed = visible(positions, jnp.arange(total_len, dtype=jnp.int32), pic_starts)[:, None, None]
    first_gain, query_weight, key_weight, value_weight, output_weight = (
        lax.all_gather(gain_attn.astype(jnp.bfloat16), ("dp", "seq"), axis=0, tiled=True).astype(
            gain_attn.dtype
        ),
        lax.all_gather(w_query, ("dp", "seq"), axis=0, tiled=True),
        lax.all_gather(w_key, ("dp", "seq"), axis=0, tiled=True),
        lax.all_gather(w_value, ("dp", "seq"), axis=0, tiled=True),
        lax.all_gather(w_out, ("dp", "seq"), axis=1, tiled=True),
    )
    first_scale = rms_scale(tokens)
    first_normed = tokens * first_scale
    normed = (first_normed * first_gain).astype(jnp.bfloat16)
    query_pre = dot_plain(normed, query_weight).reshape(seq_count, local_len, KV, groups, DH)
    key_pre = dot_plain(normed, key_weight).reshape(seq_count, local_len, KV, DH)
    value_rows = (
        dot_plain(normed, value_weight).astype(jnp.bfloat16).reshape(seq_count, local_len, KV, DH)
    )
    queries = rotate(query_pre, cos_table, sin_table).astype(jnp.bfloat16)
    keys_here = rotate(key_pre, cos_table, sin_table).astype(jnp.bfloat16)
    keys_all, values_all = (
        lax.all_gather(keys_here, "seq", axis=1, tiled=True),
        lax.all_gather(value_rows, "seq", axis=1, tiled=True),
    )

    def raw_scores():
        scores = (
            jnp.einsum("scngd,sknd->sngck", queries, keys_all, preferred_element_type=jnp.float32)
            * scale
        )
        return jnp.where(allowed, scores, -jnp.inf)

    scores = raw_scores()
    peak = jnp.max(scores, axis=-1, keepdims=True)
    log_total = peak + jnp.log(jnp.sum(jnp.exp(scores - peak), axis=-1, keepdims=True))
    probs_low = jnp.exp(scores - log_total).astype(jnp.bfloat16)
    mixed = jnp.einsum(
        "sngck,sknd->scngd", probs_low, values_all, preferred_element_type=jnp.float32
    )
    mixed_low = mixed.astype(jnp.bfloat16).reshape(tok_rows, query_width)
    hidden = tokens + keep * dot_plain(mixed_low, output_weight)
    second_gain, gate_weight, up_weight, down_weight = (
        lax.all_gather(gain_ffn.astype(jnp.bfloat16), ("dp", "seq"), axis=0, tiled=True).astype(
            gain_ffn.dtype
        ),
        lax.all_gather(w_gate, ("dp", "seq"), axis=0, tiled=True),
        lax.all_gather(w_up, ("dp", "seq"), axis=0, tiled=True),
        lax.all_gather(w_down, ("dp", "seq"), axis=1, tiled=True),
    )
    second_scale = rms_scale(hidden)
    second_normed = hidden * second_scale
    second_low = (second_normed * second_gain).astype(jnp.bfloat16)
    gate = dot_plain(second_low, gate_weight)
    upward = dot_plain(second_low, up_weight)
    sigmoid_gate = jax.nn.sigmoid(gate)
    silu_gate = gate * sigmoid_gate
    inner_low = (silu_gate * upward).astype(jnp.bfloat16)
    result = hidden + keep * dot_plain(inner_low, down_weight)
    out_hidden = result.astype(jnp.bfloat16).reshape(seq_count, local_len, width)
    upstream = cotangent.reshape(tok_rows, width).astype(jnp.float32)
    ffn_grad = (keep * upstream).astype(jnp.bfloat16)
    second_gain, gate_weight, up_weight, down_weight = (
        lax.all_gather(gain_ffn.astype(jnp.bfloat16), ("dp", "seq"), axis=0, tiled=True).astype(
            gain_ffn.dtype
        ),
        lax.all_gather(w_gate, ("dp", "seq"), axis=0, tiled=True),
        lax.all_gather(w_up, ("dp", "seq"), axis=0, tiled=True),
        lax.all_gather(w_down, ("dp", "seq"), axis=1, tiled=True),
    )
    inner_grad = dot_last(ffn_grad, down_weight)
    slope = sigmoid_gate * (1.0 + gate * (1.0 - sigmoid_gate))
    gate_grad = (inner_grad * upward * slope).astype(jnp.bfloat16)
    up_grad = (inner_grad * silu_gate).astype(jnp.bfloat16)
    norm2_grad = dot_last(gate_grad, gate_weight) + dot_last(up_grad, up_weight)
    second_gain_term = jnp.sum(norm2_grad * second_normed, axis=0)
    second_scaled = norm2_grad * second_gain
    hidden_grad = upstream + second_scale * (
        second_scaled
        - second_normed * jnp.mean(second_scaled * second_normed, axis=-1, keepdims=True)
    )
    dp_count = lax.axis_size("dp")
    seq_size = lax.axis_size("seq")
    shard_rows = width // (dp_count * seq_size)
    group_rows = width // seq_size

    def strided(matrix, count):
        view = matrix.reshape(tok_rows, dp_count, seq_size, shard_rows)
        return jnp.transpose(view, (0, 2, 1, 3)).reshape(tok_rows, count)

    normed_cols = strided(second_low, group_rows * lax.axis_size("seq"))
    partial_sums = lax.psum_scatter(
        jnp.concatenate(
            [
                dot_first(normed_cols, gate_grad),
                dot_first(normed_cols, up_grad),
                dot_first(strided(ffn_grad, group_rows * lax.axis_size("seq")), inner_low),
            ],
            axis=1,
        ).astype(jnp.bfloat16),
        "seq",
        scatter_dimension=0,
        tiled=True,
    )
    ffn_grads = lax.psum_scatter(partial_sums, "dp", scatter_dimension=0, tiled=True).astype(
        jnp.float32
    )
    branch_grad = (keep * hidden_grad).astype(jnp.bfloat16)
    first_gain, query_weight, key_weight, value_weight, output_weight = (
        lax.all_gather(gain_attn.astype(jnp.bfloat16), ("dp", "seq"), axis=0, tiled=True).astype(
            gain_attn.dtype
        ),
        lax.all_gather(w_query, ("dp", "seq"), axis=0, tiled=True),
        lax.all_gather(w_key, ("dp", "seq"), axis=0, tiled=True),
        lax.all_gather(w_value, ("dp", "seq"), axis=0, tiled=True),
        lax.all_gather(w_out, ("dp", "seq"), axis=1, tiled=True),
    )
    mixed_grad = (
        dot_last(branch_grad, output_weight)
        .astype(jnp.bfloat16)
        .reshape(seq_count, local_len, KV, groups, DH)
    )
    probs = jnp.exp(raw_scores() - log_total)
    probs_back = probs.astype(jnp.bfloat16)
    value_grad_all = jnp.einsum(
        "sngck,scngd->sknd", probs_back, mixed_grad, preferred_element_type=jnp.float32
    )
    prob_grad = jnp.einsum(
        "scngd,sknd->sngck", mixed_grad, values_all, preferred_element_type=jnp.float32
    )
    score_grad = probs * (prob_grad - jnp.sum(probs * prob_grad, axis=-1, keepdims=True))
    score_low = score_grad.astype(jnp.bfloat16)
    query_grad = (
        jnp.einsum("sngck,sknd->scngd", score_low, keys_all, preferred_element_type=jnp.float32)
        * scale
    )
    key_grad_all = (
        jnp.einsum("sngck,scngd->sknd", score_low, queries, preferred_element_type=jnp.float32)
        * scale
    )
    key_grad, value_grad = (
        lax.psum_scatter(
            key_grad_all.astype(jnp.bfloat16), "seq", scatter_dimension=1, tiled=True
        ).astype(jnp.float32),
        lax.psum_scatter(
            value_grad_all.astype(jnp.bfloat16), "seq", scatter_dimension=1, tiled=True
        ).astype(jnp.float32),
    )
    query_low = (
        rotate_back(query_grad, cos_table, sin_table)
        .astype(jnp.bfloat16)
        .reshape(tok_rows, query_width)
    )
    key_low = (
        rotate_back(key_grad, cos_table, sin_table)
        .astype(jnp.bfloat16)
        .reshape(tok_rows, key_width)
    )
    value_low = value_grad.astype(jnp.bfloat16).reshape(tok_rows, key_width)
    norm1_grad = (
        dot_last(query_low, query_weight)
        + dot_last(key_low, key_weight)
        + dot_last(value_low, value_weight)
    )
    first_gain_term = jnp.sum(norm1_grad * first_normed, axis=0)
    first_scaled = norm1_grad * first_gain
    input_grad = hidden_grad + first_scale * (
        first_scaled - first_normed * jnp.mean(first_scaled * first_normed, axis=-1, keepdims=True)
    )
    projected = jnp.concatenate([query_low, key_low, value_low], axis=1)
    attn_term = jnp.concatenate(
        [dot_first(normed, projected), dot_first(branch_grad, mixed_low)], axis=1
    )
    attn_grads, first_gain_grad, second_gain_grad = (
        lax.psum_scatter(attn_term, ("dp", "seq"), scatter_dimension=0, tiled=True),
        lax.psum_scatter(first_gain_term, ("dp", "seq"), scatter_dimension=0, tiled=True),
        lax.psum_scatter(second_gain_term, ("dp", "seq"), scatter_dimension=0, tiled=True),
    )
    return (
        out_hidden,
        input_grad.reshape(seq_count, local_len, width),
        first_gain_grad,
        attn_grads[:, :query_width],
        attn_grads[:, query_width : query_width + key_width],
        attn_grads[:, query_width + key_width : query_width + 2 * key_width],
        attn_grads[:, query_width + 2 * key_width :].T,
        second_gain_grad,
        ffn_grads[:, :FF],
        ffn_grads[:, FF : 2 * FF],
        ffn_grads[:, 2 * FF :].T,
    )


def solution(mesh):
    placed = (
        P("dp", "seq", None),
        P("dp", None),
        P("dp", "seq"),
        P(("dp", "seq")),
        P(("dp", "seq"), None),
        P(("dp", "seq"), None),
        P(("dp", "seq"), None),
        P(None, ("dp", "seq")),
        P(("dp", "seq")),
        P(("dp", "seq"), None),
        P(("dp", "seq"), None),
        P(None, ("dp", "seq")),
        P("dp", "seq", None),
    )
    return jax.shard_map(
        per_device,
        mesh=mesh,
        in_specs=placed,
        out_specs=(
            P("dp", "seq", None),
            P("dp", "seq", None),
            P(("dp", "seq")),
            P(("dp", "seq"), None),
            P(("dp", "seq"), None),
            P(("dp", "seq"), None),
            P(None, ("dp", "seq")),
            P(("dp", "seq")),
            P(("dp", "seq"), None),
            P(("dp", "seq"), None),
            P(None, ("dp", "seq")),
        ),
        check_vma=False,
    )
```

profile of v0, /device:TPU:1, one launch (start us, length us, event | category | flops | bytes accessed | tf_op | source)
XLA Modules:
  0.0 2158.2 jit_solution(14225273788975156586)
XLA Ops:
  8.0 0.7 all-gather.10.cloned.1.call-update
  11.2 41.1 %all-reduce.6 = (bf16[2048]{0:T(1024)(128)(2,1)S(1)}, bf16[2048]{0:T(1024)(128)(2,1)S(1)}) all-reduce(bf16[2048]{0:T(1024)(128)(2,1)S(1)} %dynamic-update-slice, bf16[2048]{0:T(1024)(128)(2,1)S(1)} %dynamic-update-slice.1), channel_id=1, replica_groups=mesh['dp'=8,'seq'=4] {'dp','seq'}, use_global_device_ids=true, to_apply=%add | all-reduce | flops 4096 | bytes 16384
  52.4 1.5 fusion.28
  54.2 15.4 all-gather.14.cloned.1.call-done
  69.6 2.9 copy.72
  72.5 0.8 convolution_bitcast_fusion.1
  73.5 0.7 pad_maximum_fusion.6
  74.2 53.3 %all-gather.10.cloned.1.call-done = bf16[2048,512]{1,0:T(8,128)(2,1)} async-done(((bf16[64,512]{1,0:T(8,128)(2,1)}), bf16[2048,512]{1,0:T(8,128)(2,1)}) %all-gather.10.cloned.1.call-update) | async-done | bytes 2097168 | tf_op jit(solution)/shard_map/all_gather | solution.py:122
  127.5 2.3 convolution_convert_fusion.4
  129.9 0.8 copy.101
  133.6 1.5 copy.86
  135.4 1.0 copy.87
  137.0 69.4 %all-gather.18.cloned.1.call-done = bf16[2048,2048]{1,0:T(8,128)(2,1)} async-done(((bf16[64,2048]{1,0:T(8,128)(2,1)}), bf16[2048,2048]{1,0:T(8,128)(2,1)}) %all-gather.18.cloned.1.call-update) | async-done | bytes 8388624 | tf_op jit(solution)/shard_map/all_gather | solution.py:120
  206.4 12.4 copy.73
  218.8 5.9 convolution_bitcast_fusion
  225.0 9.2 fusion.76
  234.3 8.1 exponential_reduce_fusion
  242.6 9.0 fusion.41
  251.7 70.7 %all-gather.20.cloned.1.call-done = bf16[2048,2048]{0,1:T(8,128)(2,1)} async-done(((bf16[2048,64]{0,1:T(8,128)(2,1)}), bf16[2048,2048]{0,1:T(8,128)(2,1)}) %all-gather.20.cloned.1.call-update) | async-done | bytes 8388624 | tf_op jit(solution)/shard_map/all_gather | solution.py:123
  322.4 6.1 multiply_reduce_fusion.2
  328.5 1.3 copy-done.6
  330.7 137.1 %all-gather.22.cloned.1.call-done = bf16[2048,5632]{1,0:T(8,128)(2,1)} async-done(((bf16[64,5632]{1,0:T(8,128)(2,1)}), bf16[2048,5632]{1,0:T(8,128)(2,1)}) %all-gather.22.cloned.1.call-update) | async-done | bytes 23068688 | tf_op jit(solution)/shard_map/all_gather | solution.py:160
  467.8 13.2 fusion.77
  481.0 131.7 %all-gather.24.cloned.1.call-done = bf16[2048,5632]{1,0:T(8,128)(2,1)} async-done(((bf16[64,5632]{1,0:T(8,128)(2,1)}), bf16[2048,5632]{1,0:T(8,128)(2,1)}) %all-gather.24.cloned.1.call-update) | async-done | bytes 23068688 | tf_op jit(solution)/shard_map/all_gather | solution.py:161
  612.7 13.5 fusion.78
  626.2 131.4 %all-gather.26.cloned.1.call-done = bf16[5632,2048]{0,1:T(8,128)(2,1)} async-done(((bf16[5632,64]{0,1:T(8,128)(2,1)}), bf16[5632,2048]{0,1:T(8,128)(2,1)}) %all-gather.26.cloned.1.call-update) | async-done | bytes 23068688 | tf_op jit(solution)/shard_map/all_gather | solution.py:162
  757.7 19.7 multiply_convert_fusion
  777.4 12.7 fusion.79
  790.0 13.9 multiply_reduce_fusion
  803.9 2.4 bitcast_add_fusion
  806.4 1.4 copy-done
  807.7 5.7 convolution_convert_fusion.3
  813.5 1.3 copy.106
  814.8 16.5 fusion
  831.4 10.2 fusion.5
  841.5 7.2 fusion.44
  848.8 13.0 convolution_convert_fusion.1
  861.8 10.0 fusion.45
  871.8 12.8 convolution_convert_fusion.2
  884.6 13.0 convolution_convert_fusion
  897.6 45.9 %pad_maximum_fusion = bf16[2048,16896]{1,0:T(8,128)(2,1)} fusion(bf16[2048,5632]{1,0:T(8,128)(2,1)} %convolution_convert_fusion, bf16[2048,5632]{1,0:T(8,128)(2,1)} %convolution_convert_fusion.1, bf16[2048,5632]{1,0:T(8,128)(2,1)} %convolution_convert_fusion.2), kind=kLoop, calls=%fused_computation | loop fusion | flops 207618048 | bytes 138412032 | tf_op jit(solution)/shard_map/concatenate | solution.py:206
  943.6 1.1 copy-done.16
  944.8 5.4 multiply_bitcast_fusion
  950.5 1.1 pad_maximum_fusion.3
  951.6 1.1 copy-done.1
  953.3 13.4 fusion.73
  966.7 1.1 convert_element_type.187
  968.3 19.2 fusion.35
  987.6 36.7 %pad_maximum_fusion.1 = f32[2048,5120]{1,0:T(8,128)} fusion(f32[2048,2048]{1,0:T(8,128)} %fusion.73, f32[2048,3072]{1,0:T(8,128)} %fusion.35), kind=kLoop, calls=%fused_computation.1 | loop fusion | flops 10485760 | bytes 83886080 | tf_op jit(solution)/shard_map/concatenate | solution.py:284
  1024.6 376.4 %reduce-scatter.16.cloned.1.call-done = bf16[512,16896]{1,0:T(8,128)(2,1)} async-done(((bf16[2048,16896]{1,0:T(8,128)(2,1)}), bf16[512,16896]{1,0:T(8,128)(2,1)}) %reduce-scatter.16.cloned.1.call-update) | async-done | bytes 17301520
  1401.0 7.5 fusion.80
  1408.5 14.0 fusion.16
  1422.4 3.2 convolution_add_fusion.1
  1425.7 2.5 fusion.27
  1428.2 43.6 %all-reduce.5 = (f32[2048]{0:T(1024)S(1)}, f32[2048]{0:T(1024)S(1)}) all-reduce(f32[2048]{0:T(1024)S(1)} %get-tuple-element.13, f32[2048]{0:T(1024)S(1)} %copy-done.29), channel_id=4, replica_groups=mesh['dp'=8,'seq'=4] {'dp','seq'}, use_global_device_ids=true, to_apply=%region_12.13.clone | all-reduce | flops 4096 | bytes 32768
  1473.0 3.5 fusion.26
  1476.5 377.1 %reduce-scatter.12.cloned.1.call-done = f32[64,5120]{1,0:T(8,128)} async-done(((f32[2048,5120]{1,0:T(8,128)}), f32[64,5120]{1,0:T(8,128)}) %reduce-scatter.12.cloned.1.call-update) | async-done | bytes 1310736 | tf_op jit(solution)/shard_map/reduce_scatter | solution.py:288
  1853.6 1.7 fusion.75
  1855.3 2.3 slice_bitcast_fusion.1
  1857.6 287.7 %reduce-scatter.14.cloned.1.call-done = bf16[64,16896]{1,0:T(8,128)(2,1)} async-done(((bf16[512,16896]{1,0:T(8,128)(2,1)}), bf16[64,16896]{1,0:T(8,128)(2,1)}) %reduce-scatter.14.cloned.1.call-update) | async-done | bytes 2162704 | tf_op jit(solution)/shard_map/reduce_scatter | solution.py:218
  2145.3 1.9 convert_element_type.195
  2147.2 1.2 slice_bitcast_fusion
  2148.4 0.9 copy-done.4
  2149.3 1.9 fusion.74
  (133 shorter events, 12.0 us)
Async XLA Ops:
  7.2 62.4 %all-gather.14.cloned.1.call-start = ((), (), s32[]{:S(2)}) async-start(), calls=%async_computation.7 | async-start | bytes 2162688 | tf_op jit(solution)/shard_map/all_gather | solution.py:121
  7.9 64.6 %copy-start.2 = (bf16[1,256,2048]{2,1,0:T(8,128)(2,1)S(1)}, bf16[1,256,2048]{2,1,0:T(8,128)(2,1)}, u32[]{:S(2)}) copy-start(bf16[1,256,2048]{2,1,0:T(8,128)(2,1)} %param.13) | copy-start | bytes 3145732
  7.9 119.6 %all-gather.10.cloned.1.call-start = ((), (), s32[]{:S(2)}) async-start(), calls=%async_computation.5 | async-start | bytes 2162688 | tf_op jit(solution)/shard_map/all_gather | solution.py:122
  8.7 197.7 %all-gather.18.cloned.1.call-start = ((), (), s32[]{:S(2)}) async-start(), calls=%async_computation.9 | async-start | bytes 8650752 | tf_op jit(solution)/shard_map/all_gather | solution.py:120
  9.4 215.6 %all-gather.16.cloned.1.call-start = ((), (), s32[]{:S(2)}) async-start(), calls=%async_computation.8 | async-start | bytes 1310720 | tf_op jit(solution)/shard_map/all_gather | solution.py:136
  52.3 166.4 %copy-start.25 = (f32[2048]{0:T(1024)}, f32[2048]{0:T(1024)S(1)}, u32[]{:S(2)}) copy-start(f32[2048]{0:T(1024)S(1)} %convert_element_type.160) | copy-start | bytes 24580
  53.9 164.9 %copy-start.27 = (f32[256]{0:T(256)}, f32[256]{0:T(256)S(1)}, u32[]{:S(2)}) copy-start(f32[256]{0:T(256)S(1)} %add_rsqrt_fusion.1) | copy-start | bytes 3076
  54.2 170.4 %copy-start.18 = (f32[256,64]{0,1:T(8,128)}, f32[256,64]{0,1:T(8,128)S(1)}, u32[]{:S(2)}) copy-start(f32[256,64]{0,1:T(8,128)S(1)} %get-tuple-element.36) | copy-start | bytes 196612
  54.2 170.4 %copy-start.20 = (f32[256,64]{0,1:T(8,128)}, f32[256,64]{0,1:T(8,128)S(1)}, u32[]{:S(2)}) copy-start(f32[256,64]{0,1:T(8,128)S(1)} %get-tuple-element.37) | copy-start | bytes 196612
  74.2 168.4 %all-gather.12.cloned.1.call-start = ((), (), s32[]{:S(2)}) async-start(), calls=%async_computation.6 | async-start | bytes 1310720 | tf_op jit(solution)/shard_map/all_gather | solution.py:137
  130.7 4.4 copy-start.31
  130.8 191.7 %all-gather.20.cloned.1.call-start = ((), (), s32[]{:S(2)}) async-start(), calls=%async_computation.10 | async-start | bytes 8650752 | tf_op jit(solution)/shard_map/all_gather | solution.py:123
  131.3 336.5 %all-gather.22.cloned.1.call-start = ((), (), s32[]{:S(2)}) async-start(), calls=%async_computation.11 | async-start | bytes 23789568 | tf_op jit(solution)/shard_map/all_gather | solution.py:160
  132.1 480.6 %all-gather.24.cloned.1.call-start = ((), (), s32[]{:S(2)}) async-start(), calls=%async_computation.12 | async-start | bytes 23789568 | tf_op jit(solution)/shard_map/all_gather | solution.py:161
  132.8 624.8 %all-gather.26.cloned.1.call-start = ((), (), s32[]{:S(2)}) async-start(), calls=%async_computation.13 | async-start | bytes 23789568 | tf_op jit(solution)/shard_map/all_gather | solution.py:162
  133.6 833.1 %reduce-scatter.8.cloned.1.call-start = ((), (), s32[]{:S(2)}) async-start(), calls=%async_computation.14 | async-start | bytes 1310720 | tf_op jit(solution)/shard_map/reduce_scatter | solution.py:255
  135.1 1.3 copy-start.30
  225.0 9.3 copy-start.11
  225.0 9.2 copy-start.13
  242.4 9.3 copy-start.23
  251.7 76.8 %copy-start.8 = (bf16[4,128,4,256]{3,1,2,0:T(8,128)(2,1)}, bf16[4,128,4,256]{3,1,2,0:T(8,128)(2,1)S(1)}, u32[]{:S(2)}) copy-start(bf16[4,128,4,256]{3,1,2,0:T(8,128)(2,1)S(1)} %fusion.41) | copy-start | bytes 3145732
  328.5 1.3 copy-start.6
  481.0 276.7 %copy-start.15 = (bf16[1,256,2048]{2,1,0:T(8,128)(2,1)S(1)}, bf16[1,256,2048]{2,1,0:T(8,128)(2,1)}, u32[]{:S(2)}) copy-start(bf16[1,256,2048]{2,1,0:T(8,128)(2,1)} %param.25) | copy-start | bytes 3145732
  777.4 12.7 copy-start.7
  806.4 1.4 copy-start
  814.8 16.5 slice-start
  814.8 16.5 slice-start.1
  814.8 16.5 slice-start.2
  814.8 16.5 slice-start.3
  831.3 10.2 copy-start.12
  831.3 10.2 copy-start.14
  848.7 119.2 %reduce-scatter.10.cloned.1.call-start = ((), (), s32[]{:S(2)}) async-start(), calls=%async_computation.15 | async-start | bytes 1310720 | tf_op jit(solution)/shard_map/reduce_scatter | solution.py:258
  848.8 13.0 copy-start.5
  848.8 13.0 copy-start.24
  871.8 12.8 copy-start.10
  884.6 516.4 %reduce-scatter.16.cloned.1.call-start = ((), (), s32[]{:S(2)}) async-start(), calls=%async_computation.18 | async-start | bytes 86507520
  943.5 1.2 copy-start.16
  943.6 6.6 copy-start.19
  943.6 6.6 copy-start.21
  943.6 910.0 %reduce-scatter.12.cloned.1.call-start = ((), (), s32[]{:S(2)}) async-start(), calls=%async_computation.16 | async-start | bytes 43253760 | tf_op jit(solution)/shard_map/reduce_scatter | solution.py:288
  950.2 2.6 copy-start.1
  950.2 3.1 copy-start.9
  953.3 14.7 copy-start.26
  953.3 14.7 copy-start.28
  966.7 1.6 copy-start.3
  1024.3 1121.0 %reduce-scatter.14.cloned.1.call-start = ((), (), s32[]{:S(2)}) async-start(), calls=%async_computation.17 | async-start | bytes 19464192 | tf_op jit(solution)/shard_map/reduce_scatter | solution.py:218
  1422.4 3.2 copy-start.17
  1422.4 3.2 copy-start.22
  1425.7 2.5 copy-start.29
  2147.1 2.1 copy-start.4
Sparse Core Ops, SparseCore 0:
  10.8 58.7 all-gather.13
  72.5 55.0 all-gather.9
  130.4 75.9 all-gather.17
  208.4 15.4 all-gather.15
  225.8 16.8 all-gather.11
  245.4 77.0 all-gather.19
  325.3 142.4 all-gather.21
  470.6 142.0 all-gather.23
  615.6 142.0 all-gather.25
  848.9 22.3 reduce-scatter.7
  884.7 22.4 reduce-scatter.9
  943.7 457.2 reduce-scatter.15
  1403.3 450.3 reduce-scatter.11
  1857.4 287.8 reduce-scatter.13
where the time goes:
time: 2170 us; the launch traced here: 2160 us
  waiting for transfers between devices  1660 us (76%)
  matrix products  250 us (12%)
  other arithmetic  117 us (5%)
  blocking collectives  84.7 us (4%)
  local copies, waits for them, and re-layouts  36.1 us (2%)
    unnamed x15, waiting for transfers between devices  381 us
    reduce_scatter x1, waiting for transfers between devices, per_device(): lax.psum_scatter(attn_term, ('dp', 'seq'), scatter_dimension=0, tiled=True)  377 us
    reduce_scatter x1, waiting for transfers between devices, per_device(): lax.psum_scatter(partial_sums, 'dp', scatter_dimension=0, tiled=True)  288 us
    all_gather x1, waiting for transfers between devices, per_device(): lax.all_gather(w_gate, ('dp', 'seq'), axis=0, tiled=True)  137 us
    all_gather x1, waiting for transfers between devices, per_device(): lax.all_gather(w_up, ('dp', 'seq'), axis=0, tiled=True)  132 us
    all_gather x1, waiting for transfers between devices, per_device(): lax.all_gather(w_down, ('dp', 'seq'), axis=1, tiled=True)  131 us
    unnamed x2, blocking collectives  84.7 us
    dot_general x5, matrix products, dot_first(): lax.dot_general(left, right, (((0,), (0,)), ((), ())), preferred_element_...  71.3 us
  transfers between devices with their start and end apart: 14, of which 11 were waited for; matrix products, arithmetic and copies ran while one was open for 14% of the time, Pallas kernels for 0%

commit v1 on v0

v1 whole, which is shorter than its diff:
```python
import jax
import jax.numpy as jnp
from jax import lax
from jax.sharding import Mesh
from jax.sharding import PartitionSpec as P

H = 16
KV = 4
DH = 128
PIC = 256
NPIC = 2
EPS = 1e-05
TP = 2
BF = jnp.bfloat16
F32 = jnp.float32


def rotary_tables(positions, head_dim):
    half_dim = head_dim // 2
    inverse = 10000.0 ** (-(jnp.arange(half_dim, dtype=F32) * 2.0 / head_dim))
    angles = positions.astype(F32)[:, None] * inverse[None, :]
    return (jnp.cos(angles), jnp.sin(angles))


def rotate(values, cos_table, sin_table):
    half = values.shape[-1] // 2
    shape = (cos_table.shape[0],) + (1,) * (values.ndim - 2) + (half,)
    cos_part = cos_table.reshape(shape)
    sin_part = sin_table.reshape(shape)
    first = values[..., :half]
    second = values[..., half:]
    return jnp.concatenate(
        [first * cos_part - second * sin_part, second * cos_part + first * sin_part], axis=-1
    )


def picture_ids(positions, starts):
    inside = (positions[None, :] >= starts[:, None]) & (positions[None, :] < starts[:, None] + PIC)
    labels = jnp.arange(1, NPIC + 1, dtype=jnp.int32)
    return jnp.sum(jnp.where(inside, labels[:, None], 0), axis=0)


def visible(positions, starts):
    ids = picture_ids(positions, starts)
    causal = positions[None, :] <= positions[:, None]
    same_piece = (ids[:, None] == ids[None, :]) & (ids[:, None] > 0)
    return causal | same_piece


def rms_scale(rows):
    return lax.rsqrt(jnp.mean(rows * rows, axis=-1, keepdims=True) + EPS)


def dot(left, right, contract):
    return lax.dot_general(
        left, right, ((contract[:1], contract[1:]), ((), ())), preferred_element_type=F32
    )


def nn(left, right):
    return dot(left, right, (1, 0))


def nt(left, right):
    return dot(left, right, (1, 1))


def tn(left, right):
    return dot(left, right, (0, 0))


def columns(matrix, parts):
    rows, cols = matrix.shape
    return jnp.transpose(matrix.reshape(rows, parts, cols // parts), (1, 0, 2))


def uncolumns(blocks):
    parts, rows, cols = blocks.shape
    return jnp.transpose(blocks, (1, 0, 2)).reshape(rows, parts * cols)


def per_device(
    layer_input,
    pic_starts,
    skip_mask,
    gain_attn,
    w_query,
    w_key,
    w_value,
    w_out,
    gain_ffn,
    w_gate,
    w_up,
    w_down,
    cotangent,
):
    _, local_len, width = layer_input.shape
    seq = lax.axis_size("seq")
    plane = lax.axis_size("tp") * seq
    total_len = local_len * seq
    heads = H // seq
    kv_heads = KV // seq
    groups = H // KV
    ff = w_gate.shape[1]
    ff_part = ff // plane
    q_part = heads * DH
    k_part = kv_heads * DH
    scale = DH ** (-0.5)
    in_plane = ("tp", "seq")

    gain1 = gain_attn[:, None]
    gain2 = gain_ffn[:, None]
    wq32, wk32, wv32 = w_query.astype(F32), w_key.astype(F32), w_value.astype(F32)
    wg32, wu32 = w_gate.astype(F32), w_up.astype(F32)
    attn_pack = jnp.concatenate(
        [
            columns((wq32 * gain1).astype(BF), seq),
            columns((wk32 * gain1).astype(BF), seq),
            columns((wv32 * gain1).astype(BF), seq),
            columns(w_out.T, seq),
        ],
        axis=2,
    )
    attn_rows = lax.all_to_all(attn_pack, "seq", 0, 0, tiled=True)
    attn_rows = attn_rows.reshape(-1, attn_rows.shape[2])
    attn_weight = lax.all_gather(attn_rows, ("rep", "tp"), axis=0, tiled=True)
    qkv_weight = attn_weight[:, : q_part + 2 * k_part]
    out_weight = attn_weight[:, q_part + 2 * k_part :]

    ffn_pack = jnp.concatenate(
        [
            columns((wg32 * gain2).astype(BF), plane),
            columns((wu32 * gain2).astype(BF), plane),
            columns(w_down.T, plane),
        ],
        axis=2,
    )
    ffn_rows = lax.all_to_all(ffn_pack, in_plane, 0, 0, tiled=True)
    ffn_rows = ffn_rows.reshape(-1, ffn_rows.shape[2])
    gu_weight = lax.all_gather(ffn_rows[:, : 2 * ff_part], "rep", axis=0, tiled=True)
    down_weight = lax.all_gather(ffn_rows[:, 2 * ff_part :], "rep", axis=0, tiled=True)

    tokens = layer_input.reshape(local_len, width).astype(F32)
    keep = (1 - skip_mask).astype(F32).reshape(local_len, 1)
    upstream = cotangent.reshape(local_len, width).astype(F32)
    scale1 = rms_scale(tokens)
    norm1 = tokens * scale1
    norm1_all = lax.all_gather(norm1.astype(BF), "seq", axis=0, tiled=True)
    ffn_grad = lax.all_gather((keep * upstream).astype(BF), in_plane, axis=0, tiled=True)

    positions = jnp.arange(total_len, dtype=jnp.int32)
    cos_table, sin_table = rotary_tables(positions, DH)
    allowed = visible(positions, pic_starts[0])[None, None]

    projected = nn(norm1_all, qkv_weight)
    queries = rotate(
        projected[:, :q_part].reshape(total_len, kv_heads, groups, DH), cos_table, sin_table
    ).astype(BF)
    keys = rotate(
        projected[:, q_part : q_part + k_part].reshape(total_len, kv_heads, DH),
        cos_table,
        sin_table,
    ).astype(BF)
    values = projected[:, q_part + k_part :].reshape(total_len, kv_heads, DH).astype(BF)

    def raw_scores():
        scores = jnp.einsum("qngd,knd->ngqk", queries, keys, preferred_element_type=F32) * scale
        return jnp.where(allowed, scores, -jnp.inf)

    scores = raw_scores()
    peak = jnp.max(scores, axis=-1, keepdims=True)
    log_total = peak + jnp.log(jnp.sum(jnp.exp(scores - peak), axis=-1, keepdims=True))
    probs = jnp.exp(scores - log_total)
    probs_low = probs.astype(BF)
    mixed = jnp.einsum("ngqk,knd->qngd", probs_low, values, preferred_element_type=F32)
    mixed = mixed.astype(BF).reshape(total_len, q_part)
    branch = lax.psum_scatter(
        nt(mixed, out_weight).astype(BF), "seq", scatter_dimension=0, tiled=True
    )
    hidden = tokens + keep * branch.astype(F32)

    scale2 = rms_scale(hidden)
    norm2 = hidden * scale2
    norm2_all = lax.all_gather(norm2.astype(BF), in_plane, axis=0, tiled=True)
    inner_grad = nn(ffn_grad, down_weight)
    gate_up = nn(norm2_all, gu_weight)
    gate, upward = gate_up[:, :ff_part], gate_up[:, ff_part:]
    sigmoid_gate = jax.nn.sigmoid(gate)
    silu_gate = gate * sigmoid_gate
    inner = (silu_gate * upward).astype(BF)
    slope = sigmoid_gate * (1.0 + gate * (1.0 - sigmoid_gate))
    gate_up_grad = jnp.concatenate(
        [(inner_grad * upward * slope).astype(BF), (inner_grad * silu_gate).astype(BF)], axis=1
    )
    scaled2 = lax.psum_scatter(
        nt(gate_up_grad, gu_weight).astype(BF), in_plane, scatter_dimension=0, tiled=True
    ).astype(F32)
    ffn_out = lax.psum_scatter(
        nt(inner, down_weight).astype(BF), in_plane, scatter_dimension=0, tiled=True
    )
    out_hidden = (hidden + keep * ffn_out.astype(F32)).astype(BF)
    hidden_grad = upstream + scale2 * (
        scaled2 - norm2 * jnp.mean(scaled2 * norm2, axis=-1, keepdims=True)
    )
    ffn_partial = jnp.concatenate(
        [tn(norm2_all, gate_up_grad).astype(BF), tn(ffn_grad, inner).astype(BF)], axis=1
    )
    ffn_sums = lax.psum_scatter(ffn_partial, "rep", scatter_dimension=0, tiled=True)

    branch_grad = lax.all_gather((keep * hidden_grad).astype(BF), "seq", axis=0, tiled=True)
    mixed_grad = nn(branch_grad, out_weight).astype(BF).reshape(total_len, kv_heads, groups, DH)
    values_grad = jnp.einsum(
        "ngqk,qngd->knd", probs_low, mixed_grad, preferred_element_type=F32
    ).astype(BF)
    prob_grad = jnp.einsum("qngd,knd->ngqk", mixed_grad, values, preferred_element_type=F32)
    score_grad = (
        probs * (prob_grad - jnp.sum(probs * prob_grad, axis=-1, keepdims=True))
    ).astype(BF)
    queries_grad = (
        jnp.einsum("ngqk,knd->qngd", score_grad, keys, preferred_element_type=F32) * scale
    )
    keys_grad = (
        jnp.einsum("ngqk,qngd->knd", score_grad, queries, preferred_element_type=F32) * scale
    )
    qkv_grad = jnp.concatenate(
        [
            rotate(queries_grad, cos_table, -sin_table).astype(BF).reshape(total_len, q_part),
            rotate(keys_grad, cos_table, -sin_table).astype(BF).reshape(total_len, k_part),
            values_grad.reshape(total_len, k_part),
        ],
        axis=1,
    )
    scaled1 = lax.psum_scatter(
        nt(qkv_grad, qkv_weight).astype(BF), "seq", scatter_dimension=0, tiled=True
    ).astype(F32)
    input_grad = hidden_grad + scale1 * (
        scaled1 - norm1 * jnp.mean(scaled1 * norm1, axis=-1, keepdims=True)
    )
    attn_partial = jnp.concatenate(
        [tn(norm1_all, qkv_grad).astype(BF), tn(branch_grad, mixed).astype(BF)], axis=1
    )
    attn_sums = lax.psum_scatter(attn_partial, ("rep", "tp"), scatter_dimension=0, tiled=True)

    ffn_own = lax.all_to_all(
        ffn_sums.reshape(plane, -1, ffn_sums.shape[1]), in_plane, 0, 0, tiled=True
    ).astype(F32)
    gate_own = uncolumns(ffn_own[:, :, :ff_part])
    up_own = uncolumns(ffn_own[:, :, ff_part : 2 * ff_part])
    down_own = uncolumns(ffn_own[:, :, 2 * ff_part :])
    gain_ffn_grad = jnp.sum(gate_own * wg32, axis=1) + jnp.sum(up_own * wu32, axis=1)

    attn_own = lax.all_to_all(
        attn_sums.reshape(seq, -1, attn_sums.shape[1]), "seq", 0, 0, tiled=True
    ).astype(F32)
    query_own = uncolumns(attn_own[:, :, :q_part])
    key_own = uncolumns(attn_own[:, :, q_part : q_part + k_part])
    value_own = uncolumns(attn_own[:, :, q_part + k_part : q_part + 2 * k_part])
    out_own = uncolumns(attn_own[:, :, q_part + 2 * k_part :])
    gain_attn_grad = (
        jnp.sum(query_own * wq32, axis=1)
        + jnp.sum(key_own * wk32, axis=1)
        + jnp.sum(value_own * wv32, axis=1)
    )
    return (
        out_hidden[None],
        input_grad[None],
        gain_attn_grad,
        query_own * gain1,
        key_own * gain1,
        value_own * gain1,
        out_own.T,
        gain_ffn_grad,
        gate_own * gain2,
        up_own * gain2,
        down_own.T,
    )


def solution(mesh):
    devices = mesh.devices
    dp, seq = devices.shape
    inner = Mesh(devices.reshape(dp // TP, TP, seq), ("rep", "tp", "seq"))
    dps = ("rep", "tp")
    every = ("rep", "tp", "seq")
    token = P(dps, "seq", None)
    row = P(every, None)
    col = P(None, every)
    return jax.shard_map(
        per_device,
        mesh=inner,
        in_specs=(
            token,
            P(dps, None),
            P(dps, "seq"),
            P(every),
            row,
            row,
            row,
            col,
            P(every),
            row,
            row,
            col,
            token,
        ),
        out_specs=(token, token, P(every), row, row, row, col, P(every), row, row, col),
        check_vma=False,
    )
```

time: 2170 us -> 1090 us (0.50)
  waiting for transfers between devices: 1660 us -> 642 us
  matrix products: 250 us -> 182 us
  other arithmetic: 117 us -> 66.6 us
  blocking collectives: 84.7 us -> 114 us
    reduce_scatter x4 -> x6, waiting for transfers between devices: 665 us -> 278 us  [the longest x1 91.6 us: per_device(): lax.psum_scatter(attn_partial, ('rep', 'tp'), scatter_dimension=0, tiled=...]
    unnamed x15 -> x13, waiting for transfers between devices: 381 us -> 0.88 us
    all_gather x9 -> x7, waiting for transfers between devices: 609 us -> 362 us  [the longest x1 95.9 us: per_device(): lax.all_gather(ffn_rows[:, :2 * ff_part], 'rep', axis=0, tiled=True)]
    all_to_all x0 -> x3, blocking collectives: none -> 114 us  [the longest x1 54.9 us: per_device(): ffn_rows = lax.all_to_all(ffn_pack, in_plane, 0, 0, tiled=True)]
    unnamed x2 -> x0, blocking collectives: 84.7 us -> none
    concatenate x6 -> x7, other arithmetic: 84.7 us -> 13.2 us  [the longest x4 6.1 us: rotate(): jnp.concatenate([first * cos_part - second * sin_part, second * cos_part...]
    dot_general x25 -> x18, matrix products: 250 us -> 182 us  [the longest x12 125 us: dot(): lax.dot_general(left, right, ((contract[:1], contract[1:]), ((), ())), pr...]
  transfers between devices with their start and end apart: 14 -> 14, of which waited for: 11 -> 11; matrix products, arithmetic and copies ran while one was open for 14% -> 19% of each run, Pallas kernels for 0% -> 0%
where the time goes in v1:
time: 1090 us; the launch traced here: 1080 us
  waiting for transfers between devices  642 us (59%)
  matrix products  182 us (17%)
  blocking collectives  114 us (10%)
  other arithmetic  66.6 us (6%)
  local copies, waits for them, and re-layouts  53.4 us (5%)
  between operations  17 us (2%)
    dot_general x12, matrix products, dot(): lax.dot_general(left, right, ((contract[:1], contract[1:]), ((), ())), pr...  125 us
    all_gather x1, waiting for transfers between devices, per_device(): lax.all_gather(ffn_rows[:, :2 * ff_part], 'rep', axis=0, tiled=True)  95.9 us
    reduce_scatter x1, waiting for transfers between devices, per_device(): lax.psum_scatter(attn_partial, ('rep', 'tp'), scatter_dimension=0, tiled=...  91.6 us
    all_gather x1, waiting for transfers between devices, per_device(): attn_weight = lax.all_gather(attn_rows, ('rep', 'tp'), axis=0, tiled=True)  86.9 us
    reduce_scatter x1, waiting for transfers between devices, per_device(): lax.psum_scatter(nt(gate_up_grad, gu_weight).astype(BF), in_plane, scatte...  70.8 us
    reduce_scatter x1, waiting for transfers between devices, per_device(): lax.psum_scatter(nt(inner, down_weight).astype(BF), in_plane, scatter_dim...  67.1 us
    all_gather x1, waiting for transfers between devices, per_device(): lax.all_gather((keep * upstream).astype(BF), in_plane, axis=0, tiled=True)  55.9 us
    all_gather x1, waiting for transfers between devices, per_device(): norm2_all = lax.all_gather(norm2.astype(BF), in_plane, axis=0, tiled=True)  55.1 us
  transfers between devices with their start and end apart: 14, of which 11 were waited for; matrix products, arithmetic and copies ran while one was open for 19% of the time, Pallas kernels for 0%

profile of v1, /device:TPU:1, one launch (start us, length us, event | category | flops | bytes accessed | tf_op | source)
XLA Modules:
  0.0 1080.3 jit_solution(8620445606777648327)
XLA Ops:
  9.7 2.4 fusion.10
  13.3 15.6 %all_to_all.20 = bf16[4,64,1280]{2,1,0:T(8,128)(2,1)} all-to-all(bf16[4,64,1280]{2,1,0:T(8,128)(2,1)S(1)} %copy.112), channel_id=1, replica_groups=mesh['rep'=4,'tp'=2,'seq'=4] {'seq'}, dimensions={0} | all-to-all | bytes 1310720 | tf_op jit(solution)/shard_map/all_to_all | solution.py:124
  29.2 3.0 fusion.73
  32.1 1.8 fusion.7
  34.0 17.4 %all-gather.8.cloned.1.call-done = bf16[1024,2048]{1,0:T(8,128)(2,1)} async-done(((bf16[256,2048]{1,0:T(8,128)(2,1)}), bf16[1024,2048]{1,0:T(8,128)(2,1)}) %all-gather.8.cloned.1.call-update) | async-done | bytes 4194320 | tf_op jit(solution)/shard_map/all_gather | solution.py:148
  51.4 86.9 %all-gather.10.cloned.1.call-done = bf16[2048,1280]{1,0:T(8,128)(2,1)} async-done(((bf16[256,1280]{1,0:T(8,128)(2,1)}), bf16[2048,1280]{1,0:T(8,128)(2,1)}) %all-gather.10.cloned.1.call-update) | async-done | bytes 5242896 | tf_op jit(solution)/shard_map/all_gather | solution.py:126
  138.3 6.2 fusion.12
  146.2 1.6 fusion.93
  147.8 1.8 copy.149
  149.6 3.2 copy.148
  152.8 2.2 fusion.50
  155.1 8.2 fusion.94
  163.3 8.0 exponential_reduce_fusion
  171.3 8.9 fusion.29
  180.2 6.4 convolution_convert_fusion.3
  191.9 1.9 copy_bitcast_fusion
  193.8 3.1 concatenate.65
  196.9 54.9 %all_to_all.21 = bf16[8,64,2112]{2,1,0:T(8,128)(2,1)S(1)} all-to-all(bf16[8,64,2112]{2,1,0:T(8,128)(2,1)} %concatenate.65), channel_id=1, replica_groups=mesh['rep'=4,'tp'=2,'seq'=4] {'tp','seq'}, dimensions={0} | all-to-all | bytes 4325376 | tf_op jit(solution)/shard_map/all_to_all | solution.py:138
  254.7 1.8 multiply_reduce_fusion
  256.5 3.0 fusion.23
  259.5 2.2 slice.109
  262.5 95.9 %all-gather.14.cloned.1.call-done = bf16[2048,1408]{1,0:T(8,128)(2,1)} async-done(((bf16[512,1408]{1,0:T(8,128)(2,1)}), bf16[2048,1408]{1,0:T(8,128)(2,1)}) %all-gather.14.cloned.1.call-update) | async-done | bytes 5767184 | tf_op jit(solution)/shard_map/all_gather | solution.py:140
  358.4 55.1 %all-gather.12.cloned.1.call-done = bf16[2048,2048]{1,0:T(8,128)(2,1)} async-done(((bf16[256,2048]{1,0:T(8,128)(2,1)}), bf16[2048,2048]{1,0:T(8,128)(2,1)}) %all-gather.12.cloned.1.call-update) | async-done | bytes 8388624 | tf_op jit(solution)/shard_map/all_gather | solution.py:184
  413.5 19.1 %fusion.95 = f32[2048,1408]{0,1:T(8,128)} fusion(bf16[2048,2048]{1,0:T(8,128)(2,1)} %all-gather.12.cloned.1.call-done, bf16[2048,1408]{1,0:T(8,128)(2,1)} %all-gather.14.cloned.1.call-done), kind=kOutput, calls=%fused_computation.169 | convolution fusion | flops 11811160064 | bytes 25690112 | tf_op jit(solution)/shard_map/dot_general | solution.py:55
  432.6 45.1 %all-gather.16.cloned.1.call-done = bf16[2048,704]{1,0:T(8,128)(2,1)} async-done(((bf16[512,704]{1,0:T(8,128)(2,1)}), bf16[2048,704]{1,0:T(8,128)(2,1)}) %all-gather.16.cloned.1.call-update) | async-done | bytes 2883600 | tf_op jit(solution)/shard_map/all_gather | solution.py:141
  477.7 55.9 %all-gather.18.cloned.1.call-done = bf16[2048,2048]{1,0:T(8,128)(2,1)} async-done(((bf16[256,2048]{1,0:T(8,128)(2,1)}), bf16[2048,2048]{1,0:T(8,128)(2,1)}) %all-gather.18.cloned.1.call-update) | async-done | bytes 8388624 | tf_op jit(solution)/shard_map/all_gather | solution.py:149
  533.6 16.1 %multiply_convert_fusion.1 = (bf16[2048,704]{0,1:T(8,128)(2,1)S(1)}, bf16[2048,704]{0,1:T(8,128)(2,1)}, bf16[2048,704]{0,1:T(8,128)(2,1)}) fusion(f32[2048,1408]{0,1:T(8,128)} %fusion.95, bf16[2048,2048]{1,0:T(8,128)(2,1)} %all-gather.18.cloned.1.call-done, bf16[2048,704]{1,0:T(8,128)(2,1)} %all-gather.16.cloned.1.call-done), kind=kOutput, calls=%fused_computation.17 | convolution fusion | flops 5927206912 | bytes 31457280 | tf_op jit(solution)/shard_map/dot_general | solution.py:55
  551.2 18.6 %convolution_convert_fusion.1 = bf16[2048,2048]{1,0:T(8,128)(2,1)} fusion(bf16[2048,1408]{1,0:T(8,128)(2,1)} %all-gather.14.cloned.1.call-done, bf16[2048,704]{0,1:T(8,128)(2,1)} %get-tuple-element.12, bf16[2048,704]{0,1:T(8,128)(2,1)S(1)} %get-tuple-element.11), kind=kOutput, calls=%fused_computation.13 | convolution fusion | flops 11826888704 | bytes 19922944 | tf_op jit(solution)/shard_map/dot_general | solution.py:55
  569.9 70.8 %reduce-scatter.11.cloned.1.call-done = bf16[256,2048]{1,0:T(8,128)(2,1)} async-done(((bf16[2048,2048]{1,0:T(8,128)(2,1)}), bf16[256,2048]{1,0:T(8,128)(2,1)}) %reduce-scatter.11.cloned.1.call-update) | async-done | bytes 1048592 | tf_op jit(solution)/shard_map/reduce_scatter | solution.py:195
  640.7 2.0 fusion.18
  642.7 1.9 multiply_convert_fusion.3
  644.8 10.0 convolution_convert_fusion.6
  654.8 14.7 %convolution_convert_fusion = bf16[2048,1408]{0,1:T(8,128)(2,1)S(1)} fusion(bf16[2048,2048]{1,0:T(8,128)(2,1)} %all-gather.12.cloned.1.call-done, bf16[2048,704]{0,1:T(8,128)(2,1)S(1)} %copy-done.53, bf16[2048,704]{0,1:T(8,128)(2,1)S(1)} %copy-done.52), kind=kOutput, calls=%fused_computation.12 | convolution fusion | flops 11825577984 | bytes 19922944 | tf_op jit(solution)/shard_map/dot_general | solution.py:55
  669.5 4.1 pad_maximum_fusion
  673.7 6.2 all-gather.20.cloned.1.call-done
  679.9 6.8 fusion.32
  686.8 16.1 %fusion = (f32[4,1024]{1,0:T(4,128)S(1)}, f32[1024,1024,4]{1,0,2:T(8,128)}) fusion(f32[1,4,1024,1024]{2,3,1,0:T(8,128)} %get-tuple-element.57, f32[4,1024]{1,0:T(4,128)S(1)} %log_add_fusion, bf16[1024,4,128]{0,2,1:T(8,128)(2,1)} %bitcast.195, f32[1024,768]{0,1:T(8,128)} %copy-done.8), kind=kOutput, calls=%fused_computation.3 | convolution fusion | flops 1086320640 | bytes 34897920 | tf_op jit(solution)/shard_map/qngd,knd->ngqk/dot_general | solution.py:215
  702.9 10.8 %fusion.5 = bf16[4,1024,1024]{1,2,0:T(8,128)(2,1)} fusion(f32[1024,1024,4]{1,0,2:T(8,128)} %get-tuple-element.59, f32[1,4,1024,1024]{2,3,1,0:T(8,128)S(1)} %bitcast.190, f32[4,1024]{1,0:T(4,128)S(1)} %get-tuple-element.58, f32[4,1024]{1,0:T(4,128)S(1)} %log_add_fusion), kind=kLoop, calls=%fused_computation.11 | loop fusion | flops 16777216 | bytes 41975808 | tf_op jit(solution)/shard_map/reshape.18
  713.8 7.1 multiply_bitcast_fusion
  723.2 2.3 copy.124
  725.5 7.8 fusion.43
  734.5 9.1 fusion.47
  743.7 5.4 convolution_convert_fusion.4
  749.2 5.0 convolution_convert_fusion.7
  754.2 5.0 convolution_convert_fusion.5
  759.3 2.7 pad_maximum_fusion.2
  762.1 11.4 %convolution_convert_fusion.2 = bf16[2048,2048]{1,0:T(8,128)(2,1)} fusion(bf16[2048,704]{0,1:T(8,128)(2,1)} %get-tuple-element.13, bf16[2048,704]{1,0:T(8,128)(2,1)} %all-gather.16.cloned.1.call-done), kind=kOutput, calls=%fused_computation.14 | convolution fusion | flops 5909774336 | bytes 14155776 | tf_op jit(solution)/shard_map/dot_general | solution.py:55
  773.5 48.8 %reduce-scatter.17.cloned.1.call-done = bf16[512,2112]{0,1:T(8,128)(2,1)} async-done(((bf16[2048,2112]{0,1:T(8,128)(2,1)}), bf16[512,2112]{0,1:T(8,128)(2,1)}) %reduce-scatter.17.cloned.1.call-update) | async-done | bytes 2162704 | tf_op jit(solution)/shard_map/reduce_scatter | solution.py:208
  822.3 4.1 copy.133
  826.5 43.4 %all_to_all.22 = bf16[8,64,2112]{2,1,0:T(8,128)(2,1)S(1)} all-to-all(bf16[8,64,2112]{2,1,0:T(8,128)(2,1)} %bitcast.193), channel_id=1, replica_groups=mesh['rep'=4,'tp'=2,'seq'=4] {'tp','seq'}, dimensions={0} | all-to-all | bytes 4325376 | tf_op jit(solution)/shard_map/all_to_all | solution.py:244
  870.2 2.3 slice_bitcast_fusion
  872.5 2.0 copy.136
  874.5 2.8 reshape.549
  877.3 3.5 copy.135
  880.8 2.8 reshape.548
  883.6 3.5 copy.134
  887.1 2.8 reshape.547
  889.9 4.3 broadcast_multiply_fusion
  894.7 1.7 fusion.24
  896.4 91.6 %reduce-scatter.15.cloned.1.call-done = bf16[256,1280]{0,1:T(8,128)(2,1)} async-done(((bf16[2048,1280]{0,1:T(8,128)(2,1)}), bf16[256,1280]{0,1:T(8,128)(2,1)}) %reduce-scatter.15.cloned.1.call-update) | async-done | bytes 655376 | tf_op jit(solution)/shard_map/reduce_scatter | solution.py:242
  988.0 2.2 copy.128
  990.2 5.3 all-to-all-start.2
  995.5 67.1 %reduce-scatter.9.cloned.1.call-done = bf16[256,2048]{1,0:T(8,128)(2,1)} async-done(((bf16[2048,2048]{1,0:T(8,128)(2,1)}), bf16[256,2048]{1,0:T(8,128)(2,1)}) %reduce-scatter.9.cloned.1.call-update) | async-done | bytes 1048592 | tf_op jit(solution)/shard_map/reduce_scatter | solution.py:198
  1062.6 5.1 fusion.22
  (193 shorter events, 24.5 us)
Async XLA Ops:
  8.0 4.2 copy-start.42
  8.0 4.2 copy-start.28
  8.0 4.2 copy-start.26
  8.0 4.4 copy-start.25
  8.1 4.6 copy-start.17
  8.1 43.3 %all-gather.8.cloned.1.call-start = ((), (), s32[]{:S(2)}) async-start(), calls=%async_computation.10 | async-start | bytes 5242880 | tf_op jit(solution)/shard_map/all_gather | solution.py:148
  9.7 2.5 copy-start.38
  12.2 126.1 %all-gather.10.cloned.1.call-start = ((), (), s32[]{:S(2)}) async-start(), calls=%async_computation.11 | async-start | bytes 5898240 | tf_op jit(solution)/shard_map/all_gather | solution.py:126
  12.6 16.4 %copy-start.49 = (s32[1,2]{1,0:T(1,128)S(1)}, s32[1,2]{1,0:T(1,128)}, u32[]{:S(2)}) copy-start(s32[1,2]{1,0:T(1,128)} %param.14) | copy-start | bytes 28
  28.9 225.7 %reduce-scatter.7.cloned.1.call-start = ((), (), s32[]{:S(2)}) async-start(), calls=%async_computation.12 | async-start | bytes 5242880 | tf_op jit(solution)/shard_map/reduce_scatter | solution.py:177
  29.0 115.7 %copy-start.44 = (f32[64]{0:T(128)}, f32[64]{0:T(128)S(1)}, u32[]{:S(2)}) copy-start(f32[64]{0:T(128)S(1)} %negate_power_fusion) | copy-start | bytes 772
  29.0 115.7 %copy-start.32 = (f32[1024]{0:T(1024)}, f32[1024]{0:T(1024)S(1)}, u32[]{:S(2)}) copy-start(f32[1024]{0:T(1024)S(1)} %iota_convert_fusion) | copy-start | bytes 12292
  32.1 120.6 %copy-start.6 = (f32[1024,64]{1,0:T(8,128)}, f32[1024,64]{1,0:T(8,128)S(1)}, u32[]{:S(2)}) copy-start(f32[1024,64]{1,0:T(8,128)S(1)} %get-tuple-element.45) | copy-start | bytes 786436
  146.2 8.9 copy-start.21
  146.2 8.9 copy-start.23
  155.0 8.3 copy-start.9
  155.0 8.3 copy-start.10
  180.2 6.4 copy-start.19
  186.6 2.7 copy-start.11
  186.6 2.7 copy-start.12
  186.6 2.7 copy-start.46
  186.6 171.8 %all-gather.14.cloned.1.call-start = ((), (), s32[]{:S(2)}) async-start(), calls=%async_computation.14 | async-start | bytes 7208960 | tf_op jit(solution)/shard_map/all_gather | solution.py:140
  251.9 2.7 copy-start.48
  251.9 2.8 copy-start
  253.3 3.1 copy-start.2
  254.5 159.0 %all-gather.12.cloned.1.call-start = ((), (), s32[]{:S(2)}) async-start(), calls=%async_computation.13 | async-start | bytes 9437184 | tf_op jit(solution)/shard_map/all_gather | solution.py:184
  254.6 388.1 %copy-start.34 = (f32[1,256]{1,0:T(1,128)}, f32[1,256]{1,0:T(1,128)S(1)}, u32[]{:S(2)}) copy-start(f32[1,256]{1,0:T(1,128)S(1)} %subtract_convert_fusion.2) | copy-start | bytes 3076
  256.5 386.3 %copy-start.36 = (f32[256]{0:T(256)}, f32[256]{0:T(256)S(1)}, u32[]{:S(2)}) copy-start(f32[256]{0:T(256)S(1)} %add_rsqrt_fusion) | copy-start | bytes 3076
  259.5 218.2 %all-gather.16.cloned.1.call-start = ((), (), s32[]{:S(2)}) async-start(), calls=%async_computation.15 | async-start | bytes 3932160 | tf_op jit(solution)/shard_map/all_gather | solution.py:141
  261.8 271.8 %all-gather.18.cloned.1.call-start = ((), (), s32[]{:S(2)}) async-start(), calls=%async_computation.17 | async-start | bytes 9437184 | tf_op jit(solution)/shard_map/all_gather | solution.py:149
  262.5 378.2 %reduce-scatter.11.cloned.1.call-start = ((), (), s32[]{:S(2)}) async-start(), calls=%async_computation.18 | async-start | bytes 9437184 | tf_op jit(solution)/shard_map/reduce_scatter | solution.py:195
  569.8 70.8 %copy-start.1 = (bf16[256,2048]{1,0:T(8,128)(2,1)S(1)}, bf16[256,2048]{1,0:T(8,128)(2,1)}, u32[]{:S(2)}) copy-start(bf16[256,2048]{1,0:T(8,128)(2,1)} %reduce-scatter.7.cloned.1.call-done) | copy-start | bytes 3145732
  569.9 110.0 %all-gather.20.cloned.1.call-start = ((), (), s32[]{:S(2)}) async-start(), calls=%async_computation.19 | async-start | bytes 5242880 | tf_op jit(solution)/shard_map/all_gather | solution.py:210
  644.7 177.7 %reduce-scatter.17.cloned.1.call-start = ((), (), s32[]{:S(2)}) async-start(), calls=%async_computation.22 | async-start | bytes 10813440 | tf_op jit(solution)/shard_map/reduce_scatter | solution.py:208
  644.7 10.1 copy-start.52
  644.8 10.1 copy-start.53
  673.6 221.0 %reduce-scatter.13.cloned.1.call-start = ((), (), s32[]{:S(2)}) async-start(), calls=%async_computation.20 | async-start | bytes 5242880 | tf_op jit(solution)/shard_map/reduce_scatter | solution.py:233
  686.8 16.1 %slice-start = ((s8[16777216]{0:T(1024)(128)(4,1)}), s8[4194304]{0:T(1024)(128)(4,1)S(1)}, s32[]{:S(2)}) async-start(s8[16777216]{0:T(1024)(128)(4,1)} %bitcast.189), calls=%async_computation.23 | async-start | bytes 8388608
  686.8 16.1 %slice-start.1 = ((s8[16777216]{0:T(1024)(128)(4,1)}), s8[4194304]{0:T(1024)(128)(4,1)S(1)}, s32[]{:S(2)}) async-start(s8[16777216]{0:T(1024)(128)(4,1)} %bitcast.189), calls=%async_computation.24 | async-start | bytes 8388608
  686.8 16.1 %slice-start.2 = ((s8[16777216]{0:T(1024)(128)(4,1)}), s8[4194304]{0:T(1024)(128)(4,1)S(1)}, s32[]{:S(2)}) async-start(s8[16777216]{0:T(1024)(128)(4,1)} %bitcast.189), calls=%async_computation.25 | async-start | bytes 8388608
  686.8 16.1 %slice-start.3 = ((s8[16777216]{0:T(1024)(128)(4,1)}), s8[4194304]{0:T(1024)(128)(4,1)S(1)}, s32[]{:S(2)}) async-start(s8[16777216]{0:T(1024)(128)(4,1)} %bitcast.189), calls=%async_computation.26 | async-start | bytes 8388608
  702.9 10.9 %copy-start.22 = (bf16[1024,64]{0,1:T(8,128)(2,1)S(1)}, bf16[1024,64]{0,1:T(8,128)(2,1)}, u32[]{:S(2)}) copy-start(bf16[1024,64]{0,1:T(8,128)(2,1)} %copy-done.21) | copy-start | bytes 393220
  702.9 10.9 %copy-start.24 = (bf16[1024,64]{0,1:T(8,128)(2,1)S(1)}, bf16[1024,64]{0,1:T(8,128)(2,1)}, u32[]{:S(2)}) copy-start(bf16[1024,64]{0,1:T(8,128)(2,1)} %copy-done.23) | copy-start | bytes 393220
  713.7 7.1 copy-start.7
  713.7 7.1 copy-start.13
  725.5 7.8 copy-start.33
  725.5 7.9 copy-start.45
  725.5 9.0 copy-start.5
  725.5 18.2 %slice-start.4 = ((s8[5242880]{0:T(1024)(128)(4,1)}), s8[4194304]{0:T(1024)(128)(4,1)S(1)}, s32[]{:S(2)}) async-start(s8[5242880]{0:T(1024)(128)(4,1)} %bitcast.219), calls=%async_computation.27 | async-start | bytes 8388608
  734.5 9.2 copy-start.30
  734.5 9.2 copy-start.15
  734.5 9.2 slice-start.5
  749.1 238.9 %reduce-scatter.15.cloned.1.call-start = ((), (), s32[]{:S(2)}) async-start(), calls=%async_computation.21 | async-start | bytes 5898240 | tf_op jit(solution)/shard_map/reduce_scatter | solution.py:242
  749.2 5.0 copy-start.16
  749.2 5.0 copy-start.31
  749.2 5.0 copy-start.50
  762.0 300.5 %reduce-scatter.9.cloned.1.call-start = ((), (), s32[]{:S(2)}) async-start(), calls=%async_computation.16 | async-start | bytes 9437184 | tf_op jit(solution)/shard_map/reduce_scatter | solution.py:198
  883.6 6.3 copy-start.47
  889.8 4.8 copy-start.39
  894.1 168.4 %copy-start.35 = (f32[1,256]{1,0:T(1,128)S(1)}, f32[1,256]{1,0:T(1,128)}, u32[]{:S(2)}) copy-start(f32[1,256]{1,0:T(1,128)} %copy-done.34) | copy-start | bytes 3076
  894.1 168.4 %copy-start.37 = (f32[256]{0:T(256)S(1)}, f32[256]{0:T(256)}, u32[]{:S(2)}) copy-start(f32[256]{0:T(256)} %copy-done.36) | copy-start | bytes 3076
  894.2 168.4 %copy-start.41 = (f32[256]{0:T(256)S(1)}, f32[256]{0:T(256)}, u32[]{:S(2)}) copy-start(f32[256]{0:T(256)} %copy-done.40) | copy-start | bytes 3076
  990.2 77.5 %all-to-all-start.2 = ((bf16[4,64,1280]{2,1,0:T(8,128)(2,1)}), bf16[4,64,1280]{2,1,0:T(8,128)(2,1)}, u32[]{:S(2)}, u32[]{:S(2)}) async-start(bf16[4,64,1280]{2,1,0:T(8,128)(2,1)} %bitcast.199), calls=%async_computation.7 | async-start | bytes 1310720 | tf_op jit(solution)/shard_map/all_to_all | solution.py:252
  1067.7 2.3 copy-start.43
  (10 other events, 18.5 us)
Sparse Core Ops, SparseCore 0:
  12.3 39.0 all-gather.7
  53.6 84.6 all-gather.9
  186.7 66.4 reduce-scatter.6
  644.8 35.0 all-gather.19
Sparse Core Ops, SparseCore 1:
  254.6 103.7 all-gather.13
  360.8 52.7 all-gather.11
  415.0 62.6 all-gather.15
  480.1 53.4 all-gather.17
  570.0 70.7 reduce-scatter.10
  673.7 148.6 reduce-scatter.16
  824.7 57.1 reduce-scatter.12
  885.4 102.6 reduce-scatter.14
  991.4 71.1 reduce-scatter.8

commit v2 on v1

v2 whole, which is shorter than its diff:
```python
import jax
import jax.numpy as jnp
from jax import lax
from jax.experimental import pallas as pl
from jax.experimental.pallas import tpu as pltpu
from jax.sharding import Mesh
from jax.sharding import PartitionSpec as P

H = 16
KV = 4
DH = 128
PIC = 256
NPIC = 2
EPS = 1e-05
TP = 2
BF = jnp.bfloat16
F32 = jnp.float32


def rotary_tables(positions, head_dim):
    half_dim = head_dim // 2
    inverse = 10000.0 ** (-(jnp.arange(half_dim, dtype=F32) * 2.0 / head_dim))
    angles = positions.astype(F32)[:, None] * inverse[None, :]
    return (jnp.cos(angles), jnp.sin(angles))


def rotate(values, cos_table, sin_table):
    half = values.shape[-1] // 2
    shape = (cos_table.shape[0],) + (1,) * (values.ndim - 2) + (half,)
    cos_part = cos_table.reshape(shape)
    sin_part = sin_table.reshape(shape)
    first = values[..., :half]
    second = values[..., half:]
    return jnp.concatenate(
        [first * cos_part - second * sin_part, second * cos_part + first * sin_part], axis=-1
    )


def picture_ids(positions, starts):
    inside = (positions[None, :] >= starts[:, None]) & (positions[None, :] < starts[:, None] + PIC)
    labels = jnp.arange(1, NPIC + 1, dtype=jnp.int32)
    return jnp.sum(jnp.where(inside, labels[:, None], 0), axis=0)


def visible(positions, starts):
    ids = picture_ids(positions, starts)
    causal = positions[None, :] <= positions[:, None]
    same_piece = (ids[:, None] == ids[None, :]) & (ids[:, None] > 0)
    return causal | same_piece


def rms_scale(rows):
    return lax.rsqrt(jnp.mean(rows * rows, axis=-1, keepdims=True) + EPS)


def dot(left, right, contract):
    return lax.dot_general(
        left, right, ((contract[:1], contract[1:]), ((), ())), preferred_element_type=F32
    )


def nn(left, right):
    return dot(left, right, (1, 0))


def nt(left, right):
    return dot(left, right, (1, 1))


def tn(left, right):
    return dot(left, right, (0, 0))


MESH_ID = pl.DeviceIdType.MESH
SUB = 32


def plane_place():
    tp_at = lax.axis_index("tp")
    seq_at = lax.axis_index("seq")
    seq = lax.axis_size("seq")
    half = seq // 2
    far = lax.rem(seq_at + half, seq)
    mate = seq_at + 1 - 2 * lax.rem(seq_at, 2)
    far_mate = far + 1 - 2 * lax.rem(far, 2)
    return tp_at, seq_at, far, mate, far_mate


def at_device(tp_at, seq_at):
    return (lax.axis_index("rep"), tp_at, seq_at)


def enter(devices):
    barrier = pltpu.get_barrier_semaphore()
    for device in devices:
        pl.semaphore_signal(barrier, inc=1, device_id=device, device_id_type=MESH_ID)
    pl.semaphore_wait(barrier, len(devices))


def remote(src, dst, send, recv, device):
    return pltpu.make_async_remote_copy(
        src_ref=src,
        dst_ref=dst,
        send_sem=send,
        recv_sem=recv,
        device_id=device,
        device_id_type=MESH_ID,
    )


def gather_kernel(own_ref, all_ref, sends, recvs, local):
    tp_at, seq_at, far, mate, _ = plane_place()
    seq = lax.axis_size("seq")
    other = 1 - tp_at
    to_x = at_device(tp_at, far)
    to_y = at_device(other, seq_at)
    to_c = at_device(tp_at, mate)
    rows = own_ref.shape[0]
    part = rows // 2
    enter((to_x, to_y, to_c))

    def piece(t, s, h):
        return all_ref.at[t * seq + s, pl.ds(h * part, part)]

    def pass_on(i, t, s, h, device):
        copy = remote(piece(t, s, h), piece(t, s, h), sends.at[i], recvs.at[i], device)
        copy.start()
        return copy

    def own(i, h, device):
        copy = remote(
            own_ref.at[pl.ds(h * part, part)],
            piece(tp_at, seq_at, h),
            sends.at[i],
            recvs.at[i],
            device,
        )
        copy.start()
        return copy

    x0 = own(0, 0, to_x)
    y0 = own(1, 0, to_y)
    c0 = own(2, 0, to_c)
    x1 = own(3, 1, to_x)
    y1 = own(4, 1, to_y)
    c1 = own(5, 1, to_c)
    mine = pltpu.make_async_copy(own_ref, all_ref.at[tp_at * seq + seq_at], local)
    mine.start()
    x0.wait_recv()
    diag0 = pass_on(6, tp_at, far, 0, to_y)
    rx0 = pass_on(8, tp_at, far, 0, to_c)
    y0.wait_recv()
    ry0 = pass_on(9, other, seq_at, 0, to_c)
    y1.wait_recv()
    diag1 = pass_on(7, other, seq_at, 1, to_x)
    ry1 = pass_on(10, other, seq_at, 1, to_c)
    x1.wait_recv()
    rx1 = pass_on(11, tp_at, far, 1, to_c)
    diag0.wait_recv()
    rd0 = pass_on(12, other, far, 0, to_c)
    diag1.wait_recv()
    rd1 = pass_on(13, other, far, 1, to_c)
    for copy in (c0, c1, rx0, ry0, ry1, rx1, rd0, rd1):
        copy.wait_recv()
    for copy in (x0, y0, c0, x1, y1, c1, diag0, diag1, rx0, ry0, ry1, rx1, rd0, rd1):
        copy.wait_send()
    mine.wait()


def gather_plane(block, ident):
    rows, width = block.shape
    plane = lax.axis_size("tp") * lax.axis_size("seq")
    size = rows * width * 2
    gathered = pl.pallas_call(
        gather_kernel,
        out_shape=jax.ShapeDtypeStruct((plane, rows, width), block.dtype),
        in_specs=[pl.BlockSpec(memory_space=pltpu.VMEM)],
        out_specs=pl.BlockSpec(memory_space=pltpu.HBM),
        scratch_shapes=[
            pltpu.SemaphoreType.DMA((14,)),
            pltpu.SemaphoreType.DMA((14,)),
            pltpu.SemaphoreType.DMA,
        ],
        cost_estimate=pl.CostEstimate(
            flops=0, transcendentals=0, bytes_accessed=plane * size * 12
        ),
        compiler_params=pltpu.CompilerParams(collective_id=ident, has_side_effects=True),
        name="gather_plane",
    )(block)
    return gathered.reshape(plane * rows, width)


def add_rows(target, sources, start, count, kind):
    step = min(SUB, count)

    def body(i, carry):
        at = pl.ds(start + i * step, step)
        total = sources[0][at, :].astype(F32)
        for source in sources[1:]:
            total = total + source[at, :].astype(F32)
        target[at, :] = total.astype(kind)
        return carry

    lax.fori_loop(0, count // step, body, 0)


def scatter_kernel(part_ref, sum_ref, held, chip_in, far_in, near_in, loads, sends, recvs):
    tp_at, seq_at, far, mate, far_mate = plane_place()
    seq = lax.axis_size("seq")
    other = 1 - tp_at
    to_x = at_device(tp_at, far)
    to_y = at_device(other, seq_at)
    to_c = at_device(tp_at, mate)
    rows = sum_ref.shape[0]
    part = rows // 2
    top, low = pl.ds(0, part), pl.ds(part, part)
    enter((to_x, to_y, to_c))
    chips = ((other, far, far_mate), (tp_at, far, far_mate), (other, seq_at, mate), (tp_at, seq_at, mate))
    gives, takes = [], []
    for k, (t, s, m) in enumerate(chips):
        give = remote(
            part_ref.at[t * seq + m], chip_in.at[k], sends.at[k], recvs.at[k], to_c
        )
        give.start()
        take = pltpu.make_async_copy(part_ref.at[t * seq + s], held.at[k], loads.at[k])
        take.start()
        gives.append(give)
        takes.append(take)

    def chip_sum(k):
        takes[k].wait()
        gives[k].wait_recv()
        add_rows(held.at[k], (held.at[k], chip_in.at[k]), 0, rows, held.dtype)

    def send(i, src, dst, device):
        copy = remote(src, dst, sends.at[i], recvs.at[i], device)
        copy.start()
        return copy

    chip_sum(0)
    d0 = send(4, held.at[0, top], far_in.at[0, top], to_x)
    d1 = send(5, held.at[0, low], far_in.at[1, low], to_y)
    chip_sum(1)
    x0 = send(6, held.at[1, top], near_in.at[0, top], to_x)
    chip_sum(2)
    y1 = send(7, held.at[2, low], near_in.at[1, low], to_y)
    chip_sum(3)
    d0.wait_recv()
    add_rows(held.at[2], (held.at[2], far_in.at[0]), 0, part, held.dtype)
    y0 = send(8, held.at[2, top], near_in.at[1, top], to_y)
    d1.wait_recv()
    add_rows(held.at[1], (held.at[1], far_in.at[1]), part, part, held.dtype)
    x1 = send(9, held.at[1, low], near_in.at[0, low], to_x)
    x0.wait_recv()
    y0.wait_recv()
    add_rows(sum_ref, (held.at[3], near_in.at[0], near_in.at[1]), 0, part, sum_ref.dtype)
    y1.wait_recv()
    x1.wait_recv()
    add_rows(sum_ref, (held.at[3], near_in.at[0], near_in.at[1]), part, part, sum_ref.dtype)
    for copy in gives + [d0, d1, x0, y1, y0, x1]:
        copy.wait_send()


def scatter_plane(partial, ident):
    plane = lax.axis_size("tp") * lax.axis_size("seq")
    rows, width = partial.shape[0] // plane, partial.shape[1]
    kind = partial.dtype
    size = rows * width * 2
    return pl.pallas_call(
        scatter_kernel,
        out_shape=jax.ShapeDtypeStruct((rows, width), F32),
        in_specs=[pl.BlockSpec(memory_space=pltpu.HBM)],
        out_specs=pl.BlockSpec(memory_space=pltpu.VMEM),
        scratch_shapes=[
            pltpu.VMEM((4, rows, width), kind),
            pltpu.VMEM((4, rows, width), kind),
            pltpu.VMEM((2, rows, width), kind),
            pltpu.VMEM((2, rows, width), kind),
            pltpu.SemaphoreType.DMA((4,)),
            pltpu.SemaphoreType.DMA((10,)),
            pltpu.SemaphoreType.DMA((10,)),
        ],
        cost_estimate=pl.CostEstimate(
            flops=0, transcendentals=0, bytes_accessed=plane * size * 14
        ),
        compiler_params=pltpu.CompilerParams(
            collective_id=ident, has_side_effects=True, vmem_limit_bytes=32 << 20
        ),
        name="scatter_plane",
    )(partial.reshape(plane, rows, width))


def exchange_kernel(in_ref, out_ref, stage, local, sends, recvs):
    tp_at, seq_at, _, _, _ = plane_place()
    seq = lax.axis_size("seq")
    plane = lax.axis_size("tp") * seq
    me = tp_at * seq + seq_at
    peers = [lax.rem(me + k, plane) for k in range(1, plane)]
    devices = [at_device(peer // seq, lax.rem(peer, seq)) for peer in peers]
    enter(devices)
    copies = []
    for k, (peer, device) in enumerate(zip(peers, devices)):
        copy = remote(in_ref.at[peer], out_ref.at[me], sends.at[k], recvs.at[k], device)
        copy.start()
        copies.append(copy)
    take = pltpu.make_async_copy(in_ref.at[me], stage, local.at[0])
    take.start()
    take.wait()
    put = pltpu.make_async_copy(stage, out_ref.at[me], local.at[1])
    put.start()
    for copy in copies:
        copy.wait()
    put.wait()


def exchange_plane(blocks, ident):
    plane, rows, width = blocks.shape
    size = plane * rows * width * 2
    return pl.pallas_call(
        exchange_kernel,
        out_shape=jax.ShapeDtypeStruct(blocks.shape, blocks.dtype),
        in_specs=[pl.BlockSpec(memory_space=pltpu.HBM)],
        out_specs=pl.BlockSpec(memory_space=pltpu.HBM),
        scratch_shapes=[
            pltpu.VMEM((rows, width), blocks.dtype),
            pltpu.SemaphoreType.DMA((2,)),
            pltpu.SemaphoreType.DMA((plane - 1,)),
            pltpu.SemaphoreType.DMA((plane - 1,)),
        ],
        cost_estimate=pl.CostEstimate(flops=0, transcendentals=0, bytes_accessed=size * 20),
        compiler_params=pltpu.CompilerParams(collective_id=ident, has_side_effects=True),
        name="exchange_plane",
    )(blocks)


def columns(matrix, parts):
    rows, cols = matrix.shape
    return jnp.transpose(matrix.reshape(rows, parts, cols // parts), (1, 0, 2))


def uncolumns(blocks):
    parts, rows, cols = blocks.shape
    return jnp.transpose(blocks, (1, 0, 2)).reshape(rows, parts * cols)


def after(value, *earlier):
    return lax.optimization_barrier((value,) + earlier)[0]


def per_device(
    layer_input,
    pic_starts,
    skip_mask,
    gain_attn,
    w_query,
    w_key,
    w_value,
    w_out,
    gain_ffn,
    w_gate,
    w_up,
    w_down,
    cotangent,
):
    _, local_len, width = layer_input.shape
    seq = lax.axis_size("seq")
    plane = lax.axis_size("tp") * seq
    total_len = local_len * seq
    heads = H // plane
    share = plane // KV
    ff_part = w_gate.shape[1] // plane
    q_part = heads * DH
    scale = DH ** (-0.5)

    gain1 = gain_attn[:, None]
    gain2 = gain_ffn[:, None]
    wq32, wk32, wv32 = w_query.astype(F32), w_key.astype(F32), w_value.astype(F32)
    wg32, wu32 = w_gate.astype(F32), w_up.astype(F32)
    attn_pack = jnp.concatenate(
        [
            columns((wq32 * gain1).astype(BF), plane),
            jnp.repeat(columns((wk32 * gain1).astype(BF), KV), share, axis=0),
            jnp.repeat(columns((wv32 * gain1).astype(BF), KV), share, axis=0),
            columns(w_out.T, plane),
        ],
        axis=2,
    )
    attn_rows = exchange_plane(attn_pack, 0)
    attn_rows = attn_rows.reshape(-1, attn_rows.shape[2])
    attn_weight = lax.all_gather(attn_rows, "rep", axis=0, tiled=True)
    qkv_weight = attn_weight[:, : q_part + 2 * DH]
    out_weight = attn_weight[:, q_part + 2 * DH :]

    tokens = layer_input.reshape(local_len, width).astype(F32)
    keep = (1 - skip_mask).astype(F32).reshape(local_len, 1)
    upstream = cotangent.reshape(local_len, width).astype(F32)
    scale1 = rms_scale(tokens)
    norm1 = tokens * scale1
    norm1_all = gather_plane(after(norm1.astype(BF), attn_rows), 1)

    ffn_pack = jnp.concatenate(
        [
            columns((wg32 * gain2).astype(BF), plane),
            columns((wu32 * gain2).astype(BF), plane),
            columns(w_down.T, plane),
        ],
        axis=2,
    )
    ffn_rows = exchange_plane(after(ffn_pack, norm1_all), 2)
    ffn_rows = ffn_rows.reshape(-1, ffn_rows.shape[2])
    down_weight = lax.all_gather(ffn_rows[:, 2 * ff_part :], "rep", axis=0, tiled=True)
    gu_weight = lax.all_gather(ffn_rows[:, : 2 * ff_part], "rep", axis=0, tiled=True)
    ffn_grad = gather_plane(after((keep * upstream).astype(BF), ffn_rows), 3)

    other_starts = lax.ppermute(pic_starts, "tp", [(0, 1), (1, 0)])
    starts = jnp.where(
        lax.axis_index("tp") == 0,
        jnp.concatenate([pic_starts, other_starts], axis=0),
        jnp.concatenate([other_starts, pic_starts], axis=0),
    )
    positions = jnp.arange(total_len, dtype=jnp.int32)
    cos_table, sin_table = rotary_tables(positions, DH)
    allowed = jax.vmap(visible, (None, 0))(positions, starts)[:, None]
    turn = jax.vmap(rotate, (0, None, None))

    projected = nn(norm1_all, qkv_weight).reshape(TP, total_len, q_part + 2 * DH)
    queries = turn(
        projected[..., :q_part].reshape(TP, total_len, heads, DH), cos_table, sin_table
    ).astype(BF)
    keys = turn(projected[..., q_part : q_part + DH], cos_table, sin_table).astype(BF)
    values = projected[..., q_part + DH :].astype(BF)
    scores = jnp.einsum("tqhd,tkd->thqk", queries, keys, preferred_element_type=F32) * scale
    scores = jnp.where(allowed, scores, -jnp.inf)
    peak = jnp.max(scores, axis=-1, keepdims=True)
    log_total = peak + jnp.log(jnp.sum(jnp.exp(scores - peak), axis=-1, keepdims=True))
    probs = jnp.exp(scores - log_total)
    probs_low = probs.astype(BF)
    mixed = jnp.einsum("thqk,tkd->tqhd", probs_low, values, preferred_element_type=F32)
    mixed = mixed.astype(BF).reshape(TP * total_len, q_part)
    branch = scatter_plane(nt(mixed, out_weight).astype(BF), 4)
    hidden = tokens + keep * branch

    scale2 = rms_scale(hidden)
    norm2 = hidden * scale2
    norm2_all = gather_plane(norm2.astype(BF), 5)
    inner_grad = nn(ffn_grad, down_weight)
    gate_up = nn(norm2_all, gu_weight)
    gate, upward = gate_up[:, :ff_part], gate_up[:, ff_part:]
    sigmoid_gate = jax.nn.sigmoid(gate)
    silu_gate = gate * sigmoid_gate
    inner = (silu_gate * upward).astype(BF)
    slope = sigmoid_gate * (1.0 + gate * (1.0 - sigmoid_gate))
    gate_up_grad = jnp.concatenate(
        [(inner_grad * upward * slope).astype(BF), (inner_grad * silu_gate).astype(BF)], axis=1
    )
    scaled2_partial = nt(gate_up_grad, gu_weight).astype(BF)
    down_partial = tn(ffn_grad, inner).astype(BF)
    gu_partial = tn(norm2_all, gate_up_grad).astype(BF)
    down_sums = lax.psum_scatter(down_partial, "rep", scatter_dimension=0, tiled=True)
    gu_sums = lax.psum_scatter(gu_partial, "rep", scatter_dimension=0, tiled=True)
    scaled2 = scatter_plane(after(scaled2_partial, down_partial, gu_partial), 6)
    hidden_grad = upstream + scale2 * (
        scaled2 - norm2 * jnp.mean(scaled2 * norm2, axis=-1, keepdims=True)
    )

    branch_grad = gather_plane((keep * hidden_grad).astype(BF), 7)
    mixed_grad = nn(branch_grad, out_weight).astype(BF).reshape(TP, total_len, heads, DH)
    values_grad = jnp.einsum(
        "thqk,tqhd->tkd", probs_low, mixed_grad, preferred_element_type=F32
    ).astype(BF)
    prob_grad = jnp.einsum("tqhd,tkd->thqk", mixed_grad, values, preferred_element_type=F32)
    score_grad = (
        probs * (prob_grad - jnp.sum(probs * prob_grad, axis=-1, keepdims=True))
    ).astype(BF)
    queries_grad = (
        jnp.einsum("thqk,tkd->tqhd", score_grad, keys, preferred_element_type=F32) * scale
    )
    keys_grad = (
        jnp.einsum("thqk,tqhd->tkd", score_grad, queries, preferred_element_type=F32) * scale
    )
    qkv_grad = jnp.concatenate(
        [
            turn(queries_grad, cos_table, -sin_table).astype(BF).reshape(-1, q_part),
            turn(keys_grad, cos_table, -sin_table).astype(BF).reshape(-1, DH),
            values_grad.reshape(-1, DH),
        ],
        axis=1,
    )
    attn_partial = jnp.concatenate(
        [tn(norm1_all, qkv_grad).astype(BF), tn(branch_grad, mixed).astype(BF)], axis=1
    )
    attn_sums = lax.psum_scatter(attn_partial, "rep", scatter_dimension=0, tiled=True)
    scaled1 = scatter_plane(after(nt(qkv_grad, qkv_weight).astype(BF), attn_partial), 8)
    input_grad = hidden_grad + scale1 * (
        scaled1 - norm1 * jnp.mean(scaled1 * norm1, axis=-1, keepdims=True)
    )
    ffn_out = scatter_plane(after(nt(inner, down_weight).astype(BF), scaled1), 9)
    out_hidden = (hidden + keep * ffn_out).astype(BF)

    ffn_sums = jnp.concatenate([gu_sums, down_sums], axis=1)
    ffn_sums = after(ffn_sums.reshape(plane, -1, ffn_sums.shape[1]), ffn_out)
    ffn_own = exchange_plane(ffn_sums, 10).astype(F32)
    gate_own = uncolumns(ffn_own[:, :, :ff_part])
    up_own = uncolumns(ffn_own[:, :, ff_part : 2 * ff_part])
    down_own = uncolumns(ffn_own[:, :, 2 * ff_part :])
    gain_ffn_grad = jnp.sum(gate_own * wg32, axis=1) + jnp.sum(up_own * wu32, axis=1)

    attn_own = exchange_plane(attn_sums.reshape(plane, -1, attn_sums.shape[1]), 11).astype(F32)
    query_own = uncolumns(attn_own[:, :, :q_part])
    kv_own = attn_own[:, :, q_part : q_part + 2 * DH]
    kv_own = jnp.sum(kv_own.reshape(KV, share, -1, 2 * DH), axis=1)
    key_own = uncolumns(kv_own[:, :, :DH])
    value_own = uncolumns(kv_own[:, :, DH:])
    out_own = uncolumns(attn_own[:, :, q_part + 2 * DH :])
    gain_attn_grad = (
        jnp.sum(query_own * wq32, axis=1)
        + jnp.sum(key_own * wk32, axis=1)
        + jnp.sum(value_own * wv32, axis=1)
    )
    return (
        out_hidden[None],
        input_grad[None],
        gain_attn_grad,
        query_own * gain1,
        key_own * gain1,
        value_own * gain1,
        out_own.T,
        gain_ffn_grad,
        gate_own * gain2,
        up_own * gain2,
        down_own.T,
    )


def solution(mesh):
    devices = mesh.devices
    dp, seq = devices.shape
    inner = Mesh(devices.reshape(dp // TP, TP, seq), ("rep", "tp", "seq"))
    dps = ("rep", "tp")
    every = ("rep", "tp", "seq")
    token = P(dps, "seq", None)
    row = P(every, None)
    col = P(None, every)
    return jax.shard_map(
        per_device,
        mesh=inner,
        in_specs=(
            token,
            P(dps, None),
            P(dps, "seq"),
            P(every),
            row,
            row,
            row,
            col,
            P(every),
            row,
            row,
            col,
            token,
        ),
        out_specs=(token, token, P(every), row, row, row, col, P(every), row, row, col),
        check_vma=False,
    )
```

time: 1090 us -> 783 us (0.72)
  waiting for transfers between devices: 642 us -> 45.7 us
  Pallas kernels: 0 us -> 410 us
  blocking collectives: 114 us -> 0 us
  local copies, waits for them, and re-layouts: 53.4 us -> 66.4 us
    pallas_call x0 -> x12, Pallas kernels: none -> 410 us  [the longest x4 169 us: gather_plane(): pl.pallas_call(gather_kernel, out_shape=jax.ShapeDtypeStruct((plane, rows...]
    reduce_scatter x6 -> x3, waiting for transfers between devices: 278 us -> 45 us  [the longest x1 45 us: per_device(): lax.psum_scatter(gu_partial, 'rep', scatter_dimension=0, tiled=True)]
    all_gather x5 -> x1, waiting for transfers between devices: 222 us -> 0.02 us  [per_device(): attn_weight = lax.all_gather(attn_rows, 'rep', axis=0, tiled=True)]
    all_to_all x3 -> x0, blocking collectives: 114 us -> none  [the longest x1 54.9 us: per_device(): ffn_rows = lax.all_to_all(ffn_pack, in_plane, 0, 0, tiled=True)]
    all_gather x1, waiting for transfers between devices: 95.9 us -> 0.02 us  [per_device(): lax.all_gather(ffn_rows[:, :2 * ff_part], 'rep', axis=0, tiled=True)]
    all_gather x1, waiting for transfers between devices: 45.1 us -> 0.01 us  [per_device(): lax.all_gather(ffn_rows[:, 2 * ff_part:], 'rep', axis=0, tiled=True)]
    convert_element_type x5 -> x6, other arithmetic: 8.9 us -> 19.9 us  [the longest x1 12.7 us: per_device(): score_grad = (probs * (prob_grad - jnp.sum(probs * prob_grad, axis=-1, ke...]
  transfers between devices with their start and end apart: 14 -> 7, of which waited for: 11 -> 1; matrix products, arithmetic and copies ran while one was open for 19% -> 31% of each run, Pallas kernels for 0% -> 47%
where the time goes in v2:
time: 783 us; the launch traced here: 777 us
  Pallas kernels  410 us (52%)
  matrix products  182 us (23%)
  local copies, waits for them, and re-layouts  66.4 us (8%)
  other arithmetic  57.6 us (7%)
  waiting for transfers between devices  45.7 us (6%)
  between operations  15.4 us (2%)
    pallas_call x4, Pallas kernels, gather_plane(): pl.pallas_call(gather_kernel, out_shape=jax.ShapeDtypeStruct((plane, rows...  169 us
    pallas_call x4, Pallas kernels, scatter_plane(): pl.pallas_call(scatter_kernel, out_shape=jax.ShapeDtypeStruct((rows, widt...  158 us
    dot_general x12, matrix products, dot(): lax.dot_general(left, right, ((contract[:1], contract[1:]), ((), ())), pr...  132 us
    pallas_call x4, Pallas kernels, exchange_plane(): pl.pallas_call(exchange_kernel, out_shape=jax.ShapeDtypeStruct(blocks.sha...  81.9 us
    reduce_scatter x1, waiting for transfers between devices, per_device(): lax.psum_scatter(gu_partial, 'rep', scatter_dimension=0, tiled=True)  45 us
    unnamed x93, local copies, waits for them, and re-layouts  17.9 us
  transfers between devices with their start and end apart: 7, of which 1 were waited for; matrix products, arithmetic and copies ran while one was open for 31% of the time, Pallas kernels for 47%

profile of v2, /device:TPU:1, one launch (start us, length us, event | category | flops | bytes accessed | tf_op | source)
XLA Modules:
  0.0 777.0 jit_solution(15167165138893688680)
XLA Ops:
  11.4 13.7 %exchange_plane.4 = bf16[8,64,768]{2,1,0:T(8,128)(2,1)} custom-call(bf16[8,64,768]{2,1,0:T(8,128)(2,1)} %pad_maximum_fusion.8.in_ref), custom_call_target="tpu_custom_call" | custom-call | bytes 15728640 | tf_op jit(solution)/shard_map/exchange_plane/pallas_call | solution.py:319
  25.1 2.3 copy.154
  29.6 42.5 %gather_plane.4 = bf16[8,256,2048]{2,1,0:T(8,128)(2,1)} custom-call(bf16[256,2048]{1,0:T(8,128)(2,1)} %fusion.8.own_ref), custom_call_target="tpu_custom_call" | custom-call | bytes 100663296 | tf_op jit(solution)/shard_map/gather_plane/pallas_call | solution.py:174
  73.5 1.5 reshape.435
  75.1 2.5 reshape.436
  78.4 1.7 copy_bitcast_fusion.1
  80.1 3.1 concatenate.63.in_ref
  83.2 27.9 %exchange_plane.5 = bf16[8,64,2112]{2,1,0:T(8,128)(2,1)} custom-call(bf16[8,64,2112]{2,1,0:T(8,128)(2,1)} %concatenate.63.in_ref), custom_call_target="tpu_custom_call" | custom-call | bytes 43253760 | tf_op jit(solution)/shard_map/exchange_plane/pallas_call | solution.py:319
  111.2 2.6 slice.108
  114.2 2.1 slice.111
  122.1 3.1 and_or_fusion
  125.2 8.4 %fusion.16 = f32[2,1024,512]{1,2,0:T(8,128)S(1)} fusion(bf16[2,1024,2048]{2,1,0:T(8,128)(2,1)} %bitcast.189, bf16[2048,768]{0,1:T(8,128)(2,1)} %all-gather.4.cloned.1.call-done), kind=kOutput, calls=%fused_computation.45 | convolution fusion | flops 4294967296 | bytes 14680064 | tf_op jit(solution)/shard_map/dot_general | solution.py:57
  135.7 1.5 fusion.58
  137.2 3.2 copy.206
  140.4 3.2 copy.207
  143.5 3.1 subtract_convert_fusion.1
  146.7 5.4 fusion.4
  152.2 4.2 exponential_reduce_fusion
  156.3 1.6 copy-done.1
  157.9 12.2 %fusion.24 = bf16[2,1024,2,128]{1,3,2,0:T(8,128)(2,1)} fusion(f32[2,1024,512]{1,2,0:T(8,128)} %copy-done.14, f32[2,1024,1024,2]{2,1,3,0:T(8,128)} %copy-done.1, f32[2,2,1024]{2,1,0:T(2,128)S(1)} %log_add_fusion, pred[2,1024,1024]{1,2,0:T(8,128)(4,1)S(1)} %and_or_fusion), kind=kOutput, calls=%fused_computation.71 | convolution fusion | flops 1091043328 | bytes 20463616 | tf_op jit(solution)/shard_map/thqk,tkd->tqhd/dot_general | solution.py:438
  170.1 2.4 copy.161
  172.6 4.0 convolution_convert_fusion.3
  176.6 38.7 %scatter_plane.4 = f32[256,2048]{1,0:T(8,128)S(1)} custom-call(bf16[8,256,2048]{2,1,0:T(8,128)(2,1)S(1)} %bitcast.182), custom_call_target="tpu_custom_call" | custom-call | bytes 117440512 | tf_op jit(solution)/shard_map/scatter_plane/pallas_call | solution.py:269
  215.3 1.7 multiply_reduce_fusion.1
  217.0 43.0 %gather_plane.6 = bf16[8,256,2048]{2,1,0:T(8,128)(2,1)} custom-call(bf16[256,2048]{1,0:T(8,128)(2,1)} %get-tuple-element.20.own_ref), custom_call_target="tpu_custom_call" | custom-call | bytes 100663296 | tf_op jit(solution)/shard_map/gather_plane/pallas_call | solution.py:174
  261.1 42.3 %gather_plane.5 = bf16[8,256,2048]{2,1,0:T(8,128)(2,1)} custom-call(bf16[256,2048]{1,0:T(8,128)(2,1)} %multiply_convert_fusion.4.own_ref), custom_call_target="tpu_custom_call" | custom-call | bytes 100663296 | tf_op jit(solution)/shard_map/gather_plane/pallas_call | solution.py:174
  303.4 19.2 %fusion.59 = f32[2048,1408]{0,1:T(8,128)} fusion(bf16[2048,2048]{1,0:T(8,128)(2,1)} %bitcast.193, bf16[2048,1408]{1,0:T(8,128)(2,1)} %all-gather.6.cloned.1.call-done), kind=kOutput, calls=%fused_computation.151 | convolution fusion | flops 11811160064 | bytes 25690112 | tf_op jit(solution)/shard_map/dot_general | solution.py:57
  322.7 15.8 %multiply_convert_fusion.1 = (bf16[2048,704]{0,1:T(8,128)(2,1)S(1)}, bf16[2048,704]{0,1:T(8,128)(2,1)}, bf16[2048,704]{0,1:T(8,128)(2,1)S(1)}) fusion(f32[2048,1408]{0,1:T(8,128)} %fusion.59, bf16[2048,2048]{1,0:T(8,128)(2,1)} %bitcast.195, bf16[2048,704]{1,0:T(8,128)(2,1)} %all-gather.8.cloned.1.call-done), kind=kOutput, calls=%fused_computation.18 | convolution fusion | flops 5927206912 | bytes 31457280 | tf_op jit(solution)/shard_map/dot_general | solution.py:57
  338.5 1.6 copy-done.42
  340.0 11.1 %convolution_convert_fusion.5 = bf16[2048,704]{0,1:T(8,128)(2,1)} fusion(bf16[2048,704]{0,1:T(8,128)(2,1)S(1)} %get-tuple-element.31, bf16[2048,2048]{1,0:T(8,128)(2,1)} %bitcast.196), kind=kOutput, calls=%fused_computation.23 | convolution fusion | flops 5907021824 | bytes 14155776 | tf_op jit(solution)/shard_map/dot_general | solution.py:57
  351.2 18.1 %convolution_convert_fusion.4 = bf16[2048,1408]{1,0:T(8,128)(2,1)} fusion(bf16[2048,2048]{1,0:T(8,128)(2,1)} %bitcast.194, bf16[2048,704]{0,1:T(8,128)(2,1)} %get-tuple-element.30, bf16[2048,704]{0,1:T(8,128)(2,1)S(1)} %get-tuple-element.29), kind=kOutput, calls=%fused_computation.15 | convolution fusion | flops 11825577984 | bytes 19922944 | tf_op jit(solution)/shard_map/dot_general | solution.py:57
  369.3 18.6 %convolution_convert_fusion.1 = bf16[2048,2048]{1,0:T(8,128)(2,1)} fusion(bf16[2048,1408]{1,0:T(8,128)(2,1)} %all-gather.6.cloned.1.call-done, bf16[2048,704]{0,1:T(8,128)(2,1)} %get-tuple-element.30, bf16[2048,704]{0,1:T(8,128)(2,1)S(1)} %get-tuple-element.29), kind=kOutput, calls=%fused_computation.12 | convolution fusion | flops 11826888704 | bytes 19922944 | tf_op jit(solution)/shard_map/dot_general | solution.py:57
  387.9 3.5 copy-done
  391.3 39.5 %scatter_plane.5 = f32[256,2048]{1,0:T(8,128)S(1)} custom-call(bf16[8,256,2048]{2,1,0:T(8,128)(2,1)S(1)} %bitcast.184), custom_call_target="tpu_custom_call" | custom-call | bytes 117440512 | tf_op jit(solution)/shard_map/scatter_plane/pallas_call | solution.py:269
  432.0 1.6 multiply_convert_fusion.3.own_ref
  433.6 41.7 %gather_plane.7 = bf16[8,256,2048]{2,1,0:T(8,128)(2,1)} custom-call(bf16[256,2048]{1,0:T(8,128)(2,1)} %multiply_convert_fusion.3.own_ref), custom_call_target="tpu_custom_call" | custom-call | bytes 100663296 | tf_op jit(solution)/shard_map/gather_plane/pallas_call | solution.py:174
  475.3 7.0 convolution_convert_fusion.8
  482.3 2.1 reshape.442
  484.4 13.5 %fusion = (f32[2,2,1024]{2,1,0:T(2,128)S(1)}, f32[2,1024,1024,2]{2,1,3,0:T(8,128)}) fusion(f32[2,1024,1024,2]{2,1,3,0:T(8,128)} %copy-done.1, f32[2,2,1024]{2,1,0:T(2,128)S(1)} %log_add_fusion, pred[2,1024,1024]{1,2,0:T(8,128)(4,1)} %copy-done.5, bf16[2,1024,2,128]{3,2,1,0:T(2,128)(2,1)} %reshape.442, f32[2,1024,512]{1,2,0:T(8,128)} %copy-done.14), kind=kOutput, calls=%fused_computation.2 | convolution fusion | flops 1094709248 | bytes 37257216 | tf_op jit(solution)/shard_map/tqhd,tkd->thqk/dot_general | solution.py:471
  497.9 12.7 %fusion.2 = bf16[2,2,1024,1024]{2,3,1,0:T(8,128)(2,1)S(1)} fusion(f32[2,1024,1024,2]{2,1,3,0:T(8,128)} %get-tuple-element.76, f32[2,1024,1024,2]{2,1,3,0:T(8,128)} %copy-done.1, f32[2,2,1024]{2,1,0:T(2,128)S(1)} %get-tuple-element.75, f32[2,2,1024]{2,1,0:T(2,128)S(1)} %log_add_fusion, pred[2,1024,1024]{1,2,0:T(8,128)(4,1)S(1)} %copy-done.6), kind=kLoop, calls=%fused_computation.4 | loop fusion | flops 25165824 | bytes 44072960 | tf_op jit(solution)/shard_map/convert_element_type | solution.py:474
  510.7 3.5 multiply_bitcast_fusion
  517.8 3.0 fusion.25
  521.7 2.0 copy.202
  524.7 7.0 convolution_convert_fusion.7
  531.6 12.2 %fusion.26 = bf16[2,1024,128]{2,1,0:T(8,128)(2,1)} fusion(bf16[2,1024,2,128]{3,2,1,0:T(2,128)(2,1)} %reshape.442, f32[2,1024,1024,2]{2,1,3,0:T(8,128)} %copy-done.1, f32[2,2,1024]{2,1,0:T(2,128)S(1)} %log_add_fusion, pred[2,1024,1024]{1,2,0:T(8,128)(4,1)} %copy-done.5), kind=kOutput, calls=%fused_computation.75 | convolution fusion | flops 1090781184 | bytes 20463616 | tf_op jit(solution)/shard_map/thqk,tqhd->tkd/dot_general | solution.py:468
  543.8 8.8 %convolution_convert_fusion.6 = bf16[2048,512]{0,1:T(8,128)(2,1)S(1)} fusion(bf16[2048,2048]{1,0:T(8,128)(2,1)} %bitcast.190, bf16[2048,128]{1,0:T(8,128)(2,1)} %bitcast.223, bf16[2048,64]{1,0:T(8,128)(2,1)} %bitcast.214, bf16[2048,64]{1,0:T(8,128)(2,1)} %bitcast.212, bf16[2048,256]{1,0:T(8,128)(2,1)} %bitcast.206), kind=kOutput, calls=%fused_computation.28 | convolution fusion | flops 4304404480 | bytes 12582912 | tf_op jit(solution)/shard_map/dot_general | solution.py:57
  552.6 1.9 pad_maximum_fusion.3
  555.1 6.9 convolution_convert_fusion
  562.0 39.7 %scatter_plane.6 = f32[256,2048]{1,0:T(8,128)S(1)} custom-call(bf16[8,256,2048]{2,1,0:T(8,128)(2,1)S(1)} %bitcast.183), custom_call_target="tpu_custom_call" | custom-call | bytes 117440512 | tf_op jit(solution)/shard_map/scatter_plane/pallas_call | solution.py:269
  601.7 7.2 convolution_convert_fusion.2
  609.0 40.3 %scatter_plane.7 = f32[256,2048]{1,0:T(8,128)S(1)} custom-call(bf16[8,256,2048]{2,1,0:T(8,128)(2,1)S(1)} %bitcast.185), custom_call_target="tpu_custom_call" | custom-call | bytes 117440512 | tf_op jit(solution)/shard_map/scatter_plane/pallas_call | solution.py:269
  650.9 2.8 fusion.14
  655.2 2.3 copy.178
  657.5 12.0 %exchange_plane.6 = bf16[8,64,768]{2,1,0:T(8,128)(2,1)} custom-call(bf16[8,64,768]{2,1,0:T(8,128)(2,1)} %bitcast.203), custom_call_target="tpu_custom_call" | custom-call | bytes 15728640 | tf_op jit(solution)/shard_map/exchange_plane/pallas_call | solution.py:319
  674.3 45.0 %reduce-scatter.6.cloned.1.call-done = bf16[512,1408]{1,0:T(8,128)(2,1)} async-done(((bf16[2048,1408]{1,0:T(8,128)(2,1)}), bf16[512,1408]{1,0:T(8,128)(2,1)}) %reduce-scatter.6.cloned.1.call-update) | async-done | bytes 1441808 | tf_op jit(solution)/shard_map/reduce_scatter | solution.py:460
  719.3 2.9 pad_maximum_fusion.4
  722.2 28.3 %exchange_plane.7 = bf16[8,64,2112]{2,1,0:T(8,128)(2,1)} custom-call(bf16[8,64,2112]{2,1,0:T(8,128)(2,1)} %bitcast.188), custom_call_target="tpu_custom_call" | custom-call | bytes 43253760 | tf_op jit(solution)/shard_map/exchange_plane/pallas_call | solution.py:319
  750.6 2.0 convert_element_type.204
  753.2 2.1 copy.184
  755.3 2.8 reshape.453
  758.1 2.1 copy.185
  760.2 2.8 reshape.454
  763.9 1.7 reshape.455
  765.6 3.9 broadcast_multiply_fusion
  (160 shorter events, 35.2 us)
Async XLA Ops:
  7.2 118.0 %all-gather.4.cloned.1.call-start = ((), (), s32[]{:S(2)}) async-start(), calls=%async_computation.3 | async-start | bytes 3932160 | tf_op jit(solution)/shard_map/all_gather | solution.py:390
  10.4 17.1 %copy-start.7 = (bf16[1,256,2048]{2,1,0:T(8,128)(2,1)S(1)}, bf16[1,256,2048]{2,1,0:T(8,128)(2,1)}, u32[]{:S(2)}) copy-start(bf16[1,256,2048]{2,1,0:T(8,128)(2,1)} %param.13) | copy-start | bytes 3145732
  27.4 276.0 %all-gather.6.cloned.1.call-start = ((), (), s32[]{:S(2)}) async-start(), calls=%async_computation.4 | async-start | bytes 7208960 | tf_op jit(solution)/shard_map/all_gather | solution.py:412
  27.8 0.6 copy-start.34
  29.6 42.5 %copy-start.21 = (bf16[64,5632]{1,0:T(8,128)(2,1)S(1)}, bf16[64,5632]{1,0:T(8,128)(2,1)}, u32[]{:S(2)}) copy-start(bf16[64,5632]{1,0:T(8,128)(2,1)} %param.23) | copy-start | bytes 2162692
  29.6 42.6 %copy-start.37 = (f32[64]{0:T(128)S(1)}, f32[64]{0:T(128)}, u32[]{:S(2)}) copy-start(f32[64]{0:T(128)} %param.21) | copy-start | bytes 772
  111.2 2.7 copy-start.40
  113.8 7.1 copy-start.39
  113.8 208.9 %all-gather.8.cloned.1.call-start = ((), (), s32[]{:S(2)}) async-start(), calls=%async_computation.5 | async-start | bytes 3932160 | tf_op jit(solution)/shard_map/all_gather | solution.py:411
  113.8 8.1 %collective-permute-start = (s32[1,2]{1,0:T(1,128)S(1)}, s32[1,2]{1,0:T(1,128)S(1)}, u32[]{:S(2)}, u32[]{:S(2)}) collective-permute-start(s32[1,2]{1,0:T(1,128)S(1)} %copy-done.40), channel_id=1, source_target_pairs={{0,4},{4,0},{1,5},{5,1},{2,6},{6,2},{3,7},{7,3},{8,12},{12,8},{9,1... | collective-permute-start | bytes 32 | tf_op jit(solution)/shard_map/ppermute | solution.py:415
  116.3 537.5 %reduce-scatter.8.cloned.1.call-start = ((), (), s32[]{:S(2)}) async-start(), calls=%async_computation.8 | async-start | bytes 3604480 | tf_op jit(solution)/shard_map/reduce_scatter | solution.py:459
  118.8 3.2 copy-start.22
  118.8 3.2 copy-start.24
  118.8 14.9 %copy-start.19 = (f32[1024,64]{0,1:T(8,128)}, f32[1024,64]{0,1:T(8,128)S(1)}, u32[]{:S(2)}) copy-start(f32[1024,64]{0,1:T(8,128)S(1)} %get-tuple-element.63) | copy-start | bytes 786436
  125.2 32.7 %copy-start.5 = (pred[2,1024,1024]{1,2,0:T(8,128)(4,1)}, pred[2,1024,1024]{1,2,0:T(8,128)(4,1)S(1)}, u32[]{:S(2)}) copy-start(pred[2,1024,1024]{1,2,0:T(8,128)(4,1)S(1)} %and_or_fusion) | copy-start | bytes 6291460
  133.6 2.1 copy-start.14
  133.6 1.1 copy-start.25
  143.5 3.1 copy-start.29
  146.6 5.5 copy-start.15
  146.7 5.5 copy-start.17
  152.1 5.8 copy-start.1
  172.6 4.0 copy-start.11
  176.5 38.7 %copy-start.9 = (bf16[1,256,2048]{2,1,0:T(8,128)(2,1)S(1)}, bf16[1,256,2048]{2,1,0:T(8,128)(2,1)}, u32[]{:S(2)}) copy-start(bf16[1,256,2048]{2,1,0:T(8,128)(2,1)} %param.25) | copy-start | bytes 3145732
  217.0 43.0 %copy-start.2 = (f32[256,2048]{1,0:T(8,128)}, f32[256,2048]{1,0:T(8,128)S(1)}, u32[]{:S(2)}) copy-start(f32[256,2048]{1,0:T(8,128)S(1)} %get-tuple-element.26) | copy-start | bytes 6291460
  338.5 1.6 copy-start.42
  351.1 304.0 %reduce-scatter.4.cloned.1.call-start = ((), (), s32[]{:S(2)}) async-start(), calls=%async_computation.6 | async-start | bytes 3932160 | tf_op jit(solution)/shard_map/reduce_scatter | solution.py:492
  387.8 3.5 copy-start
  391.3 39.5 %copy-start.3 = (f32[256,2048]{1,0:T(8,128)S(1)}, f32[256,2048]{1,0:T(8,128)}, u32[]{:S(2)}) copy-start(f32[256,2048]{1,0:T(8,128)} %copy-done.2) | copy-start | bytes 6291460
  430.8 1.2 copy-start.10
  484.4 13.5 %copy-start.6 = (pred[2,1024,1024]{1,2,0:T(8,128)(4,1)S(1)}, pred[2,1024,1024]{1,2,0:T(8,128)(4,1)}, u32[]{:S(2)}) copy-start(pred[2,1024,1024]{1,2,0:T(8,128)(4,1)} %copy-done.5) | copy-start | bytes 6291460
  497.9 12.7 %copy-start.30 = (bf16[2,1024,64]{1,2,0:T(8,128)(2,1)S(1)}, bf16[2,1024,64]{1,2,0:T(8,128)(2,1)}, u32[]{:S(2)}) copy-start(bf16[2,1024,64]{1,2,0:T(8,128)(2,1)} %get-tuple-element.34) | copy-start | bytes 786436
  497.9 12.7 %copy-start.31 = (bf16[2,1024,64]{1,2,0:T(8,128)(2,1)S(1)}, bf16[2,1024,64]{1,2,0:T(8,128)(2,1)}, u32[]{:S(2)}) copy-start(bf16[2,1024,64]{1,2,0:T(8,128)(2,1)} %get-tuple-element.35) | copy-start | bytes 786436
  510.7 3.6 copy-start.13
  510.7 3.6 copy-start.26
  515.0 2.8 copy-start.16
  515.6 2.2 copy-start.18
  517.8 3.0 copy-start.20
  517.8 3.0 copy-start.23
  543.8 8.8 %copy-start.28 = (bf16[2048,256]{0,1:T(8,128)(2,1)S(1)}, bf16[2048,256]{0,1:T(8,128)(2,1)}, u32[]{:S(2)}) copy-start(bf16[2048,256]{0,1:T(8,128)(2,1)} %convolution_convert_fusion.7) | copy-start | bytes 3145732
  554.5 164.8 %reduce-scatter.6.cloned.1.call-start = ((), (), s32[]{:S(2)}) async-start(), calls=%async_computation.7 | async-start | bytes 7208960 | tf_op jit(solution)/shard_map/reduce_scatter | solution.py:460
  562.0 39.7 %copy-start.41 = (bf16[2048,704]{1,0:T(8,128)(2,1)S(1)}, bf16[2048,704]{1,0:T(8,128)(2,1)}, u32[]{:S(2)}) copy-start(bf16[2048,704]{1,0:T(8,128)(2,1)} %all-gather.8.cloned.1.call-done) | copy-start | bytes 8650756
  562.0 39.7 %copy-start.43 = (bf16[2048,704]{0,1:T(8,128)(2,1)S(1)}, bf16[2048,704]{0,1:T(8,128)(2,1)}, u32[]{:S(2)}) copy-start(bf16[2048,704]{0,1:T(8,128)(2,1)} %copy-done.42) | copy-start | bytes 8650756
  608.9 40.3 %copy-start.8 = (bf16[1,256,2048]{2,1,0:T(8,128)(2,1)S(1)}, bf16[1,256,2048]{2,1,0:T(8,128)(2,1)}, u32[]{:S(2)}) copy-start(bf16[1,256,2048]{2,1,0:T(8,128)(2,1)} %param.13) | copy-start | bytes 3145732
  609.0 40.3 %copy-start.35 = (f32[256]{0:T(256)S(1)}, f32[256]{0:T(256)}, u32[]{:S(2)}) copy-start(f32[256]{0:T(256)} %copy-done.34) | copy-start | bytes 3076
  649.3 1.7 copy-start.4
  670.7 1.1 copy-start.32
  670.7 1.1 copy-start.33
  670.7 1.1 copy-start.36
  670.8 2.0 copy-start.27
  763.0 2.6 copy-start.38
  763.9 1.7 copy-start.12
Sparse Core Ops, SparseCore 0:
  27.5 63.8 all-gather.3
  113.9 106.4 all-gather.5
  222.0 61.4 all-gather.7
  351.3 55.6 reduce-scatter.7
  554.6 59.9 reduce-scatter.3
  616.7 102.5 reduce-scatter.5

commit v3 on v2

--- a/solution.py
+++ b/solution.py
@@ -396,7 +396,6 @@
     upstream = cotangent.reshape(local_len, width).astype(F32)
     scale1 = rms_scale(tokens)
     norm1 = tokens * scale1
-    norm1_all = gather_plane(after(norm1.astype(BF), attn_rows), 1)
 
     ffn_pack = jnp.concatenate(
         [
@@ -406,11 +405,12 @@
         ],
         axis=2,
     )
-    ffn_rows = exchange_plane(after(ffn_pack, norm1_all), 2)
+    ffn_rows = exchange_plane(after(ffn_pack, attn_rows), 2)
     ffn_rows = ffn_rows.reshape(-1, ffn_rows.shape[2])
     down_weight = lax.all_gather(ffn_rows[:, 2 * ff_part :], "rep", axis=0, tiled=True)
     gu_weight = lax.all_gather(ffn_rows[:, : 2 * ff_part], "rep", axis=0, tiled=True)
-    ffn_grad = gather_plane(after((keep * upstream).astype(BF), ffn_rows), 3)
+    norm1_all = gather_plane(after(norm1.astype(BF), ffn_rows), 1)
+    ffn_grad = gather_plane(after((keep * upstream).astype(BF), norm1_all), 3)
 
     other_starts = lax.ppermute(pic_starts, "tp", [(0, 1), (1, 0)])
     starts = jnp.where(
@@ -489,6 +489,7 @@
     attn_partial = jnp.concatenate(
         [tn(norm1_all, qkv_grad).astype(BF), tn(branch_grad, mixed).astype(BF)], axis=1
     )
+    attn_partial = after(attn_partial, gu_sums, down_sums)
     attn_sums = lax.psum_scatter(attn_partial, "rep", scatter_dimension=0, tiled=True)
     scaled1 = scatter_plane(after(nt(qkv_grad, qkv_weight).astype(BF), attn_partial), 8)
     input_grad = hidden_grad + scale1 * (

time: 783 us -> 755 us (0.964)
  waiting for transfers between devices: 45.7 us -> 0.15 us
  local copies, waits for them, and re-layouts: 66.4 us -> 79.7 us
    reduce_scatter x1, waiting for transfers between devices: 45 us -> 0.01 us  [per_device(): lax.psum_scatter(gu_partial, 'rep', scatter_dimension=0, tiled=True)]
    unnamed x93 -> x111, local copies, waits for them, and re-layouts: 17.9 us -> 23.7 us
  transfers between devices with their start and end apart: 7 -> 7, of which waited for: 1 -> 0; matrix products, arithmetic and copies ran while one was open for 31% -> 36% of each run, Pallas kernels for 47% -> 51%
where the time goes in v3:
time: 755 us; the launch traced here: 750 us
  Pallas kernels  409 us (54%)
  matrix products  188 us (25%)
  local copies, waits for them, and re-layouts  79.7 us (11%)
  other arithmetic  56.5 us (7%)
  between operations  15.3 us (2%)
    pallas_call x4, Pallas kernels, gather_plane(): pl.pallas_call(gather_kernel, out_shape=jax.ShapeDtypeStruct((plane, rows...  168 us
    pallas_call x4, Pallas kernels, scatter_plane(): pl.pallas_call(scatter_kernel, out_shape=jax.ShapeDtypeStruct((rows, widt...  159 us
    dot_general x12, matrix products, dot(): lax.dot_general(left, right, ((contract[:1], contract[1:]), ((), ())), pr...  138 us
    pallas_call x4, Pallas kernels, exchange_plane(): pl.pallas_call(exchange_kernel, out_shape=jax.ShapeDtypeStruct(blocks.sha...  81.2 us
    unnamed x111, local copies, waits for them, and re-layouts  23.7 us
  transfers between devices with their start and end apart: 7, of which 0 were waited for; matrix products, arithmetic and copies ran while one was open for 36% of the time, Pallas kernels for 51%

profile of v3, /device:TPU:1, one launch (start us, length us, event | category | flops | bytes accessed | tf_op | source)
XLA Modules:
  0.0 750.0 jit_solution(15031152398464525515)
XLA Ops:
  11.4 13.7 %exchange_plane.4 = bf16[8,64,768]{2,1,0:T(8,128)(2,1)} custom-call(bf16[8,64,768]{2,1,0:T(8,128)(2,1)} %pad_maximum_fusion.8.in_ref), custom_call_target="tpu_custom_call" | custom-call | bytes 15728640 | tf_op jit(solution)/shard_map/exchange_plane/pallas_call | solution.py:319
  25.1 2.3 copy.157
  28.5 2.5 reshape.425
  33.3 3.1 concatenate.58.in_ref
  36.4 28.0 %exchange_plane.5 = bf16[8,64,2112]{2,1,0:T(8,128)(2,1)} custom-call(bf16[8,64,2112]{2,1,0:T(8,128)(2,1)} %concatenate.58.in_ref), custom_call_target="tpu_custom_call" | custom-call | bytes 43253760 | tf_op jit(solution)/shard_map/exchange_plane/pallas_call | solution.py:319
  64.4 2.6 slice.108
  68.2 2.1 slice.111
  74.1 42.2 %gather_plane.4 = bf16[8,256,2048]{2,1,0:T(8,128)(2,1)} custom-call(bf16[256,2048]{1,0:T(8,128)(2,1)} %fusion.8.own_ref), custom_call_target="tpu_custom_call" | custom-call | bytes 100663296 | tf_op jit(solution)/shard_map/gather_plane/pallas_call | solution.py:174
  116.3 1.8 fusion.47
  120.3 3.0 and_or_fusion
  123.3 8.4 %fusion.16 = f32[2,1024,512]{1,2,0:T(8,128)S(1)} fusion(bf16[2,1024,2048]{2,1,0:T(8,128)(2,1)} %bitcast.189, bf16[2048,768]{0,1:T(8,128)(2,1)} %all-gather.4.cloned.1.call-done), kind=kOutput, calls=%fused_computation.45 | convolution fusion | flops 4294967296 | bytes 14680064 | tf_op jit(solution)/shard_map/dot_general | solution.py:57
  135.3 3.2 copy.206
  138.5 3.2 copy.207
  141.6 3.1 subtract_convert_fusion.1
  144.7 5.4 fusion.4
  150.2 4.5 exponential_reduce_fusion
  156.6 12.1 %fusion.24 = bf16[2,1024,2,128]{1,3,2,0:T(8,128)(2,1)} fusion(f32[2,1024,512]{1,2,0:T(8,128)} %copy-done.19, f32[2,1024,1024,2]{2,1,3,0:T(8,128)} %copy-done.7, f32[2,2,1024]{2,1,0:T(2,128)S(1)} %log_add_fusion, pred[2,1024,1024]{1,2,0:T(8,128)(4,1)S(1)} %and_or_fusion), kind=kOutput, calls=%fused_computation.71 | convolution fusion | flops 1091043328 | bytes 20463616 | tf_op jit(solution)/shard_map/thqk,tkd->tqhd/dot_general | solution.py:438
  168.7 2.5 copy.164
  171.2 4.0 convolution_convert_fusion.3
  175.2 40.3 %scatter_plane.4 = f32[256,2048]{1,0:T(8,128)S(1)} custom-call(bf16[8,256,2048]{2,1,0:T(8,128)(2,1)S(1)} %bitcast.182), custom_call_target="tpu_custom_call" | custom-call | bytes 117440512 | tf_op jit(solution)/shard_map/scatter_plane/pallas_call | solution.py:269
  215.4 1.7 multiply_reduce_fusion.1
  217.1 41.9 %gather_plane.6 = bf16[8,256,2048]{2,1,0:T(8,128)(2,1)} custom-call(bf16[256,2048]{1,0:T(8,128)(2,1)} %get-tuple-element.21.own_ref), custom_call_target="tpu_custom_call" | custom-call | bytes 100663296 | tf_op jit(solution)/shard_map/gather_plane/pallas_call | solution.py:174
  260.2 42.5 %gather_plane.5 = bf16[8,256,2048]{2,1,0:T(8,128)(2,1)} custom-call(bf16[256,2048]{1,0:T(8,128)(2,1)} %multiply_convert_fusion.4.own_ref), custom_call_target="tpu_custom_call" | custom-call | bytes 100663296 | tf_op jit(solution)/shard_map/gather_plane/pallas_call | solution.py:174
  302.7 19.0 %fusion.59 = f32[2048,1408]{0,1:T(8,128)} fusion(bf16[2048,2048]{1,0:T(8,128)(2,1)} %bitcast.193, bf16[2048,1408]{1,0:T(8,128)(2,1)} %all-gather.6.cloned.1.call-done), kind=kOutput, calls=%fused_computation.151 | convolution fusion | flops 11811160064 | bytes 25690112 | tf_op jit(solution)/shard_map/dot_general | solution.py:57
  321.7 15.6 %multiply_convert_fusion.1 = (bf16[2048,704]{0,1:T(8,128)(2,1)S(1)}, bf16[2048,704]{0,1:T(8,128)(2,1)}, bf16[2048,704]{0,1:T(8,128)(2,1)S(1)}) fusion(f32[2048,1408]{0,1:T(8,128)} %fusion.59, bf16[2048,2048]{1,0:T(8,128)(2,1)} %bitcast.195, bf16[2048,704]{1,0:T(8,128)(2,1)} %all-gather.8.cloned.1.call-done), kind=kOutput, calls=%fused_computation.18 | convolution fusion | flops 5927206912 | bytes 31457280 | tf_op jit(solution)/shard_map/dot_general | solution.py:57
  337.3 1.6 copy-done.51
  338.9 11.1 %convolution_convert_fusion.5 = bf16[2048,704]{0,1:T(8,128)(2,1)} fusion(bf16[2048,704]{0,1:T(8,128)(2,1)S(1)} %get-tuple-element.33, bf16[2048,2048]{1,0:T(8,128)(2,1)} %bitcast.196), kind=kOutput, calls=%fused_computation.23 | convolution fusion | flops 5907021824 | bytes 14155776 | tf_op jit(solution)/shard_map/dot_general | solution.py:57
  351.0 18.1 %convolution_convert_fusion.4 = bf16[2048,1408]{1,0:T(8,128)(2,1)} fusion(bf16[2048,2048]{1,0:T(8,128)(2,1)} %bitcast.194, bf16[2048,704]{0,1:T(8,128)(2,1)} %get-tuple-element.32, bf16[2048,704]{0,1:T(8,128)(2,1)S(1)} %get-tuple-element.31), kind=kOutput, calls=%fused_computation.15 | convolution fusion | flops 11825577984 | bytes 19922944 | tf_op jit(solution)/shard_map/dot_general | solution.py:57
  369.2 18.9 %convolution_convert_fusion.1 = bf16[2048,2048]{1,0:T(8,128)(2,1)} fusion(bf16[2048,1408]{1,0:T(8,128)(2,1)} %all-gather.6.cloned.1.call-done, bf16[2048,704]{0,1:T(8,128)(2,1)} %get-tuple-element.32, bf16[2048,704]{0,1:T(8,128)(2,1)S(1)} %get-tuple-element.31), kind=kOutput, calls=%fused_computation.12 | convolution fusion | flops 11826888704 | bytes 19922944 | tf_op jit(solution)/shard_map/dot_general | solution.py:57
  388.1 3.4 copy-done.6
  391.5 39.6 %scatter_plane.5 = f32[256,2048]{1,0:T(8,128)S(1)} custom-call(bf16[8,256,2048]{2,1,0:T(8,128)(2,1)S(1)} %bitcast.185), custom_call_target="tpu_custom_call" | custom-call | bytes 117440512 | tf_op jit(solution)/shard_map/scatter_plane/pallas_call | solution.py:269
  432.4 1.6 multiply_convert_fusion.3.own_ref
  434.0 41.8 %gather_plane.7 = bf16[8,256,2048]{2,1,0:T(8,128)(2,1)} custom-call(bf16[256,2048]{1,0:T(8,128)(2,1)} %multiply_convert_fusion.3.own_ref), custom_call_target="tpu_custom_call" | custom-call | bytes 100663296 | tf_op jit(solution)/shard_map/gather_plane/pallas_call | solution.py:174
  475.8 7.1 convolution_convert_fusion.8
  482.9 2.1 reshape.442
  485.0 13.6 %fusion = (f32[2,2,1024]{2,1,0:T(2,128)S(1)}, f32[2,1024,1024,2]{2,1,3,0:T(8,128)}) fusion(f32[2,1024,1024,2]{2,1,3,0:T(8,128)} %copy-done.7, f32[2,2,1024]{2,1,0:T(2,128)S(1)} %copy-done.42, pred[2,1024,1024]{1,2,0:T(8,128)(4,1)} %copy-done.11, bf16[2,1024,2,128]{3,2,1,0:T(2,128)(2,1)} %reshape.442, f32[2,1024,512]{1,2,0:T(8,128)} %copy-done.19), kind=kOutput, calls=%fused_computation.2 | convolution fusion | flops 1094709248 | bytes 37257216 | tf_op jit(solution)/shard_map/tqhd,tkd->thqk/dot_general | solution.py:471
  498.6 12.5 %fusion.2 = bf16[2,2,1024,1024]{2,3,1,0:T(8,128)(2,1)S(1)} fusion(f32[2,1024,1024,2]{2,1,3,0:T(8,128)} %get-tuple-element.78, f32[2,1024,1024,2]{2,1,3,0:T(8,128)} %copy-done.7, f32[2,2,1024]{2,1,0:T(2,128)S(1)} %get-tuple-element.77, f32[2,2,1024]{2,1,0:T(2,128)S(1)} %copy-done.42, pred[2,1024,1024]{1,2,0:T(8,128)(4,1)S(1)} %copy-done.12), kind=kLoop, calls=%fused_computation.4 | loop fusion | flops 25165824 | bytes 44072960 | tf_op jit(solution)/shard_map/convert_element_type | solution.py:474
  511.2 3.5 multiply_bitcast_fusion
  518.3 3.0 fusion.25
  522.3 2.0 copy.202
  524.3 2.0 copy.203
  526.2 7.0 convolution_convert_fusion.7
  533.2 12.2 %fusion.26 = bf16[2,1024,128]{2,1,0:T(8,128)(2,1)} fusion(bf16[2,1024,2,128]{3,2,1,0:T(2,128)(2,1)} %reshape.442, f32[2,1024,1024,2]{2,1,3,0:T(8,128)} %copy-done.7, f32[2,2,1024]{2,1,0:T(2,128)S(1)} %copy-done.42, pred[2,1024,1024]{1,2,0:T(8,128)(4,1)} %copy-done.11), kind=kOutput, calls=%fused_computation.75 | convolution fusion | flops 1090781184 | bytes 20463616 | tf_op jit(solution)/shard_map/thqk,tqhd->tkd/dot_general | solution.py:468
  545.4 8.8 %convolution_convert_fusion.6 = bf16[2048,512]{0,1:T(8,128)(2,1)S(1)} fusion(bf16[2048,2048]{1,0:T(8,128)(2,1)} %bitcast.190, bf16[2048,128]{1,0:T(8,128)(2,1)} %bitcast.223, bf16[2048,64]{1,0:T(8,128)(2,1)} %bitcast.214, bf16[2048,64]{1,0:T(8,128)(2,1)} %bitcast.212, bf16[2048,256]{1,0:T(8,128)(2,1)} %bitcast.206), kind=kOutput, calls=%fused_computation.28 | convolution fusion | flops 4304404480 | bytes 12582912 | tf_op jit(solution)/shard_map/dot_general | solution.py:57
  554.1 1.9 pad_maximum_fusion.3
  556.1 10.8 %convolution_convert_fusion = bf16[2048,2048]{1,0:T(8,128)(2,1)} fusion(bf16[2048,768]{0,1:T(8,128)(2,1)} %all-gather.4.cloned.1.call-done, bf16[2048,128]{1,0:T(8,128)(2,1)} %bitcast.224, bf16[2048,64]{1,0:T(8,128)(2,1)} %bitcast.215, bf16[2048,64]{1,0:T(8,128)(2,1)} %bitcast.213, bf16[2048,256]{1,0:T(8,128)(2,1)} %bitcast.207), kind=kOutput, calls=%fused_computation.11 | convolution fusion | flops 4307550208 | bytes 13107200 | tf_op jit(solution)/shard_map/dot_general | solution.py:57
  566.8 9.2 %convolution_convert_fusion.2 = bf16[2048,2048]{1,0:T(8,128)(2,1)} fusion(bf16[2048,704]{0,1:T(8,128)(2,1)S(1)} %copy-done.52, bf16[2048,704]{1,0:T(8,128)(2,1)S(1)} %copy-done.50), kind=kOutput, calls=%fused_computation.13 | convolution fusion | flops 5909774336 | bytes 14155776 | tf_op jit(solution)/shard_map/dot_general | solution.py:57
  576.0 2.3 copy.183
  578.3 3.4 copy-done.4
  581.6 39.7 %scatter_plane.6 = f32[256,2048]{1,0:T(8,128)S(1)} custom-call(bf16[8,256,2048]{2,1,0:T(8,128)(2,1)S(1)} %bitcast.183), custom_call_target="tpu_custom_call" | custom-call | bytes 117440512 | tf_op jit(solution)/shard_map/scatter_plane/pallas_call | solution.py:269
  622.7 39.9 %scatter_plane.7 = f32[256,2048]{1,0:T(8,128)S(1)} custom-call(bf16[8,256,2048]{2,1,0:T(8,128)(2,1)S(1)} %bitcast.184), custom_call_target="tpu_custom_call" | custom-call | bytes 117440512 | tf_op jit(solution)/shard_map/scatter_plane/pallas_call | solution.py:269
  665.5 27.4 %exchange_plane.7 = bf16[8,64,2112]{2,1,0:T(8,128)(2,1)} custom-call(bf16[8,64,2112]{2,1,0:T(8,128)(2,1)} %bitcast.188), custom_call_target="tpu_custom_call" | custom-call | bytes 43253760 | tf_op jit(solution)/shard_map/exchange_plane/pallas_call | solution.py:319
  692.9 2.0 convert_element_type.204
  694.9 2.2 slice_bitcast_fusion
  697.1 2.1 copy.184
  699.2 2.8 reshape.453
  702.0 3.5 copy.185
  705.5 2.8 reshape.454
  708.3 3.5 copy.186
  711.8 2.9 reshape.455
  714.8 4.4 broadcast_multiply_fusion
  720.8 2.8 fusion.14
  723.7 2.3 copy.178
  726.0 12.2 %exchange_plane.6 = bf16[8,64,768]{2,1,0:T(8,128)(2,1)} custom-call(bf16[8,64,768]{2,1,0:T(8,128)(2,1)} %bitcast.203), custom_call_target="tpu_custom_call" | custom-call | bytes 15728640 | tf_op jit(solution)/shard_map/exchange_plane/pallas_call | solution.py:319
  (178 shorter events, 38.7 us)
Async XLA Ops:
  7.2 116.1 %all-gather.4.cloned.1.call-start = ((), (), s32[]{:S(2)}) async-start(), calls=%async_computation.3 | async-start | bytes 3932160 | tf_op jit(solution)/shard_map/all_gather | solution.py:390
  10.4 17.1 %copy-start.27 = (bf16[64,5632]{1,0:T(8,128)(2,1)S(1)}, bf16[64,5632]{1,0:T(8,128)(2,1)}, u32[]{:S(2)}) copy-start(bf16[64,5632]{1,0:T(8,128)(2,1)} %param.23) | copy-start | bytes 2162692
  10.4 17.1 %copy-start.28 = (bf16[64,5632]{1,0:T(8,128)(2,1)S(1)}, bf16[64,5632]{1,0:T(8,128)(2,1)}, u32[]{:S(2)}) copy-start(bf16[64,5632]{1,0:T(8,128)(2,1)} %param.22) | copy-start | bytes 2162692
  10.4 17.1 %copy-start.46 = (f32[64]{0:T(128)S(1)}, f32[64]{0:T(128)}, u32[]{:S(2)}) copy-start(f32[64]{0:T(128)} %param.21) | copy-start | bytes 772
  27.4 275.2 %all-gather.6.cloned.1.call-start = ((), (), s32[]{:S(2)}) async-start(), calls=%async_computation.4 | async-start | bytes 7208960 | tf_op jit(solution)/shard_map/all_gather | solution.py:411
  64.4 2.7 copy-start.49
  66.9 5.1 copy-start.13
  67.0 254.7 %all-gather.8.cloned.1.call-start = ((), (), s32[]{:S(2)}) async-start(), calls=%async_computation.5 | async-start | bytes 3932160 | tf_op jit(solution)/shard_map/all_gather | solution.py:410
  67.0 53.1 %collective-permute-start = (s32[1,2]{1,0:T(1,128)S(1)}, s32[1,2]{1,0:T(1,128)S(1)}, u32[]{:S(2)}, u32[]{:S(2)}) collective-permute-start(s32[1,2]{1,0:T(1,128)S(1)} %copy-done.49), channel_id=1, source_target_pairs={{0,4},{4,0},{1,5},{5,1},{2,6},{6,2},{3,7},{7,3},{8,12},{12,8},{9,1... | collective-permute-start | bytes 32 | tf_op jit(solution)/shard_map/ppermute | solution.py:415
  70.3 485.7 %reduce-scatter.6.cloned.1.call-start = ((), (), s32[]{:S(2)}) async-start(), calls=%async_computation.7 | async-start | bytes 3604480 | tf_op jit(solution)/shard_map/reduce_scatter | solution.py:459
  72.3 0.6 copy-start.43
  74.1 46.0 %copy-start.48 = (s32[1,256]{1,0:T(1,128)S(1)}, s32[1,256]{1,0:T(1,128)}, u32[]{:S(2)}) copy-start(s32[1,256]{1,0:T(1,128)} %param.15) | copy-start | bytes 3076
  118.1 2.1 copy-start.30
  118.1 13.8 %copy-start.24 = (f32[1024,64]{0,1:T(8,128)}, f32[1024,64]{0,1:T(8,128)S(1)}, u32[]{:S(2)}) copy-start(f32[1024,64]{0,1:T(8,128)S(1)} %get-tuple-element.65) | copy-start | bytes 786436
  123.3 32.7 %copy-start.11 = (pred[2,1024,1024]{1,2,0:T(8,128)(4,1)}, pred[2,1024,1024]{1,2,0:T(8,128)(4,1)S(1)}, u32[]{:S(2)}) copy-start(pred[2,1024,1024]{1,2,0:T(8,128)(4,1)S(1)} %and_or_fusion) | copy-start | bytes 6291460
  131.7 2.1 copy-start.19
  131.7 1.1 copy-start.31
  141.6 3.1 copy-start.36
  144.7 5.5 copy-start.20
  144.7 5.5 copy-start.22
  150.2 5.7 copy-start.7
  156.0 0.6 copy-start.41
  171.2 4.0 copy-start.17
  175.1 40.3 %copy-start.15 = (bf16[1,256,2048]{2,1,0:T(8,128)(2,1)S(1)}, bf16[1,256,2048]{2,1,0:T(8,128)(2,1)}, u32[]{:S(2)}) copy-start(bf16[1,256,2048]{2,1,0:T(8,128)(2,1)} %param.25) | copy-start | bytes 3145732
  217.1 41.9 %copy-start.8 = (f32[256,2048]{1,0:T(8,128)}, f32[256,2048]{1,0:T(8,128)S(1)}, u32[]{:S(2)}) copy-start(f32[256,2048]{1,0:T(8,128)S(1)} %get-tuple-element.28) | copy-start | bytes 6291460
  337.3 1.6 copy-start.51
  338.9 11.2 %copy-start.29 = (f32[1024,64]{0,1:T(8,128)S(1)}, f32[1024,64]{0,1:T(8,128)}, u32[]{:S(2)}) copy-start(f32[1024,64]{0,1:T(8,128)} %get-tuple-element.63) | copy-start | bytes 786436
  350.0 206.0 %reduce-scatter.4.cloned.1.call-start = ((), (), s32[]{:S(2)}) async-start(), calls=%async_computation.6 | async-start | bytes 7208960 | tf_op jit(solution)/shard_map/reduce_scatter | solution.py:460
  369.1 354.5 %reduce-scatter.8.cloned.1.call-start = ((), (), s32[]{:S(2)}) async-start(), calls=%async_computation.8 | async-start | bytes 3932160 | tf_op jit(solution)/shard_map/reduce_scatter | solution.py:493
  388.1 3.4 copy-start.6
  391.5 39.6 %copy-start.9 = (f32[256,2048]{1,0:T(8,128)S(1)}, f32[256,2048]{1,0:T(8,128)}, u32[]{:S(2)}) copy-start(f32[256,2048]{1,0:T(8,128)} %copy-done.8) | copy-start | bytes 6291460
  431.1 1.2 copy-start.16
  475.7 9.3 %copy-start.42 = (f32[2,2,1024]{2,1,0:T(2,128)S(1)}, f32[2,2,1024]{2,1,0:T(2,128)}, u32[]{:S(2)}) copy-start(f32[2,2,1024]{2,1,0:T(2,128)} %copy-done.41) | copy-start | bytes 49156
  485.0 13.6 %copy-start.12 = (pred[2,1024,1024]{1,2,0:T(8,128)(4,1)S(1)}, pred[2,1024,1024]{1,2,0:T(8,128)(4,1)}, u32[]{:S(2)}) copy-start(pred[2,1024,1024]{1,2,0:T(8,128)(4,1)} %copy-done.11) | copy-start | bytes 6291460
  498.6 12.6 %copy-start.37 = (bf16[2,1024,64]{1,2,0:T(8,128)(2,1)S(1)}, bf16[2,1024,64]{1,2,0:T(8,128)(2,1)}, u32[]{:S(2)}) copy-start(bf16[2,1024,64]{1,2,0:T(8,128)(2,1)} %get-tuple-element.36) | copy-start | bytes 786436
  498.6 12.6 %copy-start.38 = (bf16[2,1024,64]{1,2,0:T(8,128)(2,1)S(1)}, bf16[2,1024,64]{1,2,0:T(8,128)(2,1)}, u32[]{:S(2)}) copy-start(bf16[2,1024,64]{1,2,0:T(8,128)(2,1)} %get-tuple-element.37) | copy-start | bytes 786436
  511.2 3.6 copy-start.18
  511.2 3.6 copy-start.32
  515.5 2.8 copy-start.21
  516.1 2.2 copy-start.23
  518.3 3.0 copy-start.25
  545.3 8.8 %copy-start.35 = (bf16[2048,256]{0,1:T(8,128)(2,1)S(1)}, bf16[2048,256]{0,1:T(8,128)(2,1)}, u32[]{:S(2)}) copy-start(bf16[2048,256]{0,1:T(8,128)(2,1)} %convolution_convert_fusion.7) | copy-start | bytes 3145732
  556.0 10.8 %copy-start.50 = (bf16[2048,704]{1,0:T(8,128)(2,1)S(1)}, bf16[2048,704]{1,0:T(8,128)(2,1)}, u32[]{:S(2)}) copy-start(bf16[2048,704]{1,0:T(8,128)(2,1)} %all-gather.8.cloned.1.call-done) | copy-start | bytes 8650756
  556.1 10.8 %copy-start.52 = (bf16[2048,704]{0,1:T(8,128)(2,1)S(1)}, bf16[2048,704]{0,1:T(8,128)(2,1)}, u32[]{:S(2)}) copy-start(bf16[2048,704]{0,1:T(8,128)(2,1)} %copy-done.51) | copy-start | bytes 8650756
  578.3 3.4 copy-start.4
  581.6 41.0 %copy-start.5 = (bf16[2048,2048]{1,0:T(8,128)(2,1)S(1)}, bf16[2048,2048]{1,0:T(8,128)(2,1)}, u32[]{:S(2)}) copy-start(bf16[2048,2048]{1,0:T(8,128)(2,1)} %convolution_convert_fusion.2) | copy-start | bytes 25165828
  621.3 1.3 copy-start
  622.7 41.3 %copy-start.26 = (bf16[512,704]{1,0:T(8,128)(2,1)S(1)}, bf16[512,704]{1,0:T(8,128)(2,1)}, u32[]{:S(2)}) copy-start(bf16[512,704]{1,0:T(8,128)(2,1)} %copy.183) | copy-start | bytes 2162692
  622.7 41.3 %copy-start.33 = (bf16[512,1408]{1,0:T(8,128)(2,1)S(1)}, bf16[512,1408]{1,0:T(8,128)(2,1)}, u32[]{:S(2)}) copy-start(bf16[512,1408]{1,0:T(8,128)(2,1)} %reduce-scatter.4.cloned.1.call-done) | copy-start | bytes 4325380
  662.6 1.4 copy-start.2
  708.3 6.5 copy-start.47
  714.7 5.0 copy-start.1
  714.7 5.0 copy-start.14
  714.8 5.0 copy-start.44
  714.8 5.4 copy-start.10
  719.2 1.6 copy-start.3
  738.1 1.6 copy-start.34
  738.2 1.6 copy-start.45
  739.5 2.1 copy-start.39
  739.5 2.1 copy-start.40
Sparse Core Ops, SparseCore 0:
  27.6 63.8 all-gather.3
  93.6 105.5 all-gather.5
  200.8 61.4 all-gather.7
  350.1 55.7 reduce-scatter.5
  408.1 102.3 reduce-scatter.3
  556.2 59.8 reduce-scatter.7

commit v4 on v3

--- a/solution.py
+++ b/solution.py
@@ -333,6 +333,326 @@
     )(blocks)
 
 
+def ffn_kernel(
+    own_ref,
+    grad_ref,
+    gu_hbm,
+    down_hbm,
+    all_ref,
+    inner_ref,
+    gug_ref,
+    out_ref,
+    sum_ref,
+    gu,
+    down,
+    tokens,
+    grads,
+    wide,
+    narrow,
+    inner,
+    gug,
+    part,
+    chip_in,
+    far_in,
+    near_in,
+    sends,
+    recvs,
+    local,
+):
+    tp_at, seq_at, far, mate, _ = plane_place()
+    seq = lax.axis_size("seq")
+    other = 1 - tp_at
+    kind = lax.rem(seq_at, 2)
+    to_x = at_device(tp_at, far)
+    to_y = at_device(other, seq_at)
+    to_c = at_device(tp_at, mate)
+    rows, width = own_ref.shape
+    pair = 2 * rows
+    half = rows // 2
+    ff_part = narrow.shape[1]
+    top, low = pl.ds(0, half), pl.ds(half, half)
+    enter((to_x, to_y, to_c))
+
+    def piece(t, s, h):
+        return all_ref.at[t * seq + s, pl.ds(h * half, half)]
+
+    def own(i, h, device):
+        return remote(
+            own_ref.at[pl.ds(h * half, half)],
+            piece(tp_at, seq_at, h),
+            sends.at[i],
+            recvs.at[i],
+            device,
+        )
+
+    def relay(i, t, s, h, device):
+        return remote(piece(t, s, h), piece(t, s, h), sends.at[i], recvs.at[i], device)
+
+    x0, x1 = own(0, 0, to_x), own(3, 1, to_x)
+    y0, y1 = own(1, 0, to_y), own(4, 1, to_y)
+    c0, c1 = own(2, 0, to_c), own(5, 1, to_c)
+    diag0 = relay(6, tp_at, far, 0, to_y)
+    diag1 = relay(7, other, seq_at, 1, to_x)
+    rx0, rx1 = relay(8, tp_at, far, 0, to_c), relay(11, tp_at, far, 1, to_c)
+    ry0, ry1 = relay(9, other, seq_at, 0, to_c), relay(10, other, seq_at, 1, to_c)
+    rd0, rd1 = relay(12, other, far, 0, to_c), relay(13, other, far, 1, to_c)
+
+    def give(c):
+        return remote(
+            part.at[c, 1 - kind], chip_in.at[c], sends.at[14 + c], recvs.at[14 + c], to_c
+        )
+
+    def hop(i, src, dst, device):
+        return remote(src, dst, sends.at[i], recvs.at[i], device)
+
+    def held(c):
+        return part.at[c, kind]
+
+    sum_x0 = hop(18, part.at[1, kind, top], near_in.at[0, top], to_x)
+    sum_y1 = hop(19, part.at[2, kind, low], near_in.at[1, low], to_y)
+    sum_d0 = hop(20, part.at[3, kind, top], far_in.at[0, top], to_x)
+    sum_d1 = hop(21, part.at[3, kind, low], far_in.at[1, low], to_y)
+    sum_y0 = hop(22, part.at[2, kind, top], near_in.at[1, top], to_y)
+    sum_x1 = hop(23, part.at[1, kind, low], near_in.at[0, low], to_x)
+
+    def chip_sum(c):
+        give(c).wait_recv()
+        add_rows(held(c), (held(c), chip_in.at[c]), 0, rows, part.dtype)
+
+    def chip_rows(c):
+        t = lax.rem(tp_at + c // 2, 2)
+        s = lax.rem(seq_at + (seq // 2) * lax.rem(c, 2), seq)
+        return t * seq + s - lax.rem(s, 2)
+
+    def take_tokens(c):
+        return pltpu.make_async_copy(
+            all_ref.at[pl.ds(chip_rows(c), 2)], tokens.at[lax.rem(c, 2)], local.at[lax.rem(c, 2)]
+        )
+
+    def take_grads(c):
+        return pltpu.make_async_copy(
+            grad_ref.at[pl.ds(chip_rows(c), 2)], grads.at[lax.rem(c, 2)], local.at[2 + lax.rem(c, 2)]
+        )
+
+    def put_gug(c):
+        return pltpu.make_async_copy(
+            gug.at[lax.rem(c, 2)], gug_ref.at[chip_rows(c) // 2], local.at[4 + lax.rem(c, 2)]
+        )
+
+    def put_inner(c):
+        return pltpu.make_async_copy(
+            inner.at[c], inner_ref.at[chip_rows(c) // 2], local.at[6 + c]
+        )
+
+    def put_out(c):
+        return pltpu.make_async_copy(
+            tokens.at[lax.rem(c, 2)], out_ref.at[pl.ds(chip_rows(c), 2)], local.at[10 + lax.rem(c, 2)]
+        )
+
+    take_gu = pltpu.make_async_copy(gu_hbm, gu, local.at[12])
+    take_down = pltpu.make_async_copy(down_hbm, down, local.at[13])
+    mine = pltpu.make_async_copy(own_ref, all_ref.at[tp_at * seq + seq_at], local.at[14])
+
+    for copy in (x0, y0, c0, x1, y1, c1, mine, take_gu, take_down, take_grads(0)):
+        copy.start()
+    mine.wait()
+    c0.wait_recv()
+    c1.wait_recv()
+    take_tokens(0).start()
+    take_gu.wait()
+    take_down.wait()
+
+    def after_load(c):
+        @pl.when(c == 1)
+        def _():
+            ry0.wait_recv()
+            ry1.wait_recv()
+            take_tokens(2).start()
+            chip_sum(0)
+
+        @pl.when(c == 2)
+        def _():
+            rd0.wait_recv()
+            rd1.wait_recv()
+            take_tokens(3).start()
+            chip_sum(1)
+            sum_x0.start()
+
+        @pl.when(c == 3)
+        def _():
+            chip_sum(2)
+            sum_y1.start()
+
+        @pl.when(c < 3)
+        def _():
+            take_grads(c + 1).start()
+
+    def after_chip(c):
+        @pl.when(c == 0)
+        def _():
+            x0.wait_recv()
+            diag0.start()
+            rx0.start()
+            y0.wait_recv()
+            ry0.start()
+            y1.wait_recv()
+            diag1.start()
+            ry1.start()
+            x1.wait_recv()
+            rx1.start()
+            rx0.wait_recv()
+            rx1.wait_recv()
+            take_tokens(1).start()
+
+        @pl.when(c == 1)
+        def _():
+            diag0.wait_recv()
+            rd0.start()
+            diag1.wait_recv()
+            rd1.start()
+
+    def chip_step(c, carry):
+        slot = lax.rem(c, 2)
+        take_tokens(c).wait()
+        wide[...] = nn(tokens[slot].reshape(pair, width), gu[...])
+        after_load(c)
+        take_grads(c).wait()
+        narrow[...] = nn(grads[slot].reshape(pair, width), down[...])
+
+        @pl.when(c >= 2)
+        def _():
+            put_gug(c - 2).wait()
+
+        def slopes(i, carry):
+            at = pl.ds(i * SUB, SUB)
+            gate, upward, grad = wide[at, :ff_part], wide[at, ff_part:], narrow[at, :]
+            sigmoid_gate = jax.nn.sigmoid(gate)
+            silu_gate = gate * sigmoid_gate
+            inner[c, at, :] = (silu_gate * upward).astype(BF)
+            slope = sigmoid_gate * (1.0 + gate * (1.0 - sigmoid_gate))
+            gug[slot, at, :ff_part] = (grad * upward * slope).astype(BF)
+            gug[slot, at, ff_part:] = (grad * silu_gate).astype(BF)
+            return carry
+
+        lax.fori_loop(0, pair // SUB, slopes, 0)
+        put_gug(c).start()
+        put_inner(c).start()
+        block = width // 4
+
+        def back(n, carry):
+            at = pl.ds(pl.multiple_of(n * block, block), block)
+            total = nt(gug[slot], gu[at, :]).astype(part.dtype)
+            part[c, :, :, at] = total.reshape(2, rows, block)
+            return carry
+
+        lax.fori_loop(0, 4, back, 0)
+        give(c).start()
+        after_chip(c)
+        return carry
+
+    lax.fori_loop(0, 4, chip_step, 0)
+
+    def out_step(c, carry):
+        slot = lax.rem(c, 2)
+
+        @pl.when(c >= 2)
+        def _():
+            put_out(c - 2).wait()
+
+        block = width // 4
+
+        def out_block(n, carry):
+            at = pl.ds(pl.multiple_of(n * block, block), block)
+            total = nt(inner[c], down[at, :]).astype(tokens.dtype)
+            tokens[slot, :, :, at] = total.reshape(2, rows, block)
+            return carry
+
+        lax.fori_loop(0, 4, out_block, 0)
+        put_out(c).start()
+
+        @pl.when(c == 0)
+        def _():
+            chip_sum(3)
+            sum_d0.start()
+            sum_d1.start()
+
+        return carry
+
+    lax.fori_loop(0, 4, out_step, 0)
+    sum_d0.wait_recv()
+    add_rows(held(2), (held(2), far_in.at[0]), 0, half, part.dtype)
+    sum_y0.start()
+    sum_d1.wait_recv()
+    add_rows(held(1), (held(1), far_in.at[1]), half, half, part.dtype)
+    sum_x1.start()
+    sum_x0.wait_recv()
+    sum_y0.wait_recv()
+    add_rows(sum_ref, (held(0), near_in.at[0], near_in.at[1]), 0, half, sum_ref.dtype)
+    sum_y1.wait_recv()
+    sum_x1.wait_recv()
+    add_rows(sum_ref, (held(0), near_in.at[0], near_in.at[1]), half, half, sum_ref.dtype)
+    for copy in (x0, y0, c0, x1, y1, c1, diag0, diag1, rx0, ry0, ry1, rx1, rd0, rd1):
+        copy.wait_send()
+    for c in range(4):
+        give(c).wait_send()
+        put_inner(c).wait()
+    for copy in (sum_x0, sum_y1, sum_d0, sum_d1, sum_y0, sum_x1):
+        copy.wait_send()
+    for c in (2, 3):
+        put_gug(c).wait()
+        put_out(c).wait()
+
+
+def ffn_plane(block, grads, gu_weight, down_weight, ident):
+    rows, width = block.shape
+    seq = lax.axis_size("seq")
+    plane = lax.axis_size("tp") * seq
+    chips = plane // 2
+    ff_part = down_weight.shape[1]
+    shape = jax.ShapeDtypeStruct
+    hbm = pl.BlockSpec(memory_space=pltpu.HBM)
+    vmem = pl.BlockSpec(memory_space=pltpu.VMEM)
+    tokens = plane * rows
+    return pl.pallas_call(
+        ffn_kernel,
+        out_shape=(
+            shape((plane, rows, width), BF),
+            shape((chips, 2 * rows, ff_part), BF),
+            shape((chips, 2 * rows, 2 * ff_part), BF),
+            shape((plane, rows, width), BF),
+            shape((rows, width), F32),
+        ),
+        in_specs=[vmem, hbm, hbm, hbm],
+        out_specs=(hbm, hbm, hbm, hbm, vmem),
+        scratch_shapes=[
+            pltpu.VMEM(gu_weight.shape, BF),
+            pltpu.VMEM(down_weight.shape, BF),
+            pltpu.VMEM((2, 2, rows, width), BF),
+            pltpu.VMEM((2, 2, rows, width), BF),
+            pltpu.VMEM((2 * rows, 2 * ff_part), F32),
+            pltpu.VMEM((2 * rows, ff_part), F32),
+            pltpu.VMEM((4, 2 * rows, ff_part), BF),
+            pltpu.VMEM((2, 2 * rows, 2 * ff_part), BF),
+            pltpu.VMEM((4, 2, rows, width), BF),
+            pltpu.VMEM((4, rows, width), BF),
+            pltpu.VMEM((2, rows, width), BF),
+            pltpu.VMEM((2, rows, width), BF),
+            pltpu.SemaphoreType.DMA((24,)),
+            pltpu.SemaphoreType.DMA((24,)),
+            pltpu.SemaphoreType.DMA((15,)),
+        ],
+        cost_estimate=pl.CostEstimate(
+            flops=12 * tokens * width * ff_part,
+            transcendentals=tokens * ff_part,
+            bytes_accessed=30 * tokens * width,
+        ),
+        compiler_params=pltpu.CompilerParams(
+            collective_id=ident, has_side_effects=True, vmem_limit_bytes=60 << 20
+        ),
+        name="ffn_plane",
+    )(block, grads, gu_weight, down_weight)
+
+
 def columns(matrix, parts):
     rows, cols = matrix.shape
     return jnp.transpose(matrix.reshape(rows, parts, cols // parts), (1, 0, 2))
@@ -442,28 +762,21 @@
 
     scale2 = rms_scale(hidden)
     norm2 = hidden * scale2
-    norm2_all = gather_plane(norm2.astype(BF), 5)
-    inner_grad = nn(ffn_grad, down_weight)
-    gate_up = nn(norm2_all, gu_weight)
-    gate, upward = gate_up[:, :ff_part], gate_up[:, ff_part:]
-    sigmoid_gate = jax.nn.sigmoid(gate)
-    silu_gate = gate * sigmoid_gate
-    inner = (silu_gate * upward).astype(BF)
-    slope = sigmoid_gate * (1.0 + gate * (1.0 - sigmoid_gate))
-    gate_up_grad = jnp.concatenate(
-        [(inner_grad * upward * slope).astype(BF), (inner_grad * silu_gate).astype(BF)], axis=1
-    )
-    scaled2_partial = nt(gate_up_grad, gu_weight).astype(BF)
+    norm2_all, inner, gate_up_grad, out_partial, scaled2 = ffn_plane(
+        norm2.astype(BF), ffn_grad.reshape(plane, local_len, width), gu_weight, down_weight, 5
+    )
+    norm2_all = norm2_all.reshape(-1, width)
+    inner = inner.reshape(-1, ff_part)
+    gate_up_grad = gate_up_grad.reshape(-1, 2 * ff_part)
     down_partial = tn(ffn_grad, inner).astype(BF)
-    gu_partial = tn(norm2_all, gate_up_grad).astype(BF)
     down_sums = lax.psum_scatter(down_partial, "rep", scatter_dimension=0, tiled=True)
+    gu_partial = tn(norm2_all, after(gate_up_grad, down_partial)).astype(BF)
     gu_sums = lax.psum_scatter(gu_partial, "rep", scatter_dimension=0, tiled=True)
-    scaled2 = scatter_plane(after(scaled2_partial, down_partial, gu_partial), 6)
     hidden_grad = upstream + scale2 * (
         scaled2 - norm2 * jnp.mean(scaled2 * norm2, axis=-1, keepdims=True)
     )
 
-    branch_grad = gather_plane((keep * hidden_grad).astype(BF), 7)
+    branch_grad = gather_plane(after((keep * hidden_grad).astype(BF), gu_partial, down_partial), 7)
     mixed_grad = nn(branch_grad, out_weight).astype(BF).reshape(TP, total_len, heads, DH)
     values_grad = jnp.einsum(
         "thqk,tqhd->tkd", probs_low, mixed_grad, preferred_element_type=F32
@@ -495,7 +808,7 @@
     input_grad = hidden_grad + scale1 * (
         scaled1 - norm1 * jnp.mean(scaled1 * norm1, axis=-1, keepdims=True)
     )
-    ffn_out = scatter_plane(after(nt(inner, down_weight).astype(BF), scaled1), 9)
+    ffn_out = scatter_plane(after(out_partial.reshape(-1, width), scaled1), 9)
     out_hidden = (hidden + keep * ffn_out).astype(BF)
 
     ffn_sums = jnp.concatenate([gu_sums, down_sums], axis=1)

time: 755 us -> 722 us (0.956)
  matrix products: 188 us -> 124 us
  Pallas kernels: 409 us -> 430 us
  waiting for transfers between devices: 0.15 us -> 15.7 us
    pallas_call x0 -> x1, Pallas kernels: none -> 101 us  [ffn_plane(): pl.pallas_call(ffn_kernel, out_shape=(shape((plane, rows, width), BF), sh...]
    dot_general x12 -> x8, matrix products: 138 us -> 74.3 us  [dot(): lax.dot_general(left, right, ((contract[:1], contract[1:]), ((), ())), pr...]
    pallas_call x4 -> x3, Pallas kernels: 168 us -> 127 us  [gather_plane(): pl.pallas_call(gather_kernel, out_shape=jax.ShapeDtypeStruct((plane, rows...]
    pallas_call x4 -> x3, Pallas kernels: 159 us -> 121 us  [scatter_plane(): pl.pallas_call(scatter_kernel, out_shape=jax.ShapeDtypeStruct((rows, widt...]
    reduce_scatter x1, waiting for transfers between devices: 0.01 us -> 12 us  [per_device(): lax.psum_scatter(gu_partial, 'rep', scatter_dimension=0, tiled=True)]
    unnamed x111 -> x109, local copies, waits for them, and re-layouts: 23.7 us -> 22.4 us
  transfers between devices with their start and end apart: 7 -> 7, of which waited for: 0 -> 2; matrix products, arithmetic and copies ran while one was open for 36% -> 30% of each run, Pallas kernels for 51% -> 42%
where the time goes in v4:
time: 722 us; the launch traced here: 717 us
  Pallas kernels  430 us (60%)
  matrix products  124 us (17%)
  local copies, waits for them, and re-layouts  72.4 us (10%)
  other arithmetic  58.6 us (8%)
  waiting for transfers between devices  15.7 us (2%)
  between operations  15.3 us (2%)
    pallas_call x3, Pallas kernels, gather_plane(): pl.pallas_call(gather_kernel, out_shape=jax.ShapeDtypeStruct((plane, rows...  127 us
    pallas_call x3, Pallas kernels, scatter_plane(): pl.pallas_call(scatter_kernel, out_shape=jax.ShapeDtypeStruct((rows, widt...  121 us
    pallas_call x1, Pallas kernels, ffn_plane(): pl.pallas_call(ffn_kernel, out_shape=(shape((plane, rows, width), BF), sh...  101 us
    pallas_call x4, Pallas kernels, exchange_plane(): pl.pallas_call(exchange_kernel, out_shape=jax.ShapeDtypeStruct(blocks.sha...  81.9 us
    dot_general x8, matrix products, dot(): lax.dot_general(left, right, ((contract[:1], contract[1:]), ((), ())), pr...  74.3 us
    unnamed x109, local copies, waits for them, and re-layouts  22.4 us
  transfers between devices with their start and end apart: 7, of which 2 were waited for; matrix products, arithmetic and copies ran while one was open for 30% of the time, Pallas kernels for 42%

profile of v4, /device:TPU:1, one launch (start us, length us, event | category | flops | bytes accessed | tf_op | source)
XLA Modules:
  0.0 717.2 jit_solution(6840308977163608790)
XLA Ops:
  11.4 13.7 %exchange_plane.4 = bf16[8,64,768]{2,1,0:T(8,128)(2,1)} custom-call(bf16[8,64,768]{2,1,0:T(8,128)(2,1)} %pad_maximum_fusion.5.in_ref), custom_call_target="tpu_custom_call" | custom-call | bytes 15728640 | tf_op jit(solution)/shard_map/exchange_plane/pallas_call | solution.py:319
  25.1 2.3 copy.157
  28.5 2.5 reshape.431
  33.1 3.1 concatenate.55.in_ref
  36.3 27.9 %exchange_plane.5 = bf16[8,64,2112]{2,1,0:T(8,128)(2,1)} custom-call(bf16[8,64,2112]{2,1,0:T(8,128)(2,1)} %concatenate.55.in_ref), custom_call_target="tpu_custom_call" | custom-call | bytes 43253760 | tf_op jit(solution)/shard_map/exchange_plane/pallas_call | solution.py:319
  64.2 2.2 slice.101
  70.8 1.8 fusion.46
  73.8 42.2 %gather_plane.3 = bf16[8,256,2048]{2,1,0:T(8,128)(2,1)} custom-call(bf16[256,2048]{1,0:T(8,128)(2,1)} %fusion.7.own_ref), custom_call_target="tpu_custom_call" | custom-call | bytes 100663296 | tf_op jit(solution)/shard_map/gather_plane/pallas_call | solution.py:174
  118.2 3.0 and_or_fusion
  121.3 8.4 %fusion.15 = f32[2,1024,512]{1,2,0:T(8,128)S(1)} fusion(bf16[2,1024,2048]{2,1,0:T(8,128)(2,1)} %bitcast.183, bf16[2048,768]{0,1:T(8,128)(2,1)} %all-gather.4.cloned.1.call-done), kind=kOutput, calls=%fused_computation.37 | convolution fusion | flops 4294967296 | bytes 14680064 | tf_op jit(solution)/shard_map/dot_general | solution.py:57
  129.8 1.8 copy-done.22
  131.6 1.4 fusion.55
  133.1 3.2 copy.206
  136.3 3.2 copy.207
  139.4 2.4 subtract_convert_fusion.3
  141.8 2.4 subtract_convert_fusion.1
  144.2 5.7 fusion.4
  149.9 4.2 exponential_reduce_fusion
  154.1 1.6 copy-done.4
  155.7 12.1 %fusion.23 = bf16[2,1024,2,128]{1,3,2,0:T(8,128)(2,1)} fusion(f32[2,1024,512]{1,2,0:T(8,128)} %copy-done.22, f32[2,1024,1024,2]{2,1,3,0:T(8,128)} %copy-done.4, f32[2,2,1024]{2,1,0:T(2,128)S(1)} %log_add_fusion, pred[2,1024,1024]{1,2,0:T(8,128)(4,1)S(1)} %and_or_fusion), kind=kOutput, calls=%fused_computation.63 | convolution fusion | flops 1091043328 | bytes 20463616 | tf_op jit(solution)/shard_map/thqk,tkd->tqhd/dot_general | solution.py:758
  167.8 2.5 copy.164
  170.3 4.0 convolution_convert_fusion.1
  174.3 40.3 %scatter_plane.3 = f32[256,2048]{1,0:T(8,128)S(1)} custom-call(bf16[8,256,2048]{2,1,0:T(8,128)(2,1)S(1)} %bitcast.178), custom_call_target="tpu_custom_call" | custom-call | bytes 117440512 | tf_op jit(solution)/shard_map/scatter_plane/pallas_call | solution.py:269
  214.5 1.7 multiply_reduce_fusion.1
  216.2 42.0 %gather_plane.4.grad_ref = bf16[8,256,2048]{2,1,0:T(8,128)(2,1)} custom-call(bf16[256,2048]{1,0:T(8,128)(2,1)} %get-tuple-element.27.own_ref), custom_call_target="tpu_custom_call" | custom-call | bytes 100663296 | tf_op jit(solution)/shard_map/gather_plane/pallas_call | solution.py:174
  259.4 3.5 all-gather.6.cloned.1.call-done.gu_hbm
  262.9 100.8 %ffn_plane.1 = (bf16[8,256,2048]{2,1,0:T(8,128)(2,1)}, bf16[4,512,704]{2,1,0:T(8,128)(2,1)}, bf16[4,512,1408]{2,1,0:T(8,128)(2,1)}, bf16[8,256,2048]{2,1,0:T(8,128)(2,1)}, f32[256,2048]{1,0:T(8,128)}) custom-call(bf16[256,2048]{1,0:T(8,128)(2,1)} %multiply_convert_fusion.1.own_ref, bf16[8,256,2048]{2,1,0:T(8,128)(2,1)} %gather_plane.4.grad_ref, ...), custom_call_target="tpu_custom_call" | custom-call | flops 35433480192 | bytes 125829120 | tf_op jit(solution)/shard_map/ffn_plane/pallas_call | solution.py:616
  363.7 10.7 %convolution_convert_fusion.3 = bf16[2048,704]{0,1:T(8,128)(2,1)} fusion(bf16[2048,2048]{1,0:T(8,128)(2,1)} %bitcast.187, bf16[2048,704]{1,0:T(8,128)(2,1)} %bitcast.216), kind=kOutput, calls=%fused_computation.15 | convolution fusion | flops 5907021824 | bytes 14155776 | tf_op jit(solution)/shard_map/dot_general | solution.py:57
  374.4 19.2 %convolution_convert_fusion.2 = bf16[2048,1408]{1,0:T(8,128)(2,1)} fusion(bf16[2048,2048]{1,0:T(8,128)(2,1)} %bitcast.214, bf16[2048,1408]{1,0:T(8,128)(2,1)} %bitcast.215), kind=kOutput, calls=%fused_computation.13 | convolution fusion | flops 11814043648 | bytes 19922944 | tf_op jit(solution)/shard_map/dot_general | solution.py:57
  395.6 2.1 multiply_reduce_fusion
  398.1 1.6 multiply_convert_fusion.own_ref
  399.7 42.3 %gather_plane.5 = bf16[8,256,2048]{2,1,0:T(8,128)(2,1)} custom-call(bf16[256,2048]{1,0:T(8,128)(2,1)} %multiply_convert_fusion.own_ref), custom_call_target="tpu_custom_call" | custom-call | bytes 100663296 | tf_op jit(solution)/shard_map/gather_plane/pallas_call | solution.py:174
  442.0 7.0 convolution_convert_fusion.6
  449.0 1.5 reshape.450
  450.9 13.4 %fusion = (f32[2,2,1024]{2,1,0:T(2,128)S(1)}, f32[2,1024,1024,2]{2,1,3,0:T(8,128)}) fusion(f32[2,1024,1024,2]{2,1,3,0:T(8,128)} %copy-done.4, f32[2,2,1024]{2,1,0:T(2,128)S(1)} %log_add_fusion, pred[2,1024,1024]{1,2,0:T(8,128)(4,1)S(1)} %copy-done.8, bf16[2,1024,2,128]{3,2,1,0:T(2,128)(2,1)S(1)} %reshape.450, f32[2,1024,512]{1,2,0:T(8,128)} %copy-done.22), kind=kOutput, calls=%fused_computation.2 | convolution fusion | flops 1094709248 | bytes 37257216 | tf_op jit(solution)/shard_map/tqhd,tkd->thqk/dot_general | solution.py:784
  464.3 12.7 %fusion.2 = bf16[2,2,1024,1024]{2,3,1,0:T(8,128)(2,1)S(1)} fusion(f32[2,1024,1024,2]{2,1,3,0:T(8,128)} %get-tuple-element.87, f32[2,1024,1024,2]{2,1,3,0:T(8,128)} %copy-done.4, f32[2,2,1024]{2,1,0:T(2,128)S(1)} %get-tuple-element.86, f32[2,2,1024]{2,1,0:T(2,128)S(1)} %log_add_fusion, pred[2,1024,1024]{1,2,0:T(8,128)(4,1)S(1)} %copy-done.8), kind=kLoop, calls=%fused_computation.4 | loop fusion | flops 25165824 | bytes 44072960 | tf_op jit(solution)/shard_map/convert_element_type | solution.py:787
  477.1 3.5 multiply_bitcast_fusion
  484.2 3.0 fusion.24
  488.2 2.0 copy.202
  490.2 2.0 copy.203
  492.1 6.7 convolution_convert_fusion.5
  498.9 11.7 %fusion.25 = bf16[2,1024,128]{2,1,0:T(8,128)(2,1)} fusion(bf16[2,1024,2,128]{3,2,1,0:T(2,128)(2,1)} %copy-done.21, f32[2,1024,1024,2]{2,1,3,0:T(8,128)} %copy-done.4, f32[2,2,1024]{2,1,0:T(2,128)S(1)} %log_add_fusion, pred[2,1024,1024]{1,2,0:T(8,128)(4,1)S(1)} %copy-done.8), kind=kOutput, calls=%fused_computation.67 | convolution fusion | flops 1090781184 | bytes 20463616 | tf_op jit(solution)/shard_map/thqk,tqhd->tkd/dot_general | solution.py:781
  510.6 8.4 %convolution_convert_fusion.4 = bf16[2048,512]{0,1:T(8,128)(2,1)S(1)} fusion(bf16[2048,2048]{1,0:T(8,128)(2,1)} %bitcast.184, bf16[2048,128]{1,0:T(8,128)(2,1)} %bitcast.217, bf16[2048,64]{1,0:T(8,128)(2,1)} %bitcast.205, bf16[2048,64]{1,0:T(8,128)(2,1)} %bitcast.203, bf16[2048,256]{1,0:T(8,128)(2,1)S(1)} %bitcast.197), kind=kOutput, calls=%fused_computation.20 | convolution fusion | flops 4304404480 | bytes 12582912 | tf_op jit(solution)/shard_map/dot_general | solution.py:57
  519.1 1.9 pad_maximum_fusion
  521.0 12.0 %reduce-scatter.4.cloned.1.call-done = bf16[512,1408]{1,0:T(8,128)(2,1)} async-done(((bf16[2048,1408]{1,0:T(8,128)(2,1)}), bf16[512,1408]{1,0:T(8,128)(2,1)}) %reduce-scatter.4.cloned.1.call-update) | async-done | bytes 1441808 | tf_op jit(solution)/shard_map/reduce_scatter | solution.py:774
  533.1 10.0 %convolution_convert_fusion = bf16[2048,2048]{1,0:T(8,128)(2,1)} fusion(bf16[2048,768]{0,1:T(8,128)(2,1)} %all-gather.4.cloned.1.call-done, bf16[2048,128]{1,0:T(8,128)(2,1)} %bitcast.218, bf16[2048,64]{1,0:T(8,128)(2,1)S(1)} %bitcast.206, bf16[2048,64]{1,0:T(8,128)(2,1)S(1)} %bitcast.204, bf16[2048,256]{1,0:T(8,128)(2,1)S(1)} %bitcast.198), kind=kOutput, calls=%fused_computation.11 | convolution fusion | flops 4307550208 | bytes 12582912 | tf_op jit(solution)/shard_map/dot_general | solution.py:57
  543.3 3.4 copy-done.3
  546.7 41.1 %scatter_plane.4 = f32[256,2048]{1,0:T(8,128)S(1)} custom-call(bf16[8,256,2048]{2,1,0:T(8,128)(2,1)S(1)} %bitcast.179), custom_call_target="tpu_custom_call" | custom-call | bytes 117440512 | tf_op jit(solution)/shard_map/scatter_plane/pallas_call | solution.py:269
  587.8 3.4 copy-done.2
  591.2 39.3 %scatter_plane.5 = f32[256,2048]{1,0:T(8,128)S(1)} custom-call(bf16[8,256,2048]{2,1,0:T(8,128)(2,1)S(1)} %copy-done.2), custom_call_target="tpu_custom_call" | custom-call | bytes 117440512 | tf_op jit(solution)/shard_map/scatter_plane/pallas_call | solution.py:269
  630.6 1.7 pad_maximum_fusion.1
  632.6 28.0 %exchange_plane.7 = bf16[8,64,2112]{2,1,0:T(8,128)(2,1)} custom-call(bf16[8,64,2112]{2,1,0:T(8,128)(2,1)} %bitcast.182), custom_call_target="tpu_custom_call" | custom-call | bytes 43253760 | tf_op jit(solution)/shard_map/exchange_plane/pallas_call | solution.py:319
  660.6 2.0 convert_element_type.184
  662.6 2.2 slice_bitcast_fusion
  664.8 2.1 copy.184
  666.9 1.9 reshape.461
  668.8 3.5 copy.185
  672.3 2.8 reshape.462
  675.1 3.5 copy.186
  678.6 2.8 reshape.463
  681.4 4.0 broadcast_multiply_fusion
  687.3 2.8 fusion.13
  690.1 2.3 copy.178
  692.5 12.2 %exchange_plane.6 = bf16[8,64,768]{2,1,0:T(8,128)(2,1)} custom-call(bf16[8,64,768]{2,1,0:T(8,128)(2,1)} %bitcast.194), custom_call_target="tpu_custom_call" | custom-call | bytes 15728640 | tf_op jit(solution)/shard_map/exchange_plane/pallas_call | solution.py:319
  (171 shorter events, 31.5 us)
Async XLA Ops:
  7.2 114.1 %all-gather.4.cloned.1.call-start = ((), (), s32[]{:S(2)}) async-start(), calls=%async_computation.3 | async-start | bytes 3932160 | tf_op jit(solution)/shard_map/all_gather | solution.py:710
  11.4 16.1 %copy-start.28 = (bf16[64,5632]{1,0:T(8,128)(2,1)S(1)}, bf16[64,5632]{1,0:T(8,128)(2,1)}, u32[]{:S(2)}) copy-start(bf16[64,5632]{1,0:T(8,128)(2,1)} %param.23) | copy-start | bytes 2162692
  11.4 16.1 %copy-start.29 = (bf16[64,5632]{1,0:T(8,128)(2,1)S(1)}, bf16[64,5632]{1,0:T(8,128)(2,1)}, u32[]{:S(2)}) copy-start(bf16[64,5632]{1,0:T(8,128)(2,1)} %param.22) | copy-start | bytes 2162692
  11.4 16.1 %copy-start.48 = (f32[64]{0:T(128)S(1)}, f32[64]{0:T(128)}, u32[]{:S(2)}) copy-start(f32[64]{0:T(128)} %param.21) | copy-start | bytes 772
  27.4 231.9 %all-gather.8.cloned.1.call-start = ((), (), s32[]{:S(2)}) async-start(), calls=%async_computation.5 | async-start | bytes 3932160 | tf_op jit(solution)/shard_map/all_gather | solution.py:730
  31.7 1.1 copy-start.27
  64.2 2.3 copy-start.51
  64.2 3.5 copy-start.16
  66.5 2.8 copy-start.9
  66.5 196.4 %all-gather.6.cloned.1.call-start = ((), (), s32[]{:S(2)}) async-start(), calls=%async_computation.4 | async-start | bytes 7208960 | tf_op jit(solution)/shard_map/all_gather | solution.py:731
  66.5 51.5 %collective-permute-start = (s32[1,2]{1,0:T(1,128)S(1)}, s32[1,2]{1,0:T(1,128)S(1)}, u32[]{:S(2)}, u32[]{:S(2)}) collective-permute-start(s32[1,2]{1,0:T(1,128)S(1)} %copy-done.51), channel_id=1, source_target_pairs={{0,4},{4,0},{1,5},{5,1},{2,6},{6,2},{3,7},{7,3},{8,12},{12,8},{9,1... | collective-permute-start | bytes 32 | tf_op jit(solution)/shard_map/ppermute | solution.py:735
  69.0 1.8 copy-start.50
  69.0 452.0 %reduce-scatter.6.cloned.1.call-start = ((), (), s32[]{:S(2)}) async-start(), calls=%async_computation.7 | async-start | bytes 3604480 | tf_op jit(solution)/shard_map/reduce_scatter | solution.py:772
  69.5 1.2 copy-start.45
  72.5 44.5 %copy-start.32 = (f32[1024,64]{0,1:T(8,128)}, f32[1024,64]{0,1:T(8,128)S(1)}, u32[]{:S(2)}) copy-start(f32[1024,64]{0,1:T(8,128)S(1)} %get-tuple-element.73) | copy-start | bytes 786436
  121.2 34.5 %copy-start.7 = (pred[2,1024,1024]{1,2,0:T(8,128)(4,1)}, pred[2,1024,1024]{1,2,0:T(8,128)(4,1)S(1)}, u32[]{:S(2)}) copy-start(pred[2,1024,1024]{1,2,0:T(8,128)(4,1)S(1)} %and_or_fusion) | copy-start | bytes 6291460
  129.7 2.0 copy-start.22
  139.4 2.4 copy-start.17
  144.2 5.7 copy-start.23
  144.2 5.7 copy-start.25
  149.9 5.8 copy-start.4
  170.3 4.0 copy-start.18
  174.3 40.3 %copy-start.13 = (bf16[1,256,2048]{2,1,0:T(8,128)(2,1)S(1)}, bf16[1,256,2048]{2,1,0:T(8,128)(2,1)}, u32[]{:S(2)}) copy-start(bf16[1,256,2048]{2,1,0:T(8,128)(2,1)} %param.25) | copy-start | bytes 3145732
  216.2 181.5 %copy-start.5 = (f32[256,2048]{1,0:T(8,128)}, f32[256,2048]{1,0:T(8,128)S(1)}, u32[]{:S(2)}) copy-start(f32[256,2048]{1,0:T(8,128)S(1)} %get-tuple-element.40) | copy-start | bytes 6291460
  374.4 158.6 %reduce-scatter.4.cloned.1.call-start = ((), (), s32[]{:S(2)}) async-start(), calls=%async_computation.6 | async-start | bytes 7208960 | tf_op jit(solution)/shard_map/reduce_scatter | solution.py:774
  393.6 0.9 copy-start.30
  393.7 296.5 %reduce-scatter.8.cloned.1.call-start = ((), (), s32[]{:S(2)}) async-start(), calls=%async_computation.8 | async-start | bytes 3932160 | tf_op jit(solution)/shard_map/reduce_scatter | solution.py:806
  395.6 2.2 copy-start.11
  395.6 2.5 copy-start.14
  449.0 1.9 copy-start.8
  450.9 13.4 %copy-start.21 = (bf16[2,1024,2,128]{3,2,1,0:T(2,128)(2,1)}, bf16[2,1024,2,128]{3,2,1,0:T(2,128)(2,1)S(1)}, u32[]{:S(2)}) copy-start(bf16[2,1024,2,128]{3,2,1,0:T(2,128)(2,1)S(1)} %reshape.450) | copy-start | bytes 3145732
  464.3 12.7 %copy-start.38 = (bf16[2,1024,64]{1,2,0:T(8,128)(2,1)S(1)}, bf16[2,1024,64]{1,2,0:T(8,128)(2,1)}, u32[]{:S(2)}) copy-start(bf16[2,1024,64]{1,2,0:T(8,128)(2,1)} %get-tuple-element.45) | copy-start | bytes 786436
  464.3 12.7 %copy-start.39 = (bf16[2,1024,64]{1,2,0:T(8,128)(2,1)S(1)}, bf16[2,1024,64]{1,2,0:T(8,128)(2,1)}, u32[]{:S(2)}) copy-start(bf16[2,1024,64]{1,2,0:T(8,128)(2,1)} %get-tuple-element.46) | copy-start | bytes 786436
  477.1 3.6 copy-start.20
  477.1 3.6 copy-start.33
  482.0 2.2 copy-start.24
  482.0 2.2 copy-start.26
  484.2 3.0 copy-start.31
  487.2 4.9 copy-start.19
  498.9 11.7 %copy-start.35 = (bf16[256,8,2,128]{3,1,2,0:T(8,128)(2,1)S(1)}, bf16[256,8,2,128]{3,1,2,0:T(8,128)(2,1)}, u32[]{:S(2)}) copy-start(bf16[256,8,2,128]{3,1,2,0:T(8,128)(2,1)} %copy.240) | copy-start | bytes 3145732
  510.6 8.4 %copy-start.37 = (bf16[2048,256]{0,1:T(8,128)(2,1)S(1)}, bf16[2048,256]{0,1:T(8,128)(2,1)}, u32[]{:S(2)}) copy-start(bf16[2048,256]{0,1:T(8,128)(2,1)} %convolution_convert_fusion.5) | copy-start | bytes 3145732
  521.0 12.0 %copy-start.41 = (bf16[2,1024,64]{2,1,0:T(8,128)(2,1)S(1)}, bf16[2,1024,64]{2,1,0:T(8,128)(2,1)}, u32[]{:S(2)}) copy-start(bf16[2,1024,64]{2,1,0:T(8,128)(2,1)} %copy.202) | copy-start | bytes 786436
  521.0 12.0 %copy-start.42 = (bf16[2,1024,64]{2,1,0:T(8,128)(2,1)S(1)}, bf16[2,1024,64]{2,1,0:T(8,128)(2,1)}, u32[]{:S(2)}) copy-start(bf16[2,1024,64]{2,1,0:T(8,128)(2,1)} %copy.203) | copy-start | bytes 786436
  533.0 10.0 %copy-start.40 = (bf16[512,704]{0,1:T(8,128)(2,1)S(1)}, bf16[512,704]{0,1:T(8,128)(2,1)}, u32[]{:S(2)}) copy-start(bf16[512,704]{0,1:T(8,128)(2,1)} %reduce-scatter.6.cloned.1.call-done) | copy-start | bytes 2162692
  543.3 3.4 copy-start.3
  587.8 3.4 copy-start.2
  591.2 39.3 %copy-start.34 = (bf16[512,1408]{1,0:T(8,128)(2,1)S(1)}, bf16[512,1408]{1,0:T(8,128)(2,1)}, u32[]{:S(2)}) copy-start(bf16[512,1408]{1,0:T(8,128)(2,1)} %reduce-scatter.4.cloned.1.call-done) | copy-start | bytes 4325380
  630.6 2.0 copy-start
  678.6 2.8 copy-start.49
  681.4 4.6 copy-start.10
  681.4 4.6 copy-start.46
  681.4 5.0 copy-start.6
  681.4 5.0 copy-start.12
  685.5 1.6 copy-start.1
  685.5 1.9 copy-start.15
  705.9 1.0 copy-start.36
  705.9 0.9 copy-start.47
  706.1 2.6 copy-start.43
  706.1 2.6 copy-start.44
Sparse Core Ops, SparseCore 0:
  27.5 63.8 all-gather.3
  93.0 62.0 all-gather.7
  157.3 105.5 all-gather.5
  374.5 53.9 reduce-scatter.5
  430.6 102.3 reduce-scatter.3
  535.2 60.5 reduce-scatter.7

commit v5 on v4

--- a/solution.py
+++ b/solution.py
@@ -336,15 +336,13 @@
 def ffn_kernel(
     own_ref,
     grad_ref,
-    gu_hbm,
-    down_hbm,
+    weight_hbm,
     all_ref,
     inner_ref,
     gug_ref,
     out_ref,
     sum_ref,
-    gu,
-    down,
+    weight,
     tokens,
     grads,
     wide,
@@ -370,6 +368,7 @@
     pair = 2 * rows
     half = rows // 2
     ff_part = narrow.shape[1]
+    gate_up, lower = slice(0, 2 * ff_part), slice(2 * ff_part, 3 * ff_part)
     top, low = pl.ds(0, half), pl.ds(half, half)
     enter((to_x, to_y, to_c))
 
@@ -449,18 +448,16 @@
             tokens.at[lax.rem(c, 2)], out_ref.at[pl.ds(chip_rows(c), 2)], local.at[10 + lax.rem(c, 2)]
         )
 
-    take_gu = pltpu.make_async_copy(gu_hbm, gu, local.at[12])
-    take_down = pltpu.make_async_copy(down_hbm, down, local.at[13])
-    mine = pltpu.make_async_copy(own_ref, all_ref.at[tp_at * seq + seq_at], local.at[14])
-
-    for copy in (x0, y0, c0, x1, y1, c1, mine, take_gu, take_down, take_grads(0)):
+    take_weight = pltpu.make_async_copy(weight_hbm, weight, local.at[12])
+    mine = pltpu.make_async_copy(own_ref, all_ref.at[tp_at * seq + seq_at], local.at[13])
+
+    for copy in (x0, y0, c0, x1, y1, c1, mine, take_weight, take_grads(0)):
         copy.start()
     mine.wait()
     c0.wait_recv()
     c1.wait_recv()
     take_tokens(0).start()
-    take_gu.wait()
-    take_down.wait()
+    take_weight.wait()
 
     def after_load(c):
         @pl.when(c == 1)
@@ -514,10 +511,10 @@
     def chip_step(c, carry):
         slot = lax.rem(c, 2)
         take_tokens(c).wait()
-        wide[...] = nn(tokens[slot].reshape(pair, width), gu[...])
+        wide[...] = nn(tokens[slot].reshape(pair, width), weight[:, gate_up])
         after_load(c)
         take_grads(c).wait()
-        narrow[...] = nn(grads[slot].reshape(pair, width), down[...])
+        narrow[...] = nn(grads[slot].reshape(pair, width), weight[:, lower])
 
         @pl.when(c >= 2)
         def _():
@@ -541,7 +538,7 @@
 
         def back(n, carry):
             at = pl.ds(pl.multiple_of(n * block, block), block)
-            total = nt(gug[slot], gu[at, :]).astype(part.dtype)
+            total = nt(gug[slot], weight[at, gate_up]).astype(part.dtype)
             part[c, :, :, at] = total.reshape(2, rows, block)
             return carry
 
@@ -563,7 +560,7 @@
 
         def out_block(n, carry):
             at = pl.ds(pl.multiple_of(n * block, block), block)
-            total = nt(inner[c], down[at, :]).astype(tokens.dtype)
+            total = nt(inner[c], weight[at, lower]).astype(tokens.dtype)
             tokens[slot, :, :, at] = total.reshape(2, rows, block)
             return carry
 
@@ -603,12 +600,12 @@
         put_out(c).wait()
 
 
-def ffn_plane(block, grads, gu_weight, down_weight, ident):
+def ffn_plane(block, grads, weight, ident):
     rows, width = block.shape
     seq = lax.axis_size("seq")
     plane = lax.axis_size("tp") * seq
     chips = plane // 2
-    ff_part = down_weight.shape[1]
+    ff_part = weight.shape[1] // 3
     shape = jax.ShapeDtypeStruct
     hbm = pl.BlockSpec(memory_space=pltpu.HBM)
     vmem = pl.BlockSpec(memory_space=pltpu.VMEM)
@@ -622,11 +619,10 @@
             shape((plane, rows, width), BF),
             shape((rows, width), F32),
         ),
-        in_specs=[vmem, hbm, hbm, hbm],
+        in_specs=[vmem, hbm, hbm],
         out_specs=(hbm, hbm, hbm, hbm, vmem),
         scratch_shapes=[
-            pltpu.VMEM(gu_weight.shape, BF),
-            pltpu.VMEM(down_weight.shape, BF),
+            pltpu.VMEM(weight.shape, BF),
             pltpu.VMEM((2, 2, rows, width), BF),
             pltpu.VMEM((2, 2, rows, width), BF),
             pltpu.VMEM((2 * rows, 2 * ff_part), F32),
@@ -639,7 +635,7 @@
             pltpu.VMEM((2, rows, width), BF),
             pltpu.SemaphoreType.DMA((24,)),
             pltpu.SemaphoreType.DMA((24,)),
-            pltpu.SemaphoreType.DMA((15,)),
+            pltpu.SemaphoreType.DMA((14,)),
         ],
         cost_estimate=pl.CostEstimate(
             flops=12 * tokens * width * ff_part,
@@ -650,7 +646,87 @@
             collective_id=ident, has_side_effects=True, vmem_limit_bytes=60 << 20
         ),
         name="ffn_plane",
-    )(block, grads, gu_weight, down_weight)
+    )(block, grads, weight)
+
+
+def finish_kernel(
+    gu_ref,
+    down_ref,
+    gate_weight,
+    up_weight,
+    gain_ref,
+    gate_out,
+    up_out,
+    down_out,
+    gain_out,
+    gu_in,
+    down_in,
+    local,
+    sends,
+    recvs,
+):
+    tp_at, seq_at, _, _, _ = plane_place()
+    seq = lax.axis_size("seq")
+    plane = lax.axis_size("tp") * seq
+    me = tp_at * seq + seq_at
+    peers = [lax.rem(me + k, plane) for k in range(1, plane)]
+    devices = [at_device(peer // seq, lax.rem(peer, seq)) for peer in peers]
+    enter(devices)
+    copies = []
+    for k, (peer, device) in enumerate(zip(peers, devices)):
+        copies.append(remote(gu_ref.at[peer], gu_in.at[me], sends.at[k], recvs.at[k], device))
+        i = plane - 1 + k
+        copies.append(remote(down_ref.at[peer], down_in.at[me], sends.at[i], recvs.at[i], device))
+    copies.append(pltpu.make_async_copy(gu_ref.at[me], gu_in.at[me], local.at[0]))
+    copies.append(pltpu.make_async_copy(down_ref.at[me], down_in.at[me], local.at[1]))
+    for copy in copies:
+        copy.start()
+    for copy in copies:
+        copy.wait()
+    put = pltpu.make_async_copy(down_in, down_out, local.at[2])
+    put.start()
+    gain = gain_ref[...]
+    ff_part = down_in.shape[2]
+    total = jnp.zeros(gain.shape, F32)
+    for j in range(plane):
+        at = slice(j * ff_part, (j + 1) * ff_part)
+        for k, (out, weight) in enumerate(((gate_out, gate_weight), (up_out, up_weight))):
+            own = gu_in[j, :, k * ff_part : (k + 1) * ff_part].astype(F32)
+            out[:, at] = own * gain
+            total = total + jnp.sum(own * weight[:, at].astype(F32), axis=1, keepdims=True)
+    gain_out[...] = total
+    put.wait()
+
+
+def finish_plane(gu_sums, down_sums, gate_weight, up_weight, gain, ident):
+    plane, rows, ff_part = down_sums.shape
+    shape = jax.ShapeDtypeStruct
+    hbm = pl.BlockSpec(memory_space=pltpu.HBM)
+    vmem = pl.BlockSpec(memory_space=pltpu.VMEM)
+    size = plane * rows * ff_part * 6
+    return pl.pallas_call(
+        finish_kernel,
+        out_shape=(
+            shape(gate_weight.shape, F32),
+            shape(up_weight.shape, F32),
+            shape(down_sums.shape, BF),
+            shape((rows, 1), F32),
+        ),
+        in_specs=[hbm, hbm, vmem, vmem, vmem],
+        out_specs=(vmem, vmem, hbm, vmem),
+        scratch_shapes=[
+            pltpu.VMEM(gu_sums.shape, BF),
+            pltpu.VMEM(down_sums.shape, BF),
+            pltpu.SemaphoreType.DMA((3,)),
+            pltpu.SemaphoreType.DMA((2 * plane - 2,)),
+            pltpu.SemaphoreType.DMA((2 * plane - 2,)),
+        ],
+        cost_estimate=pl.CostEstimate(flops=0, transcendentals=0, bytes_accessed=size * 20),
+        compiler_params=pltpu.CompilerParams(
+            collective_id=ident, has_side_effects=True, vmem_limit_bytes=24 << 20
+        ),
+        name="finish_plane",
+    )(gu_sums, down_sums, gate_weight, up_weight, gain)
 
 
 def columns(matrix, parts):
@@ -727,8 +803,7 @@
     )
     ffn_rows = exchange_plane(after(ffn_pack, attn_rows), 2)
     ffn_rows = ffn_rows.reshape(-1, ffn_rows.shape[2])
-    down_weight = lax.all_gather(ffn_rows[:, 2 * ff_part :], "rep", axis=0, tiled=True)
-    gu_weight = lax.all_gather(ffn_rows[:, : 2 * ff_part], "rep", axis=0, tiled=True)
+    ffn_weight = lax.all_gather(ffn_rows, "rep", axis=0, tiled=True)
     norm1_all = gather_plane(after(norm1.astype(BF), ffn_rows), 1)
     ffn_grad = gather_plane(after((keep * upstream).astype(BF), norm1_all), 3)
 
@@ -763,7 +838,7 @@
     scale2 = rms_scale(hidden)
     norm2 = hidden * scale2
     norm2_all, inner, gate_up_grad, out_partial, scaled2 = ffn_plane(
-        norm2.astype(BF), ffn_grad.reshape(plane, local_len, width), gu_weight, down_weight, 5
+        norm2.astype(BF), ffn_grad.reshape(plane, local_len, width), ffn_weight, 5
     )
     norm2_all = norm2_all.reshape(-1, width)
     inner = inner.reshape(-1, ff_part)
@@ -802,22 +877,25 @@
     attn_partial = jnp.concatenate(
         [tn(norm1_all, qkv_grad).astype(BF), tn(branch_grad, mixed).astype(BF)], axis=1
     )
-    attn_partial = after(attn_partial, gu_sums, down_sums)
+    scaled1_partial = nt(qkv_grad, qkv_weight).astype(BF)
+    attn_partial = after(attn_partial, gu_sums, down_sums, scaled1_partial)
     attn_sums = lax.psum_scatter(attn_partial, "rep", scatter_dimension=0, tiled=True)
-    scaled1 = scatter_plane(after(nt(qkv_grad, qkv_weight).astype(BF), attn_partial), 8)
+    scaled1 = scatter_plane(after(scaled1_partial, attn_partial), 8)
     input_grad = hidden_grad + scale1 * (
         scaled1 - norm1 * jnp.mean(scaled1 * norm1, axis=-1, keepdims=True)
     )
     ffn_out = scatter_plane(after(out_partial.reshape(-1, width), scaled1), 9)
     out_hidden = (hidden + keep * ffn_out).astype(BF)
 
-    ffn_sums = jnp.concatenate([gu_sums, down_sums], axis=1)
-    ffn_sums = after(ffn_sums.reshape(plane, -1, ffn_sums.shape[1]), ffn_out)
-    ffn_own = exchange_plane(ffn_sums, 10).astype(F32)
-    gate_own = uncolumns(ffn_own[:, :, :ff_part])
-    up_own = uncolumns(ffn_own[:, :, ff_part : 2 * ff_part])
-    down_own = uncolumns(ffn_own[:, :, 2 * ff_part :])
-    gain_ffn_grad = jnp.sum(gate_own * wg32, axis=1) + jnp.sum(up_own * wu32, axis=1)
+    gate_grad, up_grad, down_own, gain_ffn_grad = finish_plane(
+        after(gu_sums.reshape(plane, -1, 2 * ff_part), ffn_out),
+        down_sums.reshape(plane, -1, ff_part),
+        w_gate,
+        w_up,
+        gain2,
+        10,
+    )
+    down_grad = jnp.transpose(down_own, (0, 2, 1)).reshape(plane * ff_part, -1).astype(F32)
 
     attn_own = exchange_plane(attn_sums.reshape(plane, -1, attn_sums.shape[1]), 11).astype(F32)
     query_own = uncolumns(attn_own[:, :, :q_part])
@@ -839,10 +917,10 @@
         key_own * gain1,
         value_own * gain1,
         out_own.T,
-        gain_ffn_grad,
-        gate_own * gain2,
-        up_own * gain2,
-        down_own.T,
+        gain_ffn_grad[:, 0],
+        gate_grad,
+        up_grad,
+        down_grad,
     )
 
 

time: 722 us -> 694 us (0.961)
  local copies, waits for them, and re-layouts: 72.4 us -> 58.3 us
  waiting for transfers between devices: 15.7 us -> 6.78 us
    pallas_call x0 -> x1, Pallas kernels: none -> 30.5 us  [finish_plane(): pl.pallas_call(finish_kernel, out_shape=(shape(gate_weight.shape, F32), s...]
    pallas_call x4 -> x3, Pallas kernels: 81.9 us -> 53.8 us  [exchange_plane(): pl.pallas_call(exchange_kernel, out_shape=jax.ShapeDtypeStruct(blocks.sha...]
    transpose x4 -> x0, local copies, waits for them, and re-layouts: 11.3 us -> none  [uncolumns(): return jnp.transpose(blocks, (1, 0, 2)).reshape(rows, parts * cols)]
    reshape x5 -> x2, local copies, waits for them, and re-layouts: 8.38 us -> 0.88 us  [uncolumns(): return jnp.transpose(blocks, (1, 0, 2)).reshape(rows, parts * cols)]
    unnamed x109 -> x117, local copies, waits for them, and re-layouts: 22.4 us -> 25.5 us
  transfers between devices with their start and end apart: 7 -> 6, of which waited for: 2 -> 1; matrix products, arithmetic and copies ran while one was open for 30% -> 28% of each run, Pallas kernels for 42% -> 44%
where the time goes in v5:
time: 694 us; the launch traced here: 689 us
  Pallas kernels  431 us (62%)
  matrix products  123 us (18%)
  local copies, waits for them, and re-layouts  58.3 us (8%)
  other arithmetic  54.4 us (8%)
  between operations  15 us (2%)
    pallas_call x3, Pallas kernels, gather_plane(): pl.pallas_call(gather_kernel, out_shape=jax.ShapeDtypeStruct((plane, rows...  126 us
    pallas_call x3, Pallas kernels, scatter_plane(): pl.pallas_call(scatter_kernel, out_shape=jax.ShapeDtypeStruct((rows, widt...  121 us
    pallas_call x1, Pallas kernels, ffn_plane(): pl.pallas_call(ffn_kernel, out_shape=(shape((plane, rows, width), BF), sh...  99.4 us
    dot_general x8, matrix products, dot(): lax.dot_general(left, right, ((contract[:1], contract[1:]), ((), ())), pr...  73 us
    pallas_call x3, Pallas kernels, exchange_plane(): pl.pallas_call(exchange_kernel, out_shape=jax.ShapeDtypeStruct(blocks.sha...  53.8 us
    pallas_call x1, Pallas kernels, finish_plane(): pl.pallas_call(finish_kernel, out_shape=(shape(gate_weight.shape, F32), s...  30.5 us
    unnamed x117, local copies, waits for them, and re-layouts  25.5 us
  transfers between devices with their start and end apart: 6, of which 1 were waited for; matrix products, arithmetic and copies ran while one was open for 28% of the time, Pallas kernels for 44%

profile of v5, /device:TPU:1, one launch (start us, length us, event | category | flops | bytes accessed | tf_op | source)
XLA Modules:
  0.0 689.1 jit_solution(10948825901771333403)
XLA Ops:
  11.4 13.7 %exchange_plane.3 = bf16[8,64,768]{2,1,0:T(8,128)(2,1)} custom-call(bf16[8,64,768]{2,1,0:T(8,128)(2,1)} %pad_maximum_fusion.4.in_ref), custom_call_target="tpu_custom_call" | custom-call | bytes 15728640 | tf_op jit(solution)/shard_map/exchange_plane/pallas_call | solution.py:319
  25.1 2.4 copy.155
  28.3 1.2 multiply_convert_fusion.2
  29.5 2.5 reshape.427
  34.1 3.1 concatenate.52.in_ref
  37.3 28.0 %exchange_plane.4 = bf16[8,64,2112]{2,1,0:T(8,128)(2,1)} custom-call(bf16[8,64,2112]{2,1,0:T(8,128)(2,1)} %concatenate.52.in_ref), custom_call_target="tpu_custom_call" | custom-call | bytes 43253760 | tf_op jit(solution)/shard_map/exchange_plane/pallas_call | solution.py:319
  65.9 1.1 collective-permute-start
  67.0 1.8 fusion.42
  71.1 1.2 fusion.7.own_ref
  72.3 42.2 %gather_plane.3 = bf16[8,256,2048]{2,1,0:T(8,128)(2,1)} custom-call(bf16[256,2048]{1,0:T(8,128)(2,1)} %fusion.7.own_ref), custom_call_target="tpu_custom_call" | custom-call | bytes 100663296 | tf_op jit(solution)/shard_map/gather_plane/pallas_call | solution.py:174
  115.1 2.0 and_or_fusion
  117.1 8.4 %fusion.15 = f32[2,1024,512]{1,2,0:T(8,128)S(1)} fusion(bf16[2,1024,2048]{2,1,0:T(8,128)(2,1)} %bitcast.182, bf16[2048,768]{0,1:T(8,128)(2,1)} %all-gather.3.cloned.1.call-done), kind=kOutput, calls=%fused_computation.36 | convolution fusion | flops 4294967296 | bytes 14680064 | tf_op jit(solution)/shard_map/dot_general | solution.py:57
  125.7 1.8 copy-done.26
  127.5 1.4 fusion.51
  128.9 3.2 copy.204
  132.1 3.2 copy.203
  135.3 2.4 subtract_convert_fusion.3
  137.7 2.4 subtract_convert_fusion.1
  140.1 5.7 fusion.4
  145.8 4.2 exponential_reduce_fusion
  150.0 1.6 copy-done.13
  151.6 12.1 %fusion.19 = bf16[2,1024,2,128]{1,3,2,0:T(8,128)(2,1)} fusion(f32[2,1024,512]{1,2,0:T(8,128)} %copy-done.26, f32[2,1024,1024,2]{2,1,3,0:T(8,128)} %copy-done.13, f32[2,2,1024]{2,1,0:T(2,128)S(1)} %log_add_fusion, pred[2,1024,1024]{1,2,0:T(8,128)(4,1)S(1)} %and_or_fusion), kind=kOutput, calls=%fused_computation.54 | convolution fusion | flops 1091043328 | bytes 20463616 | tf_op jit(solution)/shard_map/thqk,tkd->tqhd/dot_general | solution.py:833
  163.7 2.4 copy.162
  166.2 4.0 convolution_convert_fusion.1
  170.1 40.2 %scatter_plane.3 = f32[256,2048]{1,0:T(8,128)S(1)} custom-call(bf16[8,256,2048]{2,1,0:T(8,128)(2,1)S(1)} %bitcast.177), custom_call_target="tpu_custom_call" | custom-call | bytes 117440512 | tf_op jit(solution)/shard_map/scatter_plane/pallas_call | solution.py:269
  210.4 1.7 multiply_reduce_fusion.1
  212.1 42.0 %gather_plane.4.grad_ref = bf16[8,256,2048]{2,1,0:T(8,128)(2,1)} custom-call(bf16[256,2048]{1,0:T(8,128)(2,1)} %get-tuple-element.31.own_ref), custom_call_target="tpu_custom_call" | custom-call | bytes 100663296 | tf_op jit(solution)/shard_map/gather_plane/pallas_call | solution.py:174
  254.1 1.1 multiply_convert_fusion.1.own_ref
  255.2 99.4 %ffn_plane.1 = (bf16[8,256,2048]{2,1,0:T(8,128)(2,1)}, bf16[4,512,704]{2,1,0:T(8,128)(2,1)}, bf16[4,512,1408]{2,1,0:T(8,128)(2,1)}, bf16[8,256,2048]{2,1,0:T(8,128)(2,1)}, f32[256,2048]{1,0:T(8,128)}) custom-call(bf16[256,2048]{1,0:T(8,128)(2,1)} %multiply_convert_fusion.1.own_ref, bf16[8,256,2048]{2,1,0:T(8,128)(2,1)} %gather_plane.4.grad_ref, ...), custom_call_target="tpu_custom_call" | custom-call | flops 35433480192 | bytes 125829120 | tf_op jit(solution)/shard_map/ffn_plane/pallas_call | solution.py:613
  354.6 10.8 %convolution_convert_fusion.3 = bf16[2048,704]{0,1:T(8,128)(2,1)} fusion(bf16[2048,2048]{1,0:T(8,128)(2,1)} %bitcast.186, bf16[2048,704]{1,0:T(8,128)(2,1)} %bitcast.215), kind=kOutput, calls=%fused_computation.15 | convolution fusion | flops 5907021824 | bytes 14155776 | tf_op jit(solution)/shard_map/dot_general | solution.py:57
  365.5 19.2 %convolution_convert_fusion.2 = bf16[2048,1408]{1,0:T(8,128)(2,1)} fusion(bf16[2048,2048]{1,0:T(8,128)(2,1)} %bitcast.213, bf16[2048,1408]{1,0:T(8,128)(2,1)} %bitcast.214), kind=kOutput, calls=%fused_computation.13 | convolution fusion | flops 11814043648 | bytes 19922944 | tf_op jit(solution)/shard_map/dot_general | solution.py:57
  386.6 2.1 multiply_reduce_fusion
  389.2 1.6 multiply_convert_fusion.own_ref
  390.8 41.9 %gather_plane.5 = bf16[8,256,2048]{2,1,0:T(8,128)(2,1)} custom-call(bf16[256,2048]{1,0:T(8,128)(2,1)} %multiply_convert_fusion.own_ref), custom_call_target="tpu_custom_call" | custom-call | bytes 100663296 | tf_op jit(solution)/shard_map/gather_plane/pallas_call | solution.py:174
  432.7 7.0 %convolution_convert_fusion.6 = bf16[2048,256]{1,0:T(8,128)(2,1)} fusion(bf16[2048,2048]{1,0:T(8,128)(2,1)} %bitcast.184, bf16[2048,768]{0,1:T(8,128)(2,1)} %all-gather.3.cloned.1.call-done), kind=kOutput, calls=%fused_computation.27 | convolution fusion | flops 2148007936 | bytes 10485760 | tf_op jit(solution)/shard_map/dot_general | solution.py:57
  439.7 1.5 reshape.447
  441.6 13.4 %fusion = (f32[2,2,1024]{2,1,0:T(2,128)S(1)}, f32[2,1024,1024,2]{2,1,3,0:T(8,128)}) fusion(f32[2,1024,1024,2]{2,1,3,0:T(8,128)} %copy-done.13, f32[2,2,1024]{2,1,0:T(2,128)S(1)} %log_add_fusion, pred[2,1024,1024]{1,2,0:T(8,128)(4,1)S(1)} %copy-done.16, bf16[2,1024,2,128]{3,2,1,0:T(2,128)(2,1)S(1)} %reshape.447, f32[2,1024,512]{1,2,0:T(8,128)} %copy-done.26), kind=kOutput, calls=%fused_computation.2 | convolution fusion | flops 1094709248 | bytes 37257216 | tf_op jit(solution)/shard_map/tqhd,tkd->thqk/dot_general | solution.py:859
  455.1 12.8 %fusion.2 = bf16[2,2,1024,1024]{2,3,1,0:T(8,128)(2,1)S(1)} fusion(f32[2,1024,1024,2]{2,1,3,0:T(8,128)} %get-tuple-element.86, f32[2,1024,1024,2]{2,1,3,0:T(8,128)} %copy-done.13, f32[2,2,1024]{2,1,0:T(2,128)S(1)} %get-tuple-element.85, f32[2,2,1024]{2,1,0:T(2,128)S(1)} %log_add_fusion, pred[2,1024,1024]{1,2,0:T(8,128)(4,1)S(1)} %copy-done.16), kind=kLoop, calls=%fused_computation.4 | loop fusion | flops 25165824 | bytes 44072960 | tf_op jit(solution)/shard_map/convert_element_type | solution.py:862
  468.0 3.5 multiply_bitcast_fusion
  474.0 1.1 copy.237
  475.2 3.0 fusion.20
  479.2 2.0 copy.199
  481.1 2.0 copy.200
  483.1 6.7 convolution_convert_fusion.5
  489.8 11.7 %fusion.21 = bf16[2,1024,128]{2,1,0:T(8,128)(2,1)} fusion(bf16[2,1024,2,128]{3,2,1,0:T(2,128)(2,1)} %copy-done.25, f32[2,1024,1024,2]{2,1,3,0:T(8,128)} %copy-done.13, f32[2,2,1024]{2,1,0:T(2,128)S(1)} %log_add_fusion, pred[2,1024,1024]{1,2,0:T(8,128)(4,1)S(1)} %copy-done.16), kind=kOutput, calls=%fused_computation.58 | convolution fusion | flops 1090781184 | bytes 20463616 | tf_op jit(solution)/shard_map/thqk,tqhd->tkd/dot_general | solution.py:856
  501.5 8.6 %convolution_convert_fusion.4 = bf16[2048,512]{0,1:T(8,128)(2,1)S(1)} fusion(bf16[2048,2048]{1,0:T(8,128)(2,1)} %bitcast.183, bf16[2048,128]{1,0:T(8,128)(2,1)} %bitcast.216, bf16[2048,64]{1,0:T(8,128)(2,1)} %bitcast.203, bf16[2048,64]{1,0:T(8,128)(2,1)} %bitcast.201, bf16[2048,256]{1,0:T(8,128)(2,1)S(1)} %bitcast.195), kind=kOutput, calls=%fused_computation.20 | convolution fusion | flops 4304404480 | bytes 12582912 | tf_op jit(solution)/shard_map/dot_general | solution.py:57
  510.2 1.9 pad_maximum_fusion
  512.1 8.4 %convolution_convert_fusion = bf16[2048,2048]{1,0:T(8,128)(2,1)} fusion(bf16[2048,768]{0,1:T(8,128)(2,1)} %all-gather.3.cloned.1.call-done, bf16[2048,128]{1,0:T(8,128)(2,1)S(1)} %bitcast.217, bf16[2048,64]{1,0:T(8,128)(2,1)S(1)} %bitcast.204, bf16[2048,64]{1,0:T(8,128)(2,1)S(1)} %bitcast.202, bf16[2048,256]{1,0:T(8,128)(2,1)S(1)} %bitcast.196), kind=kOutput, calls=%fused_computation.11 | convolution fusion | flops 4307550208 | bytes 12582912 | tf_op jit(solution)/shard_map/dot_general | solution.py:57
  520.6 6.7 reduce-scatter.4.cloned.1.call-done
  527.6 3.4 copy-done.3
  531.0 41.2 %scatter_plane.4 = f32[256,2048]{1,0:T(8,128)S(1)} custom-call(bf16[8,256,2048]{2,1,0:T(8,128)(2,1)S(1)} %bitcast.178), custom_call_target="tpu_custom_call" | custom-call | bytes 117440512 | tf_op jit(solution)/shard_map/scatter_plane/pallas_call | solution.py:269
  572.2 3.4 copy-done.2
  575.6 39.4 %scatter_plane.5 = f32[256,2048]{1,0:T(8,128)S(1)} custom-call(bf16[8,256,2048]{2,1,0:T(8,128)(2,1)S(1)} %copy-done.2), custom_call_target="tpu_custom_call" | custom-call | bytes 117440512 | tf_op jit(solution)/shard_map/scatter_plane/pallas_call | solution.py:269
  615.0 30.5 %finish_plane.1 = (f32[64,5632]{1,0:T(8,128)S(1)}, f32[64,5632]{1,0:T(8,128)S(1)}, bf16[8,64,704]{2,1,0:T(8,128)(2,1)S(1)}, f32[64,1]{1,0:T(8,128)S(1)}) custom-call(bf16[8,64,1408]{2,1,0:T(8,128)(2,1)S(1)} %bitcast.180, bf16[8,64,704]{2,1,0:T(8,128)(2,1)S(1)} %bitcast.179, bf16[64,5632]{1,0:T(8,128)(2,1)S(1)} %copy-done.7, bf16[64,5632]{1,0:T(8,128)(2,1)S(1)} %copy-done.5, ...), custom_call_target="tpu_custom_call" | custom-call | bytes 43253760 | tf_op jit(solution)/shard_map/finish_plane/pallas_call | solution.py:707
  646.6 1.1 copy-done.11
  647.8 2.1 copy.183
  649.9 2.8 reshape.461
  653.3 1.8 fusion.9
  655.2 5.6 fusion.13
  660.8 2.3 copy.176
  663.1 12.1 %exchange_plane.5 = bf16[8,64,768]{2,1,0:T(8,128)(2,1)} custom-call(bf16[8,64,768]{2,1,0:T(8,128)(2,1)} %bitcast.193), custom_call_target="tpu_custom_call" | custom-call | bytes 15728640 | tf_op jit(solution)/shard_map/exchange_plane/pallas_call | solution.py:319
  675.3 1.3 convert_element_type.189
  680.1 1.1 copy.241
  681.2 1.1 copy.242
  (168 shorter events, 22.7 us)
Async XLA Ops:
  7.2 109.9 %all-gather.3.cloned.1.call-start = ((), (), s32[]{:S(2)}) async-start(), calls=%async_computation.3 | async-start | bytes 3932160 | tf_op jit(solution)/shard_map/all_gather | solution.py:786
  11.4 16.2 %copy-start.41 = (bf16[5632,64]{0,1:T(8,128)(2,1)S(1)}, bf16[5632,64]{0,1:T(8,128)(2,1)}, u32[]{:S(2)}) copy-start(bf16[5632,64]{0,1:T(8,128)(2,1)} %param.24) | copy-start | bytes 2162692
  25.1 3.2 copy-start.4
  25.1 3.2 copy-start.6
  25.1 3.2 copy-start.50
  27.6 227.7 %all-gather.5.cloned.1.call-start = ((), (), s32[]{:S(2)}) async-start(), calls=%async_computation.4 | async-start | bytes 11141120 | tf_op jit(solution)/shard_map/all_gather | solution.py:806
  32.7 1.1 copy-start.31
  65.2 0.7 copy-start.53
  65.2 5.6 copy-start.17
  65.3 455.3 %reduce-scatter.6.cloned.1.call-start = ((), (), s32[]{:S(2)}) async-start(), calls=%async_computation.6 | async-start | bytes 3604480 | tf_op jit(solution)/shard_map/reduce_scatter | solution.py:847
  65.9 49.1 %collective-permute-start = (s32[1,2]{1,0:T(1,128)S(1)}, s32[1,2]{1,0:T(1,128)S(1)}, u32[]{:S(2)}, u32[]{:S(2)}) collective-permute-start(s32[1,2]{1,0:T(1,128)S(1)} %copy-done.53), channel_id=1, source_target_pairs={{0,4},{4,0},{1,5},{5,1},{2,6},{6,2},{3,7},{7,3},{8,12},{12,8},{9,1... | collective-permute-start | bytes 32 | tf_op jit(solution)/shard_map/ppermute | solution.py:810
  68.8 3.5 copy-start.34
  71.1 43.5 %copy-start.47 = (f32[256]{0:T(256)}, f32[256]{0:T(256)S(1)}, u32[]{:S(2)}) copy-start(f32[256]{0:T(256)S(1)} %add_rsqrt_fusion.1) | copy-start | bytes 3076
  72.3 42.6 %copy-start.52 = (s32[1,256]{1,0:T(1,128)S(1)}, s32[1,256]{1,0:T(1,128)}, u32[]{:S(2)}) copy-start(s32[1,256]{1,0:T(1,128)} %param.15) | copy-start | bytes 3076
  117.1 34.5 %copy-start.15 = (pred[2,1024,1024]{1,2,0:T(8,128)(4,1)}, pred[2,1024,1024]{1,2,0:T(8,128)(4,1)S(1)}, u32[]{:S(2)}) copy-start(pred[2,1024,1024]{1,2,0:T(8,128)(4,1)S(1)} %and_or_fusion) | copy-start | bytes 6291460
  125.5 2.0 copy-start.26
  135.3 2.4 copy-start.21
  140.0 5.7 copy-start.27
  140.1 5.7 copy-start.29
  145.8 5.8 copy-start.13
  166.1 4.0 copy-start.22
  170.1 40.3 %copy-start.19 = (bf16[1,256,2048]{2,1,0:T(8,128)(2,1)S(1)}, bf16[1,256,2048]{2,1,0:T(8,128)(2,1)}, u32[]{:S(2)}) copy-start(bf16[1,256,2048]{2,1,0:T(8,128)(2,1)} %param.25) | copy-start | bytes 3145732
  212.1 176.7 %copy-start.14 = (f32[256,2048]{1,0:T(8,128)}, f32[256,2048]{1,0:T(8,128)S(1)}, u32[]{:S(2)}) copy-start(f32[256,2048]{1,0:T(8,128)S(1)} %get-tuple-element.48) | copy-start | bytes 6291460
  365.4 161.8 %reduce-scatter.4.cloned.1.call-start = ((), (), s32[]{:S(2)}) async-start(), calls=%async_computation.5 | async-start | bytes 7208960 | tf_op jit(solution)/shard_map/reduce_scatter | solution.py:849
  384.7 0.9 copy-start.32
  384.7 276.1 %reduce-scatter.8.cloned.1.call-start = ((), (), s32[]{:S(2)}) async-start(), calls=%async_computation.7 | async-start | bytes 3932160 | tf_op jit(solution)/shard_map/reduce_scatter | solution.py:882
  386.6 2.3 copy-start.18
  386.6 2.6 copy-start.20
  439.7 1.9 copy-start.16
  441.6 13.5 %copy-start.25 = (bf16[2,1024,2,128]{3,2,1,0:T(2,128)(2,1)}, bf16[2,1024,2,128]{3,2,1,0:T(2,128)(2,1)S(1)}, u32[]{:S(2)}) copy-start(bf16[2,1024,2,128]{3,2,1,0:T(2,128)(2,1)S(1)} %reshape.447) | copy-start | bytes 3145732
  455.1 12.9 %copy-start.39 = (bf16[2,1024,64]{1,2,0:T(8,128)(2,1)S(1)}, bf16[2,1024,64]{1,2,0:T(8,128)(2,1)}, u32[]{:S(2)}) copy-start(bf16[2,1024,64]{1,2,0:T(8,128)(2,1)} %get-tuple-element.53) | copy-start | bytes 786436
  455.1 12.9 %copy-start.40 = (bf16[2,1024,64]{1,2,0:T(8,128)(2,1)S(1)}, bf16[2,1024,64]{1,2,0:T(8,128)(2,1)}, u32[]{:S(2)}) copy-start(bf16[2,1024,64]{1,2,0:T(8,128)(2,1)} %get-tuple-element.54) | copy-start | bytes 786436
  468.0 3.6 copy-start.24
  468.0 3.6 copy-start.35
  472.9 2.2 copy-start.28
  472.9 2.2 copy-start.30
  475.2 3.0 copy-start.33
  478.2 4.9 copy-start.23
  489.8 11.7 %copy-start.36 = (bf16[256,8,2,128]{3,1,2,0:T(8,128)(2,1)S(1)}, bf16[256,8,2,128]{3,1,2,0:T(8,128)(2,1)}, u32[]{:S(2)}) copy-start(bf16[256,8,2,128]{3,1,2,0:T(8,128)(2,1)} %copy.237) | copy-start | bytes 3145732
  501.5 8.6 %copy-start.38 = (bf16[2048,256]{0,1:T(8,128)(2,1)S(1)}, bf16[2048,256]{0,1:T(8,128)(2,1)}, u32[]{:S(2)}) copy-start(bf16[2048,256]{0,1:T(8,128)(2,1)} %convolution_convert_fusion.5) | copy-start | bytes 3145732
  510.1 2.0 copy-start.43
  510.1 2.0 copy-start.44
  510.1 2.0 copy-start.54
  520.5 6.7 copy-start.51
  520.5 6.8 copy-start.42
  527.6 3.4 copy-start.3
  572.2 3.4 copy-start.2
  575.6 39.4 %copy-start.5 = (bf16[64,5632]{1,0:T(8,128)(2,1)S(1)}, bf16[64,5632]{1,0:T(8,128)(2,1)}, u32[]{:S(2)}) copy-start(bf16[64,5632]{1,0:T(8,128)(2,1)} %up_weight.1) | copy-start | bytes 2162692
  575.6 39.4 %copy-start.7 = (bf16[64,5632]{1,0:T(8,128)(2,1)S(1)}, bf16[64,5632]{1,0:T(8,128)(2,1)}, u32[]{:S(2)}) copy-start(bf16[64,5632]{1,0:T(8,128)(2,1)} %gate_weight.1) | copy-start | bytes 2162692
  575.6 39.4 %copy-start.8 = (bf16[512,1408]{1,0:T(8,128)(2,1)S(1)}, bf16[512,1408]{1,0:T(8,128)(2,1)}, u32[]{:S(2)}) copy-start(bf16[512,1408]{1,0:T(8,128)(2,1)} %reduce-scatter.4.cloned.1.call-done) | copy-start | bytes 4325380
  614.9 32.9 %copy-start = (f32[256,2048]{1,0:T(8,128)}, f32[256,2048]{1,0:T(8,128)S(1)}, u32[]{:S(2)}) copy-start(f32[256,2048]{1,0:T(8,128)S(1)} %scatter_plane.5) | copy-start | bytes 6291460
  645.5 1.1 copy-start.9
  646.6 1.1 copy-start.11
  649.9 3.4 copy-start.48
  653.3 1.9 copy-start.1
  676.6 1.1 copy-start.37
  676.6 1.1 copy-start.49
  676.7 2.0 copy-start.45
  676.7 2.0 copy-start.46
  676.7 3.4 copy-start.12
  678.7 2.6 copy-start.10
Sparse Core Ops, SparseCore 0:
  27.7 63.8 all-gather.2
  93.2 157.1 all-gather.4
  365.6 57.0 reduce-scatter.5
  424.8 102.3 reduce-scatter.3
  529.4 60.5 reduce-scatter.7

commit v6 on v5

--- a/solution.py
+++ b/solution.py
@@ -204,7 +204,7 @@
     lax.fori_loop(0, count // step, body, 0)
 
 
-def scatter_kernel(part_ref, sum_ref, held, chip_in, far_in, near_in, loads, sends, recvs):
+def scatter_stages(part_ref, sum_ref, held, chip_in, far_in, near_in, loads, sends, recvs):
     tp_at, seq_at, far, mate, far_mate = plane_place()
     seq = lax.axis_size("seq")
     other = 1 - tp_at
@@ -214,51 +214,89 @@
     rows = sum_ref.shape[0]
     part = rows // 2
     top, low = pl.ds(0, part), pl.ds(part, part)
-    enter((to_x, to_y, to_c))
     chips = ((other, far, far_mate), (tp_at, far, far_mate), (other, seq_at, mate), (tp_at, seq_at, mate))
-    gives, takes = [], []
-    for k, (t, s, m) in enumerate(chips):
-        give = remote(
-            part_ref.at[t * seq + m], chip_in.at[k], sends.at[k], recvs.at[k], to_c
-        )
-        give.start()
-        take = pltpu.make_async_copy(part_ref.at[t * seq + s], held.at[k], loads.at[k])
-        take.start()
-        gives.append(give)
-        takes.append(take)
+    gives = [
+        remote(part_ref.at[t * seq + m], chip_in.at[k], sends.at[k], recvs.at[k], to_c)
+        for k, (t, s, m) in enumerate(chips)
+    ]
+    takes = [
+        pltpu.make_async_copy(part_ref.at[t * seq + s], held.at[k], loads.at[k])
+        for k, (t, s, m) in enumerate(chips)
+    ]
+
+    def hop(i, src, dst, device):
+        return remote(src, dst, sends.at[i], recvs.at[i], device)
+
+    d0 = hop(4, held.at[0, top], far_in.at[0, top], to_x)
+    d1 = hop(5, held.at[0, low], far_in.at[1, low], to_y)
+    x0 = hop(6, held.at[1, top], near_in.at[0, top], to_x)
+    y1 = hop(7, held.at[2, low], near_in.at[1, low], to_y)
+    y0 = hop(8, held.at[2, top], near_in.at[1, top], to_y)
+    x1 = hop(9, held.at[1, low], near_in.at[0, low], to_x)
+
+    def begin():
+        enter((to_x, to_y, to_c))
+        for give, take in zip(gives, takes):
+            give.start()
+            take.start()
 
     def chip_sum(k):
         takes[k].wait()
         gives[k].wait_recv()
         add_rows(held.at[k], (held.at[k], chip_in.at[k]), 0, rows, held.dtype)
 
-    def send(i, src, dst, device):
-        copy = remote(src, dst, sends.at[i], recvs.at[i], device)
-        copy.start()
-        return copy
-
-    chip_sum(0)
-    d0 = send(4, held.at[0, top], far_in.at[0, top], to_x)
-    d1 = send(5, held.at[0, low], far_in.at[1, low], to_y)
-    chip_sum(1)
-    x0 = send(6, held.at[1, top], near_in.at[0, top], to_x)
-    chip_sum(2)
-    y1 = send(7, held.at[2, low], near_in.at[1, low], to_y)
-    chip_sum(3)
-    d0.wait_recv()
-    add_rows(held.at[2], (held.at[2], far_in.at[0]), 0, part, held.dtype)
-    y0 = send(8, held.at[2, top], near_in.at[1, top], to_y)
-    d1.wait_recv()
-    add_rows(held.at[1], (held.at[1], far_in.at[1]), part, part, held.dtype)
-    x1 = send(9, held.at[1, low], near_in.at[0, low], to_x)
-    x0.wait_recv()
-    y0.wait_recv()
-    add_rows(sum_ref, (held.at[3], near_in.at[0], near_in.at[1]), 0, part, sum_ref.dtype)
-    y1.wait_recv()
-    x1.wait_recv()
-    add_rows(sum_ref, (held.at[3], near_in.at[0], near_in.at[1]), part, part, sum_ref.dtype)
-    for copy in gives + [d0, d1, x0, y1, y0, x1]:
-        copy.wait_send()
+    def diagonal():
+        chip_sum(0)
+        d0.start()
+        d1.start()
+
+    def along_x():
+        chip_sum(1)
+        x0.start()
+
+    def along_y():
+        chip_sum(2)
+        y1.start()
+
+    def own():
+        chip_sum(3)
+
+    def fold():
+        d0.wait_recv()
+        add_rows(held.at[2], (held.at[2], far_in.at[0]), 0, part, held.dtype)
+        y0.start()
+        d1.wait_recv()
+        add_rows(held.at[1], (held.at[1], far_in.at[1]), part, part, held.dtype)
+        x1.start()
+
+    def finish():
+        x0.wait_recv()
+        y0.wait_recv()
+        add_rows(sum_ref, (held.at[3], near_in.at[0], near_in.at[1]), 0, part, sum_ref.dtype)
+        y1.wait_recv()
+        x1.wait_recv()
+        add_rows(sum_ref, (held.at[3], near_in.at[0], near_in.at[1]), part, part, sum_ref.dtype)
+        for copy in gives + [d0, d1, x0, y1, y0, x1]:
+            copy.wait_send()
+
+    return begin, diagonal, along_x, along_y, own, fold, finish
+
+
+def scatter_kernel(*refs):
+    for stage in scatter_stages(*refs):
+        stage()
+
+
+def scatter_scratch(rows, width, kind):
+    return [
+        pltpu.VMEM((4, rows, width), kind),
+        pltpu.VMEM((4, rows, width), kind),
+        pltpu.VMEM((2, rows, width), kind),
+        pltpu.VMEM((2, rows, width), kind),
+        pltpu.SemaphoreType.DMA((4,)),
+        pltpu.SemaphoreType.DMA((10,)),
+        pltpu.SemaphoreType.DMA((10,)),
+    ]
 
 
 def scatter_plane(partial, ident):
@@ -271,15 +309,7 @@
         out_shape=jax.ShapeDtypeStruct((rows, width), F32),
         in_specs=[pl.BlockSpec(memory_space=pltpu.HBM)],
         out_specs=pl.BlockSpec(memory_space=pltpu.VMEM),
-        scratch_shapes=[
-            pltpu.VMEM((4, rows, width), kind),
-            pltpu.VMEM((4, rows, width), kind),
-            pltpu.VMEM((2, rows, width), kind),
-            pltpu.VMEM((2, rows, width), kind),
-            pltpu.SemaphoreType.DMA((4,)),
-            pltpu.SemaphoreType.DMA((10,)),
-            pltpu.SemaphoreType.DMA((10,)),
-        ],
+        scratch_shapes=scatter_scratch(rows, width, kind),
         cost_estimate=pl.CostEstimate(
             flops=0, transcendentals=0, bytes_accessed=plane * size * 14
         ),
@@ -288,6 +318,127 @@
         ),
         name="scatter_plane",
     )(partial.reshape(plane, rows, width))
+
+
+def attn_back_kernel(
+    starts_ref,
+    q_ref,
+    k_ref,
+    v_ref,
+    g_ref,
+    log_ref,
+    cos_ref,
+    sin_ref,
+    part_ref,
+    grad_ref,
+    sum_ref,
+    bias,
+    turned,
+    keys_sum,
+    values_sum,
+    *scatter,
+):
+    begin, diagonal, along_x, along_y, own, fold, finish = scatter_stages(
+        part_ref, sum_ref, *scatter
+    )
+    begin()
+    total, dim = cos_ref.shape
+    heads = q_ref.shape[1] // dim
+    blocks = total // PIC
+    scale = dim ** (-0.5)
+    events = {(0, 1): diagonal, (0, 2): along_x, (0, 3): along_y, (1, 0): own, (2, 2): fold}
+
+    def unturn(rows, at):
+        return rows * cos_ref[at, :] + pltpu.roll(rows, dim // 2, 1) * sin_ref[at, :]
+
+    def head_step(i, carry):
+        t, h = i // heads, lax.rem(i, heads)
+        base = pl.multiple_of(t * total, total)
+        cols = pl.ds(pl.multiple_of(h * dim, dim), dim)
+
+        @pl.when(h == 0)
+        def _():
+            turned[...] = k_ref[pl.ds(base, total), :].T
+            keys_sum[...] = jnp.zeros(keys_sum.shape, F32)
+            values_sum[...] = jnp.zeros(values_sum.shape, F32)
+            for b in range(blocks):
+                span = min(2 * PIC, total - b * PIC)
+                k_at = lax.broadcasted_iota(jnp.int32, (span, PIC), 0) + b * PIC
+                q_at = lax.broadcasted_iota(jnp.int32, (span, PIC), 1) + b * PIC
+                high, below = jnp.maximum(k_at, q_at), jnp.minimum(k_at, q_at)
+                allowed = k_at <= q_at
+                for j in range(NPIC):
+                    start = starts_ref[t, j]
+                    allowed = allowed | ((below >= start) & (high < start + PIC))
+                bias[b, :span, :] = jnp.where(allowed, 0.0, -jnp.inf)
+
+        for b in range(blocks):
+            at = pl.ds(pl.multiple_of(base + b * PIC, PIC), PIC)
+            span = min(2 * PIC, total - b * PIC)
+            count = b * PIC + span
+            seen = pl.ds(base, count)
+            queries, grads = q_ref[at, cols], g_ref[at, cols]
+            scores = nt(k_ref[seen, :], queries) * scale - log_ref[i, :, b * PIC : (b + 1) * PIC]
+            late = scores[b * PIC :] + bias[b, :span, :]
+            scores = jnp.concatenate([scores[: b * PIC], late], axis=0) if b else late
+            probs = jnp.exp(scores)
+            prob_grad = nt(v_ref[seen, :], grads)
+            mean = jnp.sum(probs * prob_grad, axis=0, keepdims=True)
+            score_grad = (probs * (prob_grad - mean)).astype(BF)
+            values_sum[:count, :] += nn(probs.astype(BF), grads)
+            keys_sum[:count, :] += nn(score_grad, queries)
+            back = nn(turned[:, :count], score_grad).T * scale
+            grad_ref[at, cols] = unturn(back, pl.ds(b * PIC, PIC)).astype(BF)
+            for (step, block), stage in events.items():
+                if block == b:
+                    pl.when(i == step)(stage)
+
+        @pl.when(h == heads - 1)
+        def _():
+            rows = pl.ds(base, total)
+            back = unturn(keys_sum[...] * scale, pl.ds(0, total))
+            grad_ref[rows, heads * dim : (heads + 1) * dim] = back.astype(BF)
+            grad_ref[rows, (heads + 1) * dim :] = values_sum[...].astype(BF)
+
+        return carry
+
+    lax.fori_loop(0, log_ref.shape[0], head_step, 0)
+    finish()
+
+
+def attn_back_plane(starts, queries, keys, values, grads, log_total, cos, sin, partial, ident):
+    plane = lax.axis_size("tp") * lax.axis_size("seq")
+    rows, width = partial.shape[0] // plane, partial.shape[1]
+    total, dim = cos.shape
+    tokens, q_part = queries.shape
+    hbm = pl.BlockSpec(memory_space=pltpu.HBM)
+    vmem = pl.BlockSpec(memory_space=pltpu.VMEM)
+    smem = pl.BlockSpec(memory_space=pltpu.SMEM)
+    return pl.pallas_call(
+        attn_back_kernel,
+        out_shape=(
+            jax.ShapeDtypeStruct((tokens, q_part + 2 * dim), BF),
+            jax.ShapeDtypeStruct((rows, width), F32),
+        ),
+        in_specs=[smem] + [vmem] * 7 + [hbm],
+        out_specs=(vmem, vmem),
+        scratch_shapes=[
+            pltpu.VMEM((total // PIC, 2 * PIC, PIC), F32),
+            pltpu.VMEM((dim, total), BF),
+            pltpu.VMEM((total, dim), F32),
+            pltpu.VMEM((total, dim), F32),
+        ]
+        + scatter_scratch(rows, width, partial.dtype),
+        cost_estimate=pl.CostEstimate(
+            flops=10 * tokens * total * q_part,
+            transcendentals=tokens * total * q_part // dim,
+            bytes_accessed=plane * rows * width * 28,
+        ),
+        compiler_params=pltpu.CompilerParams(
+            collective_id=ident, has_side_effects=True, vmem_limit_bytes=50 << 20
+        ),
+        name="attn_back_plane",
+    )(starts, queries, keys, values, grads, log_total, cos, sin, partial.reshape(plane, rows, width))
 
 
 def exchange_kernel(in_ref, out_ref, stage, local, sends, recvs):
@@ -852,27 +1003,18 @@
     )
 
     branch_grad = gather_plane(after((keep * hidden_grad).astype(BF), gu_partial, down_partial), 7)
-    mixed_grad = nn(branch_grad, out_weight).astype(BF).reshape(TP, total_len, heads, DH)
-    values_grad = jnp.einsum(
-        "thqk,tqhd->tkd", probs_low, mixed_grad, preferred_element_type=F32
-    ).astype(BF)
-    prob_grad = jnp.einsum("tqhd,tkd->thqk", mixed_grad, values, preferred_element_type=F32)
-    score_grad = (
-        probs * (prob_grad - jnp.sum(probs * prob_grad, axis=-1, keepdims=True))
-    ).astype(BF)
-    queries_grad = (
-        jnp.einsum("thqk,tkd->tqhd", score_grad, keys, preferred_element_type=F32) * scale
-    )
-    keys_grad = (
-        jnp.einsum("thqk,tqhd->tkd", score_grad, queries, preferred_element_type=F32) * scale
-    )
-    qkv_grad = jnp.concatenate(
-        [
-            turn(queries_grad, cos_table, -sin_table).astype(BF).reshape(-1, q_part),
-            turn(keys_grad, cos_table, -sin_table).astype(BF).reshape(-1, DH),
-            values_grad.reshape(-1, DH),
-        ],
-        axis=1,
+    mixed_grad = nn(branch_grad, out_weight).astype(BF)
+    qkv_grad, ffn_out = attn_back_plane(
+        starts,
+        queries.reshape(-1, q_part),
+        keys.reshape(-1, DH),
+        values.reshape(-1, DH),
+        mixed_grad,
+        log_total.reshape(TP * heads, 1, total_len),
+        jnp.concatenate([cos_table, cos_table], axis=1),
+        jnp.concatenate([sin_table, -sin_table], axis=1),
+        out_partial.reshape(-1, width),
+        9,
     )
     attn_partial = jnp.concatenate(
         [tn(norm1_all, qkv_grad).astype(BF), tn(branch_grad, mixed).astype(BF)], axis=1
@@ -884,11 +1026,10 @@
     input_grad = hidden_grad + scale1 * (
         scaled1 - norm1 * jnp.mean(scaled1 * norm1, axis=-1, keepdims=True)
     )
-    ffn_out = scatter_plane(after(out_partial.reshape(-1, width), scaled1), 9)
     out_hidden = (hidden + keep * ffn_out).astype(BF)
 
     gate_grad, up_grad, down_own, gain_ffn_grad = finish_plane(
-        after(gu_sums.reshape(plane, -1, 2 * ff_part), ffn_out),
+        after(gu_sums.reshape(plane, -1, 2 * ff_part), scaled1),
         down_sums.reshape(plane, -1, ff_part),
         w_gate,
         w_up,

time: 694 us -> 647 us (0.932)
  matrix products: 123 us -> 83.4 us
  other arithmetic: 54.4 us -> 42.9 us
    pallas_call x0 -> x1, Pallas kernels: none -> 43.4 us  [attn_back_plane(): pl.pallas_call(attn_back_kernel, out_shape=(jax.ShapeDtypeStruct((tokens,...]
    pallas_call x3 -> x2, Pallas kernels: 121 us -> 81 us  [scatter_plane(): pl.pallas_call(scatter_kernel, out_shape=jax.ShapeDtypeStruct((rows, widt...]
    dot_general x4 -> x0, matrix products: 31.7 us -> none  [the longest x1 13.4 us: per_device(): jnp.einsum('tqhd,tkd->thqk', mixed_grad, values, preferred_element_type=F32)]
    convert_element_type x1, other arithmetic: 12.8 us -> 0.58 us  [per_device(): queries = turn(projected[..., :q_part].reshape(TP, total_len, heads, DH),...]
    unnamed x117 -> x107, local copies, waits for them, and re-layouts: 25.5 us -> 23.9 us
  transfers between devices with their start and end apart: 6 -> 6, of which waited for: 1 -> 1; matrix products, arithmetic and copies ran while one was open for 28% -> 22% of each run, Pallas kernels for 44% -> 48%
where the time goes in v6:
time: 647 us; the launch traced here: 642 us
  Pallas kernels  434 us (67%)
  matrix products  83.4 us (13%)
  local copies, waits for them, and re-layouts  55.8 us (9%)
  other arithmetic  42.9 us (7%)
  between operations  14.9 us (2%)
  waiting for transfers between devices  9.39 us (1%)
    pallas_call x3, Pallas kernels, gather_plane(): pl.pallas_call(gather_kernel, out_shape=jax.ShapeDtypeStruct((plane, rows...  127 us
    pallas_call x1, Pallas kernels, ffn_plane(): pl.pallas_call(ffn_kernel, out_shape=(shape((plane, rows, width), BF), sh...  99.6 us
    pallas_call x2, Pallas kernels, scatter_plane(): pl.pallas_call(scatter_kernel, out_shape=jax.ShapeDtypeStruct((rows, widt...  81 us
    dot_general x8, matrix products, dot(): lax.dot_general(left, right, ((contract[:1], contract[1:]), ((), ())), pr...  68.1 us
    pallas_call x3, Pallas kernels, exchange_plane(): pl.pallas_call(exchange_kernel, out_shape=jax.ShapeDtypeStruct(blocks.sha...  53.9 us
    pallas_call x1, Pallas kernels, attn_back_plane(): pl.pallas_call(attn_back_kernel, out_shape=(jax.ShapeDtypeStruct((tokens,...  43.4 us
    pallas_call x1, Pallas kernels, finish_plane(): pl.pallas_call(finish_kernel, out_shape=(shape(gate_weight.shape, F32), s...  29.5 us
    unnamed x107, local copies, waits for them, and re-layouts  23.9 us
  transfers between devices with their start and end apart: 6, of which 1 were waited for; matrix products, arithmetic and copies ran while one was open for 22% of the time, Pallas kernels for 48%

profile of v6, /device:TPU:1, one launch (start us, length us, event | category | flops | bytes accessed | tf_op | source)
XLA Modules:
  0.0 642.2 jit_solution(8079150662001585566)
XLA Ops:
  8.3 1.1 fusion.26
  11.4 13.7 %exchange_plane.3 = bf16[8,64,768]{2,1,0:T(8,128)(2,1)} custom-call(bf16[8,64,768]{2,1,0:T(8,128)(2,1)} %pad_maximum_fusion.1.in_ref), custom_call_target="tpu_custom_call" | custom-call | bytes 15728640 | tf_op jit(solution)/shard_map/exchange_plane/pallas_call | solution.py:470
  25.1 2.4 copy.124
  28.3 1.2 multiply_convert_fusion.2
  29.5 2.5 reshape.383
  34.2 3.1 concatenate.50.in_ref
  37.3 28.0 %exchange_plane.4 = bf16[8,64,2112]{2,1,0:T(8,128)(2,1)} custom-call(bf16[8,64,2112]{2,1,0:T(8,128)(2,1)} %concatenate.50.in_ref), custom_call_target="tpu_custom_call" | custom-call | bytes 43253760 | tf_op jit(solution)/shard_map/exchange_plane/pallas_call | solution.py:470
  65.9 1.1 collective-permute-start
  67.4 1.2 fusion.5.own_ref
  68.6 3.0 fusion.32
  71.6 1.0 copy.126
  73.5 42.9 %gather_plane.3 = bf16[8,256,2048]{2,1,0:T(8,128)(2,1)} custom-call(bf16[256,2048]{1,0:T(8,128)(2,1)} %fusion.5.own_ref), custom_call_target="tpu_custom_call" | custom-call | bytes 100663296 | tf_op jit(solution)/shard_map/gather_plane/pallas_call | solution.py:174
  116.9 2.9 and_or_fusion
  119.9 7.7 %fusion.13 = f32[2,1024,512]{1,2,0:T(8,128)S(1)} fusion(bf16[2,1024,2048]{2,1,0:T(8,128)(2,1)} %bitcast.151, bf16[2048,768]{0,1:T(8,128)(2,1)} %all-gather.3.cloned.1.call-done), kind=kOutput, calls=%fused_computation.32 | convolution fusion | flops 4294967296 | bytes 14680064 | tf_op jit(solution)/shard_map/dot_general | solution.py:57
  127.7 1.8 copy-done.29
  129.5 1.2 fusion.41
  130.7 3.2 copy.150
  133.8 1.9 copy.149
  135.8 2.9 multiply_subtract_fusion
  139.7 1.7 subtract_convert_fusion
  141.5 4.2 fusion
  145.7 4.2 exponential_reduce_fusion
  149.9 1.5 copy-done.16
  151.5 11.2 %fusion.18 = bf16[2,1024,2,128]{1,3,2,0:T(8,128)(2,1)S(1)} fusion(f32[2,1024,1024,2]{2,1,3,0:T(8,128)} %copy-done.16, f32[2,2,1024]{2,1,0:T(2,128)S(1)} %log_add_fusion, pred[2,1024,1024]{1,2,0:T(8,128)(4,1)S(1)} %copy-done.24, f32[2,1024,512]{1,2,0:T(8,128)} %copy-done.29), kind=kOutput, calls=%fused_computation.47 | convolution fusion | flops 1091043328 | bytes 20463616 | tf_op jit(solution)/shard_map/thqk,tkd->tqhd/dot_general | solution.py:984
  163.5 4.0 convolution_convert_fusion.1
  167.5 39.6 %scatter_plane.2 = f32[256,2048]{1,0:T(8,128)S(1)} custom-call(bf16[8,256,2048]{2,1,0:T(8,128)(2,1)S(1)} %bitcast.144), custom_call_target="tpu_custom_call" | custom-call | bytes 117440512 | tf_op jit(solution)/shard_map/scatter_plane/pallas_call | solution.py:307
  207.1 1.7 multiply_reduce_fusion.1
  208.8 42.2 %gather_plane.4.grad_ref = bf16[8,256,2048]{2,1,0:T(8,128)(2,1)} custom-call(bf16[256,2048]{1,0:T(8,128)(2,1)} %get-tuple-element.32.own_ref), custom_call_target="tpu_custom_call" | custom-call | bytes 100663296 | tf_op jit(solution)/shard_map/gather_plane/pallas_call | solution.py:174
  251.0 1.1 multiply_convert_fusion.1.own_ref
  252.2 99.6 %ffn_plane.1 = (bf16[8,256,2048]{2,1,0:T(8,128)(2,1)}, bf16[4,512,704]{2,1,0:T(8,128)(2,1)}, bf16[4,512,1408]{2,1,0:T(8,128)(2,1)}, bf16[8,256,2048]{2,1,0:T(8,128)(2,1)}, f32[256,2048]{1,0:T(8,128)}) custom-call(bf16[256,2048]{1,0:T(8,128)(2,1)} %multiply_convert_fusion.1.own_ref, bf16[8,256,2048]{2,1,0:T(8,128)(2,1)} %gather_plane.4.grad_ref, ...), custom_call_target="tpu_custom_call" | custom-call | flops 35433480192 | bytes 125829120 | tf_op jit(solution)/shard_map/ffn_plane/pallas_call | solution.py:764
  351.8 10.8 %convolution_convert_fusion.3 = bf16[2048,704]{0,1:T(8,128)(2,1)} fusion(bf16[2048,2048]{1,0:T(8,128)(2,1)} %bitcast.155, bf16[2048,704]{1,0:T(8,128)(2,1)} %bitcast.182), kind=kOutput, calls=%fused_computation.11 | convolution fusion | flops 5907021824 | bytes 14155776 | tf_op jit(solution)/shard_map/dot_general | solution.py:57
  362.7 19.3 %convolution_convert_fusion.2 = bf16[2048,1408]{1,0:T(8,128)(2,1)} fusion(bf16[2048,2048]{1,0:T(8,128)(2,1)} %bitcast.180, bf16[2048,1408]{1,0:T(8,128)(2,1)} %bitcast.181), kind=kOutput, calls=%fused_computation.9 | convolution fusion | flops 11814043648 | bytes 19922944 | tf_op jit(solution)/shard_map/dot_general | solution.py:57
  383.1 1.5 pad_maximum_fusion.3
  384.6 2.0 copy.133
  387.6 2.1 slice.89
  389.7 2.0 copy.132
  391.8 1.3 copy.135
  393.1 1.5 copy.177
  394.7 1.5 pad_maximum_fusion.2.k_ref
  396.2 2.2 multiply_reduce_fusion
  398.7 1.6 multiply_convert_fusion.own_ref
  400.3 41.7 %gather_plane.5 = bf16[8,256,2048]{2,1,0:T(8,128)(2,1)} custom-call(bf16[256,2048]{1,0:T(8,128)(2,1)} %multiply_convert_fusion.own_ref), custom_call_target="tpu_custom_call" | custom-call | bytes 100663296 | tf_op jit(solution)/shard_map/gather_plane/pallas_call | solution.py:174
  442.0 7.1 %convolution_convert_fusion.6.g_ref = bf16[2048,256]{1,0:T(8,128)(2,1)} fusion(bf16[2048,2048]{1,0:T(8,128)(2,1)} %bitcast.156, bf16[2048,768]{0,1:T(8,128)(2,1)} %all-gather.3.cloned.1.call-done), kind=kOutput, calls=%fused_computation.23 | convolution fusion | flops 2148007936 | bytes 10485760 | tf_op jit(solution)/shard_map/dot_general | solution.py:57
  449.2 43.4 %attn_back_plane.1 = (bf16[2048,512]{1,0:T(8,128)(2,1)}, f32[256,2048]{1,0:T(8,128)}) custom-call(s32[2,2]{1,0:T(2,128)S(1)} %get-tuple-element.52.starts_ref, bf16[2048,256]{1,0:T(8,128)(2,1)S(1)} %bitcast.148, bf16[2048,128]{1,0:T(8,128)(2,1)S(1)} %pad_maximum_fusion.2.k_ref, bf16[2048,128]{1,0:T(8,128)(2,1)S(1)} %bitcast.149, ...), custom_call_target="tpu_custom_call" | custom-call | flops 5368709120 | bytes 117440512 | tf_op jit(solution)/shard_map/attn_back_plane/pallas_call | solution.py:417
  492.5 5.9 convolution_convert_fusion.5
  498.5 4.9 convolution_convert_fusion.4
  503.4 1.9 pad_maximum_fusion
  505.3 1.2 copy-done.37
  506.4 8.4 %convolution_convert_fusion = bf16[2048,2048]{1,0:T(8,128)(2,1)} fusion(bf16[2048,512]{1,0:T(8,128)(2,1)} %get-tuple-element.41, bf16[2048,768]{0,1:T(8,128)(2,1)S(1)} %copy-done.37), kind=kOutput, calls=%fused_computation.7 | convolution fusion | flops 4299161600 | bytes 12582912 | tf_op jit(solution)/shard_map/dot_general | solution.py:57
  514.9 9.3 %reduce-scatter.4.cloned.1.call-done = bf16[512,1408]{1,0:T(8,128)(2,1)} async-done(((bf16[2048,1408]{1,0:T(8,128)(2,1)}), bf16[512,1408]{1,0:T(8,128)(2,1)}) %reduce-scatter.4.cloned.1.call-update) | async-done | bytes 1441808 | tf_op jit(solution)/shard_map/reduce_scatter | solution.py:1000
  524.6 3.4 copy-done
  528.0 41.4 %scatter_plane.3 = f32[256,2048]{1,0:T(8,128)S(1)} custom-call(bf16[8,256,2048]{2,1,0:T(8,128)(2,1)S(1)} %bitcast.145), custom_call_target="tpu_custom_call" | custom-call | bytes 117440512 | tf_op jit(solution)/shard_map/scatter_plane/pallas_call | solution.py:307
  569.4 29.5 %finish_plane.1 = (f32[64,5632]{1,0:T(8,128)S(1)}, f32[64,5632]{1,0:T(8,128)S(1)}, bf16[8,64,704]{2,1,0:T(8,128)(2,1)S(1)}, f32[64,1]{1,0:T(8,128)S(1)}) custom-call(bf16[8,64,1408]{2,1,0:T(8,128)(2,1)S(1)} %bitcast.147, bf16[8,64,704]{2,1,0:T(8,128)(2,1)S(1)} %bitcast.146, bf16[64,5632]{1,0:T(8,128)(2,1)S(1)} %copy-done.4, bf16[64,5632]{1,0:T(8,128)(2,1)S(1)} %copy-done.2, ...), custom_call_target="tpu_custom_call" | custom-call | bytes 43253760 | tf_op jit(solution)/shard_map/finish_plane/pallas_call | solution.py:858
  599.0 1.1 copy-done.6
  600.1 1.1 copy-done.8
  601.3 2.1 copy.143
  603.4 2.9 reshape.414
  607.4 1.1 copy-done.12
  608.8 5.1 fusion.11
  613.8 2.3 copy.136
  616.1 12.2 %exchange_plane.5 = bf16[8,64,768]{2,1,0:T(8,128)(2,1)} custom-call(bf16[8,64,768]{2,1,0:T(8,128)(2,1)} %bitcast.164), custom_call_target="tpu_custom_call" | custom-call | bytes 15728640 | tf_op jit(solution)/shard_map/exchange_plane/pallas_call | solution.py:470
  628.3 1.3 convert_element_type.174
  633.2 1.1 copy.181
  634.3 1.1 copy.182
  (155 shorter events, 18.2 us)
Async XLA Ops:
  7.2 112.7 %all-gather.3.cloned.1.call-start = ((), (), s32[]{:S(2)}) async-start(), calls=%async_computation.3 | async-start | bytes 3932160 | tf_op jit(solution)/shard_map/all_gather | solution.py:937
  11.4 16.2 %copy-start.35 = (bf16[5632,64]{0,1:T(8,128)(2,1)S(1)}, bf16[5632,64]{0,1:T(8,128)(2,1)}, u32[]{:S(2)}) copy-start(bf16[5632,64]{0,1:T(8,128)(2,1)} %param.24) | copy-start | bytes 2162692
  25.1 3.2 copy-start.1
  25.1 3.2 copy-start.3
  25.1 3.2 copy-start.43
  27.6 224.6 %all-gather.5.cloned.1.call-start = ((), (), s32[]{:S(2)}) async-start(), calls=%async_computation.4 | async-start | bytes 11141120 | tf_op jit(solution)/shard_map/all_gather | solution.py:957
  32.7 1.1 copy-start.30
  65.2 0.7 copy-start.46
  65.3 1.8 copy-start.13
  65.3 449.6 %reduce-scatter.6.cloned.1.call-start = ((), (), s32[]{:S(2)}) async-start(), calls=%async_computation.6 | async-start | bytes 3604480 | tf_op jit(solution)/shard_map/reduce_scatter | solution.py:998
  65.9 50.9 %collective-permute-start = (s32[1,2]{1,0:T(1,128)S(1)}, s32[1,2]{1,0:T(1,128)S(1)}, u32[]{:S(2)}, u32[]{:S(2)}) collective-permute-start(s32[1,2]{1,0:T(1,128)S(1)} %copy-done.46), channel_id=1, source_target_pairs={{0,4},{4,0},{1,5},{5,1},{2,6},{6,2},{3,7},{7,3},{8,12},{12,8},{9,1... | collective-permute-start | bytes 32 | tf_op jit(solution)/shard_map/ppermute | solution.py:961
  67.3 5.3 copy-start.40
  71.6 64.2 %copy-start.20 = (f32[1024,64]{1,0:T(8,128)}, f32[1024,64]{1,0:T(8,128)S(1)}, u32[]{:S(2)}) copy-start(f32[1024,64]{1,0:T(8,128)S(1)} %get-tuple-element.72) | copy-start | bytes 786436
  71.6 64.2 %copy-start.22 = (f32[1024,64]{1,0:T(8,128)}, f32[1024,64]{1,0:T(8,128)S(1)}, u32[]{:S(2)}) copy-start(f32[1024,64]{1,0:T(8,128)S(1)} %get-tuple-element.73) | copy-start | bytes 786436
  73.5 43.3 %copy-start.45 = (s32[1,256]{1,0:T(1,128)S(1)}, s32[1,256]{1,0:T(1,128)}, u32[]{:S(2)}) copy-start(s32[1,256]{1,0:T(1,128)} %param.15) | copy-start | bytes 3076
  127.5 2.0 copy-start.29
  138.7 1.0 copy-start.33
  138.7 1.0 copy-start.34
  138.7 2.7 copy-start.24
  139.7 6.0 copy-start.27
  141.4 4.3 copy-start.32
  145.7 5.7 copy-start.16
  163.5 4.0 copy-start.25
  167.5 39.7 %copy-start.17 = (bf16[1,256,2048]{2,1,0:T(8,128)(2,1)S(1)}, bf16[1,256,2048]{2,1,0:T(8,128)(2,1)}, u32[]{:S(2)}) copy-start(bf16[1,256,2048]{2,1,0:T(8,128)(2,1)} %param.25) | copy-start | bytes 3145732
  208.8 42.2 %copy-start.10 = (f32[256,2048]{1,0:T(8,128)}, f32[256,2048]{1,0:T(8,128)S(1)}, u32[]{:S(2)}) copy-start(f32[256,2048]{1,0:T(8,128)S(1)} %get-tuple-element.50) | copy-start | bytes 6291460
  362.6 161.6 %reduce-scatter.4.cloned.1.call-start = ((), (), s32[]{:S(2)}) async-start(), calls=%async_computation.5 | async-start | bytes 7208960 | tf_op jit(solution)/shard_map/reduce_scatter | solution.py:1000
  381.9 1.0 copy-start.21
  381.9 1.2 copy-start.23
  382.0 231.9 %reduce-scatter.8.cloned.1.call-start = ((), (), s32[]{:S(2)}) async-start(), calls=%async_computation.7 | async-start | bytes 3932160 | tf_op jit(solution)/shard_map/reduce_scatter | solution.py:1024
  383.1 6.6 %copy-start.28 = (bf16[2,1024,2,128]{3,1,2,0:T(8,128)(2,1)S(1)}, bf16[2,1024,2,128]{3,1,2,0:T(8,128)(2,1)}, u32[]{:S(2)}) copy-start(bf16[2,1024,2,128]{3,1,2,0:T(8,128)(2,1)} %copy-done.27) | copy-start | bytes 3145732
  393.1 3.1 copy-start.11
  396.2 2.3 copy-start.15
  396.2 2.5 copy-start.18
  442.0 56.5 %slice-start = ((s8[8388608]{0:T(1024)(128)(4,1)}), s8[4194304]{0:T(1024)(128)(4,1)S(1)}, s32[]{:S(2)}) async-start(s8[8388608]{0:T(1024)(128)(4,1)} %bitcast.152), calls=%async_computation.8 | async-start | bytes 8388608
  449.2 43.4 %copy-start.26 = (bf16[2,1024,2,128]{3,2,1,0:T(2,128)(2,1)S(1)}, bf16[2,1024,2,128]{3,2,1,0:T(2,128)(2,1)}, u32[]{:S(2)}) copy-start(bf16[2,1024,2,128]{3,2,1,0:T(2,128)(2,1)} %copy-done.25) | copy-start | bytes 3145732
  449.2 49.3 %slice-start.1 = ((s8[8388608]{0:T(1024)(128)(4,1)}), s8[4194304]{0:T(1024)(128)(4,1)S(1)}, s32[]{:S(2)}) async-start(s8[8388608]{0:T(1024)(128)(4,1)} %bitcast.152), calls=%async_computation.9 | async-start | bytes 8388608
  492.5 6.0 copy-start.47
  503.4 3.0 copy-start.37
  514.9 9.3 %copy-start.44 = (f32[64]{0:T(128)S(1)}, f32[64]{0:T(128)}, u32[]{:S(2)}) copy-start(f32[64]{0:T(128)} %param.21) | copy-start | bytes 772
  514.9 9.4 %copy-start.36 = (bf16[512,704]{0,1:T(8,128)(2,1)S(1)}, bf16[512,704]{0,1:T(8,128)(2,1)}, u32[]{:S(2)}) copy-start(bf16[512,704]{0,1:T(8,128)(2,1)} %reduce-scatter.6.cloned.1.call-done) | copy-start | bytes 2162692
  524.6 3.4 copy-start
  528.0 41.4 %copy-start.2 = (bf16[64,5632]{1,0:T(8,128)(2,1)S(1)}, bf16[64,5632]{1,0:T(8,128)(2,1)}, u32[]{:S(2)}) copy-start(bf16[64,5632]{1,0:T(8,128)(2,1)} %up_weight.1) | copy-start | bytes 2162692
  528.0 41.4 %copy-start.4 = (bf16[64,5632]{1,0:T(8,128)(2,1)S(1)}, bf16[64,5632]{1,0:T(8,128)(2,1)}, u32[]{:S(2)}) copy-start(bf16[64,5632]{1,0:T(8,128)(2,1)} %gate_weight.1) | copy-start | bytes 2162692
  528.0 41.4 %copy-start.5 = (bf16[512,1408]{1,0:T(8,128)(2,1)S(1)}, bf16[512,1408]{1,0:T(8,128)(2,1)}, u32[]{:S(2)}) copy-start(bf16[512,1408]{1,0:T(8,128)(2,1)} %reduce-scatter.4.cloned.1.call-done) | copy-start | bytes 4325380
  599.0 1.1 copy-start.6
  600.1 1.1 copy-start.8
  603.4 3.5 copy-start.14
  603.4 3.5 copy-start.41
  606.9 1.6 copy-start.12
  606.9 1.9 copy-start.19
  629.6 1.1 copy-start.31
  629.7 1.1 copy-start.42
  629.8 2.0 copy-start.38
  629.8 2.0 copy-start.39
  629.8 3.4 copy-start.9
  631.7 2.6 copy-start.7
Sparse Core Ops, SparseCore 0:
  27.7 63.8 all-gather.2
  93.2 157.1 all-gather.4
  362.7 56.8 reduce-scatter.5
  421.8 102.3 reduce-scatter.3
  526.3 60.5 reduce-scatter.7

commit v7 on v6

--- a/solution.py
+++ b/solution.py
@@ -489,9 +489,9 @@
     grad_ref,
     weight_hbm,
     all_ref,
-    inner_ref,
     gug_ref,
     out_ref,
+    down_ref,
     sum_ref,
     weight,
     tokens,
@@ -500,6 +500,7 @@
     narrow,
     inner,
     gug,
+    stage,
     part,
     chip_in,
     far_in,
@@ -518,7 +519,8 @@
     rows, width = own_ref.shape
     pair = 2 * rows
     half = rows // 2
-    ff_part = narrow.shape[1]
+    block = width // 4
+    ff_part = narrow.shape[2]
     gate_up, lower = slice(0, 2 * ff_part), slice(2 * ff_part, 3 * ff_part)
     top, low = pl.ds(0, half), pl.ds(half, half)
     enter((to_x, to_y, to_c))
@@ -581,99 +583,37 @@
 
     def take_grads(c):
         return pltpu.make_async_copy(
-            grad_ref.at[pl.ds(chip_rows(c), 2)], grads.at[lax.rem(c, 2)], local.at[2 + lax.rem(c, 2)]
+            grad_ref.at[pl.ds(chip_rows(c), 2)], grads.at[c], local.at[2 + c]
         )
 
-    def put_gug(c):
+    def put_gug(c, slot):
         return pltpu.make_async_copy(
-            gug.at[lax.rem(c, 2)], gug_ref.at[chip_rows(c) // 2], local.at[4 + lax.rem(c, 2)]
+            gug.at[slot], gug_ref.at[chip_rows(c) // 2], local.at[6 + slot]
         )
 
-    def put_inner(c):
+    def put_down(n):
+        slot = lax.rem(n, 2)
         return pltpu.make_async_copy(
-            inner.at[c], inner_ref.at[chip_rows(c) // 2], local.at[6 + c]
+            stage.at[slot], down_ref.at[pl.ds(n * block, block)], local.at[9 + slot]
         )
 
     def put_out(c):
         return pltpu.make_async_copy(
-            tokens.at[lax.rem(c, 2)], out_ref.at[pl.ds(chip_rows(c), 2)], local.at[10 + lax.rem(c, 2)]
+            tokens.at[lax.rem(c, 2)], out_ref.at[pl.ds(chip_rows(c), 2)], local.at[11 + lax.rem(c, 2)]
         )
 
-    take_weight = pltpu.make_async_copy(weight_hbm, weight, local.at[12])
-    mine = pltpu.make_async_copy(own_ref, all_ref.at[tp_at * seq + seq_at], local.at[13])
-
-    for copy in (x0, y0, c0, x1, y1, c1, mine, take_weight, take_grads(0)):
+    take_weight = pltpu.make_async_copy(weight_hbm, weight, local.at[13])
+    mine = pltpu.make_async_copy(own_ref, all_ref.at[tp_at * seq + seq_at], local.at[14])
+
+    for copy in (take_weight, x0, y0, c0, x1, y1, c1, mine):
         copy.start()
-    mine.wait()
-    c0.wait_recv()
-    c1.wait_recv()
-    take_tokens(0).start()
-    take_weight.wait()
-
-    def after_load(c):
-        @pl.when(c == 1)
-        def _():
-            ry0.wait_recv()
-            ry1.wait_recv()
-            take_tokens(2).start()
-            chip_sum(0)
-
-        @pl.when(c == 2)
-        def _():
-            rd0.wait_recv()
-            rd1.wait_recv()
-            take_tokens(3).start()
-            chip_sum(1)
-            sum_x0.start()
-
-        @pl.when(c == 3)
-        def _():
-            chip_sum(2)
-            sum_y1.start()
-
-        @pl.when(c < 3)
-        def _():
-            take_grads(c + 1).start()
-
-    def after_chip(c):
-        @pl.when(c == 0)
-        def _():
-            x0.wait_recv()
-            diag0.start()
-            rx0.start()
-            y0.wait_recv()
-            ry0.start()
-            y1.wait_recv()
-            diag1.start()
-            ry1.start()
-            x1.wait_recv()
-            rx1.start()
-            rx0.wait_recv()
-            rx1.wait_recv()
-            take_tokens(1).start()
-
-        @pl.when(c == 1)
-        def _():
-            diag0.wait_recv()
-            rd0.start()
-            diag1.wait_recv()
-            rd1.start()
-
-    def chip_step(c, carry):
-        slot = lax.rem(c, 2)
-        take_tokens(c).wait()
-        wide[...] = nn(tokens[slot].reshape(pair, width), weight[:, gate_up])
-        after_load(c)
-        take_grads(c).wait()
-        narrow[...] = nn(grads[slot].reshape(pair, width), weight[:, lower])
-
-        @pl.when(c >= 2)
-        def _():
-            put_gug(c - 2).wait()
-
-        def slopes(i, carry):
+    for c in range(4):
+        take_grads(c).start()
+
+    def slopes(c, slot):
+        def body(i, carry):
             at = pl.ds(i * SUB, SUB)
-            gate, upward, grad = wide[at, :ff_part], wide[at, ff_part:], narrow[at, :]
+            gate, upward, grad = wide[at, :ff_part], wide[at, ff_part:], narrow[c, at, :]
             sigmoid_gate = jax.nn.sigmoid(gate)
             silu_gate = gate * sigmoid_gate
             inner[c, at, :] = (silu_gate * upward).astype(BF)
@@ -682,23 +622,107 @@
             gug[slot, at, ff_part:] = (grad * silu_gate).astype(BF)
             return carry
 
-        lax.fori_loop(0, pair // SUB, slopes, 0)
-        put_gug(c).start()
-        put_inner(c).start()
-        block = width // 4
-
-        def back(n, carry):
-            at = pl.ds(pl.multiple_of(n * block, block), block)
-            total = nt(gug[slot], weight[at, gate_up]).astype(part.dtype)
-            part[c, :, :, at] = total.reshape(2, rows, block)
+        lax.fori_loop(0, pair // SUB, body, 0)
+        put_gug(c, slot).start()
+
+    def back(c, slot, n):
+        at = pl.ds(pl.multiple_of(n * block, block), block)
+        total = nt(gug[slot], weight[at, gate_up]).astype(part.dtype)
+        part[c, :, :, at] = total.reshape(2, rows, block)
+
+    def widen(slot):
+        wide[...] = nn(tokens[slot].reshape(pair, width), weight[:, gate_up])
+
+    take_weight.wait()
+
+    def narrow_step(c, carry):
+        take_grads(c).wait()
+        narrow[c] = nn(grads[c].reshape(pair, width), weight[:, lower])
+        return carry
+
+    lax.fori_loop(0, 4, narrow_step, 0)
+    mine.wait()
+    c0.wait_recv()
+    c1.wait_recv()
+    take_tokens(0).start()
+    x0.wait_recv()
+    diag0.start()
+    rx0.start()
+    y0.wait_recv()
+    ry0.start()
+    take_tokens(0).wait()
+    widen(0)
+    slopes(0, 2)
+    y1.wait_recv()
+    diag1.start()
+    ry1.start()
+    x1.wait_recv()
+    rx1.start()
+    rx0.wait_recv()
+    rx1.wait_recv()
+    take_tokens(1).start()
+
+    def chip_step(c, carry):
+        slot = lax.rem(c, 2)
+        take_tokens(c).wait()
+        widen(slot)
+
+        @pl.when(c == 1)
+        def _():
+            ry0.wait_recv()
+            ry1.wait_recv()
+            take_tokens(2).start()
+
+        @pl.when(c == 2)
+        def _():
+            chip_sum(1)
+            sum_x0.start()
+
+        @pl.when(c == 3)
+        def _():
+            chip_sum(2)
+            sum_y1.start()
+            put_gug(1, 1).wait()
+
+        slopes(c, slot)
+
+        @pl.when(c == 2)
+        def _():
+            rd0.wait_recv()
+            rd1.wait_recv()
+            take_tokens(3).start()
+
+        def back_step(n, carry):
+            back(c, slot, n)
             return carry
 
-        lax.fori_loop(0, 4, back, 0)
+        lax.fori_loop(0, 4, back_step, 0)
         give(c).start()
-        after_chip(c)
+
+        @pl.when(c == 1)
+        def _():
+            diag0.wait_recv()
+            rd0.start()
+            diag1.wait_recv()
+            rd1.start()
+
         return carry
 
-    lax.fori_loop(0, 4, chip_step, 0)
+    lax.fori_loop(1, 4, chip_step, 0)
+
+    def own_step(n, carry):
+        back(0, 2, n)
+
+        @pl.when(n == 1)
+        def _():
+            chip_sum(3)
+            sum_d0.start()
+            sum_d1.start()
+
+        return carry
+
+    lax.fori_loop(0, 4, own_step, 0)
+    give(0).start()
 
     def out_step(c, carry):
         slot = lax.rem(c, 2)
@@ -706,8 +730,6 @@
         @pl.when(c >= 2)
         def _():
             put_out(c - 2).wait()
-
-        block = width // 4
 
         def out_block(n, carry):
             at = pl.ds(pl.multiple_of(n * block, block), block)
@@ -717,22 +739,32 @@
 
         lax.fori_loop(0, 4, out_block, 0)
         put_out(c).start()
-
-        @pl.when(c == 0)
+        return carry
+
+    lax.fori_loop(0, 4, out_step, 0)
+    chip_sum(0)
+
+    def down_step(n, carry):
+        @pl.when(n == 1)
         def _():
-            chip_sum(3)
-            sum_d0.start()
-            sum_d1.start()
-
+            sum_d0.wait_recv()
+            add_rows(held(2), (held(2), far_in.at[0]), 0, half, part.dtype)
+            sum_y0.start()
+            sum_d1.wait_recv()
+            add_rows(held(1), (held(1), far_in.at[1]), half, half, part.dtype)
+            sum_x1.start()
+
+        @pl.when(n >= 2)
+        def _():
+            put_down(n - 2).wait()
+
+        at = pl.ds(pl.multiple_of(n * block, block), block)
+        left = grads[:, :, :, at].reshape(4 * pair, block)
+        stage[lax.rem(n, 2)] = tn(left, inner[...].reshape(4 * pair, ff_part)).astype(BF)
+        put_down(n).start()
         return carry
 
-    lax.fori_loop(0, 4, out_step, 0)
-    sum_d0.wait_recv()
-    add_rows(held(2), (held(2), far_in.at[0]), 0, half, part.dtype)
-    sum_y0.start()
-    sum_d1.wait_recv()
-    add_rows(held(1), (held(1), far_in.at[1]), half, half, part.dtype)
-    sum_x1.start()
+    lax.fori_loop(0, 4, down_step, 0)
     sum_x0.wait_recv()
     sum_y0.wait_recv()
     add_rows(sum_ref, (held(0), near_in.at[0], near_in.at[1]), 0, half, sum_ref.dtype)
@@ -743,12 +775,13 @@
         copy.wait_send()
     for c in range(4):
         give(c).wait_send()
-        put_inner(c).wait()
     for copy in (sum_x0, sum_y1, sum_d0, sum_d1, sum_y0, sum_x1):
         copy.wait_send()
+    for c, slot in ((0, 2), (2, 0), (3, 1)):
+        put_gug(c, slot).wait()
     for c in (2, 3):
-        put_gug(c).wait()
         put_out(c).wait()
+        put_down(c).wait()
 
 
 def ffn_plane(block, grads, weight, ident):
@@ -765,9 +798,9 @@
         ffn_kernel,
         out_shape=(
             shape((plane, rows, width), BF),
-            shape((chips, 2 * rows, ff_part), BF),
             shape((chips, 2 * rows, 2 * ff_part), BF),
             shape((plane, rows, width), BF),
+            shape((width, ff_part), BF),
             shape((rows, width), F32),
         ),
         in_specs=[vmem, hbm, hbm],
@@ -775,26 +808,27 @@
         scratch_shapes=[
             pltpu.VMEM(weight.shape, BF),
             pltpu.VMEM((2, 2, rows, width), BF),
-            pltpu.VMEM((2, 2, rows, width), BF),
+            pltpu.VMEM((4, 2, rows, width), BF),
             pltpu.VMEM((2 * rows, 2 * ff_part), F32),
-            pltpu.VMEM((2 * rows, ff_part), F32),
+            pltpu.VMEM((4, 2 * rows, ff_part), F32),
             pltpu.VMEM((4, 2 * rows, ff_part), BF),
-            pltpu.VMEM((2, 2 * rows, 2 * ff_part), BF),
+            pltpu.VMEM((3, 2 * rows, 2 * ff_part), BF),
+            pltpu.VMEM((2, width // 4, ff_part), BF),
             pltpu.VMEM((4, 2, rows, width), BF),
             pltpu.VMEM((4, rows, width), BF),
             pltpu.VMEM((2, rows, width), BF),
             pltpu.VMEM((2, rows, width), BF),
             pltpu.SemaphoreType.DMA((24,)),
             pltpu.SemaphoreType.DMA((24,)),
-            pltpu.SemaphoreType.DMA((14,)),
+            pltpu.SemaphoreType.DMA((15,)),
         ],
         cost_estimate=pl.CostEstimate(
-            flops=12 * tokens * width * ff_part,
+            flops=14 * tokens * width * ff_part,
             transcendentals=tokens * ff_part,
             bytes_accessed=30 * tokens * width,
         ),
         compiler_params=pltpu.CompilerParams(
-            collective_id=ident, has_side_effects=True, vmem_limit_bytes=60 << 20
+            collective_id=ident, has_side_effects=True, vmem_limit_bytes=63 << 20
         ),
         name="ffn_plane",
     )(block, grads, weight)
@@ -988,13 +1022,11 @@
 
     scale2 = rms_scale(hidden)
     norm2 = hidden * scale2
-    norm2_all, inner, gate_up_grad, out_partial, scaled2 = ffn_plane(
+    norm2_all, gate_up_grad, out_partial, down_partial, scaled2 = ffn_plane(
         norm2.astype(BF), ffn_grad.reshape(plane, local_len, width), ffn_weight, 5
     )
     norm2_all = norm2_all.reshape(-1, width)
-    inner = inner.reshape(-1, ff_part)
     gate_up_grad = gate_up_grad.reshape(-1, 2 * ff_part)
-    down_partial = tn(ffn_grad, inner).astype(BF)
     down_sums = lax.psum_scatter(down_partial, "rep", scatter_dimension=0, tiled=True)
     gu_partial = tn(norm2_all, after(gate_up_grad, down_partial)).astype(BF)
     gu_sums = lax.psum_scatter(gu_partial, "rep", scatter_dimension=0, tiled=True)

time: 647 us -> 634 us (0.980)
  matrix products: 83.4 us -> 72.5 us
  Pallas kernels: 434 us -> 427 us
    dot_general x8 -> x7, matrix products: 68.1 us -> 57.1 us  [dot(): lax.dot_general(left, right, ((contract[:1], contract[1:]), ((), ())), pr...]
    pallas_call x1, Pallas kernels: 99.6 us -> 92.8 us  [ffn_plane(): pl.pallas_call(ffn_kernel, out_shape=(shape((plane, rows, width), BF), sh...]
    unnamed x107 -> x105, local copies, waits for them, and re-layouts: 23.9 us -> 21.7 us
  transfers between devices with their start and end apart: 6 -> 6, of which waited for: 1 -> 1; matrix products, arithmetic and copies ran while one was open for 22% -> 23% of each run, Pallas kernels for 48% -> 49%
where the time goes in v7:
time: 634 us; the launch traced here: 629 us
  Pallas kernels  427 us (67%)
  matrix products  72.5 us (11%)
  local copies, waits for them, and re-layouts  52 us (8%)
  other arithmetic  45.6 us (7%)
  waiting for transfers between devices  15.4 us (2%)
  between operations  14.9 us (2%)
    pallas_call x3, Pallas kernels, gather_plane(): pl.pallas_call(gather_kernel, out_shape=jax.ShapeDtypeStruct((plane, rows...  126 us
    pallas_call x1, Pallas kernels, ffn_plane(): pl.pallas_call(ffn_kernel, out_shape=(shape((plane, rows, width), BF), sh...  92.8 us
    pallas_call x2, Pallas kernels, scatter_plane(): pl.pallas_call(scatter_kernel, out_shape=jax.ShapeDtypeStruct((rows, widt...  80.8 us
    dot_general x7, matrix products, dot(): lax.dot_general(left, right, ((contract[:1], contract[1:]), ((), ())), pr...  57.1 us
    pallas_call x3, Pallas kernels, exchange_plane(): pl.pallas_call(exchange_kernel, out_shape=jax.ShapeDtypeStruct(blocks.sha...  53.9 us
    pallas_call x1, Pallas kernels, attn_back_plane(): pl.pallas_call(attn_back_kernel, out_shape=(jax.ShapeDtypeStruct((tokens,...  43.5 us
    pallas_call x1, Pallas kernels, finish_plane(): pl.pallas_call(finish_kernel, out_shape=(shape(gate_weight.shape, F32), s...  29.7 us
    unnamed x105, local copies, waits for them, and re-layouts  21.7 us
  transfers between devices with their start and end apart: 6, of which 1 were waited for; matrix products, arithmetic and copies ran while one was open for 23% of the time, Pallas kernels for 49%

profile of v7, /device:TPU:1, one launch (start us, length us, event | category | flops | bytes accessed | tf_op | source)
XLA Modules:
  0.0 629.1 jit_solution(16123469524551461100)
XLA Ops:
  8.3 1.1 fusion.26
  11.4 13.7 %exchange_plane.3 = bf16[8,64,768]{2,1,0:T(8,128)(2,1)} custom-call(bf16[8,64,768]{2,1,0:T(8,128)(2,1)} %pad_maximum_fusion.1.in_ref), custom_call_target="tpu_custom_call" | custom-call | bytes 15728640 | tf_op jit(solution)/shard_map/exchange_plane/pallas_call | solution.py:470
  25.1 2.4 copy.120
  28.3 1.2 multiply_convert_fusion.2
  29.5 2.5 reshape.377
  34.1 3.1 concatenate.50.in_ref
  37.2 28.0 %exchange_plane.4 = bf16[8,64,2112]{2,1,0:T(8,128)(2,1)} custom-call(bf16[8,64,2112]{2,1,0:T(8,128)(2,1)} %concatenate.50.in_ref), custom_call_target="tpu_custom_call" | custom-call | bytes 43253760 | tf_op jit(solution)/shard_map/exchange_plane/pallas_call | solution.py:470
  65.9 1.1 collective-permute-start
  67.3 1.2 fusion.5.own_ref
  68.5 3.0 fusion.32
  71.5 1.0 copy.122
  73.5 42.9 %gather_plane.3 = bf16[8,256,2048]{2,1,0:T(8,128)(2,1)} custom-call(bf16[256,2048]{1,0:T(8,128)(2,1)} %fusion.5.own_ref), custom_call_target="tpu_custom_call" | custom-call | bytes 100663296 | tf_op jit(solution)/shard_map/gather_plane/pallas_call | solution.py:174
  116.9 3.0 and_or_fusion
  119.8 7.7 %fusion.13 = f32[2,1024,512]{1,2,0:T(8,128)S(1)} fusion(bf16[2,1024,2048]{2,1,0:T(8,128)(2,1)} %bitcast.147, bf16[2048,768]{0,1:T(8,128)(2,1)} %all-gather.3.cloned.1.call-done), kind=kOutput, calls=%fused_computation.31 | convolution fusion | flops 4294967296 | bytes 14680064 | tf_op jit(solution)/shard_map/dot_general | solution.py:57
  127.7 1.8 copy-done.29
  129.5 1.2 fusion.41
  130.6 3.2 copy.145
  133.8 1.9 copy.144
  135.7 2.8 multiply_subtract_fusion
  139.6 1.8 subtract_convert_fusion
  141.3 4.3 fusion
  145.6 4.6 exponential_reduce_fusion
  150.2 1.2 copy-done.17
  151.4 11.2 %fusion.18 = bf16[2,1024,2,128]{1,3,2,0:T(8,128)(2,1)S(1)} fusion(f32[2,1024,1024,2]{2,1,3,0:T(8,128)} %copy-done.17, f32[2,2,1024]{2,1,0:T(2,128)S(1)} %log_add_fusion, pred[2,1024,1024]{1,2,0:T(8,128)(4,1)S(1)} %copy-done.24, f32[2,1024,512]{1,2,0:T(8,128)} %copy-done.29), kind=kOutput, calls=%fused_computation.46 | convolution fusion | flops 1091043328 | bytes 20463616 | tf_op jit(solution)/shard_map/thqk,tkd->tqhd/dot_general | solution.py:1018
  163.5 4.0 convolution_convert_fusion.1
  167.4 39.6 %scatter_plane.2 = f32[256,2048]{1,0:T(8,128)S(1)} custom-call(bf16[8,256,2048]{2,1,0:T(8,128)(2,1)S(1)} %bitcast.140), custom_call_target="tpu_custom_call" | custom-call | bytes 117440512 | tf_op jit(solution)/shard_map/scatter_plane/pallas_call | solution.py:307
  207.1 1.7 multiply_reduce_fusion.1
  208.7 42.2 %gather_plane.4.grad_ref = bf16[8,256,2048]{2,1,0:T(8,128)(2,1)} custom-call(bf16[256,2048]{1,0:T(8,128)(2,1)} %get-tuple-element.32.own_ref), custom_call_target="tpu_custom_call" | custom-call | bytes 100663296 | tf_op jit(solution)/shard_map/gather_plane/pallas_call | solution.py:174
  251.0 1.1 multiply_convert_fusion.1.own_ref
  252.1 92.8 %ffn_plane.1 = (bf16[8,256,2048]{2,1,0:T(8,128)(2,1)}, bf16[4,512,1408]{2,1,0:T(8,128)(2,1)}, bf16[8,256,2048]{2,1,0:T(8,128)(2,1)}, bf16[2048,704]{1,0:T(8,128)(2,1)}, f32[256,2048]{1,0:T(8,128)}) custom-call(bf16[256,2048]{1,0:T(8,128)(2,1)} %multiply_convert_fusion.1.own_ref, bf16[8,256,2048]{2,1,0:T(8,128)(2,1)} %gather_plane.4.grad_ref, ...), custom_call_target="tpu_custom_call" | custom-call | flops 41339060224 | bytes 125829120 | tf_op jit(solution)/shard_map/ffn_plane/pallas_call | solution.py:797
  345.0 19.1 %convolution_convert_fusion.2 = bf16[2048,1408]{1,0:T(8,128)(2,1)} fusion(bf16[2048,2048]{1,0:T(8,128)(2,1)} %bitcast.175, bf16[2048,1408]{1,0:T(8,128)(2,1)} %bitcast.176), kind=kOutput, calls=%fused_computation.9 | convolution fusion | flops 11814043648 | bytes 19922944 | tf_op jit(solution)/shard_map/dot_general | solution.py:57
  365.3 1.5 pad_maximum_fusion.3
  366.8 2.0 copy.129
  368.7 1.0 copy.130
  369.8 1.3 slice.89
  371.1 2.0 copy.128
  373.4 1.5 copy.172
  375.0 1.5 pad_maximum_fusion.2.k_ref
  376.5 2.2 multiply_reduce_fusion
  379.0 1.6 multiply_convert_fusion.own_ref
  380.6 41.3 %gather_plane.5 = bf16[8,256,2048]{2,1,0:T(8,128)(2,1)} custom-call(bf16[256,2048]{1,0:T(8,128)(2,1)} %multiply_convert_fusion.own_ref), custom_call_target="tpu_custom_call" | custom-call | bytes 100663296 | tf_op jit(solution)/shard_map/gather_plane/pallas_call | solution.py:174
  421.9 7.2 %convolution_convert_fusion.5.g_ref = bf16[2048,256]{1,0:T(8,128)(2,1)} fusion(bf16[2048,2048]{1,0:T(8,128)(2,1)} %bitcast.151, bf16[2048,768]{0,1:T(8,128)(2,1)} %all-gather.3.cloned.1.call-done), kind=kOutput, calls=%fused_computation.22 | convolution fusion | flops 2148007936 | bytes 10485760 | tf_op jit(solution)/shard_map/dot_general | solution.py:57
  429.1 43.5 %attn_back_plane.1 = (bf16[2048,512]{1,0:T(8,128)(2,1)}, f32[256,2048]{1,0:T(8,128)}) custom-call(s32[2,2]{1,0:T(2,128)S(1)} %get-tuple-element.52.starts_ref, bf16[2048,256]{1,0:T(8,128)(2,1)S(1)} %bitcast.143, bf16[2048,128]{1,0:T(8,128)(2,1)S(1)} %pad_maximum_fusion.2.k_ref, bf16[2048,128]{1,0:T(8,128)(2,1)S(1)} %bitcast.145, ...), custom_call_target="tpu_custom_call" | custom-call | flops 5368709120 | bytes 117440512 | tf_op jit(solution)/shard_map/attn_back_plane/pallas_call | solution.py:417
  472.7 5.9 convolution_convert_fusion.4
  478.6 4.8 convolution_convert_fusion.3
  483.4 1.8 pad_maximum_fusion
  485.3 1.2 copy-done.36
  486.4 8.4 %convolution_convert_fusion = bf16[2048,2048]{1,0:T(8,128)(2,1)} fusion(bf16[2048,512]{1,0:T(8,128)(2,1)} %get-tuple-element.41, bf16[2048,768]{0,1:T(8,128)(2,1)S(1)} %copy-done.36), kind=kOutput, calls=%fused_computation.7 | convolution fusion | flops 4299161600 | bytes 12582912 | tf_op jit(solution)/shard_map/dot_general | solution.py:57
  494.9 15.3 %reduce-scatter.4.cloned.1.call-done = bf16[512,1408]{1,0:T(8,128)(2,1)} async-done(((bf16[2048,1408]{1,0:T(8,128)(2,1)}), bf16[512,1408]{1,0:T(8,128)(2,1)}) %reduce-scatter.4.cloned.1.call-update) | async-done | bytes 1441808 | tf_op jit(solution)/shard_map/reduce_scatter | solution.py:1032
  511.0 3.4 copy-done
  514.4 41.2 %scatter_plane.3 = f32[256,2048]{1,0:T(8,128)S(1)} custom-call(bf16[8,256,2048]{2,1,0:T(8,128)(2,1)S(1)} %bitcast.141), custom_call_target="tpu_custom_call" | custom-call | bytes 117440512 | tf_op jit(solution)/shard_map/scatter_plane/pallas_call | solution.py:307
  555.6 29.7 %finish_plane.1 = (f32[64,5632]{1,0:T(8,128)S(1)}, f32[64,5632]{1,0:T(8,128)S(1)}, bf16[8,64,704]{2,1,0:T(8,128)(2,1)S(1)}, f32[64,1]{1,0:T(8,128)S(1)}) custom-call(bf16[8,64,1408]{2,1,0:T(8,128)(2,1)S(1)} %bitcast.142, bf16[8,64,704]{2,1,0:T(8,128)(2,1)S(1)} %bitcast.144, bf16[64,5632]{1,0:T(8,128)(2,1)S(1)} %copy-done.4, bf16[64,5632]{1,0:T(8,128)(2,1)S(1)} %copy-done.2, ...), custom_call_target="tpu_custom_call" | custom-call | bytes 43253760 | tf_op jit(solution)/shard_map/finish_plane/pallas_call | solution.py:892
  585.3 1.1 copy-done.6
  587.0 2.1 copy.138
  589.1 2.8 reshape.406
  591.9 1.4 reduce
  593.3 1.8 fusion.7
  595.5 5.4 fusion.11
  600.9 2.3 copy.132
  603.2 12.2 %exchange_plane.5 = bf16[8,64,768]{2,1,0:T(8,128)(2,1)} custom-call(bf16[8,64,768]{2,1,0:T(8,128)(2,1)} %bitcast.159), custom_call_target="tpu_custom_call" | custom-call | bytes 15728640 | tf_op jit(solution)/shard_map/exchange_plane/pallas_call | solution.py:470
  615.4 1.3 convert_element_type.170
  617.8 1.0 broadcast_multiply_fusion
  620.2 1.1 copy.176
  621.3 1.1 copy.177
  (151 shorter events, 16.3 us)
Async XLA Ops:
  7.2 112.7 %all-gather.3.cloned.1.call-start = ((), (), s32[]{:S(2)}) async-start(), calls=%async_computation.3 | async-start | bytes 3932160 | tf_op jit(solution)/shard_map/all_gather | solution.py:971
  11.4 16.2 %copy-start.35 = (bf16[5632,64]{0,1:T(8,128)(2,1)S(1)}, bf16[5632,64]{0,1:T(8,128)(2,1)}, u32[]{:S(2)}) copy-start(bf16[5632,64]{0,1:T(8,128)(2,1)} %param.24) | copy-start | bytes 2162692
  25.1 3.2 copy-start.1
  25.1 3.2 copy-start.3
  25.1 3.2 copy-start.42
  27.6 224.6 %all-gather.5.cloned.1.call-start = ((), (), s32[]{:S(2)}) async-start(), calls=%async_computation.4 | async-start | bytes 11141120 | tf_op jit(solution)/shard_map/all_gather | solution.py:991
  32.7 1.1 copy-start.30
  65.2 0.7 copy-start.45
  65.2 1.8 copy-start.14
  65.3 429.6 %reduce-scatter.6.cloned.1.call-start = ((), (), s32[]{:S(2)}) async-start(), calls=%async_computation.6 | async-start | bytes 3932160 | tf_op jit(solution)/shard_map/reduce_scatter | solution.py:1030
  65.9 50.9 %collective-permute-start = (s32[1,2]{1,0:T(1,128)S(1)}, s32[1,2]{1,0:T(1,128)S(1)}, u32[]{:S(2)}, u32[]{:S(2)}) collective-permute-start(s32[1,2]{1,0:T(1,128)S(1)} %copy-done.45), channel_id=1, source_target_pairs={{0,4},{4,0},{1,5},{5,1},{2,6},{6,2},{3,7},{7,3},{8,12},{12,8},{9,1... | collective-permute-start | bytes 32 | tf_op jit(solution)/shard_map/ppermute | solution.py:995
  67.3 1.2 copy-start.39
  71.5 64.2 %copy-start.20 = (f32[1024,64]{1,0:T(8,128)}, f32[1024,64]{1,0:T(8,128)S(1)}, u32[]{:S(2)}) copy-start(f32[1024,64]{1,0:T(8,128)S(1)} %get-tuple-element.72) | copy-start | bytes 786436
  71.5 64.2 %copy-start.22 = (f32[1024,64]{1,0:T(8,128)}, f32[1024,64]{1,0:T(8,128)S(1)}, u32[]{:S(2)}) copy-start(f32[1024,64]{1,0:T(8,128)S(1)} %get-tuple-element.73) | copy-start | bytes 786436
  73.5 43.3 %copy-start.44 = (s32[1,256]{1,0:T(1,128)S(1)}, s32[1,256]{1,0:T(1,128)}, u32[]{:S(2)}) copy-start(s32[1,256]{1,0:T(1,128)} %param.15) | copy-start | bytes 3076
  127.5 1.9 copy-start.29
  138.5 1.0 copy-start.33
  138.5 1.0 copy-start.34
  138.6 2.8 copy-start.24
  139.6 6.0 copy-start.27
  141.3 4.3 copy-start.32
  145.6 5.8 copy-start.17
  163.4 4.0 copy-start.25
  167.4 39.6 %copy-start.18 = (bf16[1,256,2048]{2,1,0:T(8,128)(2,1)S(1)}, bf16[1,256,2048]{2,1,0:T(8,128)(2,1)}, u32[]{:S(2)}) copy-start(bf16[1,256,2048]{2,1,0:T(8,128)(2,1)} %param.25) | copy-start | bytes 3145732
  208.7 42.2 %copy-start.11 = (f32[256,2048]{1,0:T(8,128)}, f32[256,2048]{1,0:T(8,128)S(1)}, u32[]{:S(2)}) copy-start(f32[256,2048]{1,0:T(8,128)S(1)} %get-tuple-element.50) | copy-start | bytes 6291460
  345.0 165.2 %reduce-scatter.4.cloned.1.call-start = ((), (), s32[]{:S(2)}) async-start(), calls=%async_computation.5 | async-start | bytes 7208960 | tf_op jit(solution)/shard_map/reduce_scatter | solution.py:1032
  364.1 1.0 copy-start.21
  364.1 1.2 copy-start.23
  364.1 236.7 %reduce-scatter.8.cloned.1.call-start = ((), (), s32[]{:S(2)}) async-start(), calls=%async_computation.7 | async-start | bytes 3932160 | tf_op jit(solution)/shard_map/reduce_scatter | solution.py:1056
  365.3 5.7 copy-start.28
  373.4 3.0 copy-start.12
  376.5 2.3 copy-start.16
  376.5 2.5 copy-start.19
  421.9 56.6 %slice-start = ((s8[8388608]{0:T(1024)(128)(4,1)}), s8[4194304]{0:T(1024)(128)(4,1)S(1)}, s32[]{:S(2)}) async-start(s8[8388608]{0:T(1024)(128)(4,1)} %bitcast.148), calls=%async_computation.8 | async-start | bytes 8388608
  429.1 43.5 %copy-start.26 = (bf16[2,1024,2,128]{3,2,1,0:T(2,128)(2,1)S(1)}, bf16[2,1024,2,128]{3,2,1,0:T(2,128)(2,1)}, u32[]{:S(2)}) copy-start(bf16[2,1024,2,128]{3,2,1,0:T(2,128)(2,1)} %copy-done.25) | copy-start | bytes 3145732
  429.1 49.4 %slice-start.1 = ((s8[8388608]{0:T(1024)(128)(4,1)}), s8[4194304]{0:T(1024)(128)(4,1)S(1)}, s32[]{:S(2)}) async-start(s8[8388608]{0:T(1024)(128)(4,1)} %bitcast.148), calls=%async_computation.9 | async-start | bytes 8388608
  472.7 5.9 copy-start.46
  483.4 3.0 copy-start.36
  494.9 15.4 %copy-start.43 = (f32[64]{0:T(128)S(1)}, f32[64]{0:T(128)}, u32[]{:S(2)}) copy-start(f32[64]{0:T(128)} %param.21) | copy-start | bytes 772
  511.0 3.4 copy-start
  514.3 41.2 %copy-start.2 = (bf16[64,5632]{1,0:T(8,128)(2,1)S(1)}, bf16[64,5632]{1,0:T(8,128)(2,1)}, u32[]{:S(2)}) copy-start(bf16[64,5632]{1,0:T(8,128)(2,1)} %up_weight.1) | copy-start | bytes 2162692
  514.3 41.2 %copy-start.4 = (bf16[64,5632]{1,0:T(8,128)(2,1)S(1)}, bf16[64,5632]{1,0:T(8,128)(2,1)}, u32[]{:S(2)}) copy-start(bf16[64,5632]{1,0:T(8,128)(2,1)} %gate_weight.1) | copy-start | bytes 2162692
  514.3 41.2 %copy-start.5 = (bf16[512,1408]{1,0:T(8,128)(2,1)S(1)}, bf16[512,1408]{1,0:T(8,128)(2,1)}, u32[]{:S(2)}) copy-start(bf16[512,1408]{1,0:T(8,128)(2,1)} %reduce-scatter.4.cloned.1.call-done) | copy-start | bytes 4325380
  514.3 41.2 %copy-start.8 = (bf16[512,704]{1,0:T(8,128)(2,1)S(1)}, bf16[512,704]{1,0:T(8,128)(2,1)}, u32[]{:S(2)}) copy-start(bf16[512,704]{1,0:T(8,128)(2,1)} %reduce-scatter.6.cloned.1.call-done) | copy-start | bytes 2162692
  514.4 41.3 %copy-start.9 = (f32[64,1]{1,0:T(8,128)S(1)}, f32[64,1]{1,0:T(8,128)}, u32[]{:S(2)}) copy-start(f32[64,1]{1,0:T(8,128)} %copy.137.gain_ref) | copy-start | bytes 772
  585.3 1.1 copy-start.6
  586.4 0.6 copy-start.10
  589.1 4.2 copy-start.40
  593.3 1.9 copy-start.13
  593.3 2.2 copy-start.15
  616.7 1.1 copy-start.31
  616.7 1.1 copy-start.41
  616.8 2.0 copy-start.37
  616.8 2.0 copy-start.38
  616.8 3.4 copy-start.7
Sparse Core Ops, SparseCore 0:
  27.7 63.8 all-gather.2
  93.2 157.1 all-gather.4
  345.1 60.3 reduce-scatter.5
  407.7 102.5 reduce-scatter.3
  512.4 60.5 reduce-scatter.7

commit v8 on v7

--- a/solution.py
+++ b/solution.py
@@ -24,31 +24,6 @@
     return (jnp.cos(angles), jnp.sin(angles))
 
 
-def rotate(values, cos_table, sin_table):
-    half = values.shape[-1] // 2
-    shape = (cos_table.shape[0],) + (1,) * (values.ndim - 2) + (half,)
-    cos_part = cos_table.reshape(shape)
-    sin_part = sin_table.reshape(shape)
-    first = values[..., :half]
-    second = values[..., half:]
-    return jnp.concatenate(
-        [first * cos_part - second * sin_part, second * cos_part + first * sin_part], axis=-1
-    )
-
-
-def picture_ids(positions, starts):
-    inside = (positions[None, :] >= starts[:, None]) & (positions[None, :] < starts[:, None] + PIC)
-    labels = jnp.arange(1, NPIC + 1, dtype=jnp.int32)
-    return jnp.sum(jnp.where(inside, labels[:, None], 0), axis=0)
-
-
-def visible(positions, starts):
-    ids = picture_ids(positions, starts)
-    causal = positions[None, :] <= positions[:, None]
-    same_piece = (ids[:, None] == ids[None, :]) & (ids[:, None] > 0)
-    return causal | same_piece
-
-
 def rms_scale(rows):
     return lax.rsqrt(jnp.mean(rows * rows, axis=-1, keepdims=True) + EPS)
 
@@ -108,7 +83,7 @@
     )
 
 
-def gather_kernel(own_ref, all_ref, sends, recvs, local):
+def gather_stages(own_ref, all_ref, sends, recvs, local):
     tp_at, seq_at, far, mate, _ = plane_place()
     seq = lax.axis_size("seq")
     other = 1 - tp_at
@@ -117,54 +92,75 @@
     to_c = at_device(tp_at, mate)
     rows = own_ref.shape[0]
     part = rows // 2
-    enter((to_x, to_y, to_c))
 
     def piece(t, s, h):
         return all_ref.at[t * seq + s, pl.ds(h * part, part)]
 
-    def pass_on(i, t, s, h, device):
-        copy = remote(piece(t, s, h), piece(t, s, h), sends.at[i], recvs.at[i], device)
-        copy.start()
-        return copy
+    def relay(i, t, s, h, device):
+        return remote(piece(t, s, h), piece(t, s, h), sends.at[i], recvs.at[i], device)
 
     def own(i, h, device):
-        copy = remote(
+        return remote(
             own_ref.at[pl.ds(h * part, part)],
             piece(tp_at, seq_at, h),
             sends.at[i],
             recvs.at[i],
             device,
         )
-        copy.start()
-        return copy
-
-    x0 = own(0, 0, to_x)
-    y0 = own(1, 0, to_y)
-    c0 = own(2, 0, to_c)
-    x1 = own(3, 1, to_x)
-    y1 = own(4, 1, to_y)
-    c1 = own(5, 1, to_c)
+
+    x0, x1 = own(0, 0, to_x), own(3, 1, to_x)
+    y0, y1 = own(1, 0, to_y), own(4, 1, to_y)
+    c0, c1 = own(2, 0, to_c), own(5, 1, to_c)
+    diag0 = relay(6, tp_at, far, 0, to_y)
+    diag1 = relay(7, other, seq_at, 1, to_x)
+    rx0, rx1 = relay(8, tp_at, far, 0, to_c), relay(11, tp_at, far, 1, to_c)
+    ry0, ry1 = relay(9, other, seq_at, 0, to_c), relay(10, other, seq_at, 1, to_c)
+    rd0, rd1 = relay(12, other, far, 0, to_c), relay(13, other, far, 1, to_c)
     mine = pltpu.make_async_copy(own_ref, all_ref.at[tp_at * seq + seq_at], local)
-    mine.start()
-    x0.wait_recv()
-    diag0 = pass_on(6, tp_at, far, 0, to_y)
-    rx0 = pass_on(8, tp_at, far, 0, to_c)
-    y0.wait_recv()
-    ry0 = pass_on(9, other, seq_at, 0, to_c)
-    y1.wait_recv()
-    diag1 = pass_on(7, other, seq_at, 1, to_x)
-    ry1 = pass_on(10, other, seq_at, 1, to_c)
-    x1.wait_recv()
-    rx1 = pass_on(11, tp_at, far, 1, to_c)
-    diag0.wait_recv()
-    rd0 = pass_on(12, other, far, 0, to_c)
-    diag1.wait_recv()
-    rd1 = pass_on(13, other, far, 1, to_c)
-    for copy in (c0, c1, rx0, ry0, ry1, rx1, rd0, rd1):
-        copy.wait_recv()
-    for copy in (x0, y0, c0, x1, y1, c1, diag0, diag1, rx0, ry0, ry1, rx1, rd0, rd1):
-        copy.wait_send()
-    mine.wait()
+
+    def begin():
+        enter((to_x, to_y, to_c))
+        for copy in (x0, y0, c0, x1, y1, c1, mine):
+            copy.start()
+
+    def first():
+        x0.wait_recv()
+        diag0.start()
+        rx0.start()
+        y0.wait_recv()
+        ry0.start()
+
+    def second():
+        y1.wait_recv()
+        diag1.start()
+        ry1.start()
+        x1.wait_recv()
+        rx1.start()
+
+    def finish():
+        diag0.wait_recv()
+        rd0.start()
+        diag1.wait_recv()
+        rd1.start()
+        for copy in (c0, c1, rx0, ry0, ry1, rx1, rd0, rd1):
+            copy.wait_recv()
+        for copy in (x0, y0, c0, x1, y1, c1, diag0, diag1, rx0, ry0, ry1, rx1, rd0, rd1):
+            copy.wait_send()
+        mine.wait()
+
+    return begin, first, second, finish
+
+
+def gather_kernel(*refs):
+    for stage in gather_stages(*refs):
+        stage()
+
+
+GATHER_SCRATCH = (
+    pltpu.SemaphoreType.DMA((14,)),
+    pltpu.SemaphoreType.DMA((14,)),
+    pltpu.SemaphoreType.DMA,
+)
 
 
 def gather_plane(block, ident):
@@ -176,11 +172,7 @@
         out_shape=jax.ShapeDtypeStruct((plane, rows, width), block.dtype),
         in_specs=[pl.BlockSpec(memory_space=pltpu.VMEM)],
         out_specs=pl.BlockSpec(memory_space=pltpu.HBM),
-        scratch_shapes=[
-            pltpu.SemaphoreType.DMA((14,)),
-            pltpu.SemaphoreType.DMA((14,)),
-            pltpu.SemaphoreType.DMA,
-        ],
+        scratch_shapes=GATHER_SCRATCH,
         cost_estimate=pl.CostEstimate(
             flops=0, transcendentals=0, bytes_accessed=plane * size * 12
         ),
@@ -320,11 +312,127 @@
     )(partial.reshape(plane, rows, width))
 
 
+def fill_bias(bias, starts_ref, t, blocks):
+    for b in range(blocks):
+        span = min(2, blocks - b) * PIC
+        k_at = lax.broadcasted_iota(jnp.int32, (span, PIC), 0) + b * PIC
+        q_at = lax.broadcasted_iota(jnp.int32, (span, PIC), 1) + b * PIC
+        high, below = jnp.maximum(k_at, q_at), jnp.minimum(k_at, q_at)
+        allowed = k_at <= q_at
+        for j in range(NPIC):
+            start = starts_ref[t, j]
+            allowed = allowed | ((below >= start) & (high < start + PIC))
+        bias[b, :span, :] = jnp.where(allowed, 0.0, -jnp.inf)
+
+
+def masked(scores, bias, b):
+    late = scores[b * PIC :] + bias[b, : scores.shape[0] - b * PIC, :]
+    return jnp.concatenate([scores[: b * PIC], late], axis=0) if b else late
+
+
+def attn_front_kernel(
+    starts_ref,
+    projected_ref,
+    cos_ref,
+    sin_ref,
+    own_ref,
+    qkv_ref,
+    mixed_ref,
+    log_ref,
+    all_ref,
+    bias,
+    turned,
+    *gather,
+):
+    begin, first, second, finish = gather_stages(own_ref, all_ref, *gather)
+    begin()
+    total, dim = cos_ref.shape
+    heads = mixed_ref.shape[1] // dim
+    blocks = total // PIC
+    scale = dim ** (-0.5)
+    k_cols = slice(heads * dim, (heads + 1) * dim)
+    v_cols = slice((heads + 1) * dim, (heads + 2) * dim)
+
+    def turn(rows, at):
+        return rows * cos_ref[at, :] + pltpu.roll(rows, dim // 2, 1) * sin_ref[at, :]
+
+    def head_step(i, carry):
+        t, h = i // heads, lax.rem(i, heads)
+        base = pl.multiple_of(t * total, total)
+        cols = pl.ds(pl.multiple_of(h * dim, dim), dim)
+
+        @pl.when(h == 0)
+        def _():
+            rows = pl.ds(base, total)
+            values = projected_ref[rows, v_cols].astype(BF)
+            qkv_ref[rows, k_cols] = turn(projected_ref[rows, k_cols], pl.ds(0, total)).astype(BF)
+            qkv_ref[rows, v_cols] = values
+            turned[...] = values.T
+            fill_bias(bias, starts_ref, t, blocks)
+
+        for b in range(blocks):
+            at = pl.ds(pl.multiple_of(base + b * PIC, PIC), PIC)
+            count = min(b + 2, blocks) * PIC
+            queries = turn(projected_ref[at, cols], pl.ds(b * PIC, PIC)).astype(BF)
+            qkv_ref[at, cols] = queries
+            scores = nt(qkv_ref[pl.ds(base, count), k_cols], queries) * scale
+            scores = masked(scores, bias, b)
+            peak = jnp.max(scores, axis=0, keepdims=True)
+            weights = jnp.exp(scores - peak)
+            mass = jnp.sum(weights, axis=0, keepdims=True)
+            log_ref[i, :, b * PIC : (b + 1) * PIC] = peak + jnp.log(mass)
+            probs = (weights * (1.0 / mass)).astype(BF)
+            mixed_ref[at, cols] = nn(turned[:, :count], probs).T.astype(BF)
+            if b == 0:
+                pl.when(i == 2)(first)
+
+        return carry
+
+    lax.fori_loop(0, log_ref.shape[0], head_step, 0)
+    second()
+    finish()
+
+
+def attn_front_plane(starts, projected, cos, sin, block, ident):
+    rows, width = block.shape
+    plane = lax.axis_size("tp") * lax.axis_size("seq")
+    total, dim = cos.shape
+    tokens, cols = projected.shape
+    q_part = cols - 2 * dim
+    shape = jax.ShapeDtypeStruct
+    vmem = pl.BlockSpec(memory_space=pltpu.VMEM)
+    smem = pl.BlockSpec(memory_space=pltpu.SMEM)
+    hbm = pl.BlockSpec(memory_space=pltpu.HBM)
+    return pl.pallas_call(
+        attn_front_kernel,
+        out_shape=(
+            shape((tokens, cols), BF),
+            shape((tokens, q_part), BF),
+            shape((tokens * q_part // dim // total, 1, total), F32),
+            shape((plane, rows, width), block.dtype),
+        ),
+        in_specs=[smem] + [vmem] * 4,
+        out_specs=(vmem, vmem, vmem, hbm),
+        scratch_shapes=[
+            pltpu.VMEM((total // PIC, 2 * PIC, PIC), F32),
+            pltpu.VMEM((dim, total), BF),
+            *GATHER_SCRATCH,
+        ],
+        cost_estimate=pl.CostEstimate(
+            flops=4 * tokens * total * q_part,
+            transcendentals=tokens * total * q_part // dim,
+            bytes_accessed=plane * rows * width * 24,
+        ),
+        compiler_params=pltpu.CompilerParams(
+            collective_id=ident, has_side_effects=True, vmem_limit_bytes=40 << 20
+        ),
+        name="attn_front_plane",
+    )(starts, projected, cos, sin, block)
+
+
 def attn_back_kernel(
     starts_ref,
-    q_ref,
-    k_ref,
-    v_ref,
+    qkv_ref,
     g_ref,
     log_ref,
     cos_ref,
@@ -343,13 +451,15 @@
     )
     begin()
     total, dim = cos_ref.shape
-    heads = q_ref.shape[1] // dim
+    heads = g_ref.shape[1] // dim
     blocks = total // PIC
     scale = dim ** (-0.5)
+    k_cols = slice(heads * dim, (heads + 1) * dim)
+    v_cols = slice((heads + 1) * dim, (heads + 2) * dim)
     events = {(0, 1): diagonal, (0, 2): along_x, (0, 3): along_y, (1, 0): own, (2, 2): fold}
 
     def unturn(rows, at):
-        return rows * cos_ref[at, :] + pltpu.roll(rows, dim // 2, 1) * sin_ref[at, :]
+        return rows * cos_ref[at, :] - pltpu.roll(rows, dim // 2, 1) * sin_ref[at, :]
 
     def head_step(i, carry):
         t, h = i // heads, lax.rem(i, heads)
@@ -358,31 +468,19 @@
 
         @pl.when(h == 0)
         def _():
-            turned[...] = k_ref[pl.ds(base, total), :].T
+            turned[...] = qkv_ref[pl.ds(base, total), k_cols].T
             keys_sum[...] = jnp.zeros(keys_sum.shape, F32)
             values_sum[...] = jnp.zeros(values_sum.shape, F32)
-            for b in range(blocks):
-                span = min(2 * PIC, total - b * PIC)
-                k_at = lax.broadcasted_iota(jnp.int32, (span, PIC), 0) + b * PIC
-                q_at = lax.broadcasted_iota(jnp.int32, (span, PIC), 1) + b * PIC
-                high, below = jnp.maximum(k_at, q_at), jnp.minimum(k_at, q_at)
-                allowed = k_at <= q_at
-                for j in range(NPIC):
-                    start = starts_ref[t, j]
-                    allowed = allowed | ((below >= start) & (high < start + PIC))
-                bias[b, :span, :] = jnp.where(allowed, 0.0, -jnp.inf)
+            fill_bias(bias, starts_ref, t, blocks)
 
         for b in range(blocks):
             at = pl.ds(pl.multiple_of(base + b * PIC, PIC), PIC)
-            span = min(2 * PIC, total - b * PIC)
-            count = b * PIC + span
+            count = min(b + 2, blocks) * PIC
             seen = pl.ds(base, count)
-            queries, grads = q_ref[at, cols], g_ref[at, cols]
-            scores = nt(k_ref[seen, :], queries) * scale - log_ref[i, :, b * PIC : (b + 1) * PIC]
-            late = scores[b * PIC :] + bias[b, :span, :]
-            scores = jnp.concatenate([scores[: b * PIC], late], axis=0) if b else late
-            probs = jnp.exp(scores)
-            prob_grad = nt(v_ref[seen, :], grads)
+            queries, grads = qkv_ref[at, cols], g_ref[at, cols]
+            scores = nt(qkv_ref[seen, k_cols], queries) * scale - log_ref[i, :, b * PIC : (b + 1) * PIC]
+            probs = jnp.exp(masked(scores, bias, b))
+            prob_grad = nt(qkv_ref[seen, v_cols], grads)
             mean = jnp.sum(probs * prob_grad, axis=0, keepdims=True)
             score_grad = (probs * (prob_grad - mean)).astype(BF)
             values_sum[:count, :] += nn(probs.astype(BF), grads)
@@ -397,8 +495,8 @@
         def _():
             rows = pl.ds(base, total)
             back = unturn(keys_sum[...] * scale, pl.ds(0, total))
-            grad_ref[rows, heads * dim : (heads + 1) * dim] = back.astype(BF)
-            grad_ref[rows, (heads + 1) * dim :] = values_sum[...].astype(BF)
+            grad_ref[rows, k_cols] = back.astype(BF)
+            grad_ref[rows, v_cols] = values_sum[...].astype(BF)
 
         return carry
 
@@ -406,11 +504,11 @@
     finish()
 
 
-def attn_back_plane(starts, queries, keys, values, grads, log_total, cos, sin, partial, ident):
+def attn_back_plane(starts, qkv, grads, log_total, cos, sin, partial, ident):
     plane = lax.axis_size("tp") * lax.axis_size("seq")
     rows, width = partial.shape[0] // plane, partial.shape[1]
     total, dim = cos.shape
-    tokens, q_part = queries.shape
+    tokens, q_part = grads.shape
     hbm = pl.BlockSpec(memory_space=pltpu.HBM)
     vmem = pl.BlockSpec(memory_space=pltpu.VMEM)
     smem = pl.BlockSpec(memory_space=pltpu.SMEM)
@@ -420,7 +518,7 @@
             jax.ShapeDtypeStruct((tokens, q_part + 2 * dim), BF),
             jax.ShapeDtypeStruct((rows, width), F32),
         ),
-        in_specs=[smem] + [vmem] * 7 + [hbm],
+        in_specs=[smem] + [vmem] * 5 + [hbm],
         out_specs=(vmem, vmem),
         scratch_shapes=[
             pltpu.VMEM((total // PIC, 2 * PIC, PIC), F32),
@@ -438,7 +536,7 @@
             collective_id=ident, has_side_effects=True, vmem_limit_bytes=50 << 20
         ),
         name="attn_back_plane",
-    )(starts, queries, keys, values, grads, log_total, cos, sin, partial.reshape(plane, rows, width))
+    )(starts, qkv, grads, log_total, cos, sin, partial.reshape(plane, rows, width))
 
 
 def exchange_kernel(in_ref, out_ref, stage, local, sends, recvs):
@@ -951,7 +1049,6 @@
     share = plane // KV
     ff_part = w_gate.shape[1] // plane
     q_part = heads * DH
-    scale = DH ** (-0.5)
 
     gain1 = gain_attn[:, None]
     gain2 = gain_ffn[:, None]
@@ -990,8 +1087,6 @@
     ffn_rows = ffn_rows.reshape(-1, ffn_rows.shape[2])
     ffn_weight = lax.all_gather(ffn_rows, "rep", axis=0, tiled=True)
     norm1_all = gather_plane(after(norm1.astype(BF), ffn_rows), 1)
-    ffn_grad = gather_plane(after((keep * upstream).astype(BF), norm1_all), 3)
-
     other_starts = lax.ppermute(pic_starts, "tp", [(0, 1), (1, 0)])
     starts = jnp.where(
         lax.axis_index("tp") == 0,
@@ -1000,30 +1095,19 @@
     )
     positions = jnp.arange(total_len, dtype=jnp.int32)
     cos_table, sin_table = rotary_tables(positions, DH)
-    allowed = jax.vmap(visible, (None, 0))(positions, starts)[:, None]
-    turn = jax.vmap(rotate, (0, None, None))
-
-    projected = nn(norm1_all, qkv_weight).reshape(TP, total_len, q_part + 2 * DH)
-    queries = turn(
-        projected[..., :q_part].reshape(TP, total_len, heads, DH), cos_table, sin_table
-    ).astype(BF)
-    keys = turn(projected[..., q_part : q_part + DH], cos_table, sin_table).astype(BF)
-    values = projected[..., q_part + DH :].astype(BF)
-    scores = jnp.einsum("tqhd,tkd->thqk", queries, keys, preferred_element_type=F32) * scale
-    scores = jnp.where(allowed, scores, -jnp.inf)
-    peak = jnp.max(scores, axis=-1, keepdims=True)
-    log_total = peak + jnp.log(jnp.sum(jnp.exp(scores - peak), axis=-1, keepdims=True))
-    probs = jnp.exp(scores - log_total)
-    probs_low = probs.astype(BF)
-    mixed = jnp.einsum("thqk,tkd->tqhd", probs_low, values, preferred_element_type=F32)
-    mixed = mixed.astype(BF).reshape(TP * total_len, q_part)
+    cos = jnp.concatenate([cos_table, cos_table], axis=1)
+    sin = jnp.concatenate([-sin_table, sin_table], axis=1)
+    projected = nn(norm1_all, qkv_weight)
+    qkv, mixed, log_total, ffn_grad = attn_front_plane(
+        starts, projected, cos, sin, (keep * upstream).astype(BF), 3
+    )
     branch = scatter_plane(nt(mixed, out_weight).astype(BF), 4)
     hidden = tokens + keep * branch
 
     scale2 = rms_scale(hidden)
     norm2 = hidden * scale2
     norm2_all, gate_up_grad, out_partial, down_partial, scaled2 = ffn_plane(
-        norm2.astype(BF), ffn_grad.reshape(plane, local_len, width), ffn_weight, 5
+        norm2.astype(BF), ffn_grad, ffn_weight, 5
     )
     norm2_all = norm2_all.reshape(-1, width)
     gate_up_grad = gate_up_grad.reshape(-1, 2 * ff_part)
@@ -1038,13 +1122,11 @@
     mixed_grad = nn(branch_grad, out_weight).astype(BF)
     qkv_grad, ffn_out = attn_back_plane(
         starts,
-        queries.reshape(-1, q_part),
-        keys.reshape(-1, DH),
-        values.reshape(-1, DH),
-        mixed_grad,
-        log_total.reshape(TP * heads, 1, total_len),
-        jnp.concatenate([cos_table, cos_table], axis=1),
-        jnp.concatenate([sin_table, -sin_table], axis=1),
+        qkv,
+        after(mixed_grad, down_sums),
+        log_total,
+        cos,
+        sin,
         out_partial.reshape(-1, width),
         9,
     )
@@ -1052,7 +1134,6 @@
         [tn(norm1_all, qkv_grad).astype(BF), tn(branch_grad, mixed).astype(BF)], axis=1
     )
     scaled1_partial = nt(qkv_grad, qkv_weight).astype(BF)
-    attn_partial = after(attn_partial, gu_sums, down_sums, scaled1_partial)
     attn_sums = lax.psum_scatter(attn_partial, "rep", scatter_dimension=0, tiled=True)
     scaled1 = scatter_plane(after(scaled1_partial, attn_partial), 8)
     input_grad = hidden_grad + scale1 * (
@@ -1070,6 +1151,7 @@
     )
     down_grad = jnp.transpose(down_own, (0, 2, 1)).reshape(plane * ff_part, -1).astype(F32)
 
+    attn_sums = after(attn_sums, gain_ffn_grad)
     attn_own = exchange_plane(attn_sums.reshape(plane, -1, attn_sums.shape[1]), 11).astype(F32)
     query_own = uncolumns(attn_own[:, :, :q_part])
     kv_own = attn_own[:, :, q_part : q_part + 2 * DH]

time: 634 us -> 604 us (0.953)
  other arithmetic: 45.6 us -> 22.2 us
  waiting for transfers between devices: 15.4 us -> 38.5 us
  local copies, waits for them, and re-layouts: 52 us -> 34.2 us
  matrix products: 72.5 us -> 56.7 us
    pallas_call x3 -> x2, Pallas kernels: 126 us -> 84.6 us  [gather_plane(): pl.pallas_call(gather_kernel, out_shape=jax.ShapeDtypeStruct((plane, rows...]
    pallas_call x0 -> x1, Pallas kernels: none -> 41 us  [attn_front_plane(): pl.pallas_call(attn_front_kernel, out_shape=(shape((tokens, cols), BF), s...]
    all_gather x1, waiting for transfers between devices: 0.01 us -> 38.4 us  [per_device(): ffn_weight = lax.all_gather(ffn_rows, 'rep', axis=0, tiled=True)]
    dot_general x2 -> x0, matrix products: 15.5 us -> none  [the longest x1 11.2 us: per_device(): jnp.einsum('thqk,tkd->tqhd', probs_low, values, preferred_element_type=F32)]
    reduce_scatter x1, waiting for transfers between devices: 15.3 us -> 0.01 us  [per_device(): lax.psum_scatter(gu_partial, 'rep', scatter_dimension=0, tiled=True)]
    unnamed x105 -> x78, local copies, waits for them, and re-layouts: 21.7 us -> 15.5 us
  transfers between devices with their start and end apart: 6 -> 6, of which waited for: 1 -> 1; matrix products, arithmetic and copies ran while one was open for 23% -> 15% of each run, Pallas kernels for 49% -> 52%
where the time goes in v8:
time: 604 us; the launch traced here: 597 us
  Pallas kernels  429 us (71%)
  matrix products  56.7 us (9%)
  waiting for transfers between devices  38.5 us (6%)
  local copies, waits for them, and re-layouts  34.2 us (6%)
  other arithmetic  22.2 us (4%)
  between operations  14.7 us (2%)
    pallas_call x1, Pallas kernels, ffn_plane(): pl.pallas_call(ffn_kernel, out_shape=(shape((plane, rows, width), BF), sh...  94.1 us
    pallas_call x2, Pallas kernels, gather_plane(): pl.pallas_call(gather_kernel, out_shape=jax.ShapeDtypeStruct((plane, rows...  84.6 us
    pallas_call x2, Pallas kernels, scatter_plane(): pl.pallas_call(scatter_kernel, out_shape=jax.ShapeDtypeStruct((rows, widt...  80.2 us
    dot_general x7, matrix products, dot(): lax.dot_general(left, right, ((contract[:1], contract[1:]), ((), ())), pr...  56.7 us
    pallas_call x3, Pallas kernels, exchange_plane(): pl.pallas_call(exchange_kernel, out_shape=jax.ShapeDtypeStruct(blocks.sha...  54.9 us
    pallas_call x1, Pallas kernels, attn_back_plane(): pl.pallas_call(attn_back_kernel, out_shape=(jax.ShapeDtypeStruct((tokens,...  44.4 us
    pallas_call x1, Pallas kernels, attn_front_plane(): pl.pallas_call(attn_front_kernel, out_shape=(shape((tokens, cols), BF), s...  41 us
    all_gather x1, waiting for transfers between devices, per_device(): ffn_weight = lax.all_gather(ffn_rows, 'rep', axis=0, tiled=True)  38.4 us
  transfers between devices with their start and end apart: 6, of which 1 were waited for; matrix products, arithmetic and copies ran while one was open for 15% of the time, Pallas kernels for 52%

profile of v8, /device:TPU:1, one launch (start us, length us, event | category | flops | bytes accessed | tf_op | source)
XLA Modules:
  0.0 597.0 jit_solution(2392979994221688568)
XLA Ops:
  7.2 1.1 fusion.16
  8.3 1.0 fusion.19
  9.4 1.0 bitcast_bitcast_fusion
  10.5 1.0 pad_maximum_fusion.1.in_ref
  11.4 13.7 %exchange_plane.3 = bf16[8,64,768]{2,1,0:T(8,128)(2,1)} custom-call(bf16[8,64,768]{2,1,0:T(8,128)(2,1)} %pad_maximum_fusion.1.in_ref), custom_call_target="tpu_custom_call" | custom-call | bytes 15728640 | tf_op jit(solution)/shard_map/exchange_plane/pallas_call | solution.py:568
  25.2 0.3 multiply_convert_fusion.2
  25.5 1.5 reshape.145
  27.1 2.5 reshape.146
  29.6 0.7 reshape.144
  30.4 1.0 copy-done.26
  31.4 1.5 copy_bitcast_fusion
  32.9 3.1 concatenate.23.in_ref
  36.0 28.0 %exchange_plane.4 = bf16[8,64,2112]{2,1,0:T(8,128)(2,1)} custom-call(bf16[8,64,2112]{2,1,0:T(8,128)(2,1)} %concatenate.23.in_ref), custom_call_target="tpu_custom_call" | custom-call | bytes 43253760 | tf_op jit(solution)/shard_map/exchange_plane/pallas_call | solution.py:568
  64.0 0.6 copy-done.35
  64.6 1.1 collective-permute-start
  65.7 0.3 fusion.9
  66.0 1.2 fusion.2.refs_0_
  67.2 42.9 %gather_plane.2 = bf16[8,256,2048]{2,1,0:T(8,128)(2,1)} custom-call(bf16[256,2048]{1,0:T(8,128)(2,1)} %fusion.2.refs_0_), custom_call_target="tpu_custom_call" | custom-call | bytes 100663296 | tf_op jit(solution)/shard_map/gather_plane/pallas_call | solution.py:170
  110.2 1.9 fusion.18
  112.1 0.3 pad_maximum_fusion.2
  112.8 7.7 %fusion.11.projected_ref = f32[2048,512]{1,0:T(8,128)S(1)} fusion(bf16[2048,2048]{1,0:T(8,128)(2,1)} %bitcast.99, bf16[2048,768]{1,0:T(8,128)(2,1)} %all-gather.3.cloned.1.call-done), kind=kOutput, calls=%fused_computation.27 | convolution fusion | flops 4294967296 | bytes 14680064 | tf_op jit(solution)/shard_map/dot_general | solution.py:32
  120.6 41.0 %attn_front_plane.1 = (bf16[2048,512]{1,0:T(8,128)(2,1)S(1)}, bf16[2048,256]{1,0:T(8,128)(2,1)S(1)}, f32[4,1,1024]{2,1,0:T(1,128)S(1)}, bf16[8,256,2048]{2,1,0:T(8,128)(2,1)}) custom-call(s32[2,2]{1,0:T(2,128)S(1)} %add_select_fusion.starts_ref, f32[2048,512]{1,0:T(8,128)S(1)} %fusion.11.projected_ref, f32[1024,128]{1,0:T(8,128)S(1)} %get-tuple-element.84.cos_ref, ...), custom_call_target="tpu_custom_call" | custom-call | flops 2147483648 | bytes 100663296 | tf_op jit(solution)/shard_map/attn_front_plane/pallas_call | solution.py:406
  161.6 1.3 copy-done.13
  162.9 4.0 convolution_convert_fusion.1
  166.9 39.7 %scatter_plane.2 = f32[256,2048]{1,0:T(8,128)S(1)} custom-call(bf16[8,256,2048]{2,1,0:T(8,128)(2,1)S(1)} %bitcast.94), custom_call_target="tpu_custom_call" | custom-call | bytes 117440512 | tf_op jit(solution)/shard_map/scatter_plane/pallas_call | solution.py:299
  206.6 0.5 multiply_reduce_fusion.1
  207.1 1.3 copy-done.14
  208.4 1.1 multiply_convert_fusion.1.own_ref
  209.6 38.4 %all-gather.5.cloned.1.call-done.weight_hbm = bf16[2048,2112]{1,0:T(8,128)(2,1)} async-done(((bf16[512,2112]{1,0:T(8,128)(2,1)}), bf16[2048,2112]{1,0:T(8,128)(2,1)}) %all-gather.5.cloned.1.call-update) | async-done | bytes 8650768 | tf_op jit(solution)/shard_map/all_gather | solution.py:1088
  247.9 94.1 %ffn_plane.1 = (bf16[8,256,2048]{2,1,0:T(8,128)(2,1)}, bf16[4,512,1408]{2,1,0:T(8,128)(2,1)}, bf16[8,256,2048]{2,1,0:T(8,128)(2,1)}, bf16[2048,704]{1,0:T(8,128)(2,1)}, f32[256,2048]{1,0:T(8,128)}) custom-call(bf16[256,2048]{1,0:T(8,128)(2,1)} %multiply_convert_fusion.1.own_ref, bf16[8,256,2048]{2,1,0:T(8,128)(2,1)} %get-tuple-element.38.grad_ref, ...), custom_call_target="tpu_custom_call" | custom-call | flops 41339060224 | bytes 125829120 | tf_op jit(solution)/shard_map/ffn_plane/pallas_call | solution.py:895
  342.2 19.1 %convolution_convert_fusion.2 = bf16[2048,1408]{1,0:T(8,128)(2,1)} fusion(bf16[2048,2048]{1,0:T(8,128)(2,1)} %bitcast.120, bf16[2048,1408]{1,0:T(8,128)(2,1)} %bitcast.121), kind=kOutput, calls=%fused_computation.2 | convolution fusion | flops 11814043648 | bytes 19922944 | tf_op jit(solution)/shard_map/dot_general | solution.py:32
  361.5 1.3 copy-done.15
  362.9 2.1 multiply_reduce_fusion
  365.4 1.6 multiply_convert_fusion.refs_0_
  367.0 41.7 %gather_plane.3 = bf16[8,256,2048]{2,1,0:T(8,128)(2,1)} custom-call(bf16[256,2048]{1,0:T(8,128)(2,1)} %multiply_convert_fusion.refs_0_), custom_call_target="tpu_custom_call" | custom-call | bytes 100663296 | tf_op jit(solution)/shard_map/gather_plane/pallas_call | solution.py:170
  408.7 7.2 %convolution_convert_fusion.4 = bf16[2048,256]{0,1:T(8,128)(2,1)} fusion(bf16[2048,2048]{1,0:T(8,128)(2,1)} %bitcast.101, bf16[2048,256]{1,0:T(8,128)(2,1)S(1)} %copy-done.4), kind=kOutput, calls=%fused_computation.13 | convolution fusion | flops 2148007936 | bytes 10485760 | tf_op jit(solution)/shard_map/dot_general | solution.py:32
  415.9 3.7 convolution_convert_fusion.5.g_ref
  419.6 44.4 %attn_back_plane.1 = (bf16[2048,512]{1,0:T(8,128)(2,1)}, f32[256,2048]{1,0:T(8,128)}) custom-call(s32[2,2]{1,0:T(2,128)S(1)} %add_select_fusion.starts_ref, bf16[2048,512]{1,0:T(8,128)(2,1)} %copy-done.13, bf16[2048,256]{1,0:T(8,128)(2,1)S(1)} %convolution_convert_fusion.5.g_ref, f32[4,1,1024]{2,1,0:T(1,128)S(1)} %get-tuple-element.46.log_ref, ...), custom_call_target="tpu_custom_call" | custom-call | flops 5368709120 | bytes 117440512 | tf_op jit(solution)/shard_map/attn_back_plane/pallas_call | solution.py:515
  464.1 8.7 %convolution_convert_fusion.3 = bf16[2048,512]{0,1:T(8,128)(2,1)S(1)} fusion(bf16[2048,2048]{1,0:T(8,128)(2,1)} %bitcast.100, bf16[2048,512]{1,0:T(8,128)(2,1)} %get-tuple-element.49), kind=kOutput, calls=%fused_computation.7 | convolution fusion | flops 4296015872 | bytes 12582912 | tf_op jit(solution)/shard_map/dot_general | solution.py:32
  472.8 1.9 pad_maximum_fusion
  474.7 1.5 copy-done.36
  476.2 6.4 %convolution_convert_fusion = bf16[2048,2048]{1,0:T(8,128)(2,1)S(1)} fusion(bf16[2048,512]{1,0:T(8,128)(2,1)S(1)} %copy-done.36, bf16[2048,768]{1,0:T(8,128)(2,1)} %all-gather.3.cloned.1.call-done), kind=kOutput, calls=%fused_computation | convolution fusion | flops 4299161600 | bytes 12582912 | tf_op jit(solution)/shard_map/dot_general | solution.py:32
  482.6 40.5 %scatter_plane.3 = f32[256,2048]{1,0:T(8,128)S(1)} custom-call(bf16[8,256,2048]{2,1,0:T(8,128)(2,1)S(1)} %bitcast.95), custom_call_target="tpu_custom_call" | custom-call | bytes 117440512 | tf_op jit(solution)/shard_map/scatter_plane/pallas_call | solution.py:299
  523.1 0.4 fusion.4
  523.6 1.1 copy-done.16
  524.7 0.3 copy-done.24
  525.0 2.8 fusion.8
  527.8 1.4 copy-done.5
  529.2 1.1 copy-done.8
  530.4 29.9 %finish_plane.1 = (f32[64,5632]{1,0:T(8,128)S(1)}, f32[64,5632]{1,0:T(8,128)S(1)}, bf16[8,64,704]{2,1,0:T(8,128)(2,1)S(1)}, f32[64,1]{1,0:T(8,128)S(1)}) custom-call(bf16[8,64,1408]{2,1,0:T(8,128)(2,1)S(1)} %bitcast.96, bf16[8,64,704]{2,1,0:T(8,128)(2,1)S(1)} %bitcast.97, bf16[64,5632]{1,0:T(8,128)(2,1)S(1)} %copy-done.2, bf16[64,5632]{1,0:T(8,128)(2,1)S(1)} %copy-done, ...), custom_call_target="tpu_custom_call" | custom-call | bytes 43253760 | tf_op jit(solution)/shard_map/finish_plane/pallas_call | solution.py:990
  560.3 1.1 copy-done.6
  561.5 2.1 copy.65
  563.6 2.8 reshape.171
  566.4 0.6 reduce
  567.0 2.3 copy.60
  569.3 13.2 %exchange_plane.5 = bf16[8,64,768]{2,1,0:T(8,128)(2,1)} custom-call(bf16[8,64,768]{2,1,0:T(8,128)(2,1)} %bitcast.105), custom_call_target="tpu_custom_call" | custom-call | bytes 15728640 | tf_op jit(solution)/shard_map/exchange_plane/pallas_call | solution.py:568
  582.5 1.3 convert_element_type.130
  584.0 0.7 copy-done.28
  584.8 1.0 broadcast_multiply_fusion
  585.8 0.8 copy.71
  586.6 0.9 bitcast_multiply_fusion
  587.5 0.5 add_add_fusion
  588.0 1.1 copy.84
  589.1 1.1 copy.85
  (99 shorter events, 2.0 us)
Async XLA Ops:
  7.2 105.6 %all-gather.3.cloned.1.call-start = ((), (), s32[]{:S(2)}) async-start(), calls=%async_computation.3 | async-start | bytes 3932160 | tf_op jit(solution)/shard_map/all_gather | solution.py:1068
  10.4 14.8 %copy-start = (bf16[64,5632]{1,0:T(8,128)(2,1)S(1)}, bf16[64,5632]{1,0:T(8,128)(2,1)}, u32[]{:S(2)}) copy-start(bf16[64,5632]{1,0:T(8,128)(2,1)} %up_weight.1) | copy-start | bytes 2162692
  10.4 14.8 %copy-start.1 = (bf16[64,5632]{1,0:T(8,128)(2,1)S(1)}, bf16[64,5632]{1,0:T(8,128)(2,1)}, u32[]{:S(2)}) copy-start(bf16[64,5632]{1,0:T(8,128)(2,1)} %gate_weight.1) | copy-start | bytes 2162692
  10.4 14.8 %copy-start.33 = (f32[64]{0:T(128)S(1)}, f32[64]{0:T(128)}, u32[]{:S(2)}) copy-start(f32[64]{0:T(128)} %param.21) | copy-start | bytes 772
  25.1 222.8 %all-gather.5.cloned.1.call-start = ((), (), s32[]{:S(2)}) async-start(), calls=%async_computation.4 | async-start | bytes 11141120 | tf_op jit(solution)/shard_map/all_gather | solution.py:1088
  30.3 1.1 copy-start.26
  63.9 0.7 copy-start.35
  63.9 1.8 copy-start.17
  64.0 355.6 %reduce-scatter.4.cloned.1.call-start = ((), (), s32[]{:S(2)}) async-start(), calls=%async_computation.5 | async-start | bytes 3932160 | tf_op jit(solution)/shard_map/reduce_scatter | solution.py:1114
  64.6 48.2 %collective-permute-start = (s32[1,2]{1,0:T(1,128)S(1)}, s32[1,2]{1,0:T(1,128)S(1)}, u32[]{:S(2)}, u32[]{:S(2)}) collective-permute-start(s32[1,2]{1,0:T(1,128)S(1)} %copy-done.35), channel_id=1, source_target_pairs={{0,4},{4,0},{1,5},{5,1},{2,6},{6,2},{3,7},{7,3},{8,12},{12,8},{9,1... | collective-permute-start | bytes 32 | tf_op jit(solution)/shard_map/ppermute | solution.py:1090
  110.2 2.3 copy-start.34
  110.2 2.3 copy-start.22
  112.5 8.1 %copy-start.9 = (f32[1024,128]{1,0:T(8,128)}, f32[1024,128]{1,0:T(8,128)S(1)}, u32[]{:S(2)}) copy-start(f32[1024,128]{1,0:T(8,128)S(1)} %get-tuple-element.84.cos_ref) | copy-start | bytes 1572868
  112.5 8.1 %copy-start.11 = (f32[1024,128]{1,0:T(8,128)}, f32[1024,128]{1,0:T(8,128)S(1)}, u32[]{:S(2)}) copy-start(f32[1024,128]{1,0:T(8,128)S(1)} %get-tuple-element.85.sin_ref) | copy-start | bytes 1572868
  161.6 1.3 copy-start.13
  162.9 4.0 copy-start.3
  166.9 39.7 %copy-start.18 = (bf16[1,256,2048]{2,1,0:T(8,128)(2,1)S(1)}, bf16[1,256,2048]{2,1,0:T(8,128)(2,1)}, u32[]{:S(2)}) copy-start(bf16[1,256,2048]{2,1,0:T(8,128)(2,1)} %param.13) | copy-start | bytes 3145732
  207.1 1.3 copy-start.14
  342.1 185.7 %reduce-scatter.8.cloned.1.call-start = ((), (), s32[]{:S(2)}) async-start(), calls=%async_computation.7 | async-start | bytes 7208960 | tf_op jit(solution)/shard_map/reduce_scatter | solution.py:1116
  361.3 1.6 copy-start.15
  361.3 205.7 %reduce-scatter.6.cloned.1.call-start = ((), (), s32[]{:S(2)}) async-start(), calls=%async_computation.6 | async-start | bytes 3932160 | tf_op jit(solution)/shard_map/reduce_scatter | solution.py:1137
  362.9 2.2 copy-start.20
  362.9 2.5 copy-start.23
  367.0 41.7 %copy-start.4 = (bf16[2048,256]{1,0:T(8,128)(2,1)S(1)}, bf16[2048,256]{1,0:T(8,128)(2,1)}, u32[]{:S(2)}) copy-start(bf16[2048,256]{1,0:T(8,128)(2,1)} %copy-done.3) | copy-start | bytes 3145732
  408.7 7.2 %copy-start.25 = (bf16[8,256,2048]{2,1,0:T(8,128)(2,1)S(1)}, bf16[8,256,2048]{2,1,0:T(8,128)(2,1)}, u32[]{:S(2)}) copy-start(bf16[8,256,2048]{2,1,0:T(8,128)(2,1)} %gather_plane.3) | copy-start | bytes 25165828
  415.9 3.7 copy-start.10
  415.9 3.7 copy-start.12
  464.1 8.7 %copy-start.29 = (bf16[2048,256]{0,1:T(8,128)(2,1)S(1)}, bf16[2048,256]{0,1:T(8,128)(2,1)}, u32[]{:S(2)}) copy-start(bf16[2048,256]{0,1:T(8,128)(2,1)} %convolution_convert_fusion.4) | copy-start | bytes 3145732
  474.6 1.6 copy-start.36
  482.6 40.5 %copy-start.19 = (bf16[1,256,2048]{2,1,0:T(8,128)(2,1)S(1)}, bf16[1,256,2048]{2,1,0:T(8,128)(2,1)}, u32[]{:S(2)}) copy-start(bf16[1,256,2048]{2,1,0:T(8,128)(2,1)} %param.13) | copy-start | bytes 3145732
  482.6 41.0 %copy-start.21 = (f32[256,2048]{1,0:T(8,128)S(1)}, f32[256,2048]{1,0:T(8,128)}, u32[]{:S(2)}) copy-start(f32[256,2048]{1,0:T(8,128)} %get-tuple-element.39) | copy-start | bytes 6291460
  482.6 41.0 %copy-start.27 = (f32[256,2048]{1,0:T(8,128)S(1)}, f32[256,2048]{1,0:T(8,128)}, u32[]{:S(2)}) copy-start(f32[256,2048]{1,0:T(8,128)} %get-tuple-element.48) | copy-start | bytes 6291460
  523.1 1.6 copy-start.16
  523.1 1.9 copy-start.24
  525.0 2.8 copy-start.2
  527.8 1.4 copy-start.5
  529.2 1.1 copy-start.8
  560.2 1.1 copy-start.6
  583.8 1.0 copy-start.28
  583.8 0.9 copy-start.32
  584.0 2.7 copy-start.30
  584.0 2.7 copy-start.31
  584.0 4.1 copy-start.7
Sparse Core Ops, SparseCore 0:
  25.3 63.8 all-gather.2
  90.7 157.1 all-gather.4
  342.2 57.2 reduce-scatter.3
  401.7 102.5 reduce-scatter.7
  506.4 60.5 reduce-scatter.5

commit v9 on v8

--- a/solution.py
+++ b/solution.py
@@ -582,15 +582,55 @@
     )(blocks)
 
 
-def ffn_kernel(
+def slopes(wide, narrow, inner, gug):
+    ff_part = inner.shape[1]
+
+    def body(i, carry):
+        at = pl.ds(i * SUB, SUB)
+        gate, upward, grad = wide[at, :ff_part], wide[at, ff_part:], narrow[at, :]
+        sigmoid_gate = jax.nn.sigmoid(gate)
+        silu_gate = gate * sigmoid_gate
+        inner[at, :] = (silu_gate * upward).astype(BF)
+        slope = sigmoid_gate * (1.0 + gate * (1.0 - sigmoid_gate))
+        gug[at, :ff_part] = (grad * upward * slope).astype(BF)
+        gug[at, ff_part:] = (grad * silu_gate).astype(BF)
+        return carry
+
+    lax.fori_loop(0, wide.shape[0] // SUB, body, 0)
+
+
+def weight_step(n, tokens, grads, gug, inner, stage, weight_ref, sems):
+    slot = lax.rem(n, 2)
+    block, cols = stage.shape[1:]
+    ff_part = cols // 3
+    count = gug.shape[0] * gug.shape[1]
+
+    def put(m):
+        return pltpu.make_async_copy(
+            stage.at[lax.rem(m, 2)], weight_ref.at[pl.ds(m * block, block)], sems[0].at[sems[1] + lax.rem(m, 2)]
+        )
+
+    @pl.when(n >= 2)
+    def _():
+        put(n - 2).wait()
+
+    at = pl.ds(pl.multiple_of(n * block, block), block)
+    left = tokens[:, :, :, at].reshape(count, block)
+    stage[slot, :, : 2 * ff_part] = tn(left, gug[...].reshape(count, 2 * ff_part)).astype(BF)
+    left = grads[:, :, :, at].reshape(count, block)
+    stage[slot, :, 2 * ff_part :] = tn(left, inner[...].reshape(count, ff_part)).astype(BF)
+    put(n).start()
+    return put
+
+
+def ffn_first_kernel(
     own_ref,
     grad_ref,
     weight_hbm,
     all_ref,
-    gug_ref,
+    back_ref,
     out_ref,
-    down_ref,
-    sum_ref,
+    grads_out,
     weight,
     tokens,
     grads,
@@ -599,10 +639,7 @@
     inner,
     gug,
     stage,
-    part,
-    chip_in,
-    far_in,
-    near_in,
+    columns_stage,
     sends,
     recvs,
     local,
@@ -610,7 +647,6 @@
     tp_at, seq_at, far, mate, _ = plane_place()
     seq = lax.axis_size("seq")
     other = 1 - tp_at
-    kind = lax.rem(seq_at, 2)
     to_x = at_device(tp_at, far)
     to_y = at_device(other, seq_at)
     to_c = at_device(tp_at, mate)
@@ -620,7 +656,6 @@
     block = width // 4
     ff_part = narrow.shape[2]
     gate_up, lower = slice(0, 2 * ff_part), slice(2 * ff_part, 3 * ff_part)
-    top, low = pl.ds(0, half), pl.ds(half, half)
     enter((to_x, to_y, to_c))
 
     def piece(t, s, h):
@@ -647,90 +682,29 @@
     ry0, ry1 = relay(9, other, seq_at, 0, to_c), relay(10, other, seq_at, 1, to_c)
     rd0, rd1 = relay(12, other, far, 0, to_c), relay(13, other, far, 1, to_c)
 
-    def give(c):
-        return remote(
-            part.at[c, 1 - kind], chip_in.at[c], sends.at[14 + c], recvs.at[14 + c], to_c
-        )
-
-    def hop(i, src, dst, device):
-        return remote(src, dst, sends.at[i], recvs.at[i], device)
-
-    def held(c):
-        return part.at[c, kind]
-
-    sum_x0 = hop(18, part.at[1, kind, top], near_in.at[0, top], to_x)
-    sum_y1 = hop(19, part.at[2, kind, low], near_in.at[1, low], to_y)
-    sum_d0 = hop(20, part.at[3, kind, top], far_in.at[0, top], to_x)
-    sum_d1 = hop(21, part.at[3, kind, low], far_in.at[1, low], to_y)
-    sum_y0 = hop(22, part.at[2, kind, top], near_in.at[1, top], to_y)
-    sum_x1 = hop(23, part.at[1, kind, low], near_in.at[0, low], to_x)
-
-    def chip_sum(c):
-        give(c).wait_recv()
-        add_rows(held(c), (held(c), chip_in.at[c]), 0, rows, part.dtype)
-
     def chip_rows(c):
         t = lax.rem(tp_at + c // 2, 2)
         s = lax.rem(seq_at + (seq // 2) * lax.rem(c, 2), seq)
-        return t * seq + s - lax.rem(s, 2)
+        return pl.ds(t * seq + s - lax.rem(s, 2), 2)
 
     def take_tokens(c):
-        return pltpu.make_async_copy(
-            all_ref.at[pl.ds(chip_rows(c), 2)], tokens.at[lax.rem(c, 2)], local.at[lax.rem(c, 2)]
-        )
+        return pltpu.make_async_copy(all_ref.at[chip_rows(c)], tokens.at[c], local.at[c])
 
     def take_grads(c):
-        return pltpu.make_async_copy(
-            grad_ref.at[pl.ds(chip_rows(c), 2)], grads.at[c], local.at[2 + c]
-        )
-
-    def put_gug(c, slot):
-        return pltpu.make_async_copy(
-            gug.at[slot], gug_ref.at[chip_rows(c) // 2], local.at[6 + slot]
-        )
-
-    def put_down(n):
-        slot = lax.rem(n, 2)
-        return pltpu.make_async_copy(
-            stage.at[slot], down_ref.at[pl.ds(n * block, block)], local.at[9 + slot]
-        )
+        return pltpu.make_async_copy(grad_ref.at[chip_rows(c)], grads.at[c], local.at[4 + c])
+
+    def put_back(c):
+        return pltpu.make_async_copy(stage.at[0], back_ref.at[chip_rows(c)], local.at[8])
 
     def put_out(c):
-        return pltpu.make_async_copy(
-            tokens.at[lax.rem(c, 2)], out_ref.at[pl.ds(chip_rows(c), 2)], local.at[11 + lax.rem(c, 2)]
-        )
-
-    take_weight = pltpu.make_async_copy(weight_hbm, weight, local.at[13])
-    mine = pltpu.make_async_copy(own_ref, all_ref.at[tp_at * seq + seq_at], local.at[14])
-
+        return pltpu.make_async_copy(stage.at[1], out_ref.at[chip_rows(c)], local.at[9])
+
+    take_weight = pltpu.make_async_copy(weight_hbm, weight, local.at[12])
+    mine = pltpu.make_async_copy(own_ref, all_ref.at[tp_at * seq + seq_at], local.at[13])
     for copy in (take_weight, x0, y0, c0, x1, y1, c1, mine):
         copy.start()
     for c in range(4):
         take_grads(c).start()
-
-    def slopes(c, slot):
-        def body(i, carry):
-            at = pl.ds(i * SUB, SUB)
-            gate, upward, grad = wide[at, :ff_part], wide[at, ff_part:], narrow[c, at, :]
-            sigmoid_gate = jax.nn.sigmoid(gate)
-            silu_gate = gate * sigmoid_gate
-            inner[c, at, :] = (silu_gate * upward).astype(BF)
-            slope = sigmoid_gate * (1.0 + gate * (1.0 - sigmoid_gate))
-            gug[slot, at, :ff_part] = (grad * upward * slope).astype(BF)
-            gug[slot, at, ff_part:] = (grad * silu_gate).astype(BF)
-            return carry
-
-        lax.fori_loop(0, pair // SUB, body, 0)
-        put_gug(c, slot).start()
-
-    def back(c, slot, n):
-        at = pl.ds(pl.multiple_of(n * block, block), block)
-        total = nt(gug[slot], weight[at, gate_up]).astype(part.dtype)
-        part[c, :, :, at] = total.reshape(2, rows, block)
-
-    def widen(slot):
-        wide[...] = nn(tokens[slot].reshape(pair, width), weight[:, gate_up])
-
     take_weight.wait()
 
     def narrow_step(c, carry):
@@ -743,27 +717,18 @@
     c0.wait_recv()
     c1.wait_recv()
     take_tokens(0).start()
-    x0.wait_recv()
-    diag0.start()
-    rx0.start()
-    y0.wait_recv()
-    ry0.start()
-    take_tokens(0).wait()
-    widen(0)
-    slopes(0, 2)
-    y1.wait_recv()
-    diag1.start()
-    ry1.start()
-    x1.wait_recv()
-    rx1.start()
-    rx0.wait_recv()
-    rx1.wait_recv()
-    take_tokens(1).start()
 
     def chip_step(c, carry):
-        slot = lax.rem(c, 2)
         take_tokens(c).wait()
-        widen(slot)
+        wide[...] = nn(tokens[c].reshape(pair, width), weight[:, gate_up])
+
+        @pl.when(c == 0)
+        def _():
+            x0.wait_recv()
+            diag0.start()
+            rx0.start()
+            y0.wait_recv()
+            ry0.start()
 
         @pl.when(c == 1)
         def _():
@@ -772,178 +737,353 @@
             take_tokens(2).start()
 
         @pl.when(c == 2)
-        def _():
-            chip_sum(1)
-            sum_x0.start()
-
-        @pl.when(c == 3)
-        def _():
-            chip_sum(2)
-            sum_y1.start()
-            put_gug(1, 1).wait()
-
-        slopes(c, slot)
-
-        @pl.when(c == 2)
-        def _():
-            rd0.wait_recv()
-            rd1.wait_recv()
-            take_tokens(3).start()
-
-        def back_step(n, carry):
-            back(c, slot, n)
-            return carry
-
-        lax.fori_loop(0, 4, back_step, 0)
-        give(c).start()
-
-        @pl.when(c == 1)
         def _():
             diag0.wait_recv()
             rd0.start()
             diag1.wait_recv()
             rd1.start()
 
+        slopes(wide, narrow.at[c], inner.at[c], gug.at[c])
+
+        @pl.when(c >= 1)
+        def _():
+            put_back(c - 1).wait()
+            put_out(c - 1).wait()
+
+        def back_step(n, carry):
+            at = pl.ds(pl.multiple_of(n * block, block), block)
+            total = nt(gug[c], weight[at, gate_up]).astype(BF)
+            stage[0, :, :, at] = total.reshape(2, rows, block)
+            total = nt(inner[c], weight[at, lower]).astype(BF)
+            stage[1, :, :, at] = total.reshape(2, rows, block)
+            return carry
+
+        lax.fori_loop(0, 4, back_step, 0)
+        put_back(c).start()
+        put_out(c).start()
+
+        @pl.when(c == 0)
+        def _():
+            y1.wait_recv()
+            diag1.start()
+            ry1.start()
+            x1.wait_recv()
+            rx1.start()
+            rx0.wait_recv()
+            rx1.wait_recv()
+            take_tokens(1).start()
+
+        @pl.when(c == 2)
+        def _():
+            rd0.wait_recv()
+            rd1.wait_recv()
+            take_tokens(3).start()
+
         return carry
 
-    lax.fori_loop(1, 4, chip_step, 0)
-
-    def own_step(n, carry):
-        back(0, 2, n)
-
-        @pl.when(n == 1)
-        def _():
-            chip_sum(3)
-            sum_d0.start()
-            sum_d1.start()
-
+    lax.fori_loop(0, 4, chip_step, 0)
+
+    def grads_step(n, carry):
+        weight_step(n, tokens, grads, gug, inner, columns_stage, grads_out, (local, 10))
         return carry
 
-    lax.fori_loop(0, 4, own_step, 0)
-    give(0).start()
-
-    def out_step(c, carry):
-        slot = lax.rem(c, 2)
-
-        @pl.when(c >= 2)
-        def _():
-            put_out(c - 2).wait()
-
-        def out_block(n, carry):
-            at = pl.ds(pl.multiple_of(n * block, block), block)
-            total = nt(inner[c], weight[at, lower]).astype(tokens.dtype)
-            tokens[slot, :, :, at] = total.reshape(2, rows, block)
-            return carry
-
-        lax.fori_loop(0, 4, out_block, 0)
-        put_out(c).start()
-        return carry
-
-    lax.fori_loop(0, 4, out_step, 0)
-    chip_sum(0)
-
-    def down_step(n, carry):
-        @pl.when(n == 1)
-        def _():
-            sum_d0.wait_recv()
-            add_rows(held(2), (held(2), far_in.at[0]), 0, half, part.dtype)
-            sum_y0.start()
-            sum_d1.wait_recv()
-            add_rows(held(1), (held(1), far_in.at[1]), half, half, part.dtype)
-            sum_x1.start()
-
-        @pl.when(n >= 2)
-        def _():
-            put_down(n - 2).wait()
-
-        at = pl.ds(pl.multiple_of(n * block, block), block)
-        left = grads[:, :, :, at].reshape(4 * pair, block)
-        stage[lax.rem(n, 2)] = tn(left, inner[...].reshape(4 * pair, ff_part)).astype(BF)
-        put_down(n).start()
-        return carry
-
-    lax.fori_loop(0, 4, down_step, 0)
-    sum_x0.wait_recv()
-    sum_y0.wait_recv()
-    add_rows(sum_ref, (held(0), near_in.at[0], near_in.at[1]), 0, half, sum_ref.dtype)
-    sum_y1.wait_recv()
-    sum_x1.wait_recv()
-    add_rows(sum_ref, (held(0), near_in.at[0], near_in.at[1]), half, half, sum_ref.dtype)
+    lax.fori_loop(0, 4, grads_step, 0)
     for copy in (x0, y0, c0, x1, y1, c1, diag0, diag1, rx0, ry0, ry1, rx1, rd0, rd1):
         copy.wait_send()
-    for c in range(4):
-        give(c).wait_send()
-    for copy in (sum_x0, sum_y1, sum_d0, sum_d1, sum_y0, sum_x1):
+    put_back(3).wait()
+    put_out(3).wait()
+    for n in (2, 3):
+        pltpu.make_async_copy(
+            columns_stage.at[n - 2], grads_out.at[pl.ds(n * block, block)], local.at[8 + n]
+        ).wait()
+
+
+def ffn_second_kernel(
+    all_ref,
+    grad_ref,
+    weight_hbm,
+    back_ref,
+    first_ref,
+    out_ref,
+    grads_out,
+    sum_ref,
+    weight,
+    tokens,
+    grads,
+    wide,
+    narrow,
+    inner,
+    gug,
+    part,
+    chip_in,
+    far_in,
+    near_in,
+    stage,
+    columns_stage,
+    sends,
+    recvs,
+    local,
+):
+    tp_at, seq_at, far, mate, _ = plane_place()
+    seq = lax.axis_size("seq")
+    kind = lax.rem(seq_at, 2)
+    to_x = at_device(tp_at, far)
+    to_y = at_device(1 - tp_at, seq_at)
+    to_c = at_device(tp_at, mate)
+    rows, width = sum_ref.shape
+    pair = 2 * rows
+    half = rows // 2
+    block = width // 4
+    ff_part = narrow.shape[1]
+    gate_up, lower = slice(0, 2 * ff_part), slice(2 * ff_part, 3 * ff_part)
+    top, low = pl.ds(0, half), pl.ds(half, half)
+    enter((to_x, to_y, to_c))
+
+    def chip_rows(k):
+        t = lax.rem(tp_at + 1 - lax.rem(k, 2), 2)
+        s = lax.rem(seq_at + (seq // 2) * (1 - k // 2), seq)
+        return pl.ds(t * seq + s - lax.rem(s, 2), 2)
+
+    def take(ref, target, sem):
+        return lambda k: pltpu.make_async_copy(ref.at[chip_rows(k)], target.at[k], local.at[sem + k])
+
+    take_tokens, take_grads, take_back = (
+        take(all_ref, tokens, 0),
+        take(grad_ref, grads, 4),
+        take(back_ref, part, 8),
+    )
+
+    def take_first(k):
+        slot = lax.rem(k, 2)
+        return pltpu.make_async_copy(first_ref.at[chip_rows(k)], stage.at[slot], local.at[12 + slot])
+
+    def put_out(k):
+        slot = lax.rem(k, 2)
+        return pltpu.make_async_copy(stage.at[slot], out_ref.at[chip_rows(k)], local.at[14 + slot])
+
+    def give(k):
+        return remote(part.at[k, 1 - kind], chip_in.at[k], sends.at[k], recvs.at[k], to_c)
+
+    def held(k):
+        return part.at[k, kind]
+
+    def hop(i, src, dst, device):
+        return remote(src, dst, sends.at[i], recvs.at[i], device)
+
+    d0 = hop(4, part.at[0, kind, top], far_in.at[0, top], to_x)
+    d1 = hop(5, part.at[0, kind, low], far_in.at[1, low], to_y)
+    x0 = hop(6, part.at[1, kind, top], near_in.at[0, top], to_x)
+    y1 = hop(7, part.at[2, kind, low], near_in.at[1, low], to_y)
+    y0 = hop(8, part.at[2, kind, top], near_in.at[1, top], to_y)
+    x1 = hop(9, part.at[1, kind, low], near_in.at[0, low], to_x)
+
+    def chip_sum(k):
+        give(k).wait_recv()
+        add_rows(held(k), (held(k), chip_in.at[k]), 0, rows, part.dtype)
+
+    take_weight = pltpu.make_async_copy(weight_hbm, weight, local.at[18])
+    take_weight.start()
+    for k in range(4):
+        take_grads(k).start()
+        take_tokens(k).start()
+        take_back(k).start()
+    take_first(0).start()
+    take_weight.wait()
+
+    def chip_step(k, carry):
+        slot = lax.rem(k, 2)
+        take_grads(k).wait()
+        narrow[...] = nn(grads[k].reshape(pair, width), weight[:, lower])
+
+        @pl.when(k == 1)
+        def _():
+            chip_sum(0)
+            d0.start()
+            d1.start()
+
+        @pl.when(k == 2)
+        def _():
+            chip_sum(1)
+            x0.start()
+
+        @pl.when(k == 3)
+        def _():
+            chip_sum(2)
+            y1.start()
+            d0.wait_recv()
+            add_rows(held(2), (held(2), far_in.at[0]), 0, half, part.dtype)
+            y0.start()
+            d1.wait_recv()
+            add_rows(held(1), (held(1), far_in.at[1]), half, half, part.dtype)
+            x1.start()
+
+        take_tokens(k).wait()
+        wide[...] = nn(tokens[k].reshape(pair, width), weight[:, gate_up])
+        slopes(wide, narrow, inner.at[k], gug.at[k])
+        take_back(k).wait()
+
+        def back_step(n, carry):
+            at = pl.ds(pl.multiple_of(n * block, block), block)
+            total = nt(gug[k], weight[at, gate_up]).reshape(2, rows, block)
+            part[k, :, :, at] = (part[k, :, :, at].astype(F32) + total).astype(part.dtype)
+            return carry
+
+        lax.fori_loop(0, 4, back_step, 0)
+        give(k).start()
+        take_first(k).wait()
+
+        @pl.when(k >= 1)
+        def _():
+            put_out(k - 1).wait()
+
+        @pl.when(k < 3)
+        def _():
+            take_first(k + 1).start()
+
+        def out_step(n, carry):
+            at = pl.ds(pl.multiple_of(n * block, block), block)
+            total = nt(inner[k], weight[at, lower]).reshape(2, rows, block)
+            stage[slot, :, :, at] = (stage[slot, :, :, at].astype(F32) + total).astype(stage.dtype)
+            return carry
+
+        lax.fori_loop(0, 4, out_step, 0)
+        put_out(k).start()
+        return carry
+
+    lax.fori_loop(0, 4, chip_step, 0)
+
+    def grads_step(n, carry):
+        weight_step(n, tokens, grads, gug, inner, columns_stage, grads_out, (local, 16))
+
+        @pl.when(n == 0)
+        def _():
+            chip_sum(3)
+
+        return carry
+
+    lax.fori_loop(0, 4, grads_step, 0)
+    x0.wait_recv()
+    y0.wait_recv()
+    add_rows(sum_ref, (held(3), near_in.at[0], near_in.at[1]), 0, half, sum_ref.dtype)
+    y1.wait_recv()
+    x1.wait_recv()
+    add_rows(sum_ref, (held(3), near_in.at[0], near_in.at[1]), half, half, sum_ref.dtype)
+    for k in range(4):
+        give(k).wait_send()
+    for copy in (d0, d1, x0, y1, y0, x1):
         copy.wait_send()
-    for c, slot in ((0, 2), (2, 0), (3, 1)):
-        put_gug(c, slot).wait()
-    for c in (2, 3):
-        put_out(c).wait()
-        put_down(c).wait()
-
-
-def ffn_plane(block, grads, weight, ident):
+    put_out(3).wait()
+    for n in (2, 3):
+        pltpu.make_async_copy(
+            columns_stage.at[n - 2], grads_out.at[pl.ds(n * block, block)], local.at[14 + n]
+        ).wait()
+
+
+def ffn_first_plane(block, grads, weight, ident):
     rows, width = block.shape
-    seq = lax.axis_size("seq")
-    plane = lax.axis_size("tp") * seq
-    chips = plane // 2
-    ff_part = weight.shape[1] // 3
+    plane = lax.axis_size("tp") * lax.axis_size("seq")
+    cols = weight.shape[1]
+    ff_part = cols // 3
     shape = jax.ShapeDtypeStruct
     hbm = pl.BlockSpec(memory_space=pltpu.HBM)
     vmem = pl.BlockSpec(memory_space=pltpu.VMEM)
     tokens = plane * rows
     return pl.pallas_call(
-        ffn_kernel,
+        ffn_first_kernel,
         out_shape=(
             shape((plane, rows, width), BF),
-            shape((chips, 2 * rows, 2 * ff_part), BF),
             shape((plane, rows, width), BF),
-            shape((width, ff_part), BF),
-            shape((rows, width), F32),
+            shape((plane, rows, width), BF),
+            shape((width, cols), BF),
         ),
         in_specs=[vmem, hbm, hbm],
-        out_specs=(hbm, hbm, hbm, hbm, vmem),
+        out_specs=(hbm, hbm, hbm, hbm),
         scratch_shapes=[
             pltpu.VMEM(weight.shape, BF),
-            pltpu.VMEM((2, 2, rows, width), BF),
+            pltpu.VMEM((4, 2, rows, width), BF),
             pltpu.VMEM((4, 2, rows, width), BF),
             pltpu.VMEM((2 * rows, 2 * ff_part), F32),
             pltpu.VMEM((4, 2 * rows, ff_part), F32),
             pltpu.VMEM((4, 2 * rows, ff_part), BF),
-            pltpu.VMEM((3, 2 * rows, 2 * ff_part), BF),
-            pltpu.VMEM((2, width // 4, ff_part), BF),
+            pltpu.VMEM((4, 2 * rows, 2 * ff_part), BF),
+            pltpu.VMEM((2, 2, rows, width), BF),
+            pltpu.VMEM((2, width // 4, cols), BF),
+            pltpu.SemaphoreType.DMA((14,)),
+            pltpu.SemaphoreType.DMA((14,)),
+            pltpu.SemaphoreType.DMA((14,)),
+        ],
+        cost_estimate=pl.CostEstimate(
+            flops=18 * tokens * width * ff_part,
+            transcendentals=tokens * ff_part,
+            bytes_accessed=22 * tokens * width,
+        ),
+        compiler_params=pltpu.CompilerParams(
+            collective_id=ident, has_side_effects=True, vmem_limit_bytes=60 << 20
+        ),
+        name="ffn_first_plane",
+    )(block, grads, weight)
+
+
+def ffn_second_plane(block, grads, weight, back, first, ident):
+    plane, rows, width = block.shape
+    cols = weight.shape[1]
+    ff_part = cols // 3
+    shape = jax.ShapeDtypeStruct
+    hbm = pl.BlockSpec(memory_space=pltpu.HBM)
+    vmem = pl.BlockSpec(memory_space=pltpu.VMEM)
+    tokens = plane * rows
+    return pl.pallas_call(
+        ffn_second_kernel,
+        out_shape=(
+            shape((plane, rows, width), BF),
+            shape((width, cols), BF),
+            shape((rows, width), F32),
+        ),
+        in_specs=[hbm] * 5,
+        out_specs=(hbm, hbm, vmem),
+        scratch_shapes=[
+            pltpu.VMEM(weight.shape, BF),
+            pltpu.VMEM((4, 2, rows, width), BF),
+            pltpu.VMEM((4, 2, rows, width), BF),
+            pltpu.VMEM((2 * rows, 2 * ff_part), F32),
+            pltpu.VMEM((2 * rows, ff_part), F32),
+            pltpu.VMEM((4, 2 * rows, ff_part), BF),
+            pltpu.VMEM((4, 2 * rows, 2 * ff_part), BF),
             pltpu.VMEM((4, 2, rows, width), BF),
             pltpu.VMEM((4, rows, width), BF),
             pltpu.VMEM((2, rows, width), BF),
             pltpu.VMEM((2, rows, width), BF),
-            pltpu.SemaphoreType.DMA((24,)),
-            pltpu.SemaphoreType.DMA((24,)),
-            pltpu.SemaphoreType.DMA((15,)),
+            pltpu.VMEM((2, 2, rows, width), BF),
+            pltpu.VMEM((2, width // 4, cols), BF),
+            pltpu.SemaphoreType.DMA((10,)),
+            pltpu.SemaphoreType.DMA((10,)),
+            pltpu.SemaphoreType.DMA((19,)),
         ],
         cost_estimate=pl.CostEstimate(
-            flops=14 * tokens * width * ff_part,
+            flops=18 * tokens * width * ff_part,
             transcendentals=tokens * ff_part,
-            bytes_accessed=30 * tokens * width,
+            bytes_accessed=22 * tokens * width,
         ),
         compiler_params=pltpu.CompilerParams(
             collective_id=ident, has_side_effects=True, vmem_limit_bytes=63 << 20
         ),
-        name="ffn_plane",
-    )(block, grads, weight)
+        name="ffn_second_plane",
+    )(block, grads, weight, back, first)
 
 
 def finish_kernel(
-    gu_ref,
-    down_ref,
+    first_ref,
+    second_ref,
     gate_weight,
     up_weight,
     gain_ref,
     gate_out,
     up_out,
-    down_out,
+    down_first,
+    down_second,
     gain_out,
-    gu_in,
-    down_in,
+    first_in,
+    second_in,
     local,
     sends,
     recvs,
@@ -957,50 +1097,52 @@
     enter(devices)
     copies = []
     for k, (peer, device) in enumerate(zip(peers, devices)):
-        copies.append(remote(gu_ref.at[peer], gu_in.at[me], sends.at[k], recvs.at[k], device))
         i = plane - 1 + k
-        copies.append(remote(down_ref.at[peer], down_in.at[me], sends.at[i], recvs.at[i], device))
-    copies.append(pltpu.make_async_copy(gu_ref.at[me], gu_in.at[me], local.at[0]))
-    copies.append(pltpu.make_async_copy(down_ref.at[me], down_in.at[me], local.at[1]))
+        copies.append(remote(first_ref.at[peer], first_in.at[me], sends.at[k], recvs.at[k], device))
+        copies.append(remote(second_ref.at[peer], second_in.at[me], sends.at[i], recvs.at[i], device))
+    copies.append(pltpu.make_async_copy(first_ref.at[me], first_in.at[me], local.at[0]))
+    copies.append(pltpu.make_async_copy(second_ref.at[me], second_in.at[me], local.at[1]))
     for copy in copies:
         copy.start()
     for copy in copies:
         copy.wait()
-    put = pltpu.make_async_copy(down_in, down_out, local.at[2])
-    put.start()
     gain = gain_ref[...]
-    ff_part = down_in.shape[2]
+    sizes = [ref.shape[2] // 3 for ref in (first_in, second_in)]
     total = jnp.zeros(gain.shape, F32)
     for j in range(plane):
-        at = slice(j * ff_part, (j + 1) * ff_part)
-        for k, (out, weight) in enumerate(((gate_out, gate_weight), (up_out, up_weight))):
-            own = gu_in[j, :, k * ff_part : (k + 1) * ff_part].astype(F32)
-            out[:, at] = own * gain
-            total = total + jnp.sum(own * weight[:, at].astype(F32), axis=1, keepdims=True)
+        start = j * sum(sizes)
+        for ref, down, size in ((first_in, down_first, sizes[0]), (second_in, down_second, sizes[1])):
+            at = slice(start, start + size)
+            start += size
+            for k, (out, weight) in enumerate(((gate_out, gate_weight), (up_out, up_weight))):
+                own = ref[j, :, k * size : (k + 1) * size].astype(F32)
+                out[:, at] = own * gain
+                total = total + jnp.sum(own * weight[:, at].astype(F32), axis=1, keepdims=True)
+            down[j] = ref[j, :, 2 * size :]
     gain_out[...] = total
-    put.wait()
-
-
-def finish_plane(gu_sums, down_sums, gate_weight, up_weight, gain, ident):
-    plane, rows, ff_part = down_sums.shape
+
+
+def finish_plane(first, second, gate_weight, up_weight, gain, ident):
+    plane, rows, _ = first.shape
     shape = jax.ShapeDtypeStruct
     hbm = pl.BlockSpec(memory_space=pltpu.HBM)
     vmem = pl.BlockSpec(memory_space=pltpu.VMEM)
-    size = plane * rows * ff_part * 6
+    size = plane * rows * gate_weight.shape[1] * 6 // plane
     return pl.pallas_call(
         finish_kernel,
         out_shape=(
             shape(gate_weight.shape, F32),
             shape(up_weight.shape, F32),
-            shape(down_sums.shape, BF),
+            shape((plane, rows, first.shape[2] // 3), BF),
+            shape((plane, rows, second.shape[2] // 3), BF),
             shape((rows, 1), F32),
         ),
         in_specs=[hbm, hbm, vmem, vmem, vmem],
-        out_specs=(vmem, vmem, hbm, vmem),
+        out_specs=(vmem,) * 5,
         scratch_shapes=[
-            pltpu.VMEM(gu_sums.shape, BF),
-            pltpu.VMEM(down_sums.shape, BF),
-            pltpu.SemaphoreType.DMA((3,)),
+            pltpu.VMEM(first.shape, BF),
+            pltpu.VMEM(second.shape, BF),
+            pltpu.SemaphoreType.DMA((2,)),
             pltpu.SemaphoreType.DMA((2 * plane - 2,)),
             pltpu.SemaphoreType.DMA((2 * plane - 2,)),
         ],
@@ -1009,7 +1151,7 @@
             collective_id=ident, has_side_effects=True, vmem_limit_bytes=24 << 20
         ),
         name="finish_plane",
-    )(gu_sums, down_sums, gate_weight, up_weight, gain)
+    )(first, second, gate_weight, up_weight, gain)
 
 
 def columns(matrix, parts):
@@ -1075,17 +1217,19 @@
     scale1 = rms_scale(tokens)
     norm1 = tokens * scale1
 
-    ffn_pack = jnp.concatenate(
-        [
-            columns((wg32 * gain2).astype(BF), plane),
-            columns((wu32 * gain2).astype(BF), plane),
-            columns(w_down.T, plane),
-        ],
-        axis=2,
-    )
+    first_part = (ff_part // 2 + DH - 1) // DH * DH
+    split = ((0, first_part), (first_part, ff_part))
+    ffn_parts = (
+        columns((wg32 * gain2).astype(BF), plane),
+        columns((wu32 * gain2).astype(BF), plane),
+        columns(w_down.T, plane),
+    )
+    ffn_pack = jnp.concatenate([m[:, :, a:b] for a, b in split for m in ffn_parts], axis=2)
     ffn_rows = exchange_plane(after(ffn_pack, attn_rows), 2)
     ffn_rows = ffn_rows.reshape(-1, ffn_rows.shape[2])
-    ffn_weight = lax.all_gather(ffn_rows, "rep", axis=0, tiled=True)
+    first_weight = lax.all_gather(ffn_rows[:, : 3 * first_part], "rep", axis=0, tiled=True)
+    second_rows = after(ffn_rows[:, 3 * first_part :], ffn_rows)
+    second_weight = lax.all_gather(second_rows, "rep", axis=0, tiled=True)
     norm1_all = gather_plane(after(norm1.astype(BF), ffn_rows), 1)
     other_starts = lax.ppermute(pic_starts, "tp", [(0, 1), (1, 0)])
     starts = jnp.where(
@@ -1106,24 +1250,24 @@
 
     scale2 = rms_scale(hidden)
     norm2 = hidden * scale2
-    norm2_all, gate_up_grad, out_partial, down_partial, scaled2 = ffn_plane(
-        norm2.astype(BF), ffn_grad, ffn_weight, 5
-    )
-    norm2_all = norm2_all.reshape(-1, width)
-    gate_up_grad = gate_up_grad.reshape(-1, 2 * ff_part)
-    down_sums = lax.psum_scatter(down_partial, "rep", scatter_dimension=0, tiled=True)
-    gu_partial = tn(norm2_all, after(gate_up_grad, down_partial)).astype(BF)
-    gu_sums = lax.psum_scatter(gu_partial, "rep", scatter_dimension=0, tiled=True)
+    norm2_all, back_first, out_first, first_partial = ffn_first_plane(
+        norm2.astype(BF), ffn_grad, first_weight, 5
+    )
+    first_sums = lax.psum_scatter(first_partial, "rep", scatter_dimension=0, tiled=True)
+    out_partial, second_partial, scaled2 = ffn_second_plane(
+        norm2_all, ffn_grad, second_weight, back_first, out_first, 6
+    )
+    second_sums = lax.psum_scatter(second_partial, "rep", scatter_dimension=0, tiled=True)
     hidden_grad = upstream + scale2 * (
         scaled2 - norm2 * jnp.mean(scaled2 * norm2, axis=-1, keepdims=True)
     )
 
-    branch_grad = gather_plane(after((keep * hidden_grad).astype(BF), gu_partial, down_partial), 7)
+    branch_grad = gather_plane((keep * hidden_grad).astype(BF), 7)
     mixed_grad = nn(branch_grad, out_weight).astype(BF)
     qkv_grad, ffn_out = attn_back_plane(
         starts,
         qkv,
-        after(mixed_grad, down_sums),
+        after(mixed_grad, first_sums),
         log_total,
         cos,
         sin,
@@ -1141,14 +1285,15 @@
     )
     out_hidden = (hidden + keep * ffn_out).astype(BF)
 
-    gate_grad, up_grad, down_own, gain_ffn_grad = finish_plane(
-        after(gu_sums.reshape(plane, -1, 2 * ff_part), scaled1),
-        down_sums.reshape(plane, -1, ff_part),
+    gate_grad, up_grad, down_first, down_second, gain_ffn_grad = finish_plane(
+        after(first_sums.reshape(plane, -1, first_sums.shape[1]), scaled1),
+        second_sums.reshape(plane, -1, second_sums.shape[1]),
         w_gate,
         w_up,
         gain2,
         10,
     )
+    down_own = jnp.concatenate([down_first, down_second], axis=2)
     down_grad = jnp.transpose(down_own, (0, 2, 1)).reshape(plane * ff_part, -1).astype(F32)
 
     attn_sums = after(attn_sums, gain_ffn_grad)

time: 604 us -> 587 us (0.972)
  waiting for transfers between devices: 38.5 us -> 0.19 us
  Pallas kernels: 429 us -> 461 us
  matrix products: 56.7 us -> 37.4 us
    all_gather x1 -> x2, waiting for transfers between devices: 38.4 us -> 0.02 us  [the longest x1 0.02 us: per_device(): second_weight = lax.all_gather(second_rows, 'rep', axis=0, tiled=True)]
    pallas_call x1 -> x2, Pallas kernels: 94.1 us -> 129 us  [the longest x1 66 us: ffn_first_plane(): pl.pallas_call(ffn_first_kernel, out_shape=(shape((plane, rows, width), B...]
    dot_general x7 -> x6, matrix products: 56.7 us -> 37.4 us  [dot(): lax.dot_general(left, right, ((contract[:1], contract[1:]), ((), ())), pr...]
    unnamed x78 -> x76, local copies, waits for them, and re-layouts: 15.5 us -> 16.4 us
  transfers between devices with their start and end apart: 6 -> 7, of which waited for: 1 -> 0; matrix products, arithmetic and copies ran while one was open for 15% -> 13% of each run, Pallas kernels for 52% -> 75%
where the time goes in v9:
time: 587 us; the launch traced here: 582 us
  Pallas kernels  461 us (79%)
  local copies, waits for them, and re-layouts  39.7 us (7%)
  matrix products  37.4 us (6%)
  other arithmetic  27.2 us (5%)
  between operations  15.1 us (3%)
    pallas_call x2, Pallas kernels, gather_plane(): pl.pallas_call(gather_kernel, out_shape=jax.ShapeDtypeStruct((plane, rows...  83.9 us
    pallas_call x2, Pallas kernels, scatter_plane(): pl.pallas_call(scatter_kernel, out_shape=jax.ShapeDtypeStruct((rows, widt...  80.3 us
    pallas_call x1, Pallas kernels, ffn_first_plane(): pl.pallas_call(ffn_first_kernel, out_shape=(shape((plane, rows, width), B...  66 us
    pallas_call x1, Pallas kernels, ffn_second_plane(): pl.pallas_call(ffn_second_kernel, out_shape=(shape((plane, rows, width),...  62.6 us
    pallas_call x3, Pallas kernels, exchange_plane(): pl.pallas_call(exchange_kernel, out_shape=jax.ShapeDtypeStruct(blocks.sha...  53.9 us
    pallas_call x1, Pallas kernels, attn_back_plane(): pl.pallas_call(attn_back_kernel, out_shape=(jax.ShapeDtypeStruct((tokens,...  43.4 us
    pallas_call x1, Pallas kernels, attn_front_plane(): pl.pallas_call(attn_front_kernel, out_shape=(shape((tokens, cols), BF), s...  40.9 us
    dot_general x6, matrix products, dot(): lax.dot_general(left, right, ((contract[:1], contract[1:]), ((), ())), pr...  37.4 us
  transfers between devices with their start and end apart: 7, of which 0 were waited for; matrix products, arithmetic and copies ran while one was open for 13% of the time, Pallas kernels for 75%

profile of v9, /device:TPU:1, one launch (start us, length us, event | category | flops | bytes accessed | tf_op | source)
XLA Modules:
  0.0 581.9 jit_solution(10510001675372661313)
XLA Ops:
  7.2 1.1 fusion.16
  8.3 1.0 fusion.19
  9.4 1.0 bitcast_bitcast_fusion
  10.5 1.0 pad_maximum_fusion.1.in_ref
  11.4 13.7 %exchange_plane.3 = bf16[8,64,768]{2,1,0:T(8,128)(2,1)} custom-call(bf16[8,64,768]{2,1,0:T(8,128)(2,1)} %pad_maximum_fusion.1.in_ref), custom_call_target="tpu_custom_call" | custom-call | bytes 15728640 | tf_op jit(solution)/shard_map/exchange_plane/pallas_call | solution.py:568
  25.2 0.3 multiply_convert_fusion.2
  25.5 0.7 reshape.138
  26.5 0.7 reshape.139
  27.3 0.8 slice.64
  28.1 1.8 reshape.140
  30.2 4.7 concatenate.26.in_ref
  34.9 28.0 %exchange_plane.4 = bf16[8,64,2112]{2,1,0:T(8,128)(2,1)} custom-call(bf16[8,64,2112]{2,1,0:T(8,128)(2,1)} %concatenate.26.in_ref), custom_call_target="tpu_custom_call" | custom-call | bytes 43253760 | tf_op jit(solution)/shard_map/exchange_plane/pallas_call | solution.py:568
  62.9 2.4 slice.68
  65.3 1.2 collective-permute-start
  66.5 2.3 slice.69
  69.4 1.2 fusion.2.refs_0_
  70.7 42.2 %gather_plane.2 = bf16[8,256,2048]{2,1,0:T(8,128)(2,1)} custom-call(bf16[256,2048]{1,0:T(8,128)(2,1)} %fusion.2.refs_0_), custom_call_target="tpu_custom_call" | custom-call | bytes 100663296 | tf_op jit(solution)/shard_map/gather_plane/pallas_call | solution.py:170
  112.9 3.2 fusion.18
  116.3 1.9 pad_maximum_fusion.2
  118.3 7.9 %fusion.11.projected_ref = f32[2048,512]{1,0:T(8,128)S(1)} fusion(bf16[2048,2048]{1,0:T(8,128)(2,1)} %bitcast.98, bf16[2048,768]{1,0:T(8,128)(2,1)} %all-gather.4.cloned.1.call-done), kind=kOutput, calls=%fused_computation.26 | convolution fusion | flops 4294967296 | bytes 14680064 | tf_op jit(solution)/shard_map/dot_general | solution.py:32
  126.2 40.9 %attn_front_plane.1 = (bf16[2048,512]{1,0:T(8,128)(2,1)S(1)}, bf16[2048,256]{1,0:T(8,128)(2,1)S(1)}, f32[4,1,1024]{2,1,0:T(1,128)S(1)}, bf16[8,256,2048]{2,1,0:T(8,128)(2,1)}) custom-call(s32[2,2]{1,0:T(2,128)S(1)} %add_select_fusion.starts_ref, f32[2048,512]{1,0:T(8,128)S(1)} %fusion.11.projected_ref, f32[1024,128]{1,0:T(8,128)S(1)} %get-tuple-element.86.cos_ref, ...), custom_call_target="tpu_custom_call" | custom-call | flops 2147483648 | bytes 100663296 | tf_op jit(solution)/shard_map/attn_front_plane/pallas_call | solution.py:406
  167.1 1.3 copy-done.15
  168.4 4.0 convolution_convert_fusion.1
  172.5 39.7 %scatter_plane.2 = f32[256,2048]{1,0:T(8,128)S(1)} custom-call(bf16[8,256,2048]{2,1,0:T(8,128)(2,1)S(1)} %bitcast.92), custom_call_target="tpu_custom_call" | custom-call | bytes 117440512 | tf_op jit(solution)/shard_map/scatter_plane/pallas_call | solution.py:299
  212.2 0.5 multiply_reduce_fusion.1
  212.7 1.3 copy-done.16
  214.0 1.1 multiply_convert_fusion.1.own_ref
  215.1 66.0 %ffn_first_plane.1 = (bf16[8,256,2048]{2,1,0:T(8,128)(2,1)}, bf16[8,256,2048]{2,1,0:T(8,128)(2,1)}, bf16[8,256,2048]{2,1,0:T(8,128)(2,1)}, bf16[2048,1152]{1,0:T(8,128)(2,1)}) custom-call(bf16[256,2048]{1,0:T(8,128)(2,1)} %multiply_convert_fusion.1.own_ref, bf16[8,256,2048]{2,1,0:T(8,128)(2,1)} %get-tuple-element.40.grad_ref, ...), custom_call_target="tpu_custom_call" | custom-call | flops 28991029248 | bytes 92274688 | tf_op jit(solution)/shard_map/ffn_first_plane/pallas_call | solution.py:991
  281.2 62.6 %ffn_second_plane.1 = (bf16[8,256,2048]{2,1,0:T(8,128)(2,1)}, bf16[2048,960]{1,0:T(8,128)(2,1)}, f32[256,2048]{1,0:T(8,128)}) custom-call(bf16[8,256,2048]{2,1,0:T(8,128)(2,1)} %get-tuple-element.41.all_ref, bf16[8,256,2048]{2,1,0:T(8,128)(2,1)} %get-tuple-element.40.grad_ref, bf16[2048,960]{1,0:T(8,128)(2,1)} %all-gather.8.cloned.1.call-done.weight_hbm, ...), custom_call_target="tpu_custom_call" | custom-call | flops 24159191040 | bytes 92274688 | tf_op jit(solution)/shard_map/ffn_second_plane/pallas_call | solution.py:1035
  343.9 1.5 copy-done.17
  345.4 2.1 multiply_reduce_fusion
  347.7 0.3 copy-done.24
  348.0 1.6 multiply_convert_fusion.refs_0_
  349.6 41.6 %gather_plane.3 = bf16[8,256,2048]{2,1,0:T(8,128)(2,1)} custom-call(bf16[256,2048]{1,0:T(8,128)(2,1)} %multiply_convert_fusion.refs_0_), custom_call_target="tpu_custom_call" | custom-call | bytes 100663296 | tf_op jit(solution)/shard_map/gather_plane/pallas_call | solution.py:170
  391.3 6.9 %convolution_convert_fusion.3 = bf16[2048,256]{0,1:T(8,128)(2,1)} fusion(bf16[2048,2048]{1,0:T(8,128)(2,1)} %bitcast.100, bf16[2048,256]{1,0:T(8,128)(2,1)S(1)} %copy-done.4), kind=kOutput, calls=%fused_computation.12 | convolution fusion | flops 2148007936 | bytes 10485760 | tf_op jit(solution)/shard_map/dot_general | solution.py:32
  398.2 3.7 convolution_convert_fusion.4.g_ref
  401.9 43.4 %attn_back_plane.1 = (bf16[2048,512]{1,0:T(8,128)(2,1)}, f32[256,2048]{1,0:T(8,128)}) custom-call(s32[2,2]{1,0:T(2,128)S(1)} %add_select_fusion.starts_ref, bf16[2048,512]{1,0:T(8,128)(2,1)} %copy-done.15, bf16[2048,256]{1,0:T(8,128)(2,1)S(1)} %convolution_convert_fusion.4.g_ref, f32[4,1,1024]{2,1,0:T(1,128)S(1)} %get-tuple-element.48.log_ref, ...), custom_call_target="tpu_custom_call" | custom-call | flops 5368709120 | bytes 117440512 | tf_op jit(solution)/shard_map/attn_back_plane/pallas_call | solution.py:515
  445.3 8.7 %convolution_convert_fusion.2 = bf16[2048,512]{0,1:T(8,128)(2,1)S(1)} fusion(bf16[2048,2048]{1,0:T(8,128)(2,1)} %bitcast.99, bf16[2048,512]{1,0:T(8,128)(2,1)} %get-tuple-element.51), kind=kOutput, calls=%fused_computation.6 | convolution fusion | flops 4296015872 | bytes 12582912 | tf_op jit(solution)/shard_map/dot_general | solution.py:32
  453.9 1.8 pad_maximum_fusion
  455.9 1.5 copy-done.35
  457.4 6.4 %convolution_convert_fusion = bf16[2048,2048]{1,0:T(8,128)(2,1)S(1)} fusion(bf16[2048,512]{1,0:T(8,128)(2,1)S(1)} %copy-done.35, bf16[2048,768]{1,0:T(8,128)(2,1)} %all-gather.4.cloned.1.call-done), kind=kOutput, calls=%fused_computation | convolution fusion | flops 4299161600 | bytes 12582912 | tf_op jit(solution)/shard_map/dot_general | solution.py:32
  463.7 40.6 %scatter_plane.3 = f32[256,2048]{1,0:T(8,128)S(1)} custom-call(bf16[8,256,2048]{2,1,0:T(8,128)(2,1)S(1)} %bitcast.93), custom_call_target="tpu_custom_call" | custom-call | bytes 117440512 | tf_op jit(solution)/shard_map/scatter_plane/pallas_call | solution.py:299
  504.4 1.1 copy-done.2
  505.5 1.3 copy-done.9
  506.7 1.2 copy-done.10
  508.0 29.8 %finish_plane.1 = (f32[64,5632]{1,0:T(8,128)S(1)}, f32[64,5632]{1,0:T(8,128)S(1)}, bf16[8,64,384]{2,1,0:T(8,128)(2,1)S(1)}, bf16[8,64,320]{2,1,0:T(8,128)(2,1)S(1)}, f32[64,1]{1,0:T(8,128)S(1)}) custom-call(bf16[8,64,1152]{2,1,0:T(8,128)(2,1)S(1)} %bitcast.94, bf16[8,64,960]{2,1,0:T(8,128)(2,1)S(1)} %bitcast.95, bf16[64,5632]{1,0:T(8,128)(2,1)S(1)} %copy-done.2, ...), custom_call_target="tpu_custom_call" | custom-call | bytes 43253760 | tf_op jit(solution)/shard_map/finish_plane/pallas_call | solution.py:1131
  537.8 1.1 copy-done.5
  538.9 1.1 copy-done.7
  540.2 2.1 copy.65
  542.2 2.9 reshape.163
  545.1 0.6 reduce
  545.7 0.4 fusion.4
  546.2 1.2 copy-done.18
  547.6 5.0 fusion.8
  552.6 2.3 copy.60
  554.9 12.2 %exchange_plane.5 = bf16[8,64,768]{2,1,0:T(8,128)(2,1)} custom-call(bf16[8,64,768]{2,1,0:T(8,128)(2,1)} %bitcast.109), custom_call_target="tpu_custom_call" | custom-call | bytes 15728640 | tf_op jit(solution)/shard_map/exchange_plane/pallas_call | solution.py:568
  567.1 1.3 convert_element_type.126
  568.6 0.7 copy-done.27
  569.3 1.0 broadcast_multiply_fusion
  570.4 0.8 copy.71
  571.2 0.9 bitcast_multiply_fusion
  572.1 0.5 add_add_fusion
  572.7 1.1 copy.86
  573.8 1.1 copy.87
  (109 shorter events, 2.9 us)
Async XLA Ops:
  7.2 111.1 %all-gather.4.cloned.1.call-start = ((), (), s32[]{:S(2)}) async-start(), calls=%async_computation.3 | async-start | bytes 3932160 | tf_op jit(solution)/shard_map/all_gather | solution.py:1210
  10.4 14.8 %copy-start = (bf16[64,5632]{1,0:T(8,128)(2,1)S(1)}, bf16[64,5632]{1,0:T(8,128)(2,1)}, u32[]{:S(2)}) copy-start(bf16[64,5632]{1,0:T(8,128)(2,1)} %up_weight.1) | copy-start | bytes 2162692
  10.4 14.8 %copy-start.1 = (bf16[64,5632]{1,0:T(8,128)(2,1)S(1)}, bf16[64,5632]{1,0:T(8,128)(2,1)}, u32[]{:S(2)}) copy-start(bf16[64,5632]{1,0:T(8,128)(2,1)} %gate_weight.1) | copy-start | bytes 2162692
  10.4 14.8 %copy-start.32 = (f32[64]{0:T(128)S(1)}, f32[64]{0:T(128)}, u32[]{:S(2)}) copy-start(f32[64]{0:T(128)} %param.21) | copy-start | bytes 772
  25.1 190.0 %all-gather.6.cloned.1.call-start = ((), (), s32[]{:S(2)}) async-start(), calls=%async_computation.4 | async-start | bytes 5898240 | tf_op jit(solution)/shard_map/all_gather | solution.py:1230
  62.9 2.5 copy-start.34
  65.3 3.9 copy-start.19
  65.3 215.9 %all-gather.8.cloned.1.call-start = ((), (), s32[]{:S(2)}) async-start(), calls=%async_computation.5 | async-start | bytes 5242880 | tf_op jit(solution)/shard_map/all_gather | solution.py:1232
  65.3 52.9 %collective-permute-start = (s32[1,2]{1,0:T(1,128)S(1)}, s32[1,2]{1,0:T(1,128)S(1)}, u32[]{:S(2)}, u32[]{:S(2)}) collective-permute-start(s32[1,2]{1,0:T(1,128)S(1)} %copy-done.34), channel_id=1, source_target_pairs={{0,4},{4,0},{1,5},{5,1},{2,6},{6,2},{3,7},{7,3},{8,12},{12,8},{9,1... | collective-permute-start | bytes 32 | tf_op jit(solution)/shard_map/ppermute | solution.py:1234
  68.8 333.0 %reduce-scatter.4.cloned.1.call-start = ((), (), s32[]{:S(2)}) async-start(), calls=%async_computation.6 | async-start | bytes 5898240 | tf_op jit(solution)/shard_map/reduce_scatter | solution.py:1256
  70.6 42.2 %copy-start.33 = (s32[1,256]{1,0:T(1,128)S(1)}, s32[1,256]{1,0:T(1,128)}, u32[]{:S(2)}) copy-start(s32[1,256]{1,0:T(1,128)} %param.15) | copy-start | bytes 3076
  112.9 3.2 copy-start.23
  118.2 7.9 %copy-start.11 = (f32[1024,128]{1,0:T(8,128)}, f32[1024,128]{1,0:T(8,128)S(1)}, u32[]{:S(2)}) copy-start(f32[1024,128]{1,0:T(8,128)S(1)} %get-tuple-element.86.cos_ref) | copy-start | bytes 1572868
  118.2 7.9 %copy-start.13 = (f32[1024,128]{1,0:T(8,128)}, f32[1024,128]{1,0:T(8,128)S(1)}, u32[]{:S(2)}) copy-start(f32[1024,128]{1,0:T(8,128)S(1)} %get-tuple-element.87.sin_ref) | copy-start | bytes 1572868
  167.1 1.3 copy-start.15
  168.4 4.0 copy-start.3
  172.4 39.7 %copy-start.20 = (bf16[1,256,2048]{2,1,0:T(8,128)(2,1)S(1)}, bf16[1,256,2048]{2,1,0:T(8,128)(2,1)}, u32[]{:S(2)}) copy-start(bf16[1,256,2048]{2,1,0:T(8,128)(2,1)} %param.13) | copy-start | bytes 3145732
  212.6 1.3 copy-start.16
  281.2 223.2 %reduce-scatter.8.cloned.1.call-start = ((), (), s32[]{:S(2)}) async-start(), calls=%async_computation.8 | async-start | bytes 5242880 | tf_op jit(solution)/shard_map/reduce_scatter | solution.py:1260
  343.8 1.6 copy-start.17
  343.9 208.8 %reduce-scatter.6.cloned.1.call-start = ((), (), s32[]{:S(2)}) async-start(), calls=%async_computation.7 | async-start | bytes 3932160 | tf_op jit(solution)/shard_map/reduce_scatter | solution.py:1281
  345.4 2.3 copy-start.22
  345.4 2.6 copy-start.24
  349.6 41.7 %copy-start.4 = (bf16[2048,256]{1,0:T(8,128)(2,1)S(1)}, bf16[2048,256]{1,0:T(8,128)(2,1)}, u32[]{:S(2)}) copy-start(bf16[2048,256]{1,0:T(8,128)(2,1)} %copy-done.3) | copy-start | bytes 3145732
  391.3 6.9 %copy-start.26 = (bf16[8,256,2048]{2,1,0:T(8,128)(2,1)S(1)}, bf16[8,256,2048]{2,1,0:T(8,128)(2,1)}, u32[]{:S(2)}) copy-start(bf16[8,256,2048]{2,1,0:T(8,128)(2,1)} %gather_plane.3) | copy-start | bytes 25165828
  398.2 3.7 copy-start.12
  398.2 3.7 copy-start.14
  445.3 8.7 %copy-start.28 = (bf16[2048,256]{0,1:T(8,128)(2,1)S(1)}, bf16[2048,256]{0,1:T(8,128)(2,1)}, u32[]{:S(2)}) copy-start(bf16[2048,256]{0,1:T(8,128)(2,1)} %convolution_convert_fusion.3) | copy-start | bytes 3145732
  455.8 1.6 copy-start.35
  504.4 1.1 copy-start.2
  505.5 1.3 copy-start.9
  506.7 1.2 copy-start.10
  537.8 1.1 copy-start.5
  538.9 1.1 copy-start.7
  542.2 3.5 copy-start.21
  545.7 1.6 copy-start.18
  545.7 1.9 copy-start.25
  568.4 1.0 copy-start.27
  568.4 0.9 copy-start.31
  568.6 2.7 copy-start.29
  568.6 2.7 copy-start.30
  568.6 4.1 copy-start.8
  570.4 3.4 copy-start.6
Sparse Core Ops, SparseCore 0:
  25.3 63.8 all-gather.3
  91.3 88.1 all-gather.5
  181.6 79.0 all-gather.7
  281.3 85.0 reduce-scatter.3
  368.5 77.0 reduce-scatter.7
  455.9 60.6 reduce-scatter.5

commit v10 on v9

--- a/solution.py
+++ b/solution.py
@@ -118,8 +118,8 @@
     rd0, rd1 = relay(12, other, far, 0, to_c), relay(13, other, far, 1, to_c)
     mine = pltpu.make_async_copy(own_ref, all_ref.at[tp_at * seq + seq_at], local)
 
-    def begin():
-        enter((to_x, to_y, to_c))
+    def begin(peers=(to_x, to_y, to_c)):
+        enter(peers)
         for copy in (x0, y0, c0, x1, y1, c1, mine):
             copy.start()
 
@@ -180,6 +180,74 @@
         name="gather_plane",
     )(block)
     return gathered.reshape(plane * rows, width)
+
+
+def spread_kernel(
+    own_ref, first_ref, second_ref, all_ref, first_out, second_out, first_own, second_own, copies, *gather
+):
+    begin, first, second, finish = gather_stages(own_ref, all_ref, *gather)
+    tp_at, seq_at, _, _, _ = plane_place()
+    seq = lax.axis_size("seq")
+    plane = lax.axis_size("tp") * seq
+    me = tp_at * seq + seq_at
+    peers = [lax.rem(me + k, plane) for k in range(1, plane)]
+    devices = [at_device(peer // seq, lax.rem(peer, seq)) for peer in peers]
+    sends, recvs, local = copies.at[0], copies.at[1], copies.at[2]
+    begin(devices)
+    moves, keeps = [], []
+    for n, (ref, out, kept) in enumerate(
+        ((first_ref, first_out, first_own), (second_ref, second_out, second_own))
+    ):
+        for k, (peer, device) in enumerate(zip(peers, devices)):
+            i = n * (plane - 1) + k
+            moves.append(remote(ref.at[peer], out.at[me], sends.at[i], recvs.at[i], device))
+        keeps.append(
+            (
+                pltpu.make_async_copy(ref.at[me], kept, local.at[2 * n]),
+                pltpu.make_async_copy(kept, out.at[me], local.at[2 * n + 1]),
+            )
+        )
+    for move in moves:
+        move.start()
+    for take, put in keeps:
+        take.start()
+    for take, put in keeps:
+        take.wait()
+        put.start()
+    first()
+    second()
+    for move in moves:
+        move.wait()
+    for take, put in keeps:
+        put.wait()
+    finish()
+
+
+def spread_plane(block, first, second, ident):
+    rows, width = block.shape
+    plane = lax.axis_size("tp") * lax.axis_size("seq")
+    hbm = pl.BlockSpec(memory_space=pltpu.HBM)
+    vmem = pl.BlockSpec(memory_space=pltpu.VMEM)
+    size = plane * rows * width * 2
+    return pl.pallas_call(
+        spread_kernel,
+        out_shape=(
+            jax.ShapeDtypeStruct((plane, rows, width), block.dtype),
+            jax.ShapeDtypeStruct(first.shape, first.dtype),
+            jax.ShapeDtypeStruct(second.shape, second.dtype),
+        ),
+        in_specs=[vmem, hbm, hbm],
+        out_specs=(hbm, hbm, hbm),
+        scratch_shapes=[
+            pltpu.VMEM(first.shape[1:], first.dtype),
+            pltpu.VMEM(second.shape[1:], second.dtype),
+            pltpu.SemaphoreType.DMA((3, 2 * plane)),
+            *GATHER_SCRATCH,
+        ],
+        cost_estimate=pl.CostEstimate(flops=0, transcendentals=0, bytes_accessed=size * 16),
+        compiler_params=pltpu.CompilerParams(collective_id=ident, has_side_effects=True),
+        name="spread_plane",
+    )(block, first, second)
 
 
 def add_rows(target, sources, start, count, kind):
@@ -332,21 +400,42 @@
 
 def attn_front_kernel(
     starts_ref,
-    projected_ref,
+    norm_hbm,
+    weight_hbm,
     cos_ref,
     sin_ref,
     own_ref,
     qkv_ref,
     mixed_ref,
     log_ref,
+    out_ref,
     all_ref,
     bias,
     turned,
+    norm,
+    weight,
+    projected,
+    stage,
+    local,
     *gather,
 ):
     begin, first, second, finish = gather_stages(own_ref, all_ref, *gather)
+    total, dim = cos_ref.shape
+    take_weight = pltpu.make_async_copy(weight_hbm, weight, local.at[0])
+    take_weight.start()
+
+    def take_norm(t):
+        rows = pl.ds(t * total, total)
+        return pltpu.make_async_copy(norm_hbm.at[rows], norm.at[t], local.at[1 + t])
+
+    def put_out(t, n):
+        rows = pl.ds(t * total + n * (total // 2), total // 2)
+        return pltpu.make_async_copy(stage.at[n], out_ref.at[rows], local.at[1 + TP + n])
+
+    for t in range(TP):
+        take_norm(t).start()
     begin()
-    total, dim = cos_ref.shape
+    take_weight.wait()
     heads = mixed_ref.shape[1] // dim
     blocks = total // PIC
     scale = dim ** (-0.5)
@@ -364,8 +453,16 @@
         @pl.when(h == 0)
         def _():
             rows = pl.ds(base, total)
-            values = projected_ref[rows, v_cols].astype(BF)
-            qkv_ref[rows, k_cols] = turn(projected_ref[rows, k_cols], pl.ds(0, total)).astype(BF)
+            take_norm(t).wait()
+
+            def project(n, carry):
+                some = pl.ds(pl.multiple_of(n * PIC, PIC), PIC)
+                projected[some, :] = nn(norm[t, some, :], weight[:, : (heads + 2) * dim])
+                return carry
+
+            lax.fori_loop(0, blocks, project, 0)
+            values = projected[:, v_cols].astype(BF)
+            qkv_ref[rows, k_cols] = turn(projected[:, k_cols], pl.ds(0, total)).astype(BF)
             qkv_ref[rows, v_cols] = values
             turned[...] = values.T
             fill_bias(bias, starts_ref, t, blocks)
@@ -373,7 +470,7 @@
         for b in range(blocks):
             at = pl.ds(pl.multiple_of(base + b * PIC, PIC), PIC)
             count = min(b + 2, blocks) * PIC
-            queries = turn(projected_ref[at, cols], pl.ds(b * PIC, PIC)).astype(BF)
+            queries = turn(projected[b * PIC : (b + 1) * PIC, cols], pl.ds(b * PIC, PIC)).astype(BF)
             qkv_ref[at, cols] = queries
             scores = nt(qkv_ref[pl.ds(base, count), k_cols], queries) * scale
             scores = masked(scores, bias, b)
@@ -384,21 +481,43 @@
             probs = (weights * (1.0 / mass)).astype(BF)
             mixed_ref[at, cols] = nn(turned[:, :count], probs).T.astype(BF)
             if b == 0:
-                pl.when(i == 2)(first)
+                pl.when(i == 1)(first)
+                pl.when(i == 3)(second)
+
+        @pl.when(h == heads - 1)
+        def _():
+            for n in range(2):
+
+                @pl.when(t >= 1)
+                def _():
+                    put_out(t - 1, n).wait()
+
+                rows = pl.ds(pl.multiple_of(base + n * (total // 2), total // 2), total // 2)
+                block = stage.shape[2] // 4
+
+                def out_step(m, carry):
+                    some = pl.ds(pl.multiple_of(m * block, block), block)
+                    partial = nt(mixed_ref[rows, :], weight[some, (heads + 2) * dim :])
+                    stage[n, :, some] = partial.astype(BF)
+                    return carry
+
+                lax.fori_loop(0, 4, out_step, 0)
+                put_out(t, n).start()
 
         return carry
 
     lax.fori_loop(0, log_ref.shape[0], head_step, 0)
-    second()
     finish()
-
-
-def attn_front_plane(starts, projected, cos, sin, block, ident):
+    for n in range(2):
+        put_out(TP - 1, n).wait()
+
+
+def attn_front_plane(starts, norm, weight, cos, sin, block, ident):
     rows, width = block.shape
     plane = lax.axis_size("tp") * lax.axis_size("seq")
     total, dim = cos.shape
-    tokens, cols = projected.shape
-    q_part = cols - 2 * dim
+    tokens = norm.shape[0]
+    q_part = weight.shape[1] // 2 - dim
     shape = jax.ShapeDtypeStruct
     vmem = pl.BlockSpec(memory_space=pltpu.VMEM)
     smem = pl.BlockSpec(memory_space=pltpu.SMEM)
@@ -406,16 +525,22 @@
     return pl.pallas_call(
         attn_front_kernel,
         out_shape=(
-            shape((tokens, cols), BF),
+            shape((tokens, q_part + 2 * dim), BF),
             shape((tokens, q_part), BF),
             shape((tokens * q_part // dim // total, 1, total), F32),
+            shape(norm.shape, BF),
             shape((plane, rows, width), block.dtype),
         ),
-        in_specs=[smem] + [vmem] * 4,
-        out_specs=(vmem, vmem, vmem, hbm),
+        in_specs=[smem, hbm, hbm, vmem, vmem, vmem],
+        out_specs=(vmem, vmem, vmem, hbm, hbm),
         scratch_shapes=[
             pltpu.VMEM((total // PIC, 2 * PIC, PIC), F32),
             pltpu.VMEM((dim, total), BF),
+            pltpu.VMEM((TP, total, width), BF),
+            pltpu.VMEM(weight.shape, BF),
+            pltpu.VMEM((total, q_part + 2 * dim), F32),
+            pltpu.VMEM((2, total // 2, width), BF),
+            pltpu.SemaphoreType.DMA((3 + TP,)),
             *GATHER_SCRATCH,
         ],
         cost_estimate=pl.CostEstimate(
@@ -427,7 +552,7 @@
             collective_id=ident, has_side_effects=True, vmem_limit_bytes=40 << 20
         ),
         name="attn_front_plane",
-    )(starts, projected, cos, sin, block)
+    )(starts, norm, weight, cos, sin, block)
 
 
 def attn_back_kernel(
@@ -1224,13 +1349,18 @@
         columns((wu32 * gain2).astype(BF), plane),
         columns(w_down.T, plane),
     )
-    ffn_pack = jnp.concatenate([m[:, :, a:b] for a, b in split for m in ffn_parts], axis=2)
-    ffn_rows = exchange_plane(after(ffn_pack, attn_rows), 2)
-    ffn_rows = ffn_rows.reshape(-1, ffn_rows.shape[2])
-    first_weight = lax.all_gather(ffn_rows[:, : 3 * first_part], "rep", axis=0, tiled=True)
-    second_rows = after(ffn_rows[:, 3 * first_part :], ffn_rows)
+    first_pack, second_pack = (
+        jnp.concatenate([m[:, :, a:b] for m in ffn_parts], axis=2) for a, b in split
+    )
+    norm1_all, first_rows, second_rows = spread_plane(
+        after(norm1.astype(BF), attn_rows), first_pack, second_pack, 1
+    )
+    first_rows = first_rows.reshape(-1, first_rows.shape[2])
+    second_rows = second_rows.reshape(-1, second_rows.shape[2])
+    first_weight = lax.all_gather(first_rows, "rep", axis=0, tiled=True)
     second_weight = lax.all_gather(second_rows, "rep", axis=0, tiled=True)
-    norm1_all = gather_plane(after(norm1.astype(BF), ffn_rows), 1)
+    norm1_all = norm1_all.reshape(-1, width)
+
     other_starts = lax.ppermute(pic_starts, "tp", [(0, 1), (1, 0)])
     starts = jnp.where(
         lax.axis_index("tp") == 0,
@@ -1241,11 +1371,10 @@
     cos_table, sin_table = rotary_tables(positions, DH)
     cos = jnp.concatenate([cos_table, cos_table], axis=1)
     sin = jnp.concatenate([-sin_table, sin_table], axis=1)
-    projected = nn(norm1_all, qkv_weight)
-    qkv, mixed, log_total, ffn_grad = attn_front_plane(
-        starts, projected, cos, sin, (keep * upstream).astype(BF), 3
-    )
-    branch = scatter_plane(nt(mixed, out_weight).astype(BF), 4)
+    qkv, mixed, log_total, branch_partial, ffn_grad = attn_front_plane(
+        starts, norm1_all, attn_weight, cos, sin, (keep * upstream).astype(BF), 3
+    )
+    branch = scatter_plane(branch_partial, 4)
     hidden = tokens + keep * branch
 
     scale2 = rms_scale(hidden)

time: 587 us -> 581 us (0.990)
  matrix products: 37.4 us -> 25.4 us
  waiting for transfers between devices: 0.19 us -> 7.31 us
    pallas_call x1 -> x2, Pallas kernels: 40.9 us -> 109 us  [the longest x1 66.1 us: spread_plane(): pl.pallas_call(spread_kernel, out_shape=(jax.ShapeDtypeStruct((plane, row...]
    pallas_call x2 -> x1, Pallas kernels: 83.9 us -> 42 us  [gather_plane(): pl.pallas_call(gather_kernel, out_shape=jax.ShapeDtypeStruct((plane, rows...]
    pallas_call x3 -> x2, Pallas kernels: 53.9 us -> 25.9 us  [exchange_plane(): pl.pallas_call(exchange_kernel, out_shape=jax.ShapeDtypeStruct(blocks.sha...]
    dot_general x6 -> x4, matrix products: 37.4 us -> 25.4 us  [dot(): lax.dot_general(left, right, ((contract[:1], contract[1:]), ((), ())), pr...]
    unnamed x76 -> x90, local copies, waits for them, and re-layouts: 16.4 us -> 23.6 us
    all_gather x1, waiting for transfers between devices: 0.02 us -> 6.49 us  [per_device(): second_weight = lax.all_gather(second_rows, 'rep', axis=0, tiled=True)]
  transfers between devices with their start and end apart: 7 -> 7, of which waited for: 0 -> 1; matrix products, arithmetic and copies ran while one was open for 13% -> 10% of each run, Pallas kernels for 75% -> 76%
where the time goes in v10:
time: 581 us; the launch traced here: 574 us
  Pallas kernels  460 us (79%)
  local copies, waits for them, and re-layouts  38.2 us (7%)
  other arithmetic  26.9 us (5%)
  matrix products  25.4 us (4%)
  between operations  15.3 us (3%)
  waiting for transfers between devices  7.31 us (1%)
    pallas_call x2, Pallas kernels, scatter_plane(): pl.pallas_call(scatter_kernel, out_shape=jax.ShapeDtypeStruct((rows, widt...  80.5 us
    pallas_call x1, Pallas kernels, ffn_first_plane(): pl.pallas_call(ffn_first_kernel, out_shape=(shape((plane, rows, width), B...  66.3 us
    pallas_call x1, Pallas kernels, spread_plane(): pl.pallas_call(spread_kernel, out_shape=(jax.ShapeDtypeStruct((plane, row...  66.1 us
    pallas_call x1, Pallas kernels, ffn_second_plane(): pl.pallas_call(ffn_second_kernel, out_shape=(shape((plane, rows, width),...  62.3 us
    pallas_call x1, Pallas kernels, attn_back_plane(): pl.pallas_call(attn_back_kernel, out_shape=(jax.ShapeDtypeStruct((tokens,...  43.4 us
    pallas_call x1, Pallas kernels, attn_front_plane(): pl.pallas_call(attn_front_kernel, out_shape=(shape((tokens, q_part + 2 *...  43.2 us
    pallas_call x1, Pallas kernels, gather_plane(): pl.pallas_call(gather_kernel, out_shape=jax.ShapeDtypeStruct((plane, rows...  42 us
    pallas_call x1, Pallas kernels, finish_plane(): pl.pallas_call(finish_kernel, out_shape=(shape(gate_weight.shape, F32), s...  29.7 us
  transfers between devices with their start and end apart: 7, of which 1 were waited for; matrix products, arithmetic and copies ran while one was open for 10% of the time, Pallas kernels for 76%

profile of v10, /device:TPU:1, one launch (start us, length us, event | category | flops | bytes accessed | tf_op | source)
XLA Modules:
  0.0 574.2 jit_solution(4592634524152814709)
XLA Ops:
  7.2 1.1 fusion.13
  8.3 1.0 fusion.16
  9.4 1.0 bitcast_bitcast_fusion
  10.5 1.0 pad_maximum_fusion.3.in_ref
  11.4 13.7 %exchange_plane.2 = bf16[8,64,768]{2,1,0:T(8,128)(2,1)} custom-call(bf16[8,64,768]{2,1,0:T(8,128)(2,1)} %pad_maximum_fusion.3.in_ref), custom_call_target="tpu_custom_call" | custom-call | bytes 15728640 | tf_op jit(solution)/shard_map/exchange_plane/pallas_call | solution.py:693
  25.5 0.7 reshape.148
  26.5 0.7 reshape.149
  27.3 0.8 slice.56
  28.1 1.9 reshape.150
  30.6 1.2 fusion.2.own_ref
  31.8 1.3 pad_maximum_fusion.2.second_ref
  33.1 1.2 pad_maximum_fusion.1.first_ref
  34.3 66.1 %spread_plane.1 = (bf16[8,256,2048]{2,1,0:T(8,128)(2,1)}, bf16[8,64,1152]{2,1,0:T(8,128)(2,1)}, bf16[8,64,960]{2,1,0:T(8,128)(2,1)}) custom-call(bf16[256,2048]{1,0:T(8,128)(2,1)} %fusion.2.own_ref, bf16[8,64,1152]{2,1,0:T(8,128)(2,1)} %pad_maximum_fusion.1.first_ref, bf16[8,64,960]{2,1,0:T(8,128)(2,1)} %pad_maximum_fusion.2.second_ref), custom_call_target="tpu_custom_call" | custom-call | bytes 134217728 | tf_op jit(solution)/shard_map/spread_plane/pallas_call | solution.py:232
  100.5 0.7 all-gather.8.cloned.1.call-update
  101.3 1.2 collective-permute-start
  102.5 1.9 fusion.15
  105.2 1.9 copy-done.1
  107.1 43.2 %attn_front_plane.1 = (bf16[2048,512]{1,0:T(8,128)(2,1)S(1)}, bf16[2048,256]{1,0:T(8,128)(2,1)S(1)}, f32[4,1,1024]{2,1,0:T(1,128)S(1)}, bf16[2048,2048]{1,0:T(8,128)(2,1)}, bf16[8,256,2048]{2,1,0:T(8,128)(2,1)}) custom-call(s32[2,2]{1,0:T(2,128)S(1)} %add_select_fusion.starts_ref, bf16[2048,2048]{1,0:T(8,128)(2,1)} %bitcast.97, ...), custom_call_target="tpu_custom_call" | custom-call | flops 2147483648 | bytes 100663296 | tf_op jit(solution)/shard_map/attn_front_plane/pallas_call | solution.py:525
  150.4 4.6 copy-done
  154.9 39.5 %scatter_plane.2 = f32[256,2048]{1,0:T(8,128)S(1)} custom-call(bf16[8,256,2048]{2,1,0:T(8,128)(2,1)S(1)} %bitcast.91), custom_call_target="tpu_custom_call" | custom-call | bytes 117440512 | tf_op jit(solution)/shard_map/scatter_plane/pallas_call | solution.py:367
  194.4 0.5 multiply_reduce_fusion.1
  195.0 1.3 copy-done.23
  196.3 1.1 multiply_convert_fusion.1.own_ref
  197.5 66.3 %ffn_first_plane.1 = (bf16[8,256,2048]{2,1,0:T(8,128)(2,1)}, bf16[8,256,2048]{2,1,0:T(8,128)(2,1)}, bf16[8,256,2048]{2,1,0:T(8,128)(2,1)}, bf16[2048,1152]{1,0:T(8,128)(2,1)}) custom-call(bf16[256,2048]{1,0:T(8,128)(2,1)} %multiply_convert_fusion.1.own_ref, bf16[8,256,2048]{2,1,0:T(8,128)(2,1)} %get-tuple-element.42.grad_ref, ...), custom_call_target="tpu_custom_call" | custom-call | flops 28991029248 | bytes 92274688 | tf_op jit(solution)/shard_map/ffn_first_plane/pallas_call | solution.py:1116
  263.9 6.5 %all-gather.8.cloned.1.call-done.weight_hbm = bf16[2048,960]{1,0:T(8,128)(2,1)} async-done(((bf16[512,960]{1,0:T(8,128)(2,1)}), bf16[2048,960]{1,0:T(8,128)(2,1)}) %all-gather.8.cloned.1.call-update) | async-done | bytes 3932176 | tf_op jit(solution)/shard_map/all_gather | solution.py:1361
  270.4 62.3 %ffn_second_plane.1 = (bf16[8,256,2048]{2,1,0:T(8,128)(2,1)}, bf16[2048,960]{1,0:T(8,128)(2,1)}, f32[256,2048]{1,0:T(8,128)}) custom-call(bf16[8,256,2048]{2,1,0:T(8,128)(2,1)} %get-tuple-element.44.all_ref, bf16[8,256,2048]{2,1,0:T(8,128)(2,1)} %get-tuple-element.42.grad_ref, bf16[2048,960]{1,0:T(8,128)(2,1)} %all-gather.8.cloned.1.call-done.weight_hbm, ...), custom_call_target="tpu_custom_call" | custom-call | flops 24159191040 | bytes 92274688 | tf_op jit(solution)/shard_map/ffn_second_plane/pallas_call | solution.py:1160
  332.8 1.5 copy-done.24
  334.3 2.1 multiply_reduce_fusion
  336.7 1.6 multiply_convert_fusion.refs_0_
  338.4 42.0 %gather_plane.1 = bf16[8,256,2048]{2,1,0:T(8,128)(2,1)} custom-call(bf16[256,2048]{1,0:T(8,128)(2,1)} %multiply_convert_fusion.refs_0_), custom_call_target="tpu_custom_call" | custom-call | bytes 100663296 | tf_op jit(solution)/shard_map/gather_plane/pallas_call | solution.py:170
  380.4 7.1 %convolution_convert_fusion.2 = bf16[2048,256]{0,1:T(8,128)(2,1)} fusion(bf16[2048,2048]{1,0:T(8,128)(2,1)} %bitcast.95, bf16[2048,256]{1,0:T(8,128)(2,1)} %copy-done.21), kind=kOutput, calls=%fused_computation.11 | convolution fusion | flops 2148007936 | bytes 10485760 | tf_op jit(solution)/shard_map/dot_general | solution.py:32
  387.5 3.3 convolution_convert_fusion.3.g_ref
  390.8 1.0 copy-done.8
  391.9 1.0 copy-done.10
  392.9 1.2 copy-done.22
  394.1 43.4 %attn_back_plane.1 = (bf16[2048,512]{1,0:T(8,128)(2,1)}, f32[256,2048]{1,0:T(8,128)}) custom-call(s32[2,2]{1,0:T(2,128)S(1)} %add_select_fusion.starts_ref, bf16[2048,512]{1,0:T(8,128)(2,1)} %copy-done.20, bf16[2048,256]{1,0:T(8,128)(2,1)S(1)} %copy-done.22, f32[4,1,1024]{2,1,0:T(1,128)S(1)} %get-tuple-element.51.log_ref, f32[1024,128]{1,0:T(8,128)S(1)} %copy-done.8, ...), custom_call_target="tpu_custom_call" | custom-call | flops 5368709120 | bytes 117440512 | tf_op jit(solution)/shard_map/attn_back_plane/pallas_call | solution.py:640
  437.6 8.7 %convolution_convert_fusion.1 = bf16[2048,512]{0,1:T(8,128)(2,1)S(1)} fusion(bf16[2048,2048]{1,0:T(8,128)(2,1)} %bitcast.98, bf16[2048,512]{1,0:T(8,128)(2,1)} %get-tuple-element.54), kind=kOutput, calls=%fused_computation.5 | convolution fusion | flops 4296015872 | bytes 12582912 | tf_op jit(solution)/shard_map/dot_general | solution.py:32
  446.3 1.9 pad_maximum_fusion
  448.2 0.7 copy.59.gain_ref
  448.9 6.4 %convolution_convert_fusion = bf16[2048,2048]{1,0:T(8,128)(2,1)S(1)} fusion(bf16[2048,512]{1,0:T(8,128)(2,1)} %get-tuple-element.54, bf16[2048,768]{1,0:T(8,128)(2,1)S(1)} %copy-done.2), kind=kOutput, calls=%fused_computation | convolution fusion | flops 4299161600 | bytes 12582912 | tf_op jit(solution)/shard_map/dot_general | solution.py:32
  455.3 41.0 %scatter_plane.3 = f32[256,2048]{1,0:T(8,128)S(1)} custom-call(bf16[8,256,2048]{2,1,0:T(8,128)(2,1)S(1)} %bitcast.92), custom_call_target="tpu_custom_call" | custom-call | bytes 117440512 | tf_op jit(solution)/shard_map/scatter_plane/pallas_call | solution.py:367
  496.4 1.3 copy-done.15
  497.6 1.3 copy-done.16
  498.9 0.8 copy-done.17
  499.7 29.7 %finish_plane.1 = (f32[64,5632]{1,0:T(8,128)S(1)}, f32[64,5632]{1,0:T(8,128)S(1)}, bf16[8,64,384]{2,1,0:T(8,128)(2,1)S(1)}, bf16[8,64,320]{2,1,0:T(8,128)(2,1)S(1)}, f32[64,1]{1,0:T(8,128)S(1)}) custom-call(bf16[8,64,1152]{2,1,0:T(8,128)(2,1)S(1)} %bitcast.93, bf16[8,64,960]{2,1,0:T(8,128)(2,1)S(1)} %bitcast.94, bf16[64,5632]{1,0:T(8,128)(2,1)S(1)} %copy-done.4, ...), custom_call_target="tpu_custom_call" | custom-call | bytes 43253760 | tf_op jit(solution)/shard_map/finish_plane/pallas_call | solution.py:1256
  529.4 1.1 copy-done.11
  530.6 1.1 copy-done.13
  531.8 0.5 copy-done.18
  532.3 2.1 copy.65
  534.3 2.9 reshape.167
  537.2 0.6 reduce
  537.8 0.4 fusion.4
  538.3 1.2 copy-done.25
  539.7 5.0 fusion.8
  544.7 2.3 copy.60
  547.0 12.2 %exchange_plane.3 = bf16[8,64,768]{2,1,0:T(8,128)(2,1)} custom-call(bf16[8,64,768]{2,1,0:T(8,128)(2,1)} %bitcast.106), custom_call_target="tpu_custom_call" | custom-call | bytes 15728640 | tf_op jit(solution)/shard_map/exchange_plane/pallas_call | solution.py:693
  559.2 1.3 convert_element_type.122
  560.7 0.7 copy-done.35
  561.4 1.0 broadcast_multiply_fusion
  562.4 0.8 copy.71
  563.3 0.9 bitcast_multiply_fusion
  564.2 0.5 add_add_fusion
  564.7 1.1 copy.86
  565.8 1.1 copy.87
  (119 shorter events, 3.4 us)
Async XLA Ops:
  7.2 98.0 %all-gather.4.cloned.1.call-start = ((), (), s32[]{:S(2)}) async-start(), calls=%async_computation.3 | async-start | bytes 3932160 | tf_op jit(solution)/shard_map/all_gather | solution.py:1335
  10.4 14.8 %copy-start.3 = (bf16[64,5632]{1,0:T(8,128)(2,1)S(1)}, bf16[64,5632]{1,0:T(8,128)(2,1)}, u32[]{:S(2)}) copy-start(bf16[64,5632]{1,0:T(8,128)(2,1)} %gate_weight.1) | copy-start | bytes 2162692
  10.4 14.8 %copy-start.5 = (bf16[64,5632]{1,0:T(8,128)(2,1)S(1)}, bf16[64,5632]{1,0:T(8,128)(2,1)}, u32[]{:S(2)}) copy-start(bf16[64,5632]{1,0:T(8,128)(2,1)} %up_weight.1) | copy-start | bytes 2162692
  10.4 14.8 %copy-start.40 = (f32[64]{0:T(128)S(1)}, f32[64]{0:T(128)}, u32[]{:S(2)}) copy-start(f32[64]{0:T(128)} %param.21) | copy-start | bytes 772
  25.1 172.3 %all-gather.6.cloned.1.call-start = ((), (), s32[]{:S(2)}) async-start(), calls=%async_computation.4 | async-start | bytes 5898240 | tf_op jit(solution)/shard_map/all_gather | solution.py:1360
  28.1 2.2 copy-start.26
  30.2 1.6 copy-start.34
  34.3 67.0 %copy-start.42 = (s32[1,2]{1,0:T(1,128)S(1)}, s32[1,2]{1,0:T(1,128)}, u32[]{:S(2)}) copy-start(s32[1,2]{1,0:T(1,128)} %param.14) | copy-start | bytes 28
  100.5 169.9 %all-gather.8.cloned.1.call-start = ((), (), s32[]{:S(2)}) async-start(), calls=%async_computation.5 | async-start | bytes 5242880 | tf_op jit(solution)/shard_map/all_gather | solution.py:1361
  101.2 289.6 %reduce-scatter.4.cloned.1.call-start = ((), (), s32[]{:S(2)}) async-start(), calls=%async_computation.6 | async-start | bytes 5898240 | tf_op jit(solution)/shard_map/reduce_scatter | solution.py:1385
  101.3 3.8 collective-permute-start
  102.5 2.3 copy-start.41
  102.5 2.3 copy-start.30
  104.8 45.5 %copy-start.7 = (f32[1024,128]{1,0:T(8,128)}, f32[1024,128]{1,0:T(8,128)S(1)}, u32[]{:S(2)}) copy-start(f32[1024,128]{1,0:T(8,128)S(1)} %get-tuple-element.90.cos_ref) | copy-start | bytes 1572868
  104.8 45.5 %copy-start.9 = (f32[1024,128]{1,0:T(8,128)}, f32[1024,128]{1,0:T(8,128)S(1)}, u32[]{:S(2)}) copy-start(f32[1024,128]{1,0:T(8,128)S(1)} %get-tuple-element.91.sin_ref) | copy-start | bytes 1572868
  105.1 1.9 copy-start.1
  150.3 44.1 %copy-start.20 = (bf16[2048,512]{1,0:T(8,128)(2,1)}, bf16[2048,512]{1,0:T(8,128)(2,1)S(1)}, u32[]{:S(2)}) copy-start(bf16[2048,512]{1,0:T(8,128)(2,1)S(1)} %get-tuple-element.41.qkv_ref) | copy-start | bytes 6291460
  150.3 44.6 %copy-start.21 = (bf16[2048,256]{1,0:T(8,128)(2,1)}, bf16[2048,256]{1,0:T(8,128)(2,1)S(1)}, u32[]{:S(2)}) copy-start(bf16[2048,256]{1,0:T(8,128)(2,1)S(1)} %get-tuple-element.55) | copy-start | bytes 3145732
  150.3 4.6 copy-start
  154.9 39.5 %copy-start.27 = (bf16[1,256,2048]{2,1,0:T(8,128)(2,1)S(1)}, bf16[1,256,2048]{2,1,0:T(8,128)(2,1)}, u32[]{:S(2)}) copy-start(bf16[1,256,2048]{2,1,0:T(8,128)(2,1)} %param.13) | copy-start | bytes 3145732
  194.9 1.4 copy-start.23
  263.8 232.5 %reduce-scatter.8.cloned.1.call-start = ((), (), s32[]{:S(2)}) async-start(), calls=%async_computation.8 | async-start | bytes 5242880 | tf_op jit(solution)/shard_map/reduce_scatter | solution.py:1389
  332.7 1.6 copy-start.24
  332.7 212.0 %reduce-scatter.6.cloned.1.call-start = ((), (), s32[]{:S(2)}) async-start(), calls=%async_computation.7 | async-start | bytes 3932160 | tf_op jit(solution)/shard_map/reduce_scatter | solution.py:1410
  334.3 2.2 copy-start.29
  334.3 2.5 copy-start.31
  380.4 7.1 %copy-start.2 = (bf16[2048,768]{1,0:T(8,128)(2,1)S(1)}, bf16[2048,768]{1,0:T(8,128)(2,1)}, u32[]{:S(2)}) copy-start(bf16[2048,768]{1,0:T(8,128)(2,1)} %all-gather.4.cloned.1.call-done.weight_hbm) | copy-start | bytes 9437188
  380.4 7.1 %copy-start.33 = (bf16[8,256,2048]{2,1,0:T(8,128)(2,1)S(1)}, bf16[8,256,2048]{2,1,0:T(8,128)(2,1)}, u32[]{:S(2)}) copy-start(bf16[8,256,2048]{2,1,0:T(8,128)(2,1)} %gather_plane.1) | copy-start | bytes 25165828
  390.8 1.0 copy-start.8
  391.9 1.0 copy-start.10
  392.9 1.2 copy-start.22
  437.6 8.7 %copy-start.36 = (bf16[2048,256]{0,1:T(8,128)(2,1)S(1)}, bf16[2048,256]{0,1:T(8,128)(2,1)}, u32[]{:S(2)}) copy-start(bf16[2048,256]{0,1:T(8,128)(2,1)} %convolution_convert_fusion.2) | copy-start | bytes 3145732
  455.3 41.1 %copy-start.4 = (bf16[64,5632]{1,0:T(8,128)(2,1)S(1)}, bf16[64,5632]{1,0:T(8,128)(2,1)}, u32[]{:S(2)}) copy-start(bf16[64,5632]{1,0:T(8,128)(2,1)} %gate_weight.1) | copy-start | bytes 2162692
  455.3 41.1 %copy-start.6 = (bf16[64,5632]{1,0:T(8,128)(2,1)S(1)}, bf16[64,5632]{1,0:T(8,128)(2,1)}, u32[]{:S(2)}) copy-start(bf16[64,5632]{1,0:T(8,128)(2,1)} %up_weight.1) | copy-start | bytes 2162692
  496.4 1.3 copy-start.15
  497.6 1.3 copy-start.16
  498.9 0.8 copy-start.17
  529.4 1.1 copy-start.11
  530.6 1.1 copy-start.13
  531.7 0.6 copy-start.18
  534.3 2.9 copy-start.19
  534.3 3.5 copy-start.28
  537.8 1.6 copy-start.25
  537.8 1.9 copy-start.32
  560.5 1.0 copy-start.35
  560.5 0.9 copy-start.39
  560.6 2.7 copy-start.37
  560.6 2.7 copy-start.38
  560.6 4.1 copy-start.14
  562.4 3.4 copy-start.12
Sparse Core Ops, SparseCore 0:
  25.3 63.8 all-gather.3
  100.6 89.0 all-gather.5
  191.2 79.0 all-gather.7
  272.5 83.8 reduce-scatter.3
  358.5 77.0 reduce-scatter.7
  448.3 58.3 reduce-scatter.5

commit v11 on v10

--- a/solution.py
+++ b/solution.py
@@ -183,7 +183,7 @@
 
 
 def spread_kernel(
-    own_ref, first_ref, second_ref, all_ref, first_out, second_out, first_own, second_own, copies, *gather
+    own_ref, move_ref, all_ref, move_out, kept, copies, *gather
 ):
     begin, first, second, finish = gather_stages(own_ref, all_ref, *gather)
     tp_at, seq_at, _, _, _ = plane_place()
@@ -194,36 +194,26 @@
     devices = [at_device(peer // seq, lax.rem(peer, seq)) for peer in peers]
     sends, recvs, local = copies.at[0], copies.at[1], copies.at[2]
     begin(devices)
-    moves, keeps = [], []
-    for n, (ref, out, kept) in enumerate(
-        ((first_ref, first_out, first_own), (second_ref, second_out, second_own))
-    ):
-        for k, (peer, device) in enumerate(zip(peers, devices)):
-            i = n * (plane - 1) + k
-            moves.append(remote(ref.at[peer], out.at[me], sends.at[i], recvs.at[i], device))
-        keeps.append(
-            (
-                pltpu.make_async_copy(ref.at[me], kept, local.at[2 * n]),
-                pltpu.make_async_copy(kept, out.at[me], local.at[2 * n + 1]),
-            )
-        )
+    moves = [
+        remote(move_ref.at[peer], move_out.at[me], sends.at[k], recvs.at[k], device)
+        for k, (peer, device) in enumerate(zip(peers, devices))
+    ]
     for move in moves:
         move.start()
-    for take, put in keeps:
-        take.start()
-    for take, put in keeps:
-        take.wait()
-        put.start()
+    take = pltpu.make_async_copy(move_ref.at[me], kept, local.at[0])
+    put = pltpu.make_async_copy(kept, move_out.at[me], local.at[1])
+    take.start()
+    take.wait()
+    put.start()
     first()
     second()
     for move in moves:
         move.wait()
-    for take, put in keeps:
-        put.wait()
+    put.wait()
     finish()
 
 
-def spread_plane(block, first, second, ident):
+def spread_plane(block, blocks, ident):
     rows, width = block.shape
     plane = lax.axis_size("tp") * lax.axis_size("seq")
     hbm = pl.BlockSpec(memory_space=pltpu.HBM)
@@ -233,21 +223,19 @@
         spread_kernel,
         out_shape=(
             jax.ShapeDtypeStruct((plane, rows, width), block.dtype),
-            jax.ShapeDtypeStruct(first.shape, first.dtype),
-            jax.ShapeDtypeStruct(second.shape, second.dtype),
-        ),
-        in_specs=[vmem, hbm, hbm],
-        out_specs=(hbm, hbm, hbm),
+            jax.ShapeDtypeStruct(blocks.shape, blocks.dtype),
+        ),
+        in_specs=[vmem, hbm],
+        out_specs=(hbm, hbm),
         scratch_shapes=[
-            pltpu.VMEM(first.shape[1:], first.dtype),
-            pltpu.VMEM(second.shape[1:], second.dtype),
-            pltpu.SemaphoreType.DMA((3, 2 * plane)),
+            pltpu.VMEM(blocks.shape[1:], blocks.dtype),
+            pltpu.SemaphoreType.DMA((3, plane)),
             *GATHER_SCRATCH,
         ],
         cost_estimate=pl.CostEstimate(flops=0, transcendentals=0, bytes_accessed=size * 16),
         compiler_params=pltpu.CompilerParams(collective_id=ident, has_side_effects=True),
         name="spread_plane",
-    )(block, first, second)
+    )(block, blocks)
 
 
 def add_rows(target, sources, start, count, kind):
@@ -374,7 +362,7 @@
             flops=0, transcendentals=0, bytes_accessed=plane * size * 14
         ),
         compiler_params=pltpu.CompilerParams(
-            collective_id=ident, has_side_effects=True, vmem_limit_bytes=32 << 20
+            collective_id=ident, has_side_effects=True, vmem_limit_bytes=60 << 20
         ),
         name="scatter_plane",
     )(partial.reshape(plane, rows, width))
@@ -1199,16 +1187,27 @@
 def finish_kernel(
     first_ref,
     second_ref,
+    attn_ref,
     gate_weight,
     up_weight,
-    gain_ref,
+    query_weight,
+    key_weight,
+    value_weight,
+    gain2_ref,
+    gain1_ref,
     gate_out,
     up_out,
     down_first,
     down_second,
-    gain_out,
+    gain2_out,
+    query_out,
+    key_out,
+    value_out,
+    out_out,
+    gain1_out,
     first_in,
     second_in,
+    attn_in,
     local,
     sends,
     recvs,
@@ -1220,63 +1219,99 @@
     peers = [lax.rem(me + k, plane) for k in range(1, plane)]
     devices = [at_device(peer // seq, lax.rem(peer, seq)) for peer in peers]
     enter(devices)
-    copies = []
-    for k, (peer, device) in enumerate(zip(peers, devices)):
-        i = plane - 1 + k
-        copies.append(remote(first_ref.at[peer], first_in.at[me], sends.at[k], recvs.at[k], device))
-        copies.append(remote(second_ref.at[peer], second_in.at[me], sends.at[i], recvs.at[i], device))
-    copies.append(pltpu.make_async_copy(first_ref.at[me], first_in.at[me], local.at[0]))
-    copies.append(pltpu.make_async_copy(second_ref.at[me], second_in.at[me], local.at[1]))
-    for copy in copies:
-        copy.start()
-    for copy in copies:
-        copy.wait()
-    gain = gain_ref[...]
+    groups = []
+    for n, (ref, into) in enumerate(
+        ((first_ref, first_in), (second_ref, second_in), (attn_ref, attn_in))
+    ):
+        copies = [pltpu.make_async_copy(ref.at[me], into.at[me], local.at[n])]
+        for k, (peer, device) in enumerate(zip(peers, devices)):
+            i = n * (plane - 1) + k
+            copies.append(remote(ref.at[peer], into.at[me], sends.at[i], recvs.at[i], device))
+        for copy in copies:
+            copy.start()
+        groups.append(copies)
+
+    def arrive(n):
+        for copy in groups[n]:
+            copy.wait()
+
+    gain = gain2_ref[...]
     sizes = [ref.shape[2] // 3 for ref in (first_in, second_in)]
     total = jnp.zeros(gain.shape, F32)
-    for j in range(plane):
-        start = j * sum(sizes)
-        for ref, down, size in ((first_in, down_first, sizes[0]), (second_in, down_second, sizes[1])):
+    for n, (ref, down) in enumerate(((first_in, down_first), (second_in, down_second))):
+        arrive(n)
+        size = sizes[n]
+        for j in range(plane):
+            start = j * sum(sizes) + n * sizes[0]
             at = slice(start, start + size)
-            start += size
             for k, (out, weight) in enumerate(((gate_out, gate_weight), (up_out, up_weight))):
                 own = ref[j, :, k * size : (k + 1) * size].astype(F32)
                 out[:, at] = own * gain
                 total = total + jnp.sum(own * weight[:, at].astype(F32), axis=1, keepdims=True)
             down[j] = ref[j, :, 2 * size :]
-    gain_out[...] = total
-
-
-def finish_plane(first, second, gate_weight, up_weight, gain, ident):
+    gain2_out[...] = total
+
+    arrive(2)
+    gain = gain1_ref[...]
+    q_part = query_out.shape[1] // plane
+    share = plane // KV
+    total = jnp.zeros(gain.shape, F32)
+    for j in range(plane):
+        at = slice(j * q_part, (j + 1) * q_part)
+        own = attn_in[j, :, :q_part].astype(F32)
+        query_out[:, at] = own * gain
+        total = total + jnp.sum(own * query_weight[:, at].astype(F32), axis=1, keepdims=True)
+        out_out[:, at] = attn_in[j, :, q_part + 2 * DH :].astype(F32)
+    for j in range(KV):
+        at = slice(j * DH, (j + 1) * DH)
+        for k, (out, weight) in enumerate(((key_out, key_weight), (value_out, value_weight))):
+            cols = slice(q_part + k * DH, q_part + (k + 1) * DH)
+            own = attn_in[j * share, :, cols].astype(F32)
+            for i in range(1, share):
+                own = own + attn_in[j * share + i, :, cols].astype(F32)
+            out[:, at] = own * gain
+            total = total + jnp.sum(own * weight[:, at].astype(F32), axis=1, keepdims=True)
+    gain1_out[...] = total
+
+
+def finish_plane(first, second, attn, weights, gain2, gain1, ident):
     plane, rows, _ = first.shape
     shape = jax.ShapeDtypeStruct
     hbm = pl.BlockSpec(memory_space=pltpu.HBM)
     vmem = pl.BlockSpec(memory_space=pltpu.VMEM)
-    size = plane * rows * gate_weight.shape[1] * 6 // plane
+    gate, up, query, key, value = (shape(w.shape, F32) for w in weights)
+    column = shape((rows, 1), F32)
+    size = (first.size + second.size + attn.size) * 2
     return pl.pallas_call(
         finish_kernel,
         out_shape=(
-            shape(gate_weight.shape, F32),
-            shape(up_weight.shape, F32),
+            gate,
+            up,
             shape((plane, rows, first.shape[2] // 3), BF),
             shape((plane, rows, second.shape[2] // 3), BF),
-            shape((rows, 1), F32),
-        ),
-        in_specs=[hbm, hbm, vmem, vmem, vmem],
-        out_specs=(vmem,) * 5,
+            column,
+            query,
+            key,
+            value,
+            query,
+            column,
+        ),
+        in_specs=[hbm] * 3 + [vmem] * 7,
+        out_specs=(vmem,) * 10,
         scratch_shapes=[
             pltpu.VMEM(first.shape, BF),
             pltpu.VMEM(second.shape, BF),
-            pltpu.SemaphoreType.DMA((2,)),
-            pltpu.SemaphoreType.DMA((2 * plane - 2,)),
-            pltpu.SemaphoreType.DMA((2 * plane - 2,)),
+            pltpu.VMEM(attn.shape, BF),
+            pltpu.SemaphoreType.DMA((3,)),
+            pltpu.SemaphoreType.DMA((3 * plane - 3,)),
+            pltpu.SemaphoreType.DMA((3 * plane - 3,)),
         ],
         cost_estimate=pl.CostEstimate(flops=0, transcendentals=0, bytes_accessed=size * 20),
         compiler_params=pltpu.CompilerParams(
-            collective_id=ident, has_side_effects=True, vmem_limit_bytes=24 << 20
+            collective_id=ident, has_side_effects=True, vmem_limit_bytes=32 << 20
         ),
         name="finish_plane",
-    )(first, second, gate_weight, up_weight, gain)
+    )(first, second, attn, *weights, gain2, gain1)
 
 
 def columns(matrix, parts):
@@ -1352,9 +1387,8 @@
     first_pack, second_pack = (
         jnp.concatenate([m[:, :, a:b] for m in ffn_parts], axis=2) for a, b in split
     )
-    norm1_all, first_rows, second_rows = spread_plane(
-        after(norm1.astype(BF), attn_rows), first_pack, second_pack, 1
-    )
+    first_rows = exchange_plane(after(first_pack, attn_rows), 2)
+    norm1_all, second_rows = spread_plane(after(norm1.astype(BF), first_rows), second_pack, 1)
     first_rows = first_rows.reshape(-1, first_rows.shape[2])
     second_rows = second_rows.reshape(-1, second_rows.shape[2])
     first_weight = lax.all_gather(first_rows, "rep", axis=0, tiled=True)
@@ -1408,45 +1442,33 @@
     )
     scaled1_partial = nt(qkv_grad, qkv_weight).astype(BF)
     attn_sums = lax.psum_scatter(attn_partial, "rep", scatter_dimension=0, tiled=True)
-    scaled1 = scatter_plane(after(scaled1_partial, attn_partial), 8)
+    scaled1 = scatter_plane(after(scaled1_partial, attn_partial, second_sums), 8)
     input_grad = hidden_grad + scale1 * (
         scaled1 - norm1 * jnp.mean(scaled1 * norm1, axis=-1, keepdims=True)
     )
     out_hidden = (hidden + keep * ffn_out).astype(BF)
 
-    gate_grad, up_grad, down_first, down_second, gain_ffn_grad = finish_plane(
-        after(first_sums.reshape(plane, -1, first_sums.shape[1]), scaled1),
+    gate_grad, up_grad, down_first, down_second, gain2_grad, *attn_grads = finish_plane(
+        after(first_sums, input_grad, out_hidden).reshape(plane, -1, first_sums.shape[1]),
         second_sums.reshape(plane, -1, second_sums.shape[1]),
-        w_gate,
-        w_up,
+        attn_sums.reshape(plane, -1, attn_sums.shape[1]),
+        (w_gate, w_up, w_query, w_key, w_value),
         gain2,
+        gain1,
         10,
     )
+    query_grad, key_grad, value_grad, out_grad, gain1_grad = attn_grads
     down_own = jnp.concatenate([down_first, down_second], axis=2)
     down_grad = jnp.transpose(down_own, (0, 2, 1)).reshape(plane * ff_part, -1).astype(F32)
-
-    attn_sums = after(attn_sums, gain_ffn_grad)
-    attn_own = exchange_plane(attn_sums.reshape(plane, -1, attn_sums.shape[1]), 11).astype(F32)
-    query_own = uncolumns(attn_own[:, :, :q_part])
-    kv_own = attn_own[:, :, q_part : q_part + 2 * DH]
-    kv_own = jnp.sum(kv_own.reshape(KV, share, -1, 2 * DH), axis=1)
-    key_own = uncolumns(kv_own[:, :, :DH])
-    value_own = uncolumns(kv_own[:, :, DH:])
-    out_own = uncolumns(attn_own[:, :, q_part + 2 * DH :])
-    gain_attn_grad = (
-        jnp.sum(query_own * wq32, axis=1)
-        + jnp.sum(key_own * wk32, axis=1)
-        + jnp.sum(value_own * wv32, axis=1)
-    )
     return (
         out_hidden[None],
         input_grad[None],
-        gain_attn_grad,
-        query_own * gain1,
-        key_own * gain1,
-        value_own * gain1,
-        out_own.T,
-        gain_ffn_grad[:, 0],
+        gain1_grad[:, 0],
+        query_grad,
+        key_grad,
+        value_grad,
+        out_grad.T,
+        gain2_grad[:, 0],
         gate_grad,
         up_grad,
         down_grad,

time: 581 us -> 580 us (level)
  waiting for transfers between devices: 7.31 us -> 0.23 us
    pallas_call x1, Pallas kernels: 66.1 us -> 53.2 us  [spread_plane(): pl.pallas_call(spread_kernel, out_shape=(jax.ShapeDtypeStruct((plane, row...]
    pallas_call x1, Pallas kernels: 29.7 us -> 37.5 us  [finish_plane(): pl.pallas_call(finish_kernel, out_shape=(gate, up, shape((plane, rows, fi...]
    all_gather x1, waiting for transfers between devices: 6.49 us -> 0.02 us  [per_device(): second_weight = lax.all_gather(second_rows, 'rep', axis=0, tiled=True)]
    unnamed x90 -> x114, local copies, waits for them, and re-layouts: 23.6 us -> 24.5 us
  transfers between devices with their start and end apart: 7 -> 7, of which waited for: 1 -> 1; matrix products, arithmetic and copies ran while one was open for 10% -> 10% of each run, Pallas kernels for 76% -> 72%
where the time goes in v11:
time: 580 us; the launch traced here: 573 us
  Pallas kernels  462 us (80%)
  local copies, waits for them, and re-layouts  37.7 us (7%)
  other arithmetic  29 us (5%)
  matrix products  27.6 us (5%)
  between operations  15.2 us (3%)
    pallas_call x2, Pallas kernels, scatter_plane(): pl.pallas_call(scatter_kernel, out_shape=jax.ShapeDtypeStruct((rows, widt...  83.7 us
    pallas_call x1, Pallas kernels, ffn_first_plane(): pl.pallas_call(ffn_first_kernel, out_shape=(shape((plane, rows, width), B...  66.1 us
    pallas_call x1, Pallas kernels, ffn_second_plane(): pl.pallas_call(ffn_second_kernel, out_shape=(shape((plane, rows, width),...  62 us
    pallas_call x1, Pallas kernels, spread_plane(): pl.pallas_call(spread_kernel, out_shape=(jax.ShapeDtypeStruct((plane, row...  53.2 us
    pallas_call x1, Pallas kernels, attn_back_plane(): pl.pallas_call(attn_back_kernel, out_shape=(jax.ShapeDtypeStruct((tokens,...  43.3 us
    pallas_call x1, Pallas kernels, attn_front_plane(): pl.pallas_call(attn_front_kernel, out_shape=(shape((tokens, q_part + 2 *...  43.2 us
    pallas_call x1, Pallas kernels, gather_plane(): pl.pallas_call(gather_kernel, out_shape=jax.ShapeDtypeStruct((plane, rows...  42.3 us
    pallas_call x1, Pallas kernels, finish_plane(): pl.pallas_call(finish_kernel, out_shape=(gate, up, shape((plane, rows, fi...  37.5 us
  transfers between devices with their start and end apart: 7, of which 1 were waited for; matrix products, arithmetic and copies ran while one was open for 10% of the time, Pallas kernels for 72%

profile of v11, /device:TPU:1, one launch (start us, length us, event | category | flops | bytes accessed | tf_op | source)
XLA Modules:
  0.0 572.9 jit_solution(10520118474496814384)
XLA Ops:
  7.2 1.1 multiply_convert_fusion.4
  8.3 1.0 multiply_convert_fusion.6
  9.4 1.0 bitcast_bitcast_fusion
  10.5 1.0 pad_maximum_fusion.3.in_ref
  11.4 13.7 %exchange_plane.2 = bf16[8,64,768]{2,1,0:T(8,128)(2,1)} custom-call(bf16[8,64,768]{2,1,0:T(8,128)(2,1)} %pad_maximum_fusion.3.in_ref), custom_call_target="tpu_custom_call" | custom-call | bytes 15728640 | tf_op jit(solution)/shard_map/exchange_plane/pallas_call | solution.py:681
  25.5 0.7 reshape.126
  26.4 0.8 slice.32
  27.1 0.7 reshape.127
  28.0 0.8 slice.33
  28.8 0.7 reshape.128
  29.6 0.8 copy-done.47
  30.4 2.2 pad_maximum_fusion.1.in_ref
  32.6 16.7 %exchange_plane.3 = bf16[8,64,1152]{2,1,0:T(8,128)(2,1)} custom-call(bf16[8,64,1152]{2,1,0:T(8,128)(2,1)} %pad_maximum_fusion.1.in_ref), custom_call_target="tpu_custom_call" | custom-call | bytes 23592960 | tf_op jit(solution)/shard_map/exchange_plane/pallas_call | solution.py:681
  49.5 1.0 copy-done.39
  50.8 1.2 fusion.2.own_ref
  52.0 1.3 pad_maximum_fusion.2.move_ref
  53.3 53.2 %spread_plane.1 = (bf16[8,256,2048]{2,1,0:T(8,128)(2,1)}, bf16[8,64,960]{2,1,0:T(8,128)(2,1)}) custom-call(bf16[256,2048]{1,0:T(8,128)(2,1)} %fusion.2.own_ref, bf16[8,64,960]{2,1,0:T(8,128)(2,1)} %pad_maximum_fusion.2.move_ref), custom_call_target="tpu_custom_call" | custom-call | bytes 134217728 | tf_op jit(solution)/shard_map/spread_plane/pallas_call | solution.py:222
  106.6 1.2 collective-permute-start
  107.9 1.9 fusion.11
  110.5 1.9 copy-done
  112.5 43.2 %attn_front_plane.1 = (bf16[2048,512]{1,0:T(8,128)(2,1)S(1)}, bf16[2048,256]{1,0:T(8,128)(2,1)S(1)}, f32[4,1,1024]{2,1,0:T(1,128)S(1)}, bf16[2048,2048]{1,0:T(8,128)(2,1)}, bf16[8,256,2048]{2,1,0:T(8,128)(2,1)}) custom-call(s32[2,2]{1,0:T(2,128)S(1)} %add_select_fusion.starts_ref, bf16[2048,2048]{1,0:T(8,128)(2,1)} %bitcast.75, ...), custom_call_target="tpu_custom_call" | custom-call | flops 2147483648 | bytes 100663296 | tf_op jit(solution)/shard_map/attn_front_plane/pallas_call | solution.py:513
  155.7 1.3 copy-done.33
  157.0 41.2 %scatter_plane.2 = f32[256,2048]{1,0:T(8,128)} custom-call(bf16[8,256,2048]{2,1,0:T(8,128)(2,1)} %bitcast.71), custom_call_target="tpu_custom_call" | custom-call | bytes 117440512 | tf_op jit(solution)/shard_map/scatter_plane/pallas_call | solution.py:355
  198.2 2.1 multiply_reduce_fusion.1
  200.3 1.3 copy-done.36
  201.6 1.1 multiply_convert_fusion.1.own_ref
  202.8 66.1 %ffn_first_plane.1 = (bf16[8,256,2048]{2,1,0:T(8,128)(2,1)}, bf16[8,256,2048]{2,1,0:T(8,128)(2,1)}, bf16[8,256,2048]{2,1,0:T(8,128)(2,1)}, bf16[2048,1152]{1,0:T(8,128)(2,1)}) custom-call(bf16[256,2048]{1,0:T(8,128)(2,1)} %multiply_convert_fusion.1.own_ref, bf16[8,256,2048]{2,1,0:T(8,128)(2,1)} %get-tuple-element.47.grad_ref, ...), custom_call_target="tpu_custom_call" | custom-call | flops 28991029248 | bytes 92274688 | tf_op jit(solution)/shard_map/ffn_first_plane/pallas_call | solution.py:1104
  269.0 62.0 %ffn_second_plane.1 = (bf16[8,256,2048]{2,1,0:T(8,128)(2,1)}, bf16[2048,960]{1,0:T(8,128)(2,1)}, f32[256,2048]{1,0:T(8,128)}) custom-call(bf16[8,256,2048]{2,1,0:T(8,128)(2,1)} %get-tuple-element.48.all_ref, bf16[8,256,2048]{2,1,0:T(8,128)(2,1)} %get-tuple-element.47.grad_ref, bf16[2048,960]{1,0:T(8,128)(2,1)} %all-gather.8.cloned.1.call-done.weight_hbm, ...), custom_call_target="tpu_custom_call" | custom-call | flops 24159191040 | bytes 92274688 | tf_op jit(solution)/shard_map/ffn_second_plane/pallas_call | solution.py:1148
  331.1 1.5 copy-done.37
  332.6 2.1 multiply_reduce_fusion
  335.1 1.6 multiply_convert_fusion.refs_0_
  336.7 42.3 %gather_plane.1 = bf16[8,256,2048]{2,1,0:T(8,128)(2,1)} custom-call(bf16[256,2048]{1,0:T(8,128)(2,1)} %multiply_convert_fusion.refs_0_), custom_call_target="tpu_custom_call" | custom-call | bytes 100663296 | tf_op jit(solution)/shard_map/gather_plane/pallas_call | solution.py:170
  379.0 7.1 %convolution_convert_fusion.2 = bf16[2048,256]{0,1:T(8,128)(2,1)} fusion(bf16[2048,2048]{1,0:T(8,128)(2,1)} %bitcast.73, bf16[2048,256]{1,0:T(8,128)(2,1)} %copy-done.34), kind=kOutput, calls=%fused_computation.11 | convolution fusion | flops 2148007936 | bytes 10485760 | tf_op jit(solution)/shard_map/dot_general | solution.py:32
  386.1 3.3 convolution_convert_fusion.3.g_ref
  389.5 1.0 copy-done.7
  390.5 1.0 copy-done.9
  391.5 1.3 copy-done.35
  392.8 43.3 %attn_back_plane.1 = (bf16[2048,512]{1,0:T(8,128)(2,1)}, f32[256,2048]{1,0:T(8,128)}) custom-call(s32[2,2]{1,0:T(2,128)S(1)} %add_select_fusion.starts_ref, bf16[2048,512]{1,0:T(8,128)(2,1)} %copy-done.33, bf16[2048,256]{1,0:T(8,128)(2,1)S(1)} %copy-done.35, f32[4,1,1024]{2,1,0:T(1,128)S(1)} %get-tuple-element.55.log_ref, f32[1024,128]{1,0:T(8,128)S(1)} %copy-done.7, ...), custom_call_target="tpu_custom_call" | custom-call | flops 5368709120 | bytes 117440512 | tf_op jit(solution)/shard_map/attn_back_plane/pallas_call | solution.py:628
  436.1 8.7 %convolution_convert_fusion.1 = bf16[2048,512]{0,1:T(8,128)(2,1)S(1)} fusion(bf16[2048,2048]{1,0:T(8,128)(2,1)} %bitcast.76, bf16[2048,512]{1,0:T(8,128)(2,1)} %get-tuple-element.58), kind=kOutput, calls=%fused_computation.5 | convolution fusion | flops 4296015872 | bytes 12582912 | tf_op jit(solution)/shard_map/dot_general | solution.py:32
  444.8 1.8 pad_maximum_fusion
  446.7 0.7 copy.37.gain2_ref
  447.4 0.7 copy.38.gain1_ref
  448.1 8.5 %convolution_convert_fusion = bf16[2048,2048]{1,0:T(8,128)(2,1)} fusion(bf16[2048,512]{1,0:T(8,128)(2,1)} %get-tuple-element.58, bf16[2048,768]{1,0:T(8,128)(2,1)S(1)} %copy-done.1), kind=kOutput, calls=%fused_computation | convolution fusion | flops 4299161600 | bytes 12582912 | tf_op jit(solution)/shard_map/dot_general | solution.py:32
  456.6 42.6 %scatter_plane.3 = f32[256,2048]{1,0:T(8,128)} custom-call(bf16[8,256,2048]{2,1,0:T(8,128)(2,1)} %bitcast.72), custom_call_target="tpu_custom_call" | custom-call | bytes 117440512 | tf_op jit(solution)/shard_map/scatter_plane/pallas_call | solution.py:355
  499.2 2.2 fusion.4
  501.6 5.9 %fusion.7 = (f32[256,2048]{1,0:T(8,128)}, bf16[256,2048]{1,0:T(8,128)(2,1)}) fusion(f32[256,2048]{1,0:T(8,128)} %scatter_plane.3, bf16[1,256,2048]{2,1,0:T(8,128)(2,1)S(1)} %copy-done.41, f32[256]{0:T(256)S(1)} %broadcast_multiply_fusion, f32[256]{0:T(256)S(1)} %add_rsqrt_fusion.1, f32[256,2048]{1,0:T(8,128)} %get-tuple-element.52, ...), kind=kLoop, calls=%fused_computation.17 | loop fusion | flops 7864320 | bytes 13636608 | tf_op jit(solution)/shard_map/add | solution.py:1446
  507.6 1.5 copy.36
  509.1 1.2 copy-done.15
  510.3 0.9 copy-done.16
  511.3 0.8 copy-done.23
  512.1 0.8 copy-done.24
  512.8 37.5 %finish_plane.1 = (f32[64,5632]{1,0:T(8,128)S(1)}, f32[64,5632]{1,0:T(8,128)S(1)}, bf16[8,64,384]{2,1,0:T(8,128)(2,1)S(1)}, bf16[8,64,320]{2,1,0:T(8,128)(2,1)S(...) custom-call(bf16[8,64,1152]{2,1,0:T(8,128)(2,1)S(1)} %bitcast.68, ...), custom_call_target="tpu_custom_call" | custom-call | bytes 58982400 | tf_op jit(solution)/shard_map/finish_plane/pallas_call | solution.py:1285
  550.3 1.1 copy-done.10
  551.4 1.1 copy-done.12
  552.5 0.8 copy-done.17
  553.5 0.6 copy-done.19
  554.2 2.1 copy.39
  556.3 2.9 reshape.147
  560.5 0.8 copy.56
  561.3 0.7 copy.57
  561.9 0.7 copy.58
  562.6 0.8 copy.59
  563.4 1.1 copy.60
  564.5 1.1 copy.61
  (138 shorter events, 4.7 us)
Async XLA Ops:
  7.2 103.4 %all-gather.4.cloned.1.call-start = ((), (), s32[]{:S(2)}) async-start(), calls=%async_computation.3 | async-start | bytes 3932160 | tf_op jit(solution)/shard_map/all_gather | solution.py:1370
  10.4 14.8 %copy-start.2 = (bf16[64,5632]{1,0:T(8,128)(2,1)S(1)}, bf16[64,5632]{1,0:T(8,128)(2,1)}, u32[]{:S(2)}) copy-start(bf16[64,5632]{1,0:T(8,128)(2,1)} %gate_weight.1) | copy-start | bytes 2162692
  10.4 14.8 %copy-start.4 = (bf16[64,5632]{1,0:T(8,128)(2,1)S(1)}, bf16[64,5632]{1,0:T(8,128)(2,1)}, u32[]{:S(2)}) copy-start(bf16[64,5632]{1,0:T(8,128)(2,1)} %up_weight.1) | copy-start | bytes 2162692
  10.4 14.8 %copy-start.51 = (f32[64]{0:T(128)S(1)}, f32[64]{0:T(128)}, u32[]{:S(2)}) copy-start(f32[64]{0:T(128)} %param.21) | copy-start | bytes 772
  25.1 177.6 %all-gather.6.cloned.1.call-start = ((), (), s32[]{:S(2)}) async-start(), calls=%async_computation.4 | async-start | bytes 5898240 | tf_op jit(solution)/shard_map/all_gather | solution.py:1394
  27.1 1.6 copy-start.49
  29.4 1.0 copy-start.47
  49.3 1.2 copy-start.39
  49.3 219.6 %all-gather.8.cloned.1.call-start = ((), (), s32[]{:S(2)}) async-start(), calls=%async_computation.5 | async-start | bytes 5242880 | tf_op jit(solution)/shard_map/all_gather | solution.py:1395
  53.3 53.3 %copy-start.53 = (s32[1,2]{1,0:T(1,128)S(1)}, s32[1,2]{1,0:T(1,128)}, u32[]{:S(2)}) copy-start(s32[1,2]{1,0:T(1,128)} %param.14) | copy-start | bytes 28
  106.6 282.9 %reduce-scatter.4.cloned.1.call-start = ((), (), s32[]{:S(2)}) async-start(), calls=%async_computation.6 | async-start | bytes 5898240 | tf_op jit(solution)/shard_map/reduce_scatter | solution.py:1419
  106.6 3.8 collective-permute-start
  107.9 2.3 copy-start.52
  107.9 2.3 copy-start.43
  110.2 45.5 %copy-start.6 = (f32[1024,128]{1,0:T(8,128)}, f32[1024,128]{1,0:T(8,128)S(1)}, u32[]{:S(2)}) copy-start(f32[1024,128]{1,0:T(8,128)S(1)} %get-tuple-element.86.cos_ref) | copy-start | bytes 1572868
  110.2 45.5 %copy-start.8 = (f32[1024,128]{1,0:T(8,128)}, f32[1024,128]{1,0:T(8,128)S(1)}, u32[]{:S(2)}) copy-start(f32[1024,128]{1,0:T(8,128)S(1)} %get-tuple-element.87.sin_ref) | copy-start | bytes 1572868
  110.5 1.9 copy-start
  155.7 1.3 copy-start.33
  157.0 43.3 %copy-start.34 = (bf16[2048,256]{1,0:T(8,128)(2,1)}, bf16[2048,256]{1,0:T(8,128)(2,1)S(1)}, u32[]{:S(2)}) copy-start(bf16[2048,256]{1,0:T(8,128)(2,1)S(1)} %get-tuple-element.59) | copy-start | bytes 3145732
  157.0 41.2 %copy-start.40 = (bf16[1,256,2048]{2,1,0:T(8,128)(2,1)S(1)}, bf16[1,256,2048]{2,1,0:T(8,128)(2,1)}, u32[]{:S(2)}) copy-start(bf16[1,256,2048]{2,1,0:T(8,128)(2,1)} %param.13) | copy-start | bytes 3145732
  200.3 1.3 copy-start.36
  268.9 187.6 %reduce-scatter.6.cloned.1.call-start = ((), (), s32[]{:S(2)}) async-start(), calls=%async_computation.7 | async-start | bytes 5242880 | tf_op jit(solution)/shard_map/reduce_scatter | solution.py:1423
  331.0 1.6 copy-start.37
  331.1 176.5 %reduce-scatter.8.cloned.1.call-start = ((), (), s32[]{:S(2)}) async-start(), calls=%async_computation.8 | async-start | bytes 3932160 | tf_op jit(solution)/shard_map/reduce_scatter | solution.py:1444
  332.6 2.2 copy-start.42
  332.6 2.5 copy-start.44
  379.0 7.1 %copy-start.1 = (bf16[2048,768]{1,0:T(8,128)(2,1)S(1)}, bf16[2048,768]{1,0:T(8,128)(2,1)}, u32[]{:S(2)}) copy-start(bf16[2048,768]{1,0:T(8,128)(2,1)} %all-gather.4.cloned.1.call-done.weight_hbm) | copy-start | bytes 9437188
  379.0 7.1 %copy-start.46 = (bf16[8,256,2048]{2,1,0:T(8,128)(2,1)S(1)}, bf16[8,256,2048]{2,1,0:T(8,128)(2,1)}, u32[]{:S(2)}) copy-start(bf16[8,256,2048]{2,1,0:T(8,128)(2,1)} %gather_plane.1) | copy-start | bytes 25165828
  389.5 1.0 copy-start.7
  390.5 1.0 copy-start.9
  391.5 1.3 copy-start.35
  436.1 8.7 %copy-start.48 = (bf16[2048,256]{0,1:T(8,128)(2,1)S(1)}, bf16[2048,256]{0,1:T(8,128)(2,1)}, u32[]{:S(2)}) copy-start(bf16[2048,256]{0,1:T(8,128)(2,1)} %convolution_convert_fusion.2) | copy-start | bytes 3145732
  446.6 0.7 copy-start.50
  456.6 42.6 %copy-start.41 = (bf16[1,256,2048]{2,1,0:T(8,128)(2,1)S(1)}, bf16[1,256,2048]{2,1,0:T(8,128)(2,1)}, u32[]{:S(2)}) copy-start(bf16[1,256,2048]{2,1,0:T(8,128)(2,1)} %param.13) | copy-start | bytes 3145732
  499.1 2.2 copy-start.38
  499.2 2.5 copy-start.45
  501.6 7.4 %copy-start.3 = (bf16[64,5632]{1,0:T(8,128)(2,1)S(1)}, bf16[64,5632]{1,0:T(8,128)(2,1)}, u32[]{:S(2)}) copy-start(bf16[64,5632]{1,0:T(8,128)(2,1)} %gate_weight.1) | copy-start | bytes 2162692
  501.6 7.4 %copy-start.5 = (bf16[64,5632]{1,0:T(8,128)(2,1)S(1)}, bf16[64,5632]{1,0:T(8,128)(2,1)}, u32[]{:S(2)}) copy-start(bf16[64,5632]{1,0:T(8,128)(2,1)} %up_weight.1) | copy-start | bytes 2162692
  501.6 7.5 %copy-start.21 = (bf16[64,512]{1,0:T(8,128)(2,1)S(1)}, bf16[64,512]{1,0:T(8,128)(2,1)}, u32[]{:S(2)}) copy-start(bf16[64,512]{1,0:T(8,128)(2,1)} %key_weight.1) | copy-start | bytes 196612
  501.6 7.5 %copy-start.22 = (bf16[64,512]{1,0:T(8,128)(2,1)S(1)}, bf16[64,512]{1,0:T(8,128)(2,1)}, u32[]{:S(2)}) copy-start(bf16[64,512]{1,0:T(8,128)(2,1)} %value_weight.1) | copy-start | bytes 196612
  507.5 1.6 copy-start.14
  509.1 1.2 copy-start.15
  510.3 0.9 copy-start.16
  511.3 0.8 copy-start.23
  512.1 0.8 copy-start.24
  550.3 1.1 copy-start.10
  551.4 1.1 copy-start.12
  552.5 0.8 copy-start.17
  553.3 0.8 copy-start.19
  553.3 0.8 copy-start.25
  553.3 0.9 copy-start.27
  553.3 0.9 copy-start.29
  553.3 0.9 copy-start.31
  556.3 2.9 copy-start.32
  556.3 3.6 copy-start.30
  556.3 4.2 copy-start.20
  556.3 5.0 copy-start.28
  556.3 5.6 copy-start.26
  556.3 6.3 %copy-start.18 = (f32[64,2048]{1,0:T(8,128)S(1)}, f32[64,2048]{1,0:T(8,128)}, u32[]{:S(2)}) copy-start(f32[64,2048]{1,0:T(8,128)} %copy-done.17) | copy-start | bytes 1572868
  559.2 4.2 copy-start.13
  561.9 2.6 copy-start.11
Sparse Core Ops, SparseCore 0:
  25.3 63.8 all-gather.3
  90.7 88.1 all-gather.5
  180.5 79.0 all-gather.7
  269.0 85.0 reduce-scatter.3
  356.3 77.0 reduce-scatter.5
  446.8 60.7 reduce-scatter.7

commit v12 on v11

--- a/solution.py
+++ b/solution.py
@@ -137,23 +137,24 @@
         x1.wait_recv()
         rx1.start()
 
-    def finish():
+    def far_start():
         diag0.wait_recv()
         rd0.start()
         diag1.wait_recv()
         rd1.start()
-        for copy in (c0, c1, rx0, ry0, ry1, rx1, rd0, rd1):
+
+    def near_arrive():
+        mine.wait()
+        for copy in (c0, c1, rx0, ry0, ry1, rx1):
             copy.wait_recv()
+
+    def far_arrive():
+        rd0.wait_recv()
+        rd1.wait_recv()
         for copy in (x0, y0, c0, x1, y1, c1, diag0, diag1, rx0, ry0, ry1, rx1, rd0, rd1):
             copy.wait_send()
-        mine.wait()
-
-    return begin, first, second, finish
-
-
-def gather_kernel(*refs):
-    for stage in gather_stages(*refs):
-        stage()
+
+    return begin, first, second, near_arrive, far_start, far_arrive
 
 
 GATHER_SCRATCH = (
@@ -163,29 +164,96 @@
 )
 
 
-def gather_plane(block, ident):
+def gather_mix_kernel(
+    own_ref, mixed_ref, weight_ref, all_ref, grad_ref, columns_ref, tokens, total, local, *gather
+):
+    begin, first, second, near_arrive, far_start, far_arrive = gather_stages(
+        own_ref, all_ref, *gather
+    )
+    tp_at, seq_at, _, _, _ = plane_place()
+    seq = lax.axis_size("seq")
+    rows, width = own_ref.shape
+    pair = 2 * rows
+    block = width // 4
+    begin()
+
+    def chip_rows(c):
+        t = lax.rem(tp_at + c // 2, 2)
+        s = lax.rem(seq_at + (seq // 2) * lax.rem(c, 2), seq)
+        return t * seq + s - lax.rem(s, 2)
+
+    def take(c):
+        return pltpu.make_async_copy(
+            all_ref.at[pl.ds(chip_rows(c), 2)], tokens.at[c], local.at[c]
+        )
+
+    total[...] = jnp.zeros(total.shape, F32)
+
+    def chip_step(c, carry):
+        take(c).wait()
+        at = pl.ds(pl.multiple_of(chip_rows(c) * rows, pair), pair)
+        chip = nn(tokens[c].reshape(pair, width), weight_ref[...])
+        grad_ref[at, :] = chip.astype(BF)
+
+        def grads_step(n, carry):
+            some = pl.ds(pl.multiple_of(n * block, block), block)
+            total[some, :] += tn(tokens[c, :, :, some].reshape(pair, block), mixed_ref[at, :])
+            return carry
+
+        lax.fori_loop(0, 4, grads_step, 0)
+        return carry
+
+    first()
+    second()
+    near_arrive()
+    for c in range(3):
+        take(c).start()
+    lax.fori_loop(0, 3, chip_step, 0)
+    far_start()
+    far_arrive()
+    take(3).start()
+    chip_step(3, 0)
+    columns_ref[...] = total[...].astype(BF)
+
+
+def gather_mix_plane(block, mixed, weight, ident):
     rows, width = block.shape
     plane = lax.axis_size("tp") * lax.axis_size("seq")
-    size = rows * width * 2
-    gathered = pl.pallas_call(
-        gather_kernel,
-        out_shape=jax.ShapeDtypeStruct((plane, rows, width), block.dtype),
-        in_specs=[pl.BlockSpec(memory_space=pltpu.VMEM)],
-        out_specs=pl.BlockSpec(memory_space=pltpu.HBM),
-        scratch_shapes=GATHER_SCRATCH,
+    tokens, q_part = mixed.shape
+    shape = jax.ShapeDtypeStruct
+    hbm = pl.BlockSpec(memory_space=pltpu.HBM)
+    vmem = pl.BlockSpec(memory_space=pltpu.VMEM)
+    return pl.pallas_call(
+        gather_mix_kernel,
+        out_shape=(
+            shape((plane, rows, width), BF),
+            shape((tokens, q_part), BF),
+            shape((width, q_part), BF),
+        ),
+        in_specs=[vmem] * 3,
+        out_specs=(hbm, vmem, vmem),
+        scratch_shapes=[
+            pltpu.VMEM((4, 2, rows, width), BF),
+            pltpu.VMEM((width, q_part), F32),
+            pltpu.SemaphoreType.DMA((4,)),
+            *GATHER_SCRATCH,
+        ],
         cost_estimate=pl.CostEstimate(
-            flops=0, transcendentals=0, bytes_accessed=plane * size * 12
-        ),
-        compiler_params=pltpu.CompilerParams(collective_id=ident, has_side_effects=True),
-        name="gather_plane",
-    )(block)
-    return gathered.reshape(plane * rows, width)
+            flops=4 * tokens * width * q_part,
+            transcendentals=0,
+            bytes_accessed=plane * rows * width * 24,
+        ),
+        compiler_params=pltpu.CompilerParams(
+            collective_id=ident, has_side_effects=True, vmem_limit_bytes=40 << 20
+        ),
+        name="gather_mix_plane",
+    )(block, mixed, weight)
 
 
 def spread_kernel(
     own_ref, move_ref, all_ref, move_out, kept, copies, *gather
 ):
-    begin, first, second, finish = gather_stages(own_ref, all_ref, *gather)
+    begin, first, second, *last = gather_stages(own_ref, all_ref, *gather)
     tp_at, seq_at, _, _, _ = plane_place()
     seq = lax.axis_size("seq")
     plane = lax.axis_size("tp") * seq
@@ -210,7 +278,8 @@
     for move in moves:
         move.wait()
     put.wait()
-    finish()
+    for stage in last:
+        stage()
 
 
 def spread_plane(block, blocks, ident):
@@ -407,7 +476,7 @@
     local,
     *gather,
 ):
-    begin, first, second, finish = gather_stages(own_ref, all_ref, *gather)
+    begin, first, second, *last = gather_stages(own_ref, all_ref, *gather)
     total, dim = cos_ref.shape
     take_weight = pltpu.make_async_copy(weight_hbm, weight, local.at[0])
     take_weight.start()
@@ -495,7 +564,8 @@
         return carry
 
     lax.fori_loop(0, log_ref.shape[0], head_step, 0)
-    finish()
+    for stage_step in last:
+        stage_step()
     for n in range(2):
         put_out(TP - 1, n).wait()
 
@@ -1184,33 +1254,8 @@
     )(block, grads, weight, back, first)
 
 
-def finish_kernel(
-    first_ref,
-    second_ref,
-    attn_ref,
-    gate_weight,
-    up_weight,
-    query_weight,
-    key_weight,
-    value_weight,
-    gain2_ref,
-    gain1_ref,
-    gate_out,
-    up_out,
-    down_first,
-    down_second,
-    gain2_out,
-    query_out,
-    key_out,
-    value_out,
-    out_out,
-    gain1_out,
-    first_in,
-    second_in,
-    attn_in,
-    local,
-    sends,
-    recvs,
+def exchange_all_kernel(
+    first_ref, second_ref, attn_ref, first_in, second_in, attn_in, local, sends, recvs
 ):
     tp_at, seq_at, _, _, _ = plane_place()
     seq = lax.axis_size("seq")
@@ -1231,15 +1276,58 @@
             copy.start()
         groups.append(copies)
 
-    def arrive(n):
-        for copy in groups[n]:
+    for copies in groups:
+        for copy in copies:
             copy.wait()
 
+
+def exchange_all_plane(blocks, ident):
+    plane = blocks[0].shape[0]
+    hbm = pl.BlockSpec(memory_space=pltpu.HBM)
+    vmem = pl.BlockSpec(memory_space=pltpu.VMEM)
+    size = sum(block.size for block in blocks) * 2
+    return pl.pallas_call(
+        exchange_all_kernel,
+        out_shape=tuple(jax.ShapeDtypeStruct(b.shape, b.dtype) for b in blocks),
+        in_specs=[hbm] * 3,
+        out_specs=(vmem,) * 3,
+        scratch_shapes=[
+            pltpu.SemaphoreType.DMA((3,)),
+            pltpu.SemaphoreType.DMA((3 * plane - 3,)),
+            pltpu.SemaphoreType.DMA((3 * plane - 3,)),
+        ],
+        cost_estimate=pl.CostEstimate(flops=0, transcendentals=0, bytes_accessed=size * 20),
+        compiler_params=pltpu.CompilerParams(collective_id=ident, has_side_effects=True),
+        name="exchange_all_plane",
+    )(*blocks)
+
+
+def finish_kernel(
+    first_in,
+    second_in,
+    attn_in,
+    gate_weight,
+    up_weight,
+    query_weight,
+    key_weight,
+    value_weight,
+    gain2_ref,
+    gain1_ref,
+    gate_out,
+    up_out,
+    down_out,
+    gain2_out,
+    query_out,
+    key_out,
+    value_out,
+    out_out,
+    gain1_out,
+):
+    plane = first_in.shape[0]
     gain = gain2_ref[...]
     sizes = [ref.shape[2] // 3 for ref in (first_in, second_in)]
     total = jnp.zeros(gain.shape, F32)
-    for n, (ref, down) in enumerate(((first_in, down_first), (second_in, down_second))):
-        arrive(n)
+    for n, ref in enumerate((first_in, second_in)):
         size = sizes[n]
         for j in range(plane):
             start = j * sum(sizes) + n * sizes[0]
@@ -1248,10 +1336,9 @@
                 own = ref[j, :, k * size : (k + 1) * size].astype(F32)
                 out[:, at] = own * gain
                 total = total + jnp.sum(own * weight[:, at].astype(F32), axis=1, keepdims=True)
-            down[j] = ref[j, :, 2 * size :]
+            down_out[at, :] = ref[j, :, 2 * size :].astype(F32).T
     gain2_out[...] = total
 
-    arrive(2)
     gain = gain1_ref[...]
     q_part = query_out.shape[1] // plane
     share = plane // KV
@@ -1261,7 +1348,7 @@
         own = attn_in[j, :, :q_part].astype(F32)
         query_out[:, at] = own * gain
         total = total + jnp.sum(own * query_weight[:, at].astype(F32), axis=1, keepdims=True)
-        out_out[:, at] = attn_in[j, :, q_part + 2 * DH :].astype(F32)
+        out_out[at, :] = attn_in[j, :, q_part + 2 * DH :].astype(F32).T
     for j in range(KV):
         at = slice(j * DH, (j + 1) * DH)
         for k, (out, weight) in enumerate(((key_out, key_weight), (value_out, value_weight))):
@@ -1274,43 +1361,23 @@
     gain1_out[...] = total
 
 
-def finish_plane(first, second, attn, weights, gain2, gain1, ident):
-    plane, rows, _ = first.shape
+def finish(first, second, attn, weights, gain2, gain1):
+    rows = first.shape[1]
     shape = jax.ShapeDtypeStruct
-    hbm = pl.BlockSpec(memory_space=pltpu.HBM)
     vmem = pl.BlockSpec(memory_space=pltpu.VMEM)
     gate, up, query, key, value = (shape(w.shape, F32) for w in weights)
+    down, out = (shape(w.shape[::-1], F32) for w in (gate, query))
     column = shape((rows, 1), F32)
-    size = (first.size + second.size + attn.size) * 2
     return pl.pallas_call(
         finish_kernel,
-        out_shape=(
-            gate,
-            up,
-            shape((plane, rows, first.shape[2] // 3), BF),
-            shape((plane, rows, second.shape[2] // 3), BF),
-            column,
-            query,
-            key,
-            value,
-            query,
-            column,
-        ),
-        in_specs=[hbm] * 3 + [vmem] * 7,
-        out_specs=(vmem,) * 10,
-        scratch_shapes=[
-            pltpu.VMEM(first.shape, BF),
-            pltpu.VMEM(second.shape, BF),
-            pltpu.VMEM(attn.shape, BF),
-            pltpu.SemaphoreType.DMA((3,)),
-            pltpu.SemaphoreType.DMA((3 * plane - 3,)),
-            pltpu.SemaphoreType.DMA((3 * plane - 3,)),
-        ],
-        cost_estimate=pl.CostEstimate(flops=0, transcendentals=0, bytes_accessed=size * 20),
-        compiler_params=pltpu.CompilerParams(
-            collective_id=ident, has_side_effects=True, vmem_limit_bytes=32 << 20
-        ),
-        name="finish_plane",
+        out_shape=(gate, up, down, column, query, key, value, out, column),
+        in_specs=[vmem] * 10,
+        out_specs=(vmem,) * 9,
+        cost_estimate=pl.CostEstimate(
+            flops=4 * gate.size, transcendentals=0, bytes_accessed=16 * gate.size
+        ),
+        compiler_params=pltpu.CompilerParams(vmem_limit_bytes=40 << 20),
+        name="finish",
     )(first, second, attn, *weights, gain2, gain1)
 
 
@@ -1425,8 +1492,9 @@
         scaled2 - norm2 * jnp.mean(scaled2 * norm2, axis=-1, keepdims=True)
     )
 
-    branch_grad = gather_plane((keep * hidden_grad).astype(BF), 7)
-    mixed_grad = nn(branch_grad, out_weight).astype(BF)
+    _, mixed_grad, out_columns = gather_mix_plane(
+        (keep * hidden_grad).astype(BF), mixed, out_weight, 7
+    )
     qkv_grad, ffn_out = attn_back_plane(
         starts,
         qkv,
@@ -1438,7 +1506,7 @@
         9,
     )
     attn_partial = jnp.concatenate(
-        [tn(norm1_all, qkv_grad).astype(BF), tn(branch_grad, mixed).astype(BF)], axis=1
+        [tn(norm1_all, qkv_grad).astype(BF), out_columns], axis=1
     )
     scaled1_partial = nt(qkv_grad, qkv_weight).astype(BF)
     attn_sums = lax.psum_scatter(attn_partial, "rep", scatter_dimension=0, tiled=True)
@@ -1448,18 +1516,17 @@
     )
     out_hidden = (hidden + keep * ffn_out).astype(BF)
 
-    gate_grad, up_grad, down_first, down_second, gain2_grad, *attn_grads = finish_plane(
-        after(first_sums, input_grad, out_hidden).reshape(plane, -1, first_sums.shape[1]),
-        second_sums.reshape(plane, -1, second_sums.shape[1]),
-        attn_sums.reshape(plane, -1, attn_sums.shape[1]),
-        (w_gate, w_up, w_query, w_key, w_value),
-        gain2,
-        gain1,
+    sums = exchange_all_plane(
+        (
+            after(first_sums, input_grad, out_hidden).reshape(plane, -1, first_sums.shape[1]),
+            second_sums.reshape(plane, -1, second_sums.shape[1]),
+            attn_sums.reshape(plane, -1, attn_sums.shape[1]),
+        ),
         10,
     )
+    weights = (w_gate, w_up, w_query, w_key, w_value)
+    gate_grad, up_grad, down_grad, gain2_grad, *attn_grads = finish(*sums, weights, gain2, gain1)
     query_grad, key_grad, value_grad, out_grad, gain1_grad = attn_grads
-    down_own = jnp.concatenate([down_first, down_second], axis=2)
-    down_grad = jnp.transpose(down_own, (0, 2, 1)).reshape(plane * ff_part, -1).astype(F32)
     return (
         out_hidden[None],
         input_grad[None],
@@ -1467,7 +1534,7 @@
         query_grad,
         key_grad,
         value_grad,
-        out_grad.T,
+        out_grad,
         gain2_grad[:, 0],
         gate_grad,
         up_grad,

time: 580 us -> 577 us (level)
  matrix products: 27.6 us -> 17.3 us
  Pallas kernels: 462 us -> 471 us
    dot_general x4 -> x2, matrix products: 27.6 us -> 17.3 us  [dot(): lax.dot_general(left, right, ((contract[:1], contract[1:]), ((), ())), pr...]
    pallas_call x2 -> x3, Pallas kernels: 79.8 us -> 89.3 us  [the longest x1 44.8 us: gather_mix_plane(): pl.pallas_call(gather_mix_kernel, out_shape=(shape((plane, rows, width),...]
    unnamed x114 -> x80, local copies, waits for them, and re-layouts: 24.5 us -> 26.3 us
  transfers between devices with their start and end apart: 7 -> 7, of which waited for: 1 -> 1; matrix products, arithmetic and copies ran while one was open for 10% -> 8% of each run, Pallas kernels for 72% -> 72%
where the time goes in v12:
time: 577 us; the launch traced here: 569 us
  Pallas kernels  471 us (82%)
  local copies, waits for them, and re-layouts  37.1 us (6%)
  other arithmetic  26.2 us (5%)
  matrix products  17.3 us (3%)
  between operations  15 us (3%)
    pallas_call x2, Pallas kernels, scatter_plane(): pl.pallas_call(scatter_kernel, out_shape=jax.ShapeDtypeStruct((rows, widt...  83.2 us
    pallas_call x1, Pallas kernels, ffn_first_plane(): pl.pallas_call(ffn_first_kernel, out_shape=(shape((plane, rows, width), B...  66 us
    pallas_call x1, Pallas kernels, ffn_second_plane(): pl.pallas_call(ffn_second_kernel, out_shape=(shape((plane, rows, width),...  61.9 us
    pallas_call x1, Pallas kernels, spread_plane(): pl.pallas_call(spread_kernel, out_shape=(jax.ShapeDtypeStruct((plane, row...  53.2 us
    pallas_call x1, Pallas kernels, gather_mix_plane(): pl.pallas_call(gather_mix_kernel, out_shape=(shape((plane, rows, width),...  44.8 us
    pallas_call x1, Pallas kernels, attn_back_plane(): pl.pallas_call(attn_back_kernel, out_shape=(jax.ShapeDtypeStruct((tokens,...  43.5 us
    pallas_call x1, Pallas kernels, attn_front_plane(): pl.pallas_call(attn_front_kernel, out_shape=(shape((tokens, q_part + 2 *...  43 us
    pallas_call x1, Pallas kernels, exchange_all_plane(): pl.pallas_call(exchange_all_kernel, out_shape=tuple((jax.ShapeDtypeStruct...  39 us
  transfers between devices with their start and end apart: 7, of which 1 were waited for; matrix products, arithmetic and copies ran while one was open for 8% of the time, Pallas kernels for 72%

profile of v12, /device:TPU:1, one launch (start us, length us, event | category | flops | bytes accessed | tf_op | source)
XLA Modules:
  0.0 569.5 jit_solution(13665630693587155837)
XLA Ops:
  7.2 1.1 multiply_convert_fusion.4
  8.3 1.0 multiply_convert_fusion.6
  9.4 1.0 bitcast_bitcast_fusion
  10.5 1.0 pad_maximum_fusion.3.in_ref
  11.4 13.7 %exchange_plane.2 = bf16[8,64,768]{2,1,0:T(8,128)(2,1)} custom-call(bf16[8,64,768]{2,1,0:T(8,128)(2,1)} %pad_maximum_fusion.3.in_ref), custom_call_target="tpu_custom_call" | custom-call | bytes 15728640 | tf_op jit(solution)/shard_map/exchange_plane/pallas_call | solution.py:751
  25.2 0.3 multiply_convert_fusion.3
  25.5 0.7 reshape.120
  26.4 0.7 reshape.121
  27.3 1.9 reshape.122
  29.3 0.9 copy-done.34
  30.2 1.2 pad_maximum_fusion.1.in_ref
  31.4 16.7 %exchange_plane.3 = bf16[8,64,1152]{2,1,0:T(8,128)(2,1)} custom-call(bf16[8,64,1152]{2,1,0:T(8,128)(2,1)} %pad_maximum_fusion.1.in_ref), custom_call_target="tpu_custom_call" | custom-call | bytes 23592960 | tf_op jit(solution)/shard_map/exchange_plane/pallas_call | solution.py:751
  48.3 1.2 slice.37
  49.4 0.3 fusion.8
  49.7 1.2 fusion.2.own_ref
  51.0 1.3 pad_maximum_fusion.2.move_ref
  52.2 53.2 %spread_plane.1 = (bf16[8,256,2048]{2,1,0:T(8,128)(2,1)}, bf16[8,64,960]{2,1,0:T(8,128)(2,1)}) custom-call(bf16[256,2048]{1,0:T(8,128)(2,1)} %fusion.2.own_ref, bf16[8,64,960]{2,1,0:T(8,128)(2,1)} %pad_maximum_fusion.2.move_ref), custom_call_target="tpu_custom_call" | custom-call | bytes 134217728 | tf_op jit(solution)/shard_map/spread_plane/pallas_call | solution.py:291
  105.6 1.2 collective-permute-start
  106.9 1.9 fusion.10
  108.8 0.3 pad_maximum_fusion.4
  109.5 1.9 copy-done
  111.4 43.0 %attn_front_plane.1 = (bf16[2048,512]{1,0:T(8,128)(2,1)S(1)}, bf16[2048,256]{1,0:T(8,128)(2,1)S(1)}, f32[4,1,1024]{2,1,0:T(1,128)S(1)}, bf16[2048,2048]{1,0:T(8,128)(2,1)}, bf16[8,256,2048]{2,1,0:T(8,128)(2,1)}) custom-call(s32[2,2]{1,0:T(2,128)S(1)} %add_select_fusion.starts_ref, bf16[2048,2048]{1,0:T(8,128)(2,1)} %bitcast.60, ...), custom_call_target="tpu_custom_call" | custom-call | flops 2147483648 | bytes 100663296 | tf_op jit(solution)/shard_map/attn_front_plane/pallas_call | solution.py:583
  154.4 1.3 copy-done.18
  155.7 1.0 copy-done.19
  156.7 41.2 %scatter_plane.2 = f32[256,2048]{1,0:T(8,128)} custom-call(bf16[8,256,2048]{2,1,0:T(8,128)(2,1)} %bitcast.58), custom_call_target="tpu_custom_call" | custom-call | bytes 117440512 | tf_op jit(solution)/shard_map/scatter_plane/pallas_call | solution.py:424
  197.9 2.1 multiply_reduce_fusion.1
  200.0 1.4 copy-done.23
  201.4 1.1 multiply_convert_fusion.1.own_ref
  202.5 66.0 %ffn_first_plane.1 = (bf16[8,256,2048]{2,1,0:T(8,128)(2,1)}, bf16[8,256,2048]{2,1,0:T(8,128)(2,1)}, bf16[8,256,2048]{2,1,0:T(8,128)(2,1)}, bf16[2048,1152]{1,0:T(8,128)(2,1)}) custom-call(bf16[256,2048]{1,0:T(8,128)(2,1)} %multiply_convert_fusion.1.own_ref, bf16[8,256,2048]{2,1,0:T(8,128)(2,1)} %get-tuple-element.51.grad_ref, ...), custom_call_target="tpu_custom_call" | custom-call | flops 28991029248 | bytes 92274688 | tf_op jit(solution)/shard_map/ffn_first_plane/pallas_call | solution.py:1174
  268.7 61.9 %ffn_second_plane.1 = (bf16[8,256,2048]{2,1,0:T(8,128)(2,1)}, bf16[2048,960]{1,0:T(8,128)(2,1)}, f32[256,2048]{1,0:T(8,128)}) custom-call(bf16[8,256,2048]{2,1,0:T(8,128)(2,1)} %get-tuple-element.52.all_ref, bf16[8,256,2048]{2,1,0:T(8,128)(2,1)} %get-tuple-element.51.grad_ref, bf16[2048,960]{1,0:T(8,128)(2,1)} %all-gather.8.cloned.1.call-done.weight_hbm, ...), custom_call_target="tpu_custom_call" | custom-call | flops 24159191040 | bytes 92274688 | tf_op jit(solution)/shard_map/ffn_second_plane/pallas_call | solution.py:1218
  330.7 1.8 copy-done.1
  332.6 1.5 copy-done.24
  334.1 2.1 multiply_reduce_fusion
  336.4 0.3 copy-done.31
  336.7 0.7 multiply_convert_fusion.own_ref
  337.4 0.5 copy-done.20
  337.9 44.8 %gather_mix_plane.1 = (bf16[8,256,2048]{2,1,0:T(8,128)(2,1)}, bf16[2048,256]{1,0:T(8,128)(2,1)S(1)}, bf16[2048,256]{1,0:T(8,128)(2,1)S(1)}) custom-call(bf16[256,2048]{1,0:T(8,128)(2,1)S(1)} %multiply_convert_fusion.own_ref, bf16[2048,256]{1,0:T(8,128)(2,1)S(1)} %copy-done.20, bf16[2048,256]{1,0:T(8,128)(2,1)S(1)} %slice.38.weight_ref), custom_call_target="tpu_custom_call" | custom-call | flops 4294967296 | bytes 100663296 | tf_op jit(solution)/shard_map/gather_mix_plane/pallas_call | solution.py:226
  382.7 1.0 copy-done.14
  383.7 1.0 copy-done.21
  384.6 2.3 copy.39
  386.9 1.0 copy-done.8
  387.9 1.0 copy-done.10
  389.0 1.2 copy-done.22
  390.2 43.5 %attn_back_plane.1 = (bf16[2048,512]{1,0:T(8,128)(2,1)}, f32[256,2048]{1,0:T(8,128)}) custom-call(s32[2,2]{1,0:T(2,128)S(1)} %add_select_fusion.starts_ref, bf16[2048,512]{1,0:T(8,128)(2,1)} %copy-done.18, bf16[2048,256]{1,0:T(8,128)(2,1)S(1)} %copy-done.22, f32[4,1,1024]{2,1,0:T(1,128)S(1)} %get-tuple-element.61.log_ref, f32[1024,128]{1,0:T(8,128)S(1)} %copy-done.8, ...), custom_call_target="tpu_custom_call" | custom-call | flops 5368709120 | bytes 117440512 | tf_op jit(solution)/shard_map/attn_back_plane/pallas_call | solution.py:698
  433.8 8.7 %convolution_convert_fusion.1 = bf16[2048,512]{0,1:T(8,128)(2,1)S(1)} fusion(bf16[2048,2048]{1,0:T(8,128)(2,1)} %bitcast.61, bf16[2048,512]{1,0:T(8,128)(2,1)} %get-tuple-element.64), kind=kOutput, calls=%fused_computation.5 | convolution fusion | flops 4296015872 | bytes 12582912 | tf_op jit(solution)/shard_map/dot_general | solution.py:32
  442.4 1.8 pad_maximum_fusion
  444.4 0.5 copy-done.35
  445.0 8.7 %convolution_convert_fusion = bf16[2048,2048]{1,0:T(8,128)(2,1)} fusion(bf16[2048,512]{1,0:T(8,128)(2,1)} %get-tuple-element.64, bf16[2048,768]{1,0:T(8,128)(2,1)S(1)} %copy-done.1), kind=kOutput, calls=%fused_computation | convolution fusion | flops 4299161600 | bytes 12582912 | tf_op jit(solution)/shard_map/dot_general | solution.py:32
  453.7 42.0 %scatter_plane.3 = f32[256,2048]{1,0:T(8,128)} custom-call(bf16[8,256,2048]{2,1,0:T(8,128)(2,1)} %bitcast.59), custom_call_target="tpu_custom_call" | custom-call | bytes 117440512 | tf_op jit(solution)/shard_map/scatter_plane/pallas_call | solution.py:424
  495.7 2.2 fusion.4
  498.0 0.3 copy-done.32
  498.3 5.0 fusion.7
  503.3 1.6 reduce-scatter.8.cloned.1.call-done
  505.0 2.3 copy.40
  507.2 39.0 %exchange_all_plane.1 = (bf16[8,64,1152]{2,1,0:T(8,128)(2,1)}, bf16[8,64,960]{2,1,0:T(8,128)(2,1)}, bf16[8,64,768]{2,1,0:T(8,128)(2,1)}) custom-call(bf16[8,64,1152]{2,1,0:T(8,128)(2,1)} %bitcast.72, bf16[8,64,960]{2,1,0:T(8,128)(2,1)} %bitcast.73, bf16[8,64,768]{2,1,0:T(8,128)(2,1)} %bitcast.70), custom_call_target="tpu_custom_call" | custom-call | bytes 58982400 | tf_op jit(solution)/shard_map/exchange_all_plane/pallas_call | solution.py:1289
  546.3 1.3 copy-done.11
  547.5 1.2 copy-done.12
  548.8 1.1 copy-done.15
  549.9 5.5 finish.1
  555.4 1.5 copy-done.6
  557.0 3.1 copy.44
  560.1 1.1 copy.43
  561.2 0.6 reduce
  561.8 0.6 reduce.1
  (102 shorter events, 2.0 us)
Async XLA Ops:
  7.2 102.3 %all-gather.4.cloned.1.call-start = ((), (), s32[]{:S(2)}) async-start(), calls=%async_computation.3 | async-start | bytes 3932160 | tf_op jit(solution)/shard_map/all_gather | solution.py:1437
  10.4 14.8 %copy-start.2 = (bf16[64,5632]{1,0:T(8,128)(2,1)S(1)}, bf16[64,5632]{1,0:T(8,128)(2,1)}, u32[]{:S(2)}) copy-start(bf16[64,5632]{1,0:T(8,128)(2,1)} %gate_weight.1) | copy-start | bytes 2162692
  10.4 14.8 %copy-start.4 = (bf16[64,5632]{1,0:T(8,128)(2,1)S(1)}, bf16[64,5632]{1,0:T(8,128)(2,1)}, u32[]{:S(2)}) copy-start(bf16[64,5632]{1,0:T(8,128)(2,1)} %up_weight.1) | copy-start | bytes 2162692
  10.4 14.8 %copy-start.36 = (f32[64]{0:T(128)S(1)}, f32[64]{0:T(128)}, u32[]{:S(2)}) copy-start(f32[64]{0:T(128)} %param.21) | copy-start | bytes 772
  25.1 177.4 %all-gather.6.cloned.1.call-start = ((), (), s32[]{:S(2)}) async-start(), calls=%async_computation.4 | async-start | bytes 5898240 | tf_op jit(solution)/shard_map/all_gather | solution.py:1461
  29.3 0.9 copy-start.34
  48.1 1.4 copy-start.26
  48.1 220.5 %all-gather.8.cloned.1.call-start = ((), (), s32[]{:S(2)}) async-start(), calls=%async_computation.5 | async-start | bytes 5242880 | tf_op jit(solution)/shard_map/all_gather | solution.py:1462
  52.2 53.3 %copy-start.38 = (s32[1,2]{1,0:T(1,128)S(1)}, s32[1,2]{1,0:T(1,128)}, u32[]{:S(2)}) copy-start(s32[1,2]{1,0:T(1,128)} %param.14) | copy-start | bytes 28
  105.5 281.4 %reduce-scatter.4.cloned.1.call-start = ((), (), s32[]{:S(2)}) async-start(), calls=%async_computation.6 | async-start | bytes 5898240 | tf_op jit(solution)/shard_map/reduce_scatter | solution.py:1486
  105.6 3.8 collective-permute-start
  106.8 2.3 copy-start.37
  106.8 2.3 copy-start.30
  109.1 45.3 %copy-start.7 = (f32[1024,128]{1,0:T(8,128)}, f32[1024,128]{1,0:T(8,128)S(1)}, u32[]{:S(2)}) copy-start(f32[1024,128]{1,0:T(8,128)S(1)} %get-tuple-element.116.cos_ref) | copy-start | bytes 1572868
  109.1 45.3 %copy-start.9 = (f32[1024,128]{1,0:T(8,128)}, f32[1024,128]{1,0:T(8,128)S(1)}, u32[]{:S(2)}) copy-start(f32[1024,128]{1,0:T(8,128)S(1)} %get-tuple-element.117.sin_ref) | copy-start | bytes 1572868
  109.5 2.0 copy-start
  154.4 1.3 copy-start.18
  155.7 1.0 copy-start.19
  200.0 1.4 copy-start.23
  268.6 185.1 %reduce-scatter.6.cloned.1.call-start = ((), (), s32[]{:S(2)}) async-start(), calls=%async_computation.7 | async-start | bytes 5242880 | tf_op jit(solution)/shard_map/reduce_scatter | solution.py:1490
  330.6 1.9 copy-start.1
  330.7 174.3 %reduce-scatter.8.cloned.1.call-start = ((), (), s32[]{:S(2)}) async-start(), calls=%async_computation.8 | async-start | bytes 3932160 | tf_op jit(solution)/shard_map/reduce_scatter | solution.py:1512
  332.5 1.6 copy-start.24
  334.1 2.3 copy-start.28
  334.1 2.6 copy-start.31
  336.7 1.2 copy-start.20
  382.7 1.0 copy-start.14
  383.7 1.0 copy-start.21
  386.9 1.0 copy-start.8
  387.9 1.0 copy-start.10
  389.0 1.2 copy-start.22
  433.7 8.7 %copy-start.33 = (bf16[2048,256]{0,1:T(8,128)(2,1)S(1)}, bf16[2048,256]{0,1:T(8,128)(2,1)}, u32[]{:S(2)}) copy-start(bf16[2048,256]{0,1:T(8,128)(2,1)} %copy.39) | copy-start | bytes 3145732
  444.3 0.7 copy-start.35
  453.7 42.0 %copy-start.27 = (bf16[1,256,2048]{2,1,0:T(8,128)(2,1)S(1)}, bf16[1,256,2048]{2,1,0:T(8,128)(2,1)}, u32[]{:S(2)}) copy-start(bf16[1,256,2048]{2,1,0:T(8,128)(2,1)} %param.13) | copy-start | bytes 3145732
  453.7 44.3 %copy-start.29 = (f32[256,2048]{1,0:T(8,128)S(1)}, f32[256,2048]{1,0:T(8,128)}, u32[]{:S(2)}) copy-start(f32[256,2048]{1,0:T(8,128)} %get-tuple-element.56) | copy-start | bytes 6291460
  495.7 2.3 copy-start.25
  495.7 2.5 copy-start.32
  503.3 42.9 %copy-start.3 = (bf16[64,5632]{1,0:T(8,128)(2,1)S(1)}, bf16[64,5632]{1,0:T(8,128)(2,1)}, u32[]{:S(2)}) copy-start(bf16[64,5632]{1,0:T(8,128)(2,1)} %gate_weight.1) | copy-start | bytes 2162692
  503.3 42.9 %copy-start.5 = (bf16[64,5632]{1,0:T(8,128)(2,1)S(1)}, bf16[64,5632]{1,0:T(8,128)(2,1)}, u32[]{:S(2)}) copy-start(bf16[64,5632]{1,0:T(8,128)(2,1)} %up_weight.1) | copy-start | bytes 2162692
  503.3 42.9 %copy-start.13 = (bf16[64,2048]{1,0:T(8,128)(2,1)S(1)}, bf16[64,2048]{1,0:T(8,128)(2,1)}, u32[]{:S(2)}) copy-start(bf16[64,2048]{1,0:T(8,128)(2,1)} %query_weight.1) | copy-start | bytes 786436
  503.3 43.0 %copy-start.16 = (bf16[64,512]{1,0:T(8,128)(2,1)S(1)}, bf16[64,512]{1,0:T(8,128)(2,1)}, u32[]{:S(2)}) copy-start(bf16[64,512]{1,0:T(8,128)(2,1)} %key_weight.1) | copy-start | bytes 196612
  503.3 43.0 %copy-start.17 = (bf16[64,512]{1,0:T(8,128)(2,1)S(1)}, bf16[64,512]{1,0:T(8,128)(2,1)}, u32[]{:S(2)}) copy-start(bf16[64,512]{1,0:T(8,128)(2,1)} %value_weight.1) | copy-start | bytes 196612
  546.3 1.3 copy-start.11
  547.5 1.2 copy-start.12
  548.8 1.1 copy-start.15
  555.4 1.5 copy-start.6
Sparse Core Ops, SparseCore 0:
  25.3 63.8 all-gather.3
  90.7 88.1 all-gather.5
  180.5 79.0 all-gather.7
  268.7 85.1 reduce-scatter.3
  356.0 77.0 reduce-scatter.5
  444.4 60.4 reduce-scatter.7

commit v13 on v12

--- a/solution.py
+++ b/solution.py
@@ -1254,9 +1254,9 @@
     )(block, grads, weight, back, first)
 
 
-def exchange_all_kernel(
-    first_ref, second_ref, attn_ref, first_in, second_in, attn_in, local, sends, recvs
-):
+def exchange_all_kernel(*refs):
+    *blocks, local, sends, recvs = refs
+    count = len(blocks) // 2
     tp_at, seq_at, _, _, _ = plane_place()
     seq = lax.axis_size("seq")
     plane = lax.axis_size("tp") * seq
@@ -1265,9 +1265,7 @@
     devices = [at_device(peer // seq, lax.rem(peer, seq)) for peer in peers]
     enter(devices)
     groups = []
-    for n, (ref, into) in enumerate(
-        ((first_ref, first_in), (second_ref, second_in), (attn_ref, attn_in))
-    ):
+    for n, (ref, into) in enumerate(zip(blocks[:count], blocks[count:])):
         copies = [pltpu.make_async_copy(ref.at[me], into.at[me], local.at[n])]
         for k, (peer, device) in enumerate(zip(peers, devices)):
             i = n * (plane - 1) + k
@@ -1282,24 +1280,161 @@
 
 
 def exchange_all_plane(blocks, ident):
-    plane = blocks[0].shape[0]
+    plane, count = blocks[0].shape[0], len(blocks)
     hbm = pl.BlockSpec(memory_space=pltpu.HBM)
     vmem = pl.BlockSpec(memory_space=pltpu.VMEM)
     size = sum(block.size for block in blocks) * 2
     return pl.pallas_call(
         exchange_all_kernel,
         out_shape=tuple(jax.ShapeDtypeStruct(b.shape, b.dtype) for b in blocks),
-        in_specs=[hbm] * 3,
-        out_specs=(vmem,) * 3,
+        in_specs=[hbm] * count,
+        out_specs=(vmem,) * count,
         scratch_shapes=[
-            pltpu.SemaphoreType.DMA((3,)),
-            pltpu.SemaphoreType.DMA((3 * plane - 3,)),
-            pltpu.SemaphoreType.DMA((3 * plane - 3,)),
+            pltpu.SemaphoreType.DMA((count,)),
+            pltpu.SemaphoreType.DMA((count * (plane - 1),)),
+            pltpu.SemaphoreType.DMA((count * (plane - 1),)),
         ],
         cost_estimate=pl.CostEstimate(flops=0, transcendentals=0, bytes_accessed=size * 20),
         compiler_params=pltpu.CompilerParams(collective_id=ident, has_side_effects=True),
         name="exchange_all_plane",
     )(*blocks)
+
+
+def attn_grads_kernel(
+    norm_hbm,
+    grad_ref,
+    columns_ref,
+    weight_hbm,
+    move_ref,
+    grads_out,
+    back_out,
+    move_out,
+    norm,
+    weight,
+    stage,
+    back,
+    kept,
+    local,
+    sends,
+    recvs,
+):
+    tp_at, seq_at, _, _, _ = plane_place()
+    seq = lax.axis_size("seq")
+    plane = lax.axis_size("tp") * seq
+    me = tp_at * seq + seq_at
+    tokens, width = norm.shape
+    cols = grad_ref.shape[1]
+    block, some = width // 4, tokens // 4
+    peers = [lax.rem(me + k, plane) for k in range(1, plane)]
+    devices = [at_device(peer // seq, lax.rem(peer, seq)) for peer in peers]
+
+    def at(n):
+        return pl.ds(pl.multiple_of(n * block, block), block)
+
+    def take(n):
+        return pltpu.make_async_copy(norm_hbm.at[:, at(n)], norm.at[:, at(n)], local.at[n])
+
+    def put(n):
+        slot = lax.rem(n, 2)
+        return pltpu.make_async_copy(stage.at[slot], grads_out.at[at(n)], local.at[4 + slot])
+
+    def put_back(n):
+        slot = lax.rem(n, 2)
+        rows = pl.ds(pl.multiple_of(n * some, some), some)
+        return pltpu.make_async_copy(back.at[slot], back_out.at[rows], local.at[6 + slot])
+
+    for n in range(4):
+        take(n).start()
+    take_weight = pltpu.make_async_copy(weight_hbm, weight, local.at[8])
+    take_weight.start()
+    take_kept = pltpu.make_async_copy(move_ref.at[me], kept, local.at[9])
+    put_kept = pltpu.make_async_copy(kept, move_out.at[me], local.at[10])
+    take_kept.start()
+    enter(devices)
+    moves = [
+        remote(move_ref.at[peer], move_out.at[me], sends.at[k], recvs.at[k], device)
+        for k, (peer, device) in enumerate(zip(peers, devices))
+    ]
+    for move in moves:
+        move.start()
+
+    def grads_step(n, carry):
+        @pl.when(n >= 2)
+        def _():
+            put(n - 2).wait()
+
+        slot = lax.rem(n, 2)
+        take(n).wait()
+        stage[slot, :, :cols] = tn(norm[:, at(n)], grad_ref[...]).astype(BF)
+        stage[slot, :, cols:] = columns_ref[at(n), :]
+        put(n).start()
+        return carry
+
+    lax.fori_loop(0, 4, grads_step, 0)
+    take_kept.wait()
+    put_kept.start()
+    take_weight.wait()
+
+    def back_step(n, carry):
+        @pl.when(n >= 2)
+        def _():
+            put_back(n - 2).wait()
+
+        slot = lax.rem(n, 2)
+        left = grad_ref[pl.ds(pl.multiple_of(n * some, some), some), :]
+
+        def back_block(m, carry):
+            back[slot, :, at(m)] = nt(left, weight[at(m), :cols]).astype(BF)
+            return carry
+
+        lax.fori_loop(0, 4, back_block, 0)
+        put_back(n).start()
+        return carry
+
+    lax.fori_loop(0, 4, back_step, 0)
+    for n in (2, 3):
+        put(n).wait()
+        put_back(n).wait()
+    for move in moves:
+        move.wait()
+    put_kept.wait()
+
+
+def attn_grads_plane(norm, grads, columns, weight, blocks, ident):
+    tokens, width = norm.shape
+    plane = blocks.shape[0]
+    shape = jax.ShapeDtypeStruct
+    hbm = pl.BlockSpec(memory_space=pltpu.HBM)
+    vmem = pl.BlockSpec(memory_space=pltpu.VMEM)
+    return pl.pallas_call(
+        attn_grads_kernel,
+        out_shape=(
+            shape(weight.shape, BF),
+            shape((tokens, width), BF),
+            shape(blocks.shape, blocks.dtype),
+        ),
+        in_specs=[hbm, vmem, vmem, hbm, hbm],
+        out_specs=(hbm,) * 3,
+        scratch_shapes=[
+            pltpu.VMEM(norm.shape, BF),
+            pltpu.VMEM(weight.shape, BF),
+            pltpu.VMEM((2, width // 4, weight.shape[1]), BF),
+            pltpu.VMEM((2, tokens // 4, width), BF),
+            pltpu.VMEM(blocks.shape[1:], blocks.dtype),
+            pltpu.SemaphoreType.DMA((11,)),
+            pltpu.SemaphoreType.DMA((plane - 1,)),
+            pltpu.SemaphoreType.DMA((plane - 1,)),
+        ],
+        cost_estimate=pl.CostEstimate(
+            flops=4 * tokens * width * grads.shape[1],
+            transcendentals=0,
+            bytes_accessed=12 * tokens * width,
+        ),
+        compiler_params=pltpu.CompilerParams(
+            collective_id=ident, has_side_effects=True, vmem_limit_bytes=48 << 20
+        ),
+        name="attn_grads_plane",
+    )(norm, grads, columns, weight, blocks)
 
 
 def finish_kernel(
@@ -1505,12 +1640,16 @@
         out_partial.reshape(-1, width),
         9,
     )
-    attn_partial = jnp.concatenate(
-        [tn(norm1_all, qkv_grad).astype(BF), out_columns], axis=1
-    )
-    scaled1_partial = nt(qkv_grad, qkv_weight).astype(BF)
+    attn_partial, scaled1_partial, first_own = attn_grads_plane(
+        norm1_all,
+        qkv_grad,
+        out_columns,
+        attn_weight,
+        first_sums.reshape(plane, -1, first_sums.shape[1]),
+        11,
+    )
     attn_sums = lax.psum_scatter(attn_partial, "rep", scatter_dimension=0, tiled=True)
-    scaled1 = scatter_plane(after(scaled1_partial, attn_partial, second_sums), 8)
+    scaled1 = scatter_plane(after(scaled1_partial, second_sums), 8)
     input_grad = hidden_grad + scale1 * (
         scaled1 - norm1 * jnp.mean(scaled1 * norm1, axis=-1, keepdims=True)
     )
@@ -1518,14 +1657,13 @@
 
     sums = exchange_all_plane(
         (
-            after(first_sums, input_grad, out_hidden).reshape(plane, -1, first_sums.shape[1]),
-            second_sums.reshape(plane, -1, second_sums.shape[1]),
+            after(second_sums, input_grad, out_hidden).reshape(plane, -1, second_sums.shape[1]),
             attn_sums.reshape(plane, -1, attn_sums.shape[1]),
         ),
         10,
     )
     weights = (w_gate, w_up, w_query, w_key, w_value)
-    gate_grad, up_grad, down_grad, gain2_grad, *attn_grads = finish(*sums, weights, gain2, gain1)
+    gate_grad, up_grad, down_grad, gain2_grad, *attn_grads = finish(first_own, *sums, weights, gain2, gain1)
     query_grad, key_grad, value_grad, out_grad, gain1_grad = attn_grads
     return (
         out_hidden[None],

time: 577 us -> 563 us (0.976)
  matrix products: 17.3 us -> 0 us
  waiting for transfers between devices: 1.78 us -> 9.96 us
  local copies, waits for them, and re-layouts: 37.1 us -> 29.6 us
    dot_general x2 -> x0, matrix products: 17.3 us -> none  [dot(): lax.dot_general(left, right, ((contract[:1], contract[1:]), ((), ())), pr...]
    pallas_call x0 -> x1, Pallas kernels: none -> 17.2 us  [attn_grads_plane(): pl.pallas_call(attn_grads_kernel, out_shape=(shape(weight.shape, BF), sha...]
    pallas_call x1, Pallas kernels: 39 us -> 25.8 us  [exchange_all_plane(): pl.pallas_call(exchange_all_kernel, out_shape=tuple((jax.ShapeDtypeStruct...]
    reduce_scatter x1, waiting for transfers between devices: 1.63 us -> 9.81 us  [per_device(): lax.psum_scatter(attn_partial, 'rep', scatter_dimension=0, tiled=True)]
    unnamed x80, local copies, waits for them, and re-layouts: 26.3 us -> 20.4 us
  transfers between devices with their start and end apart: 7 -> 7, of which waited for: 1 -> 1; matrix products, arithmetic and copies ran while one was open for 8% -> 5% of each run, Pallas kernels for 72% -> 77%
where the time goes in v13:
time: 563 us; the launch traced here: 556 us
  Pallas kernels  474 us (84%)
  local copies, waits for them, and re-layouts  29.6 us (5%)
  other arithmetic  25.9 us (5%)
  between operations  15 us (3%)
  waiting for transfers between devices  9.96 us (2%)
    pallas_call x2, Pallas kernels, scatter_plane(): pl.pallas_call(scatter_kernel, out_shape=jax.ShapeDtypeStruct((rows, widt...  82.4 us
    pallas_call x1, Pallas kernels, ffn_first_plane(): pl.pallas_call(ffn_first_kernel, out_shape=(shape((plane, rows, width), B...  66.1 us
    pallas_call x1, Pallas kernels, ffn_second_plane(): pl.pallas_call(ffn_second_kernel, out_shape=(shape((plane, rows, width),...  62.1 us
    pallas_call x1, Pallas kernels, spread_plane(): pl.pallas_call(spread_kernel, out_shape=(jax.ShapeDtypeStruct((plane, row...  53.2 us
    pallas_call x1, Pallas kernels, gather_mix_plane(): pl.pallas_call(gather_mix_kernel, out_shape=(shape((plane, rows, width),...  44.9 us
    pallas_call x1, Pallas kernels, attn_back_plane(): pl.pallas_call(attn_back_kernel, out_shape=(jax.ShapeDtypeStruct((tokens,...  43.5 us
    pallas_call x1, Pallas kernels, attn_front_plane(): pl.pallas_call(attn_front_kernel, out_shape=(shape((tokens, q_part + 2 *...  43.2 us
    pallas_call x2, Pallas kernels, exchange_plane(): pl.pallas_call(exchange_kernel, out_shape=jax.ShapeDtypeStruct(blocks.sha...  30.4 us
  transfers between devices with their start and end apart: 7, of which 1 were waited for; matrix products, arithmetic and copies ran while one was open for 5% of the time, Pallas kernels for 77%

profile of v13, /device:TPU:1, one launch (start us, length us, event | category | flops | bytes accessed | tf_op | source)
XLA Modules:
  0.0 556.3 jit_solution(17115075240523208509)
XLA Ops:
  7.2 1.1 multiply_convert_fusion.4
  8.3 1.0 multiply_convert_fusion.6
  9.4 1.0 bitcast_bitcast_fusion
  10.5 1.0 pad_maximum_fusion.2.in_ref
  11.4 13.7 %exchange_plane.2 = bf16[8,64,768]{2,1,0:T(8,128)(2,1)} custom-call(bf16[8,64,768]{2,1,0:T(8,128)(2,1)} %pad_maximum_fusion.2.in_ref), custom_call_target="tpu_custom_call" | custom-call | bytes 15728640 | tf_op jit(solution)/shard_map/exchange_plane/pallas_call | solution.py:751
  25.2 0.3 multiply_convert_fusion.3
  25.5 0.7 reshape.120
  26.2 0.1 copy.50
  26.4 0.8 slice.28
  27.1 0.7 reshape.121
  27.8 0.1 copy.49
  28.0 0.8 slice.29
  28.7 1.8 reshape.122
  30.6 0.1 copy.48
  30.8 0.9 copy-done.33
  31.7 2.2 pad_maximum_fusion.in_ref
  33.9 16.7 %exchange_plane.3 = bf16[8,64,1152]{2,1,0:T(8,128)(2,1)} custom-call(bf16[8,64,1152]{2,1,0:T(8,128)(2,1)} %pad_maximum_fusion.in_ref), custom_call_target="tpu_custom_call" | custom-call | bytes 23592960 | tf_op jit(solution)/shard_map/exchange_plane/pallas_call | solution.py:751
  50.8 1.1 slice.33
  51.9 0.3 fusion.8
  52.2 1.2 fusion.2.own_ref
  53.4 1.3 pad_maximum_fusion.1.move_ref
  54.7 53.2 %spread_plane.1 = (bf16[8,256,2048]{2,1,0:T(8,128)(2,1)}, bf16[8,64,960]{2,1,0:T(8,128)(2,1)}) custom-call(bf16[256,2048]{1,0:T(8,128)(2,1)} %fusion.2.own_ref, bf16[8,64,960]{2,1,0:T(8,128)(2,1)} %pad_maximum_fusion.1.move_ref), custom_call_target="tpu_custom_call" | custom-call | bytes 134217728 | tf_op jit(solution)/shard_map/spread_plane/pallas_call | solution.py:291
  108.0 1.2 collective-permute-start
  109.3 1.9 fusion.9
  111.2 0.3 pad_maximum_fusion.3
  111.6 0.2 fusion.3.own_ref
  111.9 1.9 copy-done
  113.9 43.2 %attn_front_plane.1 = (bf16[2048,512]{1,0:T(8,128)(2,1)S(1)}, bf16[2048,256]{1,0:T(8,128)(2,1)S(1)}, f32[4,1,1024]{2,1,0:T(1,128)S(1)}, bf16[2048,2048]{1,0:T(8,128)(2,1)}, bf16[8,256,2048]{2,1,0:T(8,128)(2,1)}) custom-call(s32[2,2]{1,0:T(2,128)S(1)} %add_select_fusion.starts_ref, bf16[2048,2048]{1,0:T(8,128)(2,1)} %bitcast.58, ...), custom_call_target="tpu_custom_call" | custom-call | flops 2147483648 | bytes 100663296 | tf_op jit(solution)/shard_map/attn_front_plane/pallas_call | solution.py:583
  157.1 1.3 copy-done.16
  158.4 1.0 copy-done.18
  159.4 41.2 %scatter_plane.2 = f32[256,2048]{1,0:T(8,128)} custom-call(bf16[8,256,2048]{2,1,0:T(8,128)(2,1)} %bitcast.57), custom_call_target="tpu_custom_call" | custom-call | bytes 117440512 | tf_op jit(solution)/shard_map/scatter_plane/pallas_call | solution.py:424
  200.6 2.1 multiply_reduce_fusion.1
  202.7 1.4 copy-done.23
  204.1 1.1 multiply_convert_fusion.1.own_ref
  205.2 66.1 %ffn_first_plane.1 = (bf16[8,256,2048]{2,1,0:T(8,128)(2,1)}, bf16[8,256,2048]{2,1,0:T(8,128)(2,1)}, bf16[8,256,2048]{2,1,0:T(8,128)(2,1)}, bf16[2048,1152]{1,0:T(8,128)(2,1)}) custom-call(bf16[256,2048]{1,0:T(8,128)(2,1)} %multiply_convert_fusion.1.own_ref, bf16[8,256,2048]{2,1,0:T(8,128)(2,1)} %get-tuple-element.53.grad_ref, ...), custom_call_target="tpu_custom_call" | custom-call | flops 28991029248 | bytes 92274688 | tf_op jit(solution)/shard_map/ffn_first_plane/pallas_call | solution.py:1174
  271.4 62.1 %ffn_second_plane.1 = (bf16[8,256,2048]{2,1,0:T(8,128)(2,1)}, bf16[2048,960]{1,0:T(8,128)(2,1)}, f32[256,2048]{1,0:T(8,128)}) custom-call(bf16[8,256,2048]{2,1,0:T(8,128)(2,1)} %get-tuple-element.54.all_ref, bf16[8,256,2048]{2,1,0:T(8,128)(2,1)} %get-tuple-element.53.grad_ref, bf16[2048,960]{1,0:T(8,128)(2,1)} %all-gather.8.cloned.1.call-done.weight_hbm, ...), custom_call_target="tpu_custom_call" | custom-call | flops 24159191040 | bytes 92274688 | tf_op jit(solution)/shard_map/ffn_second_plane/pallas_call | solution.py:1218
  333.5 1.4 slice.34.weight_ref
  335.0 0.4 copy-done.24
  335.4 2.1 multiply_reduce_fusion
  337.5 0.1 copy-done.29
  337.6 0.3 copy-done.31
  338.0 0.7 multiply_convert_fusion.own_ref
  338.7 0.5 copy-done.19
  339.2 44.9 %gather_mix_plane.1 = (bf16[8,256,2048]{2,1,0:T(8,128)(2,1)}, bf16[2048,256]{1,0:T(8,128)(2,1)S(1)}, bf16[2048,256]{1,0:T(8,128)(2,1)S(1)}) custom-call(bf16[256,2048]{1,0:T(8,128)(2,1)S(1)} %multiply_convert_fusion.own_ref, bf16[2048,256]{1,0:T(8,128)(2,1)S(1)} %copy-done.19, bf16[2048,256]{1,0:T(8,128)(2,1)S(1)} %slice.34.weight_ref), custom_call_target="tpu_custom_call" | custom-call | flops 4294967296 | bytes 100663296 | tf_op jit(solution)/shard_map/gather_mix_plane/pallas_call | solution.py:226
  384.1 1.0 copy-done.21
  385.1 43.5 %attn_back_plane.1 = (bf16[2048,512]{1,0:T(8,128)(2,1)}, f32[256,2048]{1,0:T(8,128)}) custom-call(s32[2,2]{1,0:T(2,128)S(1)} %add_select_fusion.starts_ref, bf16[2048,512]{1,0:T(8,128)(2,1)} %copy-done.16, bf16[2048,256]{1,0:T(8,128)(2,1)S(1)} %get-tuple-element.62.g_ref, f32[4,1,1024]{2,1,0:T(1,128)S(1)} %get-tuple-element.63.log_ref, ...), custom_call_target="tpu_custom_call" | custom-call | flops 5368709120 | bytes 117440512 | tf_op jit(solution)/shard_map/attn_back_plane/pallas_call | solution.py:698
  428.7 1.6 copy-done.20
  430.2 17.2 %attn_grads_plane.1 = (bf16[2048,768]{1,0:T(8,128)(2,1)}, bf16[2048,2048]{1,0:T(8,128)(2,1)}, bf16[8,64,1152]{2,1,0:T(8,128)(2,1)S(1)}) custom-call(bf16[2048,2048]{1,0:T(8,128)(2,1)} %bitcast.59, bf16[2048,512]{1,0:T(8,128)(2,1)S(1)} %copy-done.20, bf16[2048,256]{1,0:T(8,128)(2,1)S(1)} %copy-done.22, ...), custom_call_target="tpu_custom_call" | custom-call | flops 8589934592 | bytes 50331648 | tf_op jit(solution)/shard_map/attn_grads_plane/pallas_call | solution.py:1409
  447.5 0.5 copy-done.35
  448.2 41.2 %scatter_plane.3 = f32[256,2048]{1,0:T(8,128)} custom-call(bf16[8,256,2048]{2,1,0:T(8,128)(2,1)} %bitcast.56), custom_call_target="tpu_custom_call" | custom-call | bytes 117440512 | tf_op jit(solution)/shard_map/scatter_plane/pallas_call | solution.py:424
  489.4 2.2 fusion.4
  491.6 0.3 copy-done.32
  491.9 5.7 %fusion.7 = (f32[256,2048]{1,0:T(8,128)}, bf16[256,2048]{1,0:T(8,128)(2,1)}) fusion(f32[256,2048]{1,0:T(8,128)} %scatter_plane.3, bf16[1,256,2048]{2,1,0:T(8,128)(2,1)S(1)} %copy-done.28, f32[256]{0:T(256)S(1)} %broadcast_multiply_fusion, f32[256]{0:T(256)S(1)} %add_rsqrt_fusion.1, f32[256,2048]{1,0:T(8,128)} %get-tuple-element.58, ...), kind=kLoop, calls=%fused_computation.12 | loop fusion | flops 7864320 | bytes 13636608 | tf_op jit(solution)/shard_map/add | solution.py:1653
  497.6 9.8 %reduce-scatter.8.cloned.1.call-done = bf16[512,768]{1,0:T(8,128)(2,1)} async-done(((bf16[2048,768]{1,0:T(8,128)(2,1)}), bf16[512,768]{1,0:T(8,128)(2,1)}) %reduce-scatter.8.cloned.1.call-update) | async-done | bytes 786448 | tf_op jit(solution)/shard_map/reduce_scatter | solution.py:1651
  507.4 25.8 %exchange_all_plane.1 = (bf16[8,64,960]{2,1,0:T(8,128)(2,1)}, bf16[8,64,768]{2,1,0:T(8,128)(2,1)}) custom-call(bf16[8,64,960]{2,1,0:T(8,128)(2,1)} %bitcast.70, bf16[8,64,768]{2,1,0:T(8,128)(2,1)} %bitcast.73), custom_call_target="tpu_custom_call" | custom-call | bytes 35389440 | tf_op jit(solution)/shard_map/exchange_all_plane/pallas_call | solution.py:1287
  533.3 1.2 copy-done.9
  534.5 1.1 copy-done.13
  535.6 5.5 finish.1
  541.2 1.5 copy-done.4
  542.7 1.0 copy-done.11
  543.7 3.2 copy.40
  546.8 1.1 copy.39
  548.0 0.6 reduce
  548.6 0.6 reduce.1
  (98 shorter events, 1.1 us)
Async XLA Ops:
  7.2 104.7 %all-gather.4.cloned.1.call-start = ((), (), s32[]{:S(2)}) async-start(), calls=%async_computation.3 | async-start | bytes 3932160 | tf_op jit(solution)/shard_map/all_gather | solution.py:1572
  10.4 14.8 %copy-start.1 = (bf16[64,5632]{1,0:T(8,128)(2,1)S(1)}, bf16[64,5632]{1,0:T(8,128)(2,1)}, u32[]{:S(2)}) copy-start(bf16[64,5632]{1,0:T(8,128)(2,1)} %gate_weight.1) | copy-start | bytes 2162692
  10.4 14.8 %copy-start.2 = (bf16[64,5632]{1,0:T(8,128)(2,1)S(1)}, bf16[64,5632]{1,0:T(8,128)(2,1)}, u32[]{:S(2)}) copy-start(bf16[64,5632]{1,0:T(8,128)(2,1)} %up_weight.1) | copy-start | bytes 2162692
  10.4 14.8 %copy-start.36 = (f32[64]{0:T(128)S(1)}, f32[64]{0:T(128)}, u32[]{:S(2)}) copy-start(f32[64]{0:T(128)} %param.21) | copy-start | bytes 772
  25.2 180.1 %all-gather.6.cloned.1.call-start = ((), (), s32[]{:S(2)}) async-start(), calls=%async_computation.4 | async-start | bytes 5898240 | tf_op jit(solution)/shard_map/all_gather | solution.py:1596
  30.6 1.1 copy-start.34
  30.8 0.9 copy-start.33
  50.6 1.3 copy-start.26
  50.6 220.8 %all-gather.8.cloned.1.call-start = ((), (), s32[]{:S(2)}) async-start(), calls=%async_computation.5 | async-start | bytes 5242880 | tf_op jit(solution)/shard_map/all_gather | solution.py:1597
  54.7 53.3 %copy-start.38 = (s32[1,2]{1,0:T(1,128)S(1)}, s32[1,2]{1,0:T(1,128)}, u32[]{:S(2)}) copy-start(s32[1,2]{1,0:T(1,128)} %param.14) | copy-start | bytes 28
  108.0 277.1 %reduce-scatter.4.cloned.1.call-start = ((), (), s32[]{:S(2)}) async-start(), calls=%async_computation.6 | async-start | bytes 5898240 | tf_op jit(solution)/shard_map/reduce_scatter | solution.py:1621
  108.0 3.8 collective-permute-start
  109.3 2.3 copy-start.37
  109.3 2.3 copy-start.30
  111.6 45.5 %copy-start.5 = (f32[1024,128]{1,0:T(8,128)}, f32[1024,128]{1,0:T(8,128)S(1)}, u32[]{:S(2)}) copy-start(f32[1024,128]{1,0:T(8,128)S(1)} %get-tuple-element.120.cos_ref) | copy-start | bytes 1572868
  111.6 45.5 %copy-start.7 = (f32[1024,128]{1,0:T(8,128)}, f32[1024,128]{1,0:T(8,128)S(1)}, u32[]{:S(2)}) copy-start(f32[1024,128]{1,0:T(8,128)S(1)} %get-tuple-element.121.sin_ref) | copy-start | bytes 1572868
  111.9 1.9 copy-start
  157.1 1.3 copy-start.16
  158.4 1.0 copy-start.18
  159.4 41.2 %copy-start.27 = (bf16[1,256,2048]{2,1,0:T(8,128)(2,1)S(1)}, bf16[1,256,2048]{2,1,0:T(8,128)(2,1)}, u32[]{:S(2)}) copy-start(bf16[1,256,2048]{2,1,0:T(8,128)(2,1)} %param.13) | copy-start | bytes 3145732
  202.7 1.4 copy-start.23
  271.3 176.9 %reduce-scatter.6.cloned.1.call-start = ((), (), s32[]{:S(2)}) async-start(), calls=%async_computation.7 | async-start | bytes 5242880 | tf_op jit(solution)/shard_map/reduce_scatter | solution.py:1625
  333.5 1.9 copy-start.24
  333.5 173.9 %reduce-scatter.8.cloned.1.call-start = ((), (), s32[]{:S(2)}) async-start(), calls=%async_computation.8 | async-start | bytes 3932160 | tf_op jit(solution)/shard_map/reduce_scatter | solution.py:1651
  335.4 2.2 copy-start.29
  335.4 2.5 copy-start.31
  337.9 1.2 copy-start.19
  339.2 45.9 %copy-start.6 = (f32[1024,128]{1,0:T(8,128)S(1)}, f32[1024,128]{1,0:T(8,128)}, u32[]{:S(2)}) copy-start(f32[1024,128]{1,0:T(8,128)} %copy-done.5) | copy-start | bytes 1572868
  339.2 45.9 %copy-start.8 = (f32[1024,128]{1,0:T(8,128)S(1)}, f32[1024,128]{1,0:T(8,128)}, u32[]{:S(2)}) copy-start(f32[1024,128]{1,0:T(8,128)} %copy-done.7) | copy-start | bytes 1572868
  384.1 1.0 copy-start.21
  385.1 43.5 %copy-start.17 = (bf16[512,1152]{1,0:T(8,128)(2,1)S(1)}, bf16[512,1152]{1,0:T(8,128)(2,1)}, u32[]{:S(2)}) copy-start(bf16[512,1152]{1,0:T(8,128)(2,1)} %reduce-scatter.4.cloned.1.call-done) | copy-start | bytes 3538948
  385.1 43.5 %copy-start.22 = (bf16[2048,256]{1,0:T(8,128)(2,1)S(1)}, bf16[2048,256]{1,0:T(8,128)(2,1)}, u32[]{:S(2)}) copy-start(bf16[2048,256]{1,0:T(8,128)(2,1)} %copy-done.21) | copy-start | bytes 3145732
  428.6 1.6 copy-start.20
  447.4 0.7 copy-start.35
  448.2 41.2 %copy-start.28 = (bf16[1,256,2048]{2,1,0:T(8,128)(2,1)S(1)}, bf16[1,256,2048]{2,1,0:T(8,128)(2,1)}, u32[]{:S(2)}) copy-start(bf16[1,256,2048]{2,1,0:T(8,128)(2,1)} %param.13) | copy-start | bytes 3145732
  489.4 2.2 copy-start.25
  489.4 2.5 copy-start.32
  491.9 41.3 %copy-start.10 = (bf16[64,2048]{1,0:T(8,128)(2,1)S(1)}, bf16[64,2048]{1,0:T(8,128)(2,1)}, u32[]{:S(2)}) copy-start(bf16[64,2048]{1,0:T(8,128)(2,1)} %query_weight.1) | copy-start | bytes 786436
  491.9 41.3 %copy-start.14 = (bf16[64,512]{1,0:T(8,128)(2,1)S(1)}, bf16[64,512]{1,0:T(8,128)(2,1)}, u32[]{:S(2)}) copy-start(bf16[64,512]{1,0:T(8,128)(2,1)} %key_weight.1) | copy-start | bytes 196612
  491.9 41.3 %copy-start.15 = (bf16[64,512]{1,0:T(8,128)(2,1)S(1)}, bf16[64,512]{1,0:T(8,128)(2,1)}, u32[]{:S(2)}) copy-start(bf16[64,512]{1,0:T(8,128)(2,1)} %value_weight.1) | copy-start | bytes 196612
  497.6 35.6 %copy-start.3 = (bf16[64,5632]{1,0:T(8,128)(2,1)S(1)}, bf16[64,5632]{1,0:T(8,128)(2,1)}, u32[]{:S(2)}) copy-start(bf16[64,5632]{1,0:T(8,128)(2,1)} %up_weight.1) | copy-start | bytes 2162692
  533.3 1.2 copy-start.9
  534.5 1.1 copy-start.13
  541.2 1.6 copy-start.4
  542.7 1.0 copy-start.11
  543.7 3.2 copy-start.12
Sparse Core Ops, SparseCore 0:
  25.3 63.8 all-gather.3
  90.7 88.1 all-gather.5
  180.5 79.0 all-gather.7
  271.4 85.1 reduce-scatter.3
  358.8 77.0 reduce-scatter.5
  447.6 59.8 reduce-scatter.7

commit v14 on v13

--- a/solution.py
+++ b/solution.py
@@ -1471,7 +1471,7 @@
                 own = ref[j, :, k * size : (k + 1) * size].astype(F32)
                 out[:, at] = own * gain
                 total = total + jnp.sum(own * weight[:, at].astype(F32), axis=1, keepdims=True)
-            down_out[at, :] = ref[j, :, 2 * size :].astype(F32).T
+            down_out[:, at] = ref[j, :, 2 * size :].astype(F32)
     gain2_out[...] = total
 
     gain = gain1_ref[...]
@@ -1483,7 +1483,7 @@
         own = attn_in[j, :, :q_part].astype(F32)
         query_out[:, at] = own * gain
         total = total + jnp.sum(own * query_weight[:, at].astype(F32), axis=1, keepdims=True)
-        out_out[at, :] = attn_in[j, :, q_part + 2 * DH :].astype(F32).T
+        out_out[:, at] = attn_in[j, :, q_part + 2 * DH :].astype(F32)
     for j in range(KV):
         at = slice(j * DH, (j + 1) * DH)
         for k, (out, weight) in enumerate(((key_out, key_weight), (value_out, value_weight))):
@@ -1501,11 +1501,10 @@
     shape = jax.ShapeDtypeStruct
     vmem = pl.BlockSpec(memory_space=pltpu.VMEM)
     gate, up, query, key, value = (shape(w.shape, F32) for w in weights)
-    down, out = (shape(w.shape[::-1], F32) for w in (gate, query))
     column = shape((rows, 1), F32)
     return pl.pallas_call(
         finish_kernel,
-        out_shape=(gate, up, down, column, query, key, value, out, column),
+        out_shape=(gate, up, gate, column, query, key, value, query, column),
         in_specs=[vmem] * 10,
         out_specs=(vmem,) * 9,
         cost_estimate=pl.CostEstimate(
@@ -1655,15 +1654,17 @@
     )
     out_hidden = (hidden + keep * ffn_out).astype(BF)
 
-    sums = exchange_all_plane(
-        (
-            after(second_sums, input_grad, out_hidden).reshape(plane, -1, second_sums.shape[1]),
-            attn_sums.reshape(plane, -1, attn_sums.shape[1]),
-        ),
-        10,
+    (second_own,) = exchange_all_plane(
+        (after(second_sums, scaled1).reshape(plane, -1, second_sums.shape[1]),), 10
+    )
+    (attn_own,) = exchange_all_plane(
+        (after(attn_sums, second_own, input_grad, out_hidden).reshape(plane, -1, attn_sums.shape[1]),),
+        12,
     )
     weights = (w_gate, w_up, w_query, w_key, w_value)
-    gate_grad, up_grad, down_grad, gain2_grad, *attn_grads = finish(first_own, *sums, weights, gain2, gain1)
+    gate_grad, up_grad, down_grad, gain2_grad, *attn_grads = finish(
+        first_own, second_own, attn_own, weights, gain2, gain1
+    )
     query_grad, key_grad, value_grad, out_grad, gain1_grad = attn_grads
     return (
         out_hidden[None],
@@ -1672,11 +1673,11 @@
         query_grad,
         key_grad,
         value_grad,
-        out_grad,
+        out_grad.T,
         gain2_grad[:, 0],
         gate_grad,
         up_grad,
-        down_grad,
+        down_grad.T,
     )
 
 

time: 563 us -> 555 us (0.986)
  waiting for transfers between devices: 9.96 us -> 0.15 us
    reduce_scatter x1, waiting for transfers between devices: 9.81 us -> 0.01 us  [per_device(): lax.psum_scatter(attn_partial, 'rep', scatter_dimension=0, tiled=True)]
    pallas_call x1 -> x2, Pallas kernels: 25.8 us -> 29.8 us  [exchange_all_plane(): pl.pallas_call(exchange_all_kernel, out_shape=tuple((jax.ShapeDtypeStruct...]
  transfers between devices with their start and end apart: 7 -> 7, of which waited for: 1 -> 0; matrix products, arithmetic and copies ran while one was open for 5% -> 6% of each run, Pallas kernels for 77% -> 81%
where the time goes in v14:
time: 555 us; the launch traced here: 548 us
  Pallas kernels  479 us (86%)
  local copies, waits for them, and re-layouts  26.5 us (5%)
  other arithmetic  25.9 us (5%)
  between operations  15.1 us (3%)
    pallas_call x2, Pallas kernels, scatter_plane(): pl.pallas_call(scatter_kernel, out_shape=jax.ShapeDtypeStruct((rows, widt...  82.6 us
    pallas_call x1, Pallas kernels, ffn_first_plane(): pl.pallas_call(ffn_first_kernel, out_shape=(shape((plane, rows, width), B...  66.1 us
    pallas_call x1, Pallas kernels, ffn_second_plane(): pl.pallas_call(ffn_second_kernel, out_shape=(shape((plane, rows, width),...  62 us
    pallas_call x1, Pallas kernels, spread_plane(): pl.pallas_call(spread_kernel, out_shape=(jax.ShapeDtypeStruct((plane, row...  53.2 us
    pallas_call x1, Pallas kernels, gather_mix_plane(): pl.pallas_call(gather_mix_kernel, out_shape=(shape((plane, rows, width),...  44.9 us
    pallas_call x1, Pallas kernels, attn_back_plane(): pl.pallas_call(attn_back_kernel, out_shape=(jax.ShapeDtypeStruct((tokens,...  43.6 us
    pallas_call x1, Pallas kernels, attn_front_plane(): pl.pallas_call(attn_front_kernel, out_shape=(shape((tokens, q_part + 2 *...  43.2 us
    pallas_call x2, Pallas kernels, exchange_plane(): pl.pallas_call(exchange_kernel, out_shape=jax.ShapeDtypeStruct(blocks.sha...  30.4 us
  transfers between devices with their start and end apart: 7, of which 0 were waited for; matrix products, arithmetic and copies ran while one was open for 6% of the time, Pallas kernels for 81%

profile of v14, /device:TPU:1, one launch (start us, length us, event | category | flops | bytes accessed | tf_op | source)
XLA Modules:
  0.0 547.8 jit_solution(17408904542789863463)
XLA Ops:
  7.2 1.1 multiply_convert_fusion.4
  8.3 1.0 multiply_convert_fusion.6
  9.4 1.0 bitcast_bitcast_fusion
  10.5 1.0 pad_maximum_fusion.2.in_ref
  11.4 13.7 %exchange_plane.2 = bf16[8,64,768]{2,1,0:T(8,128)(2,1)} custom-call(bf16[8,64,768]{2,1,0:T(8,128)(2,1)} %pad_maximum_fusion.2.in_ref), custom_call_target="tpu_custom_call" | custom-call | bytes 15728640 | tf_op jit(solution)/shard_map/exchange_plane/pallas_call | solution.py:751
  25.2 1.2 multiply_convert_fusion.3
  26.4 0.7 reshape.120
  27.1 0.1 copy.46
  27.3 1.9 reshape.121
  29.1 0.1 copy.45
  29.3 0.8 slice.29
  30.1 1.8 reshape.122
  31.9 0.1 copy.44
  32.1 0.9 copy-done.34
  33.0 1.2 pad_maximum_fusion.in_ref
  34.2 16.7 %exchange_plane.3 = bf16[8,64,1152]{2,1,0:T(8,128)(2,1)} custom-call(bf16[8,64,1152]{2,1,0:T(8,128)(2,1)} %pad_maximum_fusion.in_ref), custom_call_target="tpu_custom_call" | custom-call | bytes 23592960 | tf_op jit(solution)/shard_map/exchange_plane/pallas_call | solution.py:751
  51.1 1.1 slice.33
  52.2 0.3 fusion.8
  52.5 1.2 fusion.2.own_ref
  53.8 1.3 pad_maximum_fusion.1.move_ref
  55.0 53.2 %spread_plane.1 = (bf16[8,256,2048]{2,1,0:T(8,128)(2,1)}, bf16[8,64,960]{2,1,0:T(8,128)(2,1)}) custom-call(bf16[256,2048]{1,0:T(8,128)(2,1)} %fusion.2.own_ref, bf16[8,64,960]{2,1,0:T(8,128)(2,1)} %pad_maximum_fusion.1.move_ref), custom_call_target="tpu_custom_call" | custom-call | bytes 134217728 | tf_op jit(solution)/shard_map/spread_plane/pallas_call | solution.py:291
  108.4 1.2 collective-permute-start
  109.6 1.9 fusion.9
  111.5 0.3 pad_maximum_fusion.3
  111.9 0.2 fusion.3.own_ref
  112.3 1.9 copy-done
  114.2 43.2 %attn_front_plane.1 = (bf16[2048,512]{1,0:T(8,128)(2,1)S(1)}, bf16[2048,256]{1,0:T(8,128)(2,1)S(1)}, f32[4,1,1024]{2,1,0:T(1,128)S(1)}, bf16[2048,2048]{1,0:T(8,128)(2,1)}, bf16[8,256,2048]{2,1,0:T(8,128)(2,1)}) custom-call(s32[2,2]{1,0:T(2,128)S(1)} %add_select_fusion.starts_ref, bf16[2048,2048]{1,0:T(8,128)(2,1)} %bitcast.60, ...), custom_call_target="tpu_custom_call" | custom-call | flops 2147483648 | bytes 100663296 | tf_op jit(solution)/shard_map/attn_front_plane/pallas_call | solution.py:583
  157.5 1.3 copy-done.15
  158.8 1.0 copy-done.17
  159.7 41.2 %scatter_plane.2 = f32[256,2048]{1,0:T(8,128)} custom-call(bf16[8,256,2048]{2,1,0:T(8,128)(2,1)} %bitcast.59), custom_call_target="tpu_custom_call" | custom-call | bytes 117440512 | tf_op jit(solution)/shard_map/scatter_plane/pallas_call | solution.py:424
  201.0 2.1 multiply_reduce_fusion.1
  203.1 1.4 copy-done.24
  204.4 1.1 multiply_convert_fusion.1.own_ref
  205.6 66.1 %ffn_first_plane.1 = (bf16[8,256,2048]{2,1,0:T(8,128)(2,1)}, bf16[8,256,2048]{2,1,0:T(8,128)(2,1)}, bf16[8,256,2048]{2,1,0:T(8,128)(2,1)}, bf16[2048,1152]{1,0:T(8,128)(2,1)}) custom-call(bf16[256,2048]{1,0:T(8,128)(2,1)} %multiply_convert_fusion.1.own_ref, bf16[8,256,2048]{2,1,0:T(8,128)(2,1)} %get-tuple-element.52.grad_ref, ...), custom_call_target="tpu_custom_call" | custom-call | flops 28991029248 | bytes 92274688 | tf_op jit(solution)/shard_map/ffn_first_plane/pallas_call | solution.py:1174
  271.8 62.0 %ffn_second_plane.1 = (bf16[8,256,2048]{2,1,0:T(8,128)(2,1)}, bf16[2048,960]{1,0:T(8,128)(2,1)}, f32[256,2048]{1,0:T(8,128)}) custom-call(bf16[8,256,2048]{2,1,0:T(8,128)(2,1)} %get-tuple-element.53.all_ref, bf16[8,256,2048]{2,1,0:T(8,128)(2,1)} %get-tuple-element.52.grad_ref, bf16[2048,960]{1,0:T(8,128)(2,1)} %all-gather.8.cloned.1.call-done.weight_hbm, ...), custom_call_target="tpu_custom_call" | custom-call | flops 24159191040 | bytes 92274688 | tf_op jit(solution)/shard_map/ffn_second_plane/pallas_call | solution.py:1218
  333.9 1.4 slice.34.weight_ref
  335.3 0.4 copy-done.25
  335.8 2.1 multiply_reduce_fusion
  337.9 0.1 copy-done.30
  338.0 0.3 copy-done.32
  338.3 0.7 multiply_convert_fusion.own_ref
  339.0 0.5 copy-done.18
  339.5 44.9 %gather_mix_plane.1 = (bf16[8,256,2048]{2,1,0:T(8,128)(2,1)}, bf16[2048,256]{1,0:T(8,128)(2,1)S(1)}, bf16[2048,256]{1,0:T(8,128)(2,1)S(1)}) custom-call(bf16[256,2048]{1,0:T(8,128)(2,1)S(1)} %multiply_convert_fusion.own_ref, bf16[2048,256]{1,0:T(8,128)(2,1)S(1)} %copy-done.18, bf16[2048,256]{1,0:T(8,128)(2,1)S(1)} %slice.34.weight_ref), custom_call_target="tpu_custom_call" | custom-call | flops 4294967296 | bytes 100663296 | tf_op jit(solution)/shard_map/gather_mix_plane/pallas_call | solution.py:226
  384.5 1.0 copy-done.20
  385.5 1.0 copy-done.22
  386.4 1.2 copy-done.21
  387.7 43.6 %attn_back_plane.1 = (bf16[2048,512]{1,0:T(8,128)(2,1)}, f32[256,2048]{1,0:T(8,128)}) custom-call(s32[2,2]{1,0:T(2,128)S(1)} %add_select_fusion.starts_ref, bf16[2048,512]{1,0:T(8,128)(2,1)} %copy-done.15, bf16[2048,256]{1,0:T(8,128)(2,1)S(1)} %copy-done.21, f32[4,1,1024]{2,1,0:T(1,128)S(1)} %get-tuple-element.62.log_ref, f32[1024,128]{1,0:T(8,128)S(1)} %copy-done.7, ...), custom_call_target="tpu_custom_call" | custom-call | flops 5368709120 | bytes 117440512 | tf_op jit(solution)/shard_map/attn_back_plane/pallas_call | solution.py:698
  431.3 1.6 copy-done.19
  432.8 17.1 %attn_grads_plane.1 = (bf16[2048,768]{1,0:T(8,128)(2,1)}, bf16[2048,2048]{1,0:T(8,128)(2,1)}, bf16[8,64,1152]{2,1,0:T(8,128)(2,1)S(1)}) custom-call(bf16[2048,2048]{1,0:T(8,128)(2,1)} %bitcast.61, bf16[2048,512]{1,0:T(8,128)(2,1)S(1)} %copy-done.19, bf16[2048,256]{1,0:T(8,128)(2,1)S(1)} %copy-done.23, ...), custom_call_target="tpu_custom_call" | custom-call | flops 8589934592 | bytes 50331648 | tf_op jit(solution)/shard_map/attn_grads_plane/pallas_call | solution.py:1409
  450.0 1.0 copy-done.10
  451.0 0.1 copy.35.gain2_ref
  451.1 0.5 copy-done.36
  451.6 0.1 copy.36.gain1_ref
  451.7 41.3 %scatter_plane.3 = f32[256,2048]{1,0:T(8,128)} custom-call(bf16[8,256,2048]{2,1,0:T(8,128)(2,1)} %bitcast.58), custom_call_target="tpu_custom_call" | custom-call | bytes 117440512 | tf_op jit(solution)/shard_map/scatter_plane/pallas_call | solution.py:424
  493.1 16.9 %exchange_all_plane.2.second_in = bf16[8,64,960]{2,1,0:T(8,128)(2,1)} custom-call(bf16[8,64,960]{2,1,0:T(8,128)(2,1)} %bitcast.73), custom_call_target="tpu_custom_call" | custom-call | bytes 19660800 | tf_op jit(solution)/shard_map/exchange_all_plane/pallas_call | solution.py:1287
  510.0 2.2 fusion.4
  512.3 0.3 copy-done.33
  512.6 5.8 %fusion.7 = (f32[256,2048]{1,0:T(8,128)}, bf16[256,2048]{1,0:T(8,128)(2,1)}) fusion(f32[256,2048]{1,0:T(8,128)} %scatter_plane.3, bf16[1,256,2048]{2,1,0:T(8,128)(2,1)S(1)} %copy-done.29, f32[256]{0:T(256)S(1)} %broadcast_multiply_fusion, f32[256]{0:T(256)S(1)} %add_rsqrt_fusion.1, f32[256,2048]{1,0:T(8,128)} %get-tuple-element.57, ...), kind=kLoop, calls=%fused_computation.12 | loop fusion | flops 7864320 | bytes 13636608 | tf_op jit(solution)/shard_map/add | solution.py:1652
  518.3 12.9 %exchange_all_plane.3.attn_in = bf16[8,64,768]{2,1,0:T(8,128)(2,1)} custom-call(bf16[8,64,768]{2,1,0:T(8,128)(2,1)} %bitcast.75), custom_call_target="tpu_custom_call" | custom-call | bytes 15728640 | tf_op jit(solution)/shard_map/exchange_all_plane/pallas_call | solution.py:1287
  531.3 1.1 copy-done.2
  532.4 1.3 copy-done.11
  533.7 5.7 %finish.1 = (f32[64,5632]{1,0:T(8,128)}, f32[64,5632]{1,0:T(8,128)}, f32[64,5632]{1,0:T(8,128)}, f32[64,1]{1,0:T(8,128)S(1)}, f32[64,2048]{1,0:T(8,128)}, /*inde...) custom-call(bf16[8,64,1152]{2,1,0:T(8,128)(2,1)S(1)} %copy-done.11, ...), custom_call_target="tpu_custom_call" | custom-call | flops 1441792 | bytes 5767168 | tf_op jit(solution)/shard_map/finish/pallas_call | solution.py:1505
  539.4 0.6 reduce
  540.1 0.6 reduce.1
  (99 shorter events, 0.9 us)
Async XLA Ops:
  7.2 105.1 %all-gather.4.cloned.1.call-start = ((), (), s32[]{:S(2)}) async-start(), calls=%async_computation.3 | async-start | bytes 3932160 | tf_op jit(solution)/shard_map/all_gather | solution.py:1571
  10.4 14.8 %copy-start.3 = (bf16[64,5632]{1,0:T(8,128)(2,1)S(1)}, bf16[64,5632]{1,0:T(8,128)(2,1)}, u32[]{:S(2)}) copy-start(bf16[64,5632]{1,0:T(8,128)(2,1)} %gate_weight.1) | copy-start | bytes 2162692
  10.4 14.8 %copy-start.4 = (bf16[64,5632]{1,0:T(8,128)(2,1)S(1)}, bf16[64,5632]{1,0:T(8,128)(2,1)}, u32[]{:S(2)}) copy-start(bf16[64,5632]{1,0:T(8,128)(2,1)} %up_weight.1) | copy-start | bytes 2162692
  10.4 14.8 %copy-start.37 = (f32[64]{0:T(128)S(1)}, f32[64]{0:T(128)}, u32[]{:S(2)}) copy-start(f32[64]{0:T(128)} %param.21) | copy-start | bytes 772
  25.2 180.4 %all-gather.6.cloned.1.call-start = ((), (), s32[]{:S(2)}) async-start(), calls=%async_computation.4 | async-start | bytes 5898240 | tf_op jit(solution)/shard_map/all_gather | solution.py:1595
  31.9 1.1 copy-start.35
  32.1 0.9 copy-start.34
  50.9 1.4 copy-start.27
  50.9 220.9 %all-gather.8.cloned.1.call-start = ((), (), s32[]{:S(2)}) async-start(), calls=%async_computation.5 | async-start | bytes 5242880 | tf_op jit(solution)/shard_map/all_gather | solution.py:1596
  55.0 53.3 %copy-start.39 = (s32[1,2]{1,0:T(1,128)S(1)}, s32[1,2]{1,0:T(1,128)}, u32[]{:S(2)}) copy-start(s32[1,2]{1,0:T(1,128)} %param.14) | copy-start | bytes 28
  108.3 278.1 %reduce-scatter.4.cloned.1.call-start = ((), (), s32[]{:S(2)}) async-start(), calls=%async_computation.6 | async-start | bytes 5898240 | tf_op jit(solution)/shard_map/reduce_scatter | solution.py:1620
  108.4 3.8 collective-permute-start
  109.6 2.3 copy-start.38
  109.6 2.3 copy-start.31
  111.9 45.5 %copy-start.6 = (f32[1024,128]{1,0:T(8,128)}, f32[1024,128]{1,0:T(8,128)S(1)}, u32[]{:S(2)}) copy-start(f32[1024,128]{1,0:T(8,128)S(1)} %get-tuple-element.96.cos_ref) | copy-start | bytes 1572868
  111.9 45.5 %copy-start.8 = (f32[1024,128]{1,0:T(8,128)}, f32[1024,128]{1,0:T(8,128)S(1)}, u32[]{:S(2)}) copy-start(f32[1024,128]{1,0:T(8,128)S(1)} %get-tuple-element.97.sin_ref) | copy-start | bytes 1572868
  112.3 1.9 copy-start
  157.4 1.3 copy-start.15
  158.8 1.0 copy-start.17
  159.7 41.2 %copy-start.28 = (bf16[1,256,2048]{2,1,0:T(8,128)(2,1)S(1)}, bf16[1,256,2048]{2,1,0:T(8,128)(2,1)}, u32[]{:S(2)}) copy-start(bf16[1,256,2048]{2,1,0:T(8,128)(2,1)} %param.13) | copy-start | bytes 3145732
  203.1 1.4 copy-start.24
  271.7 180.0 %reduce-scatter.6.cloned.1.call-start = ((), (), s32[]{:S(2)}) async-start(), calls=%async_computation.7 | async-start | bytes 5242880 | tf_op jit(solution)/shard_map/reduce_scatter | solution.py:1624
  333.9 1.9 copy-start.25
  333.9 184.5 %reduce-scatter.8.cloned.1.call-start = ((), (), s32[]{:S(2)}) async-start(), calls=%async_computation.8 | async-start | bytes 3932160 | tf_op jit(solution)/shard_map/reduce_scatter | solution.py:1650
  335.8 2.2 copy-start.30
  335.8 2.5 copy-start.32
  338.3 1.2 copy-start.18
  339.5 46.9 %copy-start.7 = (f32[1024,128]{1,0:T(8,128)S(1)}, f32[1024,128]{1,0:T(8,128)}, u32[]{:S(2)}) copy-start(f32[1024,128]{1,0:T(8,128)} %copy-done.6) | copy-start | bytes 1572868
  339.5 46.9 %copy-start.9 = (f32[1024,128]{1,0:T(8,128)S(1)}, f32[1024,128]{1,0:T(8,128)}, u32[]{:S(2)}) copy-start(f32[1024,128]{1,0:T(8,128)} %copy-done.8) | copy-start | bytes 1572868
  384.5 1.0 copy-start.20
  385.5 1.0 copy-start.22
  386.4 1.2 copy-start.21
  387.7 43.6 %copy-start.16 = (bf16[512,1152]{1,0:T(8,128)(2,1)S(1)}, bf16[512,1152]{1,0:T(8,128)(2,1)}, u32[]{:S(2)}) copy-start(bf16[512,1152]{1,0:T(8,128)(2,1)} %reduce-scatter.4.cloned.1.call-done) | copy-start | bytes 3538948
  387.7 43.6 %copy-start.23 = (bf16[2048,256]{1,0:T(8,128)(2,1)S(1)}, bf16[2048,256]{1,0:T(8,128)(2,1)}, u32[]{:S(2)}) copy-start(bf16[2048,256]{1,0:T(8,128)(2,1)} %copy-done.22) | copy-start | bytes 3145732
  431.2 1.6 copy-start.19
  450.0 1.0 copy-start.10
  451.0 0.7 copy-start.36
  493.1 16.9 %copy-start.29 = (bf16[1,256,2048]{2,1,0:T(8,128)(2,1)S(1)}, bf16[1,256,2048]{2,1,0:T(8,128)(2,1)}, u32[]{:S(2)}) copy-start(bf16[1,256,2048]{2,1,0:T(8,128)(2,1)} %param.13) | copy-start | bytes 3145732
  510.0 2.3 copy-start.26
  510.0 2.5 copy-start.33
  512.6 18.7 %copy-start.5 = (bf16[64,5632]{1,0:T(8,128)(2,1)S(1)}, bf16[64,5632]{1,0:T(8,128)(2,1)}, u32[]{:S(2)}) copy-start(bf16[64,5632]{1,0:T(8,128)(2,1)} %up_weight.1) | copy-start | bytes 2162692
  512.6 18.7 %copy-start.12 = (bf16[64,2048]{1,0:T(8,128)(2,1)S(1)}, bf16[64,2048]{1,0:T(8,128)(2,1)}, u32[]{:S(2)}) copy-start(bf16[64,2048]{1,0:T(8,128)(2,1)} %query_weight.1) | copy-start | bytes 786436
  512.6 18.7 %copy-start.13 = (bf16[64,512]{1,0:T(8,128)(2,1)S(1)}, bf16[64,512]{1,0:T(8,128)(2,1)}, u32[]{:S(2)}) copy-start(bf16[64,512]{1,0:T(8,128)(2,1)} %key_weight.1) | copy-start | bytes 196612
  512.6 18.7 %copy-start.14 = (bf16[64,512]{1,0:T(8,128)(2,1)S(1)}, bf16[64,512]{1,0:T(8,128)(2,1)}, u32[]{:S(2)}) copy-start(bf16[64,512]{1,0:T(8,128)(2,1)} %value_weight.1) | copy-start | bytes 196612
  518.3 13.0 %copy-start.1 = (bf16[8,64,960]{2,1,0:T(8,128)(2,1)S(1)}, bf16[8,64,960]{2,1,0:T(8,128)(2,1)}, u32[]{:S(2)}) copy-start(bf16[8,64,960]{2,1,0:T(8,128)(2,1)} %exchange_all_plane.2.second_in) | copy-start | bytes 2949124
  531.3 1.1 copy-start.2
  532.4 1.3 copy-start.11
Sparse Core Ops, SparseCore 0:
  25.3 63.8 all-gather.3
  90.7 88.1 all-gather.5
  180.5 79.0 all-gather.7
  271.8 85.1 reduce-scatter.3
  359.1 77.0 reduce-scatter.5
  451.1 59.7 reduce-scatter.7

commit v15 on v14

--- a/solution.py
+++ b/solution.py
@@ -1,5 +1,6 @@
 import jax
 import jax.numpy as jnp
+import numpy as np
 from jax import lax
 from jax.experimental import pallas as pl
 from jax.experimental.pallas import tpu as pltpu
@@ -17,11 +18,12 @@
 F32 = jnp.float32
 
 
-def rotary_tables(positions, head_dim):
-    half_dim = head_dim // 2
-    inverse = 10000.0 ** (-(jnp.arange(half_dim, dtype=F32) * 2.0 / head_dim))
-    angles = positions.astype(F32)[:, None] * inverse[None, :]
-    return (jnp.cos(angles), jnp.sin(angles))
+def rotary_tables(total, head_dim):
+    half = np.arange(head_dim // 2, dtype=np.float32)
+    inverse = np.float32(10000.0) ** (half * np.float32(-2.0 / head_dim))
+    angles = np.arange(total, dtype=np.float32)[:, None] * inverse[None, :]
+    cos, sin = np.cos(angles), np.sin(angles)
+    return np.concatenate([cos, cos], axis=1), np.concatenate([-sin, sin], axis=1)
 
 
 def rms_scale(rows):
@@ -1602,10 +1604,7 @@
         jnp.concatenate([pic_starts, other_starts], axis=0),
         jnp.concatenate([other_starts, pic_starts], axis=0),
     )
-    positions = jnp.arange(total_len, dtype=jnp.int32)
-    cos_table, sin_table = rotary_tables(positions, DH)
-    cos = jnp.concatenate([cos_table, cos_table], axis=1)
-    sin = jnp.concatenate([-sin_table, sin_table], axis=1)
+    cos, sin = rotary_tables(total_len, DH)
     qkv, mixed, log_total, branch_partial, ffn_grad = attn_front_plane(
         starts, norm1_all, attn_weight, cos, sin, (keep * upstream).astype(BF), 3
     )

time: 555 us -> 558 us (level)
    unnamed x80 -> x78, local copies, waits for them, and re-layouts: 16.9 us -> 16.9 us
  transfers between devices with their start and end apart: 7 -> 7, of which waited for: 0 -> 1; matrix products, arithmetic and copies ran while one was open for 6% -> 5% of each run, Pallas kernels for 81% -> 82%
where the time goes in v15:
time: 558 us; the launch traced here: 547 us
  Pallas kernels  479 us (86%)
  local copies, waits for them, and re-layouts  26.1 us (5%)
  other arithmetic  25 us (4%)
  between operations  15.2 us (3%)
    pallas_call x2, Pallas kernels, scatter_plane(): pl.pallas_call(scatter_kernel, out_shape=jax.ShapeDtypeStruct((rows, widt...  82.6 us
    pallas_call x1, Pallas kernels, ffn_first_plane(): pl.pallas_call(ffn_first_kernel, out_shape=(shape((plane, rows, width), B...  66.1 us
    pallas_call x1, Pallas kernels, ffn_second_plane(): pl.pallas_call(ffn_second_kernel, out_shape=(shape((plane, rows, width),...  62 us
    pallas_call x1, Pallas kernels, spread_plane(): pl.pallas_call(spread_kernel, out_shape=(jax.ShapeDtypeStruct((plane, row...  53.2 us
    pallas_call x1, Pallas kernels, gather_mix_plane(): pl.pallas_call(gather_mix_kernel, out_shape=(shape((plane, rows, width),...  44.9 us
    pallas_call x1, Pallas kernels, attn_back_plane(): pl.pallas_call(attn_back_kernel, out_shape=(jax.ShapeDtypeStruct((tokens,...  43.6 us
    pallas_call x1, Pallas kernels, attn_front_plane(): pl.pallas_call(attn_front_kernel, out_shape=(shape((tokens, q_part + 2 *...  43.3 us
    pallas_call x2, Pallas kernels, exchange_plane(): pl.pallas_call(exchange_kernel, out_shape=jax.ShapeDtypeStruct(blocks.sha...  30.4 us
  transfers between devices with their start and end apart: 7, of which 1 were waited for; matrix products, arithmetic and copies ran while one was open for 5% of the time, Pallas kernels for 82%

profile of v15, /device:TPU:1, one launch (start us, length us, event | category | flops | bytes accessed | tf_op | source)
XLA Modules:
  0.0 547.4 jit_solution(12307212445683513305)
XLA Ops:
  7.2 1.1 multiply_convert_fusion.4
  8.3 1.0 multiply_convert_fusion.6
  9.4 1.0 bitcast_bitcast_fusion
  10.5 1.0 pad_maximum_fusion.2.in_ref
  11.4 13.7 %exchange_plane.2 = bf16[8,64,768]{2,1,0:T(8,128)(2,1)} custom-call(bf16[8,64,768]{2,1,0:T(8,128)(2,1)} %pad_maximum_fusion.2.in_ref), custom_call_target="tpu_custom_call" | custom-call | bytes 15728640 | tf_op jit(solution)/shard_map/exchange_plane/pallas_call | solution.py:753
  25.2 0.3 multiply_convert_fusion.3
  25.5 0.7 reshape.110
  26.2 0.1 copy.48
  26.4 0.8 slice.28
  27.1 0.7 reshape.111
  27.8 0.1 copy.47
  28.0 0.8 slice.29
  28.7 1.8 reshape.112
  30.6 0.1 copy.46
  30.8 0.9 copy-done.33
  31.7 2.2 pad_maximum_fusion.in_ref
  33.9 16.7 %exchange_plane.3 = bf16[8,64,1152]{2,1,0:T(8,128)(2,1)} custom-call(bf16[8,64,1152]{2,1,0:T(8,128)(2,1)} %pad_maximum_fusion.in_ref), custom_call_target="tpu_custom_call" | custom-call | bytes 23592960 | tf_op jit(solution)/shard_map/exchange_plane/pallas_call | solution.py:753
  50.8 1.1 slice.33
  51.9 0.3 fusion.8
  52.2 1.2 fusion.2.own_ref
  53.4 1.3 pad_maximum_fusion.1.move_ref
  54.7 53.2 %spread_plane.1 = (bf16[8,256,2048]{2,1,0:T(8,128)(2,1)}, bf16[8,64,960]{2,1,0:T(8,128)(2,1)}) custom-call(bf16[256,2048]{1,0:T(8,128)(2,1)} %fusion.2.own_ref, bf16[8,64,960]{2,1,0:T(8,128)(2,1)} %pad_maximum_fusion.1.move_ref), custom_call_target="tpu_custom_call" | custom-call | bytes 134217728 | tf_op jit(solution)/shard_map/spread_plane/pallas_call | solution.py:293
  108.0 0.2 reduce-scatter.4.cloned.1.call-start
  108.3 1.2 collective-permute-start
  109.5 1.5 fusion.3.own_ref
  111.0 0.2 collective-permute-done
  111.2 1.9 copy-done
  113.1 43.3 %attn_front_plane.1 = (bf16[2048,512]{1,0:T(8,128)(2,1)S(1)}, bf16[2048,256]{1,0:T(8,128)(2,1)S(1)}, f32[4,1,1024]{2,1,0:T(1,128)S(1)}, bf16[2048,2048]{1,0:T(8,128)(2,1)}, bf16[8,256,2048]{2,1,0:T(8,128)(2,1)}) custom-call(s32[2,2]{1,0:T(2,128)S(1)} %add_select_fusion.starts_ref, bf16[2048,2048]{1,0:T(8,128)(2,1)} %bitcast.60, ...), custom_call_target="tpu_custom_call" | custom-call | flops 2147483648 | bytes 100663296 | tf_op jit(solution)/shard_map/attn_front_plane/pallas_call | solution.py:585
  156.4 1.3 copy-done.15
  157.7 1.0 copy-done.17
  158.7 41.3 %scatter_plane.2 = f32[256,2048]{1,0:T(8,128)} custom-call(bf16[8,256,2048]{2,1,0:T(8,128)(2,1)} %bitcast.59), custom_call_target="tpu_custom_call" | custom-call | bytes 117440512 | tf_op jit(solution)/shard_map/scatter_plane/pallas_call | solution.py:426
  200.0 2.1 multiply_reduce_fusion.1
  202.1 1.3 copy-done.24
  203.5 1.1 multiply_convert_fusion.1.own_ref
  204.6 66.1 %ffn_first_plane.1 = (bf16[8,256,2048]{2,1,0:T(8,128)(2,1)}, bf16[8,256,2048]{2,1,0:T(8,128)(2,1)}, bf16[8,256,2048]{2,1,0:T(8,128)(2,1)}, bf16[2048,1152]{1,0:T(8,128)(2,1)}) custom-call(bf16[256,2048]{1,0:T(8,128)(2,1)} %multiply_convert_fusion.1.own_ref, bf16[8,256,2048]{2,1,0:T(8,128)(2,1)} %get-tuple-element.52.grad_ref, ...), custom_call_target="tpu_custom_call" | custom-call | flops 28991029248 | bytes 92274688 | tf_op jit(solution)/shard_map/ffn_first_plane/pallas_call | solution.py:1176
  270.7 0.3 reduce-scatter.6.cloned.1.call-start
  271.0 62.0 %ffn_second_plane.1 = (bf16[8,256,2048]{2,1,0:T(8,128)(2,1)}, bf16[2048,960]{1,0:T(8,128)(2,1)}, f32[256,2048]{1,0:T(8,128)}) custom-call(bf16[8,256,2048]{2,1,0:T(8,128)(2,1)} %get-tuple-element.53.all_ref, bf16[8,256,2048]{2,1,0:T(8,128)(2,1)} %get-tuple-element.52.grad_ref, bf16[2048,960]{1,0:T(8,128)(2,1)} %all-gather.8.cloned.1.call-done.weight_hbm, ...), custom_call_target="tpu_custom_call" | custom-call | flops 24159191040 | bytes 92274688 | tf_op jit(solution)/shard_map/ffn_second_plane/pallas_call | solution.py:1220
  333.0 1.4 slice.34.weight_ref
  334.5 0.4 copy-done.25
  334.9 2.1 multiply_reduce_fusion
  337.0 0.1 copy-done.30
  337.2 0.3 copy-done.31
  337.5 0.7 multiply_convert_fusion.own_ref
  338.2 0.5 copy-done.18
  338.7 44.9 %gather_mix_plane.1 = (bf16[8,256,2048]{2,1,0:T(8,128)(2,1)}, bf16[2048,256]{1,0:T(8,128)(2,1)S(1)}, bf16[2048,256]{1,0:T(8,128)(2,1)S(1)}) custom-call(bf16[256,2048]{1,0:T(8,128)(2,1)S(1)} %multiply_convert_fusion.own_ref, bf16[2048,256]{1,0:T(8,128)(2,1)S(1)} %copy-done.18, bf16[2048,256]{1,0:T(8,128)(2,1)S(1)} %slice.34.weight_ref), custom_call_target="tpu_custom_call" | custom-call | flops 4294967296 | bytes 100663296 | tf_op jit(solution)/shard_map/gather_mix_plane/pallas_call | solution.py:228
  383.6 1.0 copy-done.20
  384.6 1.0 copy-done.22
  385.5 1.2 copy-done.21
  386.8 43.6 %attn_back_plane.1 = (bf16[2048,512]{1,0:T(8,128)(2,1)}, f32[256,2048]{1,0:T(8,128)}) custom-call(s32[2,2]{1,0:T(2,128)S(1)} %add_select_fusion.starts_ref, bf16[2048,512]{1,0:T(8,128)(2,1)} %copy-done.15, bf16[2048,256]{1,0:T(8,128)(2,1)S(1)} %copy-done.21, f32[4,1,1024]{2,1,0:T(1,128)S(1)} %get-tuple-element.62.log_ref, f32[1024,128]{1,0:T(8,128)S(1)} %copy-done.10, ...), custom_call_target="tpu_custom_call" | custom-call | flops 5368709120 | bytes 117440512 | tf_op jit(solution)/shard_map/attn_back_plane/pallas_call | solution.py:700
  430.4 1.6 copy-done.19
  432.0 17.4 %attn_grads_plane.1 = (bf16[2048,768]{1,0:T(8,128)(2,1)}, bf16[2048,2048]{1,0:T(8,128)(2,1)}, bf16[8,64,1152]{2,1,0:T(8,128)(2,1)S(1)}) custom-call(bf16[2048,2048]{1,0:T(8,128)(2,1)} %bitcast.61, bf16[2048,512]{1,0:T(8,128)(2,1)S(1)} %copy-done.19, bf16[2048,256]{1,0:T(8,128)(2,1)S(1)} %copy-done.23, ...), custom_call_target="tpu_custom_call" | custom-call | flops 8589934592 | bytes 50331648 | tf_op jit(solution)/shard_map/attn_grads_plane/pallas_call | solution.py:1411
  449.4 1.0 copy-done.6
  450.5 0.5 copy-done.35
  451.1 41.2 %scatter_plane.3 = f32[256,2048]{1,0:T(8,128)} custom-call(bf16[8,256,2048]{2,1,0:T(8,128)(2,1)} %bitcast.58), custom_call_target="tpu_custom_call" | custom-call | bytes 117440512 | tf_op jit(solution)/shard_map/scatter_plane/pallas_call | solution.py:426
  492.4 17.0 %exchange_all_plane.2.second_in = bf16[8,64,960]{2,1,0:T(8,128)(2,1)} custom-call(bf16[8,64,960]{2,1,0:T(8,128)(2,1)} %bitcast.73), custom_call_target="tpu_custom_call" | custom-call | bytes 19660800 | tf_op jit(solution)/shard_map/exchange_all_plane/pallas_call | solution.py:1289
  509.5 2.2 fusion.4
  511.7 0.3 copy-done.32
  512.0 5.8 %fusion.7 = (f32[256,2048]{1,0:T(8,128)}, bf16[256,2048]{1,0:T(8,128)(2,1)}) fusion(f32[256,2048]{1,0:T(8,128)} %scatter_plane.3, bf16[1,256,2048]{2,1,0:T(8,128)(2,1)S(1)} %copy-done.29, f32[256]{0:T(256)S(1)} %broadcast_multiply_fusion, f32[256]{0:T(256)S(1)} %add_rsqrt_fusion.1, f32[256,2048]{1,0:T(8,128)} %get-tuple-element.57, ...), kind=kLoop, calls=%fused_computation.12 | loop fusion | flops 7864320 | bytes 13636608 | tf_op jit(solution)/shard_map/add | solution.py:1651
  517.7 12.9 %exchange_all_plane.3.attn_in = bf16[8,64,768]{2,1,0:T(8,128)(2,1)} custom-call(bf16[8,64,768]{2,1,0:T(8,128)(2,1)} %bitcast.75), custom_call_target="tpu_custom_call" | custom-call | bytes 15728640 | tf_op jit(solution)/shard_map/exchange_all_plane/pallas_call | solution.py:1289
  530.7 1.1 copy-done.2
  531.9 1.3 copy-done.7
  533.1 5.7 %finish.1 = (f32[64,5632]{1,0:T(8,128)}, f32[64,5632]{1,0:T(8,128)}, f32[64,5632]{1,0:T(8,128)}, f32[64,1]{1,0:T(8,128)S(1)}, f32[64,2048]{1,0:T(8,128)}, /*inde...) custom-call(bf16[8,64,1152]{2,1,0:T(8,128)(2,1)S(1)} %copy-done.7, ...), custom_call_target="tpu_custom_call" | custom-call | flops 1441792 | bytes 5767168 | tf_op jit(solution)/shard_map/finish/pallas_call | solution.py:1507
  538.9 0.6 reduce
  539.5 0.6 reduce.1
  (93 shorter events, 1.0 us)
Async XLA Ops:
  7.2 104.0 %all-gather.4.cloned.1.call-start = ((), (), s32[]{:S(2)}) async-start(), calls=%async_computation.3 | async-start | bytes 3932160 | tf_op jit(solution)/shard_map/all_gather | solution.py:1573
  10.4 14.8 %copy-start.3 = (bf16[64,5632]{1,0:T(8,128)(2,1)S(1)}, bf16[64,5632]{1,0:T(8,128)(2,1)}, u32[]{:S(2)}) copy-start(bf16[64,5632]{1,0:T(8,128)(2,1)} %gate_weight.1) | copy-start | bytes 2162692
  10.4 14.8 %copy-start.4 = (bf16[64,5632]{1,0:T(8,128)(2,1)S(1)}, bf16[64,5632]{1,0:T(8,128)(2,1)}, u32[]{:S(2)}) copy-start(bf16[64,5632]{1,0:T(8,128)(2,1)} %up_weight.1) | copy-start | bytes 2162692
  10.4 14.8 %copy-start.36 = (f32[64]{0:T(128)S(1)}, f32[64]{0:T(128)}, u32[]{:S(2)}) copy-start(f32[64]{0:T(128)} %param.23) | copy-start | bytes 772
  25.2 179.5 %all-gather.6.cloned.1.call-start = ((), (), s32[]{:S(2)}) async-start(), calls=%async_computation.4 | async-start | bytes 5898240 | tf_op jit(solution)/shard_map/all_gather | solution.py:1597
  30.6 1.1 copy-start.34
  30.8 0.9 copy-start.33
  50.6 1.3 copy-start.27
  50.6 220.4 %all-gather.8.cloned.1.call-start = ((), (), s32[]{:S(2)}) async-start(), calls=%async_computation.5 | async-start | bytes 5242880 | tf_op jit(solution)/shard_map/all_gather | solution.py:1598
  54.7 53.5 %copy-start.38 = (s32[1,2]{1,0:T(1,128)S(1)}, s32[1,2]{1,0:T(1,128)}, u32[]{:S(2)}) copy-start(s32[1,2]{1,0:T(1,128)} %param.16) | copy-start | bytes 28
  54.7 54.8 %copy-start.37 = (s32[1,256]{1,0:T(1,128)S(1)}, s32[1,256]{1,0:T(1,128)}, u32[]{:S(2)}) copy-start(s32[1,256]{1,0:T(1,128)} %param.17) | copy-start | bytes 3076
  108.0 3.2 copy-start.9
  108.0 3.2 copy-start.11
  108.0 277.5 %reduce-scatter.4.cloned.1.call-start = ((), (), s32[]{:S(2)}) async-start(), calls=%async_computation.6 | async-start | bytes 5898240 | tf_op jit(solution)/shard_map/reduce_scatter | solution.py:1619
  108.3 2.9 collective-permute-start
  111.2 1.9 copy-start
  156.4 1.3 copy-start.15
  157.7 1.0 copy-start.17
  158.7 41.3 %copy-start.28 = (bf16[1,256,2048]{2,1,0:T(8,128)(2,1)S(1)}, bf16[1,256,2048]{2,1,0:T(8,128)(2,1)}, u32[]{:S(2)}) copy-start(bf16[1,256,2048]{2,1,0:T(8,128)(2,1)} %param.15) | copy-start | bytes 3145732
  202.1 1.4 copy-start.24
  270.7 180.4 %reduce-scatter.6.cloned.1.call-start = ((), (), s32[]{:S(2)}) async-start(), calls=%async_computation.7 | async-start | bytes 5242880 | tf_op jit(solution)/shard_map/reduce_scatter | solution.py:1623
  333.0 1.9 copy-start.25
  333.0 184.7 %reduce-scatter.8.cloned.1.call-start = ((), (), s32[]{:S(2)}) async-start(), calls=%async_computation.8 | async-start | bytes 3932160 | tf_op jit(solution)/shard_map/reduce_scatter | solution.py:1649
  334.9 2.2 copy-start.30
  334.9 2.5 copy-start.31
  337.5 1.2 copy-start.18
  338.7 46.8 %copy-start.10 = (f32[1024,128]{1,0:T(8,128)S(1)}, f32[1024,128]{1,0:T(8,128)}, u32[]{:S(2)}) copy-start(f32[1024,128]{1,0:T(8,128)} %constant.24.clone.cos_ref) | copy-start | bytes 1572868
  338.7 46.8 %copy-start.12 = (f32[1024,128]{1,0:T(8,128)S(1)}, f32[1024,128]{1,0:T(8,128)}, u32[]{:S(2)}) copy-start(f32[1024,128]{1,0:T(8,128)} %constant.25.clone.sin_ref) | copy-start | bytes 1572868
  383.6 1.0 copy-start.20
  384.6 1.0 copy-start.22
  385.5 1.2 copy-start.21
  386.8 43.6 %copy-start.16 = (bf16[512,1152]{1,0:T(8,128)(2,1)S(1)}, bf16[512,1152]{1,0:T(8,128)(2,1)}, u32[]{:S(2)}) copy-start(bf16[512,1152]{1,0:T(8,128)(2,1)} %reduce-scatter.4.cloned.1.call-done) | copy-start | bytes 3538948
  386.8 43.6 %copy-start.23 = (bf16[2048,256]{1,0:T(8,128)(2,1)S(1)}, bf16[2048,256]{1,0:T(8,128)(2,1)}, u32[]{:S(2)}) copy-start(bf16[2048,256]{1,0:T(8,128)(2,1)} %copy-done.22) | copy-start | bytes 3145732
  430.4 1.6 copy-start.19
  449.4 1.0 copy-start.6
  450.4 0.7 copy-start.35
  492.4 17.0 %copy-start.29 = (bf16[1,256,2048]{2,1,0:T(8,128)(2,1)S(1)}, bf16[1,256,2048]{2,1,0:T(8,128)(2,1)}, u32[]{:S(2)}) copy-start(bf16[1,256,2048]{2,1,0:T(8,128)(2,1)} %param.15) | copy-start | bytes 3145732
  509.4 2.3 copy-start.26
  509.4 2.5 copy-start.32
  512.0 18.7 %copy-start.5 = (bf16[64,5632]{1,0:T(8,128)(2,1)S(1)}, bf16[64,5632]{1,0:T(8,128)(2,1)}, u32[]{:S(2)}) copy-start(bf16[64,5632]{1,0:T(8,128)(2,1)} %up_weight.1) | copy-start | bytes 2162692
  512.0 18.7 %copy-start.8 = (bf16[64,2048]{1,0:T(8,128)(2,1)S(1)}, bf16[64,2048]{1,0:T(8,128)(2,1)}, u32[]{:S(2)}) copy-start(bf16[64,2048]{1,0:T(8,128)(2,1)} %query_weight.1) | copy-start | bytes 786436
  512.0 18.7 %copy-start.13 = (bf16[64,512]{1,0:T(8,128)(2,1)S(1)}, bf16[64,512]{1,0:T(8,128)(2,1)}, u32[]{:S(2)}) copy-start(bf16[64,512]{1,0:T(8,128)(2,1)} %key_weight.1) | copy-start | bytes 196612
  512.0 18.7 %copy-start.14 = (bf16[64,512]{1,0:T(8,128)(2,1)S(1)}, bf16[64,512]{1,0:T(8,128)(2,1)}, u32[]{:S(2)}) copy-start(bf16[64,512]{1,0:T(8,128)(2,1)} %value_weight.1) | copy-start | bytes 196612
  517.7 13.0 %copy-start.1 = (bf16[8,64,960]{2,1,0:T(8,128)(2,1)S(1)}, bf16[8,64,960]{2,1,0:T(8,128)(2,1)}, u32[]{:S(2)}) copy-start(bf16[8,64,960]{2,1,0:T(8,128)(2,1)} %exchange_all_plane.2.second_in) | copy-start | bytes 2949124
  530.7 1.1 copy-start.2
  531.9 1.3 copy-start.7
Sparse Core Ops, SparseCore 0:
  25.3 63.8 all-gather.3
  90.7 88.1 all-gather.5
  180.5 79.0 all-gather.7
  270.8 85.1 reduce-scatter.3
  358.1 77.0 reduce-scatter.5
  450.5 59.6 reduce-scatter.7
